TPU v7x, 128 devices: a whole 4x4x4 slice. The times are simulated.
128 devices in a mesh: patch: 8 (over x, core), proto: 16 (over z, y).
Axes of the slice: x: 4, y: 4, z: 4, core: 2. Of those that a mesh axis runs over, the one named last changes fastest.
Arguments:
- student_feats: bfloat16 [32768, 256], P(('patch', 'proto')), may hold values from -50 to 50
- teacher_feats: bfloat16 [32768, 256], P(('patch', 'proto')), may hold values from -50 to 50
- proto_weight: bfloat16 [256, 131072], P(None, 'proto'), may hold values from -4 to 4
- mask_index: int32 [4096], P(('patch', 'proto')), may hold values from 0 to 255, as said below
- row_weight: bfloat16 [4096], P(('patch', 'proto')), may hold values from 0.5 to 4
Outputs:
- grad_student: float32 [4096, 256], P(('patch', 'proto'))
- grad_proto: float32 [256, 131072], P('patch', 'proto')
- loss: float32 [], replicated
Inputs may be any that keep to these rules, and one draw needn't show every extreme that they name: `mask_index`: entries k * 32 to (k + 1) * 32 - 1 are distinct patch positions of image k, counted from that image's first patch.
All inputs are finite; a program needn't handle non-finite values.
Results may differ from a plain program's by a relative error of at most 0.0057.
Values may be sent and summed in bfloat16 or wider, within the bound.
No kernel may reach another device: no remote copies, remote signals or barrier semaphores. Data moves between devices by JAX's collectives and lax.ppermute only.
A program may use at most 128 MiB of HBM per device.

v0:
```python
import functools

import jax
import jax.numpy as jnp
from jax import lax
from jax.experimental import pallas as pl
from jax.experimental.pallas import tpu as pltpu
from jax.sharding import PartitionSpec as P

SK_ITERS = 3
EPS = 1e-06
TEACHER_TEMP = 0.07
STUDENT_TEMP = 0.1
F32 = jnp.float32
BF16 = jnp.bfloat16
LANES = 128
PIECES = (3, 3, 2)
VMEM_LIMIT = 20 * 1024 * 1024

NN = (((1,), (0,)), ((), ()))
NT = (((1,), (1,)), ((), ()))
TN = (((0,), (0,)), ((), ()))
SMEM = pl.BlockSpec(memory_space=pltpu.SMEM)
VMEM = pl.BlockSpec(memory_space=pltpu.VMEM)
ANY = pl.BlockSpec(memory_space=pl.ANY)
HBM = pl.BlockSpec(memory_space=pltpu.HBM)


def mm(a, b, dims=NN):
    return lax.dot_general(a, b, dims, preferred_element_type=F32)


def shape(dims, dtype):
    return jax.ShapeDtypeStruct(dims, dtype)


def call(body, name, out_shape, args, flops, specs=None, after=(), scratch=(), limit=VMEM_LIMIT):
    specs = specs or [VMEM] * len(args)
    skip = len(after)
    args = [
        pltpu.with_memory_space_constraint(arg, pltpu.HBM) if spec is HBM else arg
        for arg, spec in zip(args, specs)
    ]

    def ordered(*refs):
        body(*refs[skip:])

    def out_spec(out):
        return VMEM if isinstance(out, jax.ShapeDtypeStruct) else HBM

    many = isinstance(out_shape, tuple)
    return pl.pallas_call(
        ordered,
        name=name,
        out_shape=out_shape,
        in_specs=[ANY] * skip + specs,
        out_specs=tuple(map(out_spec, out_shape)) if many else out_spec(out_shape),
        scratch_shapes=list(scratch),
        compiler_params=pltpu.CompilerParams(vmem_limit_bytes=limit),
        cost_estimate=pl.CostEstimate(flops=flops, bytes_accessed=1 << 16, transcendentals=0),
    )(*after, *args)


def three_terms(row):
    high = row.astype(BF16).astype(F32)
    rest = row - high
    mid = rest.astype(BF16).astype(F32)
    low = rest - mid
    index = lax.broadcasted_iota(jnp.int32, (16, row.shape[1]), 0)
    terms = jnp.where(
        index == 0, high, jnp.where(index == 1, mid, jnp.where(index == 2, low, 0.0))
    )
    return terms.astype(BF16)


def column_sum(refs):
    total = refs[0][...]
    for ref in refs[1:]:
        total = total + ref[...]
    return total


def chunks(table_ref, count=8):
    width = table_ref.shape[1] // count
    return [(j, pl.ds(j * width, width)) for j in range(count)]


def move(source, start, target, sems, count):
    width = target.shape[1] // count
    copies = [
        pltpu.make_async_copy(
            source.at[:, pl.ds(start + j * width, width)],
            target.at[:, pl.ds(j * width, width)],
            sems.at[j],
        )
        for j in range(count)
    ]
    for copy in copies:
        copy.start()
    return copies


def store(source, target, cols, sem):
    copy = pltpu.make_async_copy(source.at[:, cols], target.at[:, cols], sem)
    copy.start()
    return copy


def read_rows(message_ref, start, n):
    total = jnp.sum(message_ref[...], axis=0)
    pieces = [total[start + k : start + k + 1, :] for k in range(n // LANES)]
    return jnp.concatenate(pieces, axis=1)


def write_rows(message_ref, start, row):
    count = message_ref.shape[0]
    for k in range(row.shape[1] // LANES):
        piece = row[:, k * LANES : (k + 1) * LANES]
        message_ref[:, start + k, :] = jnp.broadcast_to(piece, (count, LANES))


def rows_body(
    place_ref,
    student_hbm,
    teacher_hbm,
    index_hbm,
    weight_hbm,
    rows_ref,
    x_ref,
    w_ref,
    student_ref,
    teacher_ref,
    index_ref,
    weight_ref,
    sems,
):
    copies = [
        pltpu.make_async_copy(index_hbm, index_ref, sems.at[0]),
        pltpu.make_async_copy(teacher_hbm, teacher_ref, sems.at[1]),
        pltpu.make_async_copy(student_hbm, student_ref, sems.at[2]),
        pltpu.make_async_copy(weight_hbm, weight_ref, sems.at[3]),
    ]
    for copy in copies:
        copy.start()
    for copy in copies:
        copy.wait()
    picks = index_ref[...]
    length = student_ref.shape[0]
    count = picks.shape[1]
    one_hot = (lax.broadcasted_iota(jnp.int32, (length, count), 0) == picks).astype(BF16)
    x = mm(one_hot, student_ref[...], TN)
    y = mm(one_hot, teacher_ref[...], TN)
    x_ref[...] = x
    unit_x = x * lax.rsqrt(jnp.sum(x * x, axis=1, keepdims=True) + EPS)
    unit_y = y * lax.rsqrt(jnp.sum(y * y, axis=1, keepdims=True) + EPS)
    both = jnp.concatenate([unit_y.astype(BF16), unit_x.astype(BF16)], axis=0)
    rows_ref[...] = jnp.broadcast_to(both[None], rows_ref.shape)
    lanes = w_ref.shape[1]
    spot = lax.broadcasted_iota(jnp.int32, (count, lanes), 1) - place_ref[0] * count
    spread = (spot == lax.broadcasted_iota(jnp.int32, (count, lanes), 0)).astype(BF16)
    w_ref[...] = jnp.broadcast_to(mm(weight_ref[...], spread), w_ref.shape)


def proto_body(w_hbm, unit_hbm, inverse_ref, w_ref, unit_ref, in_sems, out_sems):
    copies = move(w_hbm, 0, w_ref, in_sems, 8)
    stores = []
    for j, cols in chunks(w_ref):
        copies[j].wait()
        w = w_ref[:, cols].astype(F32)
        inverse = lax.rsqrt(jnp.sum(w * w, axis=0, keepdims=True) + EPS)
        inverse_ref[pl.ds(j, 1), :] = inverse
        unit_ref[:, cols] = (w * inverse).astype(BF16)
        stores.append(store(unit_ref, unit_hbm, cols, out_sems.at[j]))
    for copy in stores:
        copy.wait()


def table_body(rows_ref, unit_hbm, table_ref, sums_ref, unit_ref, sems):
    copies = move(unit_hbm, 0, unit_ref, sems, 8)
    half = rows_ref.shape[1] // 2
    teacher = rows_ref[:, :half, :].reshape(-1, rows_ref.shape[2])
    for j, cols in chunks(table_ref):
        copies[j].wait()
        table = jnp.exp(mm(teacher, unit_ref[:, cols]) * (1.0 / TEACHER_TEMP)).astype(BF16)
        table_ref[:, cols] = table
        sums_ref[pl.ds(j, 1), :] = jnp.sum(table.astype(F32), axis=0, keepdims=True)


def row_pass_body(parts, *refs):
    sums_refs, table_ref, extra_refs, out_ref = refs[:parts], refs[parts], refs[parts + 1 : -1], refs[-1]
    scale = 1.0 / column_sum(sums_refs)
    n = table_ref.shape[0]
    total = jnp.zeros((16, n), F32)
    for j, cols in chunks(table_ref):
        total += mm(three_terms(scale[j : j + 1, :]), table_ref[:, cols], NT)
    write_rows(out_ref, 0, jnp.sum(total, axis=0, keepdims=True))
    write_rows(out_ref, n // LANES, column_sum(extra_refs)[0:1, :])


def col_pass_body(message_ref, table_ref, out_ref):
    terms = three_terms(1.0 / read_rows(message_ref, 0, table_ref.shape[0]))
    for j, cols in chunks(table_ref):
        out_ref[pl.ds(j, 1), :] = jnp.sum(mm(terms, table_ref[:, cols]), axis=0, keepdims=True)


def student_body(first, rows_ref, unit_hbm, table_ref, sums_ref, feature_ref, *refs):
    unit_ref, sems = refs[-2:]
    count = PIECES[first]
    width = table_ref.shape[1] // count
    copies = move(unit_hbm, sum(PIECES[:first]) * width, unit_ref, sems, count)
    half = rows_ref.shape[1] // 2
    student = rows_ref[:, half:, :].reshape(-1, rows_ref.shape[2])
    total = jnp.zeros((16, student.shape[0]), F32)
    for j, cols in chunks(table_ref, count):
        copies[j].wait()
        unit = unit_ref[:, cols]
        table = jnp.exp(mm(student, unit) * (1.0 / STUDENT_TEMP)).astype(BF16)
        table_ref[:, cols] = table
        total += mm(jnp.ones((16, table.shape[1]), BF16), table, NT)
        part = mm(unit, table, NT)
        if j == 0:
            feature_ref[...] = part
        else:
            feature_ref[...] += part
    sums_ref[...] = total[0:8]
    if len(refs) > 2:
        d = student.shape[1]
        eye = (
            lax.broadcasted_iota(jnp.int32, (d, d), 0)
            == lax.broadcasted_iota(jnp.int32, (d, d), 1)
        ).astype(BF16)
        refs[0][...] = mm(eye, student, NT).astype(BF16)


def codes_feature_body(*refs):
    *sums_refs, table_ref, unit_hbm, feature_ref, unit_ref, sems = refs
    copies = move(unit_hbm, 0, unit_ref, sems, 8)
    scale = 1.0 / column_sum(sums_refs)
    for j, cols in chunks(table_ref):
        copies[j].wait()
        scaled = (unit_ref[:, cols].astype(F32) * scale[j : j + 1, :]).astype(BF16)
        part = mm(scaled, table_ref[:, cols], NT)
        if j == 0:
            feature_ref[...] = part
        else:
            feature_ref[...] += part


def row_factors(first_ref, last_ref, n):
    tile = n // LANES
    return read_rows(first_ref, tile, n), read_rows(last_ref, tile, n), read_rows(last_ref, 0, n)


def head_body(parts, *refs):
    place_ref, first_ref, last_ref = refs[:3]
    sums_refs = refs[3 : 3 + parts]
    turned_ref, inverse_ref, codes_ref, *piece_refs, w_hbm = refs[3 + parts : -6]
    own_ref, keep_ref, near_ref, turn_ref, w_ref, sems = refs[-6:]
    x, core = place_ref[1], place_ref[2]
    chips = near_ref.shape[0]
    share = near_ref.shape[1]
    protos = codes_ref.shape[1]
    count = 8
    width = protos // count
    spots = []
    for k in range(chips):
        spots += [2 * (x ^ k) + core, 2 * (x ^ k) + 1 - core]
    copies = []
    for j in range(count):
        copies.append([])
        for m, spot in enumerate(spots):
            copy = pltpu.make_async_copy(
                w_hbm.at[pl.ds(pl.multiple_of(spot * share, share), share), pl.ds(j * width, width)],
                w_ref.at[pl.ds(m * share, share), pl.ds(j * width, width)],
                sems.at[j, m],
            )
            copy.start()
            copies[j].append(copy)
    for m, spot in enumerate(spots):
        turn_ref[pl.ds(m * share, share), :] = turned_ref[
            pl.ds(pl.multiple_of(spot * share, share), share), :
        ]
    weights, exp_total, total = row_factors(first_ref, last_ref, codes_ref.shape[0])
    turned = turn_ref[...].astype(F32)
    left_probs = (turned * (weights / exp_total * (1.0 / STUDENT_TEMP))).astype(BF16)
    left_codes = (turned * (weights / total * (1.0 / STUDENT_TEMP))).astype(BF16)
    scale = 1.0 / column_sum(sums_refs)
    piece, at = 0, 0
    for j, cols in chunks(codes_ref, count):
        probs = piece_refs[piece][:, pl.ds(at * width, width)]
        at += 1
        if at == PIECES[piece]:
            piece, at = piece + 1, 0
        head = mm(left_probs, probs) - scale[j : j + 1, :] * mm(left_codes, codes_ref[:, cols])
        for copy in copies[j]:
            copy.wait()
        inverse = inverse_ref[pl.ds(j, 1), :]
        unit = w_ref[:, cols].astype(F32) * inverse
        inner = jnp.sum(unit * head, axis=0, keepdims=True)
        grad = inverse * (head - unit * inner)
        own_ref[:, cols] = grad[0:share]
        for k in range(chips):
            low = 2 * k * share
            if k:
                keep_ref[k - 1, :, cols] = grad[low : low + share]
            near_ref[k, :, cols] = grad[low + share : low + 2 * share].astype(BF16)


def pair_body(own_ref, keep_ref, near_ref, out_ref, *pair_refs):
    out_ref[...] = own_ref[...] + near_ref[0].astype(F32)
    for k, pair_ref in enumerate(pair_refs):
        pair_ref[...] = (keep_ref[k] + near_ref[k + 1].astype(F32)).astype(BF16)


def final_body(own_ref, *refs):
    *far_refs, out_ref = refs
    total = own_ref[...]
    for far_ref in far_refs:
        total = total + far_ref[...].astype(F32)
    out_ref[...] = total


def owner_body(sent_ref, x_ref, grad_ref, tail_ref):
    sent = jnp.sum(sent_ref[...], axis=0)
    own = x_ref.shape[0]
    x = x_ref[...]
    feature = sent[:own]
    inverse = lax.rsqrt(jnp.sum(x * x, axis=1, keepdims=True) + EPS)
    unit = x * inverse
    grad_ref[...] = inverse * (feature - unit * jnp.sum(unit * feature, axis=1, keepdims=True))
    tail_ref[...] = jnp.broadcast_to(sent[own:, :LANES][None], tail_ref.shape)


def feature_body(first_ref, last_ref, codes_ref, turned_ref, *refs):
    *probs_refs, out_ref = refs
    n = codes_ref.shape[1]
    weights, exp_total, total = row_factors(first_ref, last_ref, n)
    codes = codes_ref[...]
    probs = column_sum(probs_refs)
    over = weights / total * (1.0 / STUDENT_TEMP)
    feature = probs * (weights / exp_total * (1.0 / STUDENT_TEMP)) - codes * over
    own = n // out_ref.shape[0]
    out_ref[:, :own, :] = feature.T.reshape(out_ref.shape[0], own, out_ref.shape[2])
    share = 1.0 / out_ref.shape[0]
    cross = jnp.sum(turned_ref[...].astype(F32) * codes, axis=0, keepdims=True)
    part = jnp.sum(weights * jnp.log(exp_total) * share - over * cross)
    count = jnp.sum(weights) * share
    tail = (out_ref.shape[0], out_ref.shape[1] - own, out_ref.shape[2])
    lane = lax.broadcasted_iota(jnp.int32, tail, 2)
    out_ref[:, own:, :] = jnp.where(lane == 0, part, jnp.where(lane == 1, count, 0.0))


def on_device(student_feats, teacher_feats, proto_weight, mask_index, row_weight):
    n_patch, n_proto = lax.axis_size("patch"), lax.axis_size("proto")
    d, protos = proto_weight.shape
    length = student_feats.shape[0]
    own = mask_index.shape[0]
    rows = own * n_proto
    chips = n_patch // 2
    share = d // n_patch
    width = protos // 8
    patch, proto = lax.axis_index("patch"), lax.axis_index("proto")
    place = jnp.stack([proto, patch // 2, patch % 2]).astype(jnp.int32)
    product = 2 * rows * d * protos

    def exchange(array, axis):
        return lax.all_to_all(array, axis, 0, 0)

    def hop(array, bits):
        return lax.ppermute(array, "patch", [(i, i ^ bits) for i in range(n_patch)])

    own_rows, x_rows, own_weights = call(
        rows_body,
        "own_rows",
        (
            shape((n_proto, 2 * own, d), BF16),
            shape((own, d), F32),
            shape((8, rows), F32),
        ),
        (place, student_feats, teacher_feats, mask_index[None, :], row_weight[None, :]),
        1 << 28,
        specs=[SMEM, HBM, HBM, HBM, HBM],
        scratch=[
            pltpu.VMEM((length, d), BF16),
            pltpu.VMEM((length, d), BF16),
            pltpu.VMEM((1, own), jnp.int32),
            pltpu.VMEM((1, own), BF16),
            pltpu.SemaphoreType.DMA((4,)),
        ],
    )
    all_rows = exchange(own_rows, "proto")
    unit, inverse = call(
        proto_body,
        "proto_unit",
        (pltpu.HBM((d, protos), BF16), shape((8, width), F32)),
        (proto_weight,),
        product,
        specs=[HBM],
        scratch=[
            pltpu.VMEM((d, protos), BF16),
            pltpu.VMEM((d, protos), BF16),
            pltpu.SemaphoreType.DMA((8,)),
            pltpu.SemaphoreType.DMA((8,)),
        ],
    )
    codes, sums = call(
        table_body,
        "teacher_table",
        (shape((rows, protos), BF16), shape((8, width), F32)),
        (all_rows, unit),
        2 * product,
        specs=[VMEM, HBM],
        scratch=[pltpu.VMEM((d, protos), BF16), pltpu.SemaphoreType.DMA((8,))],
    )

    messages = []
    pieces = []
    for sweep in range(SK_ITERS):
        sums = sums + hop(sums, 1)
        parts = [sums] + [hop(sums, 2 * k) for k in range(1, chips)]
        span = PIECES[sweep] * width
        last = sweep == SK_ITERS - 1
        pieces.append(
            call(
                functools.partial(student_body, sweep),
                "student_table",
                (shape((rows, span), BF16), shape((8, rows), F32), shape((d, rows), F32))
                + ((shape((d, rows), BF16),) if last else ()),
                (all_rows, unit),
                product,
                specs=[VMEM, HBM],
                after=(sums,),
                scratch=[pltpu.VMEM((d, span), BF16), pltpu.SemaphoreType.DMA((PIECES[sweep],))],
            )
        )
        part = call(
            functools.partial(row_pass_body, chips),
            "row_pass",
            shape((n_proto, 8, LANES), F32),
            (*parts, codes, *([piece[1] for piece in pieces] if last else [own_weights])),
            product,
            after=() if last else (pieces[-1][1],),
        )
        messages.append(exchange(part, "proto"))
        if not last:
            sums = call(
                col_pass_body,
                "col_pass",
                shape((8, width), F32),
                (messages[-1], codes),
                product // 2,
            )

    turned = pieces[-1][3]
    factors = (messages[0], messages[-1])
    own_block, keep, near = call(
        functools.partial(head_body, chips),
        "head",
        (
            shape((share, protos), F32),
            shape((chips - 1, share, protos), F32),
            shape((chips, share, protos), BF16),
        ),
        (
            place,
            *factors,
            *parts,
            turned,
            inverse,
            codes,
            *[piece[0] for piece in pieces],
            proto_weight,
        ),
        4 * product,
        specs=[SMEM] + [VMEM] * (len(factors) + chips + 3 + len(pieces)) + [HBM],
        scratch=[
            pltpu.VMEM((d, rows), BF16),
            pltpu.VMEM((d, protos), BF16),
            pltpu.SemaphoreType.DMA((8, n_patch)),
        ],
    )
    codes_feature = call(
        codes_feature_body,
        "codes_feature",
        shape((d, rows), F32),
        (*parts, codes, unit),
        product,
        specs=[VMEM] * (chips + 1) + [HBM],
        after=(own_block,),
        scratch=[pltpu.VMEM((d, protos), BF16), pltpu.SemaphoreType.DMA((8,))],
    )
    own_block, *pairs = call(
        pair_body,
        "pair_sums",
        (shape((share, protos), F32),)
        + tuple(shape((share, protos), BF16) for _ in range(chips - 1)),
        (own_block, keep, hop(near, 1)),
        product // 4,
        after=(codes_feature,),
    )
    far = [hop(pair, 2 * (k + 1)) for k, pair in enumerate(pairs)]
    feature_part = call(
        feature_body,
        "feature",
        shape((n_proto, own + 8, d), F32),
        (*factors, codes_feature, turned, *[piece[2] for piece in pieces]),
        product // 4,
        after=(own_block,),
    )
    grad_student, tails = call(
        owner_body,
        "owner",
        (shape((own, d), F32), shape((n_patch, 8, LANES), F32)),
        (exchange(feature_part, "proto"), x_rows),
        product // 8,
    )
    grad_proto = call(
        final_body,
        "assemble",
        shape((share, protos), F32),
        (own_block, *far),
        product // 4,
        after=(tails,),
    )
    losses = jnp.sum(exchange(tails, "patch"), axis=0)
    return (grad_student, grad_proto, losses[0, 0] / losses[0, 1])


def solution(mesh):
    both = ("patch", "proto")
    in_specs = (P(both, None), P(both, None), P(None, "proto"), P(both), P(both))
    out_specs = (P(both, None), P("patch", "proto"), P())
    return jax.shard_map(
        on_device, mesh=mesh, in_specs=in_specs, out_specs=out_specs, check_vma=False
    )
```

profile of v0, /device:TPU:1, one launch (start us, length us, event | category | flops | bytes accessed | tf_op | source)
XLA Modules:
  0.0 154.7 jit_solution(8764846528901984309)
XLA Ops:
  0.6 0.1 pad_add_fusion.refs_0_
  0.7 2.7 %own_rows.1 = (bf16[16,64,256]{2,1,0:T(8,128)(2,1)}, f32[32,256]{1,0:T(8,128)S(1)}, f32[8,512]{1,0:T(8,128)S(1)}) custom-call(s32[3]{0:T(128)S(1)} %pad_add_fusion.refs_0_, bf16[256,256]{1,0:T(8,128)(2,1)} %refs_1_.1, bf16[256,256]{1,0:T(8,128)(2,1)} %refs_2_.1, s32[1,32]{1,0:T(1,128)} %bitcast.6, bf16[1,32]{1,0:T(2,128)(2,1)} %bitcast.7), custom_call_target="tpu_custom_call" | custom-call | flops 268435456 | bytes 65536 | tf_op jit(solution)/shard_map/own_rows/pallas_call | solution.py:52
  3.4 8.6 %all-to-all-start = ((bf16[16,64,256]{2,1,0:T(8,128)(2,1)}), bf16[16,64,256]{2,1,0:T(8,128)(2,1)S(1)}, u32[]{:S(2)}, u32[]{:S(2)}) async-start(bf16[16,64,256]{2,1,0:T(8,128)(2,1)} %get-tuple-element.29), calls=%async_computation | async-start | bytes 1048576 | tf_op jit(solution)/shard_map/all_to_all | solution.py:367
  12.0 3.7 %proto_unit.1 = (bf16[256,8192]{1,0:T(8,128)(2,1)}, f32[8,1024]{1,0:T(8,128)S(1)}) custom-call(bf16[256,8192]{1,0:T(8,128)(2,1)} %refs_13_.1), custom_call_target="tpu_custom_call" | custom-call | flops 2147483648 | bytes 65536 | tf_op jit(solution)/shard_map/proto_unit/pallas_call | solution.py:52
  15.7 6.8 %all-to-all-done.refs_0_.refs_1_ = bf16[16,64,256]{2,1,0:T(8,128)(2,1)S(1)} async-done(((bf16[16,64,256]{2,1,0:T(8,128)(2,1)}), bf16[16,64,256]{2,1,0:T(8,128)(2,1)S(1)}, u32[]{:S(2)}, u32[]{:S(2)}) %all-to-all-start) | async-done | bytes 524320 | tf_op jit(solution)/shard_map/all_to_all | solution.py:367
  22.5 6.0 %teacher_table.1 = (bf16[512,8192]{1,0:T(8,128)(2,1)S(1)}, f32[8,1024]{1,0:T(8,128)S(1)}) custom-call(bf16[16,64,256]{2,1,0:T(8,128)(2,1)S(1)} %all-to-all-done.refs_0_.refs_1_, bf16[256,8192]{1,0:T(8,128)(2,1)} %get-tuple-element.30.refs_1_.refs_2_.refs_6_), custom_call_target="tpu_custom_call" | custom-call | flops 4294967296 | bytes 65536 | tf_op jit(solution)/shard_map/teacher_table/pallas_call | solution.py:52
  28.5 2.1 %collective-permute-start = (f32[8,1024]{1,0:T(8,128)S(1)}, f32[8,1024]{1,0:T(8,128)S(1)}, u32[]{:S(2)}, u32[]{:S(2)}) collective-permute-start(f32[8,1024]{1,0:T(8,128)S(1)} %get-tuple-element.31), channel_id=1, source_target_pairs={{0,16},{16,0},{32,48},{48,32},{64,80},{80,64},{96,112},{112,96},{1... | collective-permute-start | bytes 98312 | tf_op jit(solution)/shard_map/ppermute | solution.py:370
  30.6 0.9 collective-permute-done
  31.4 2.5 %collective-permute-start.3 = (f32[8,1024]{1,0:T(8,128)S(1)}, f32[8,1024]{1,0:T(8,128)S(1)}, u32[]{:S(2)}, u32[]{:S(2)}) collective-permute-start(f32[8,1024]{1,0:T(8,128)S(1)} %add.15.refs_0_.refs_1_), channel_id=1, source_target_pairs={{0,96},{16,112},{32,64},{48,80},{64,32},{80,48},{96,0},{112,16},{1... | collective-permute-start | bytes 98312 | tf_op jit(solution)/shard_map/ppermute | solution.py:370
  33.9 0.5 collective-permute-start.2
  34.4 0.3 collective-permute-start.1
  34.7 3.8 %student_table.3 = (bf16[512,3072]{1,0:T(8,128)(2,1)S(1)}, f32[8,512]{1,0:T(8,128)S(1)}, f32[256,512]{1,0:T(8,128)S(1)}) custom-call(f32[8,1024]{1,0:T(8,128)S(1)} %add.15.refs_0_.refs_1_, bf16[16,64,256]{2,1,0:T(8,128)(2,1)S(1)} %all-to-all-done.refs_0_.refs_1_, bf16[256,8192]{1,0:T(8,128)(2,1)} %get-tuple-element.30.refs_1_.refs_2_.refs_6_), custom_call_target="tpu_custom_call" | custom-call | flops 2147483648 | bytes 65536 | tf_op jit(solution)/shard_map/student_table/pallas_call | solution.py:52
  38.5 0.0 collective-permute-done.3.refs_4_
  38.5 0.0 collective-permute-done.2.refs_3_
  38.6 0.0 collective-permute-done.1.refs_2_
  38.6 2.3 %row_pass.3 = f32[16,8,128]{2,1,0:T(8,128)S(1)} custom-call(f32[8,512]{1,0:T(8,128)S(1)} %get-tuple-element.32.refs_0_.refs_5_, f32[8,1024]{1,0:T(8,128)S(1)} %add.15.refs_0_.refs_1_, f32[8,1024]{1,0:T(8,128)S(1)} %collective-permute-done.1.refs_2_, f32[8,1024]{1,0:T(8,128)S(1)} %collective-permute-done.2.refs_3_, ...), custom_call_target="tpu_custom_call" | custom-call | flops 2147483648 | bytes 65536 | tf_op jit(solution)/shard_map/row_pass/pallas_call | solution.py:52
  40.9 9.2 %all_to_all.30.refs_0_.refs_1_ = f32[16,8,128]{2,1,0:T(8,128)S(1)} all-to-all(f32[16,8,128]{2,1,0:T(8,128)S(1)} %row_pass.3), channel_id=1, replica_groups=mesh['patch'=8,'proto'=16] {'proto'}, dimensions={0} | all-to-all | bytes 131072 | tf_op jit(solution)/shard_map/all_to_all | solution.py:367
  50.1 1.2 col_pass.2
  51.3 2.9 %collective-permute-start.4 = (f32[8,1024]{1,0:T(8,128)S(1)}, f32[8,1024]{1,0:T(8,128)S(1)}, u32[]{:S(2)}, u32[]{:S(2)}) collective-permute-start(f32[8,1024]{1,0:T(8,128)S(1)} %col_pass.2), channel_id=1, source_target_pairs={{0,16},{16,0},{32,48},{48,32},{64,80},{80,64},{96,112},{112,96},{1... | collective-permute-start | bytes 98312 | tf_op jit(solution)/shard_map/ppermute | solution.py:370
  54.2 0.9 collective-permute-done.4
  55.1 2.3 %collective-permute-start.7 = (f32[8,1024]{1,0:T(8,128)S(1)}, f32[8,1024]{1,0:T(8,128)S(1)}, u32[]{:S(2)}, u32[]{:S(2)}) collective-permute-start(f32[8,1024]{1,0:T(8,128)S(1)} %add.16.refs_0_.refs_1_), channel_id=1, source_target_pairs={{0,96},{16,112},{32,64},{48,80},{64,32},{80,48},{96,0},{112,16},{1... | collective-permute-start | bytes 98312 | tf_op jit(solution)/shard_map/ppermute | solution.py:370
  57.3 0.5 collective-permute-start.6
  57.8 0.5 collective-permute-start.5
  58.3 3.8 %student_table.4 = (bf16[512,3072]{1,0:T(8,128)(2,1)S(1)}, f32[8,512]{1,0:T(8,128)S(1)}, f32[256,512]{1,0:T(8,128)S(1)}) custom-call(f32[8,1024]{1,0:T(8,128)S(1)} %add.16.refs_0_.refs_1_, bf16[16,64,256]{2,1,0:T(8,128)(2,1)S(1)} %all-to-all-done.refs_0_.refs_1_, bf16[256,8192]{1,0:T(8,128)(2,1)} %get-tuple-element.30.refs_1_.refs_2_.refs_6_), custom_call_target="tpu_custom_call" | custom-call | flops 2147483648 | bytes 65536 | tf_op jit(solution)/shard_map/student_table/pallas_call | solution.py:52
  62.2 0.0 collective-permute-done.7.refs_4_
  62.2 0.0 collective-permute-done.6.refs_3_
  62.2 0.0 collective-permute-done.5.refs_2_
  62.2 2.3 %row_pass.4 = f32[16,8,128]{2,1,0:T(8,128)S(1)} custom-call(f32[8,512]{1,0:T(8,128)S(1)} %get-tuple-element.35.refs_0_.refs_6_, f32[8,1024]{1,0:T(8,128)S(1)} %add.16.refs_0_.refs_1_, f32[8,1024]{1,0:T(8,128)S(1)} %collective-permute-done.5.refs_2_, f32[8,1024]{1,0:T(8,128)S(1)} %collective-permute-done.6.refs_3_, ...), custom_call_target="tpu_custom_call" | custom-call | flops 2147483648 | bytes 65536 | tf_op jit(solution)/shard_map/row_pass/pallas_call | solution.py:52
  64.5 9.4 %all_to_all.31.refs_0_ = f32[16,8,128]{2,1,0:T(8,128)S(1)} all-to-all(f32[16,8,128]{2,1,0:T(8,128)S(1)} %row_pass.4), channel_id=1, replica_groups=mesh['patch'=8,'proto'=16] {'proto'}, dimensions={0} | all-to-all | bytes 131072 | tf_op jit(solution)/shard_map/all_to_all | solution.py:367
  73.9 1.2 col_pass.3
  75.1 2.7 %collective-permute-start.8 = (f32[8,1024]{1,0:T(8,128)S(1)}, f32[8,1024]{1,0:T(8,128)S(1)}, u32[]{:S(2)}, u32[]{:S(2)}) collective-permute-start(f32[8,1024]{1,0:T(8,128)S(1)} %col_pass.3), channel_id=1, source_target_pairs={{0,16},{16,0},{32,48},{48,32},{64,80},{80,64},{96,112},{112,96},{1... | collective-permute-start | bytes 98312 | tf_op jit(solution)/shard_map/ppermute | solution.py:370
  77.8 0.9 collective-permute-done.8
  78.7 2.3 %collective-permute-start.11 = (f32[8,1024]{1,0:T(8,128)S(1)}, f32[8,1024]{1,0:T(8,128)S(1)}, u32[]{:S(2)}, u32[]{:S(2)}) collective-permute-start(f32[8,1024]{1,0:T(8,128)S(1)} %add.17.refs_0_.refs_3_.refs_1_), channel_id=1, source_target_pairs={{0,96},{16,112},{32,64},{48,80},{64,32},{80,48},{96,0},{112,16},{1... | collective-permute-start | bytes 98312 | tf_op jit(solution)/shard_map/ppermute | solution.py:370
  80.9 0.5 collective-permute-start.10
  81.4 0.5 collective-permute-start.9
  81.9 3.0 %student_table.5 = (bf16[512,2048]{1,0:T(8,128)(2,1)S(1)}, f32[8,512]{1,0:T(8,128)S(1)}, f32[256,512]{1,0:T(8,128)S(1)}, bf16[256,512]{1,0:T(8,128)(2,1)S(1)}) custom-call(f32[8,1024]{1,0:T(8,128)S(1)} %add.17.refs_0_.refs_3_.refs_1_, bf16[16,64,256]{2,1,0:T(8,128)(2,1)S(1)} %all-to-all-done.refs_0_.refs_1_, ...), custom_call_target="tpu_custom_call" | custom-call | flops 2147483648 | bytes 65536 | tf_op jit(solution)/shard_map/student_table/pallas_call | solution.py:52
  84.9 0.0 collective-permute-done.11.refs_3_.refs_6_.refs_4_
  84.9 0.3 collective-permute-done.10.refs_2_.refs_5_.refs_3_
  85.2 0.0 collective-permute-done.9.refs_1_.refs_4_.refs_2_
  85.2 2.3 %row_pass.5 = f32[16,8,128]{2,1,0:T(8,128)S(1)} custom-call(f32[8,1024]{1,0:T(8,128)S(1)} %add.17.refs_0_.refs_3_.refs_1_, f32[8,1024]{1,0:T(8,128)S(1)} %collective-permute-done.9.refs_1_.refs_4_.refs_2_, f32[8,1024]{1,0:T(8,128)S(1)} %collective-permute-done.10.refs_2_.refs_5_.refs_3_, f32[8,1024]{1,0:T(8,128)S(1)} %collective-permute-done.11.refs_3_.refs_6_.refs_4_, ...), custom_call_target="tpu_custom_call" | custom-call | flops 2147483648 | bytes 65536 | tf_op jit(solution)/shard_map/row_pass/pallas_call | solution.py:52
  87.5 9.4 %all_to_all.32.refs_2_ = f32[16,8,128]{2,1,0:T(8,128)S(1)} all-to-all(f32[16,8,128]{2,1,0:T(8,128)S(1)} %row_pass.5), channel_id=1, replica_groups=mesh['patch'=8,'proto'=16] {'proto'}, dimensions={0} | all-to-all | bytes 131072 | tf_op jit(solution)/shard_map/all_to_all | solution.py:367
  96.9 11.0 %head.1 = (f32[32,8192]{1,0:T(8,128)S(1)}, f32[3,32,8192]{2,1,0:T(8,128)S(1)}, bf16[4,32,8192]{2,1,0:T(8,128)(2,1)S(1)}) custom-call(s32[3]{0:T(128)S(1)} %pad_add_fusion.refs_0_, f32[16,8,128]{2,1,0:T(8,128)S(1)} %all_to_all.30.refs_0_.refs_1_, f32[16,8,128]{2,1,0:T(8,128)S(1)} %all_to_all.32.refs_2_, f32[8,1024]{1,0:T(8,128)S(1)} %add.17.refs_0_.refs_3_.refs_1_, ...), custom_call_target="tpu_custom_call" | custom-call | flops 8589934592 | bytes 65536 | tf_op jit(solution)/shard_map/head/pallas_call | solution.py:52
  107.8 3.3 %collective-permute-start.12 = (bf16[4,32,8192]{2,1,0:T(8,128)(2,1)S(1)}, bf16[4,32,8192]{2,1,0:T(8,128)(2,1)S(1)}, u32[]{:S(2)}, u32[]{:S(2)}) collective-permute-start(bf16[4,32,8192]{2,1,0:T(8,128)(2,1)S(1)} %get-tuple-element.44), channel_id=1, source_target_pairs={{0,16},{16,0},{32,48},{48,32},{64,80},{80,64},{96,112},{112,96},{1... | collective-permute-start | bytes 6291464 | tf_op jit(solution)/shard_map/ppermute | solution.py:370
  111.1 4.1 %codes_feature.1.refs_0_.refs_3_ = f32[256,512]{1,0:T(8,128)S(1)} custom-call(f32[32,8192]{1,0:T(8,128)S(1)} %get-tuple-element.42.refs_0_.refs_1_, f32[8,1024]{1,0:T(8,128)S(1)} %add.17.refs_0_.refs_3_.refs_1_, f32[8,1024]{1,0:T(8,128)S(1)} %collective-permute-done.9.refs_1_.refs_4_.refs_2_, f32[8,1024]{1,0:T(8,128)S(1)} %collective-permute-done.10.refs_2_.refs_5_.refs_3_, ...), custom_call_target="tpu_custom_call" | custom-call | flops 2147483648 | bytes 65536 | tf_op jit(solution)/shard_map/codes_feature/pallas_call | solution.py:52
  115.2 0.0 collective-permute-done.12.refs_3_
  115.2 1.3 pair_sums.1
  116.5 0.0 copy-start
  116.5 0.8 copy-done
  117.3 1.2 feature.1
  118.5 3.6 %all-to-all-start.4 = ((f32[16,40,256]{2,1,0:T(8,128)}), f32[16,40,256]{2,1,0:T(8,128)S(1)}, u32[]{:S(2)}, u32[]{:S(2)}) async-start(f32[16,40,256]{2,1,0:T(8,128)} %feature.1), calls=%async_computation.4 | async-start | bytes 1310720 | tf_op jit(solution)/shard_map/all_to_all | solution.py:367
  122.1 0.2 collective-permute-start.13
  122.3 2.5 %collective-permute-start.14 = (bf16[32,8192]{1,0:T(8,128)(2,1)}, bf16[32,8192]{1,0:T(8,128)(2,1)S(1)}, u32[]{:S(2)}, u32[]{:S(2)}) collective-permute-start(bf16[32,8192]{1,0:T(8,128)(2,1)} %get-tuple-element.53), channel_id=1, source_target_pairs={{0,64},{16,80},{32,96},{48,112},{64,0},{80,16},{96,32},{112,48},{1... | collective-permute-start | bytes 1572872 | tf_op jit(solution)/shard_map/ppermute | solution.py:370
  124.8 1.2 collective-permute-start.15
  126.0 8.8 %all-to-all-done.4.refs_0_ = f32[16,40,256]{2,1,0:T(8,128)S(1)} async-done(((f32[16,40,256]{2,1,0:T(8,128)}), f32[16,40,256]{2,1,0:T(8,128)S(1)}, u32[]{:S(2)}, u32[]{:S(2)}) %all-to-all-start.4) | async-done | bytes 655392 | tf_op jit(solution)/shard_map/all_to_all | solution.py:367
  134.8 0.8 owner.1
  135.6 4.4 %all-to-all-start.5 = ((f32[8,8,128]{2,1,0:T(8,128)}), f32[8,8,128]{2,1,0:T(8,128)S(1)}, u32[]{:S(2)}, u32[]{:S(2)}) async-start(f32[8,8,128]{2,1,0:T(8,128)} %get-tuple-element.51.refs_0_), calls=%async_computation.5 | async-start | bytes 65536 | tf_op jit(solution)/shard_map/all_to_all | solution.py:367
  140.1 0.0 collective-permute-done.13.refs_2_
  140.1 8.2 %collective-permute-done.14.refs_3_ = bf16[32,8192]{1,0:T(8,128)(2,1)S(1)} collective-permute-done((bf16[32,8192]{1,0:T(8,128)(2,1)}, bf16[32,8192]{1,0:T(8,128)(2,1)S(1)}, u32[]{:S(2)}, u32[]{:S(2)}) %collective-permute-start.14) | collective-permute-done | bytes 524320 | tf_op jit(solution)/shard_map/ppermute | solution.py:370
  148.3 2.2 %collective-permute-done.15.refs_4_ = bf16[32,8192]{1,0:T(8,128)(2,1)S(1)} collective-permute-done((bf16[32,8192]{1,0:T(8,128)(2,1)}, bf16[32,8192]{1,0:T(8,128)(2,1)S(1)}, u32[]{:S(2)}, u32[]{:S(2)}) %collective-permute-start.15) | collective-permute-done | bytes 524320 | tf_op jit(solution)/shard_map/ppermute | solution.py:370
  150.5 1.2 assemble.1
  151.6 0.0 all-to-all-done.5
  151.7 0.6 fusion
  (4 shorter events, 0.0 us)
Async XLA Ops:
  3.4 19.1 %all-to-all-start = ((bf16[16,64,256]{2,1,0:T(8,128)(2,1)}), bf16[16,64,256]{2,1,0:T(8,128)(2,1)S(1)}, u32[]{:S(2)}, u32[]{:S(2)}) async-start(bf16[16,64,256]{2,1,0:T(8,128)(2,1)} %get-tuple-element.29), calls=%async_computation | async-start | bytes 1048576 | tf_op jit(solution)/shard_map/all_to_all | solution.py:367
  28.5 2.9 %collective-permute-start = (f32[8,1024]{1,0:T(8,128)S(1)}, f32[8,1024]{1,0:T(8,128)S(1)}, u32[]{:S(2)}, u32[]{:S(2)}) collective-permute-start(f32[8,1024]{1,0:T(8,128)S(1)} %get-tuple-element.31), channel_id=1, source_target_pairs={{0,16},{16,0},{32,48},{48,32},{64,80},{80,64},{96,112},{112,96},{1... | collective-permute-start | bytes 98312 | tf_op jit(solution)/shard_map/ppermute | solution.py:370
  31.4 7.1 %collective-permute-start.3 = (f32[8,1024]{1,0:T(8,128)S(1)}, f32[8,1024]{1,0:T(8,128)S(1)}, u32[]{:S(2)}, u32[]{:S(2)}) collective-permute-start(f32[8,1024]{1,0:T(8,128)S(1)} %add.15.refs_0_.refs_1_), channel_id=1, source_target_pairs={{0,96},{16,112},{32,64},{48,80},{64,32},{80,48},{96,0},{112,16},{1... | collective-permute-start | bytes 98312 | tf_op jit(solution)/shard_map/ppermute | solution.py:370
  33.9 4.6 %collective-permute-start.2 = (f32[8,1024]{1,0:T(8,128)S(1)}, f32[8,1024]{1,0:T(8,128)S(1)}, u32[]{:S(2)}, u32[]{:S(2)}) collective-permute-start(f32[8,1024]{1,0:T(8,128)S(1)} %add.15.refs_0_.refs_1_), channel_id=1, source_target_pairs={{0,64},{16,80},{32,96},{48,112},{64,0},{80,16},{96,32},{112,48},{1... | collective-permute-start | bytes 98312 | tf_op jit(solution)/shard_map/ppermute | solution.py:370
  34.4 4.1 %collective-permute-start.1 = (f32[8,1024]{1,0:T(8,128)S(1)}, f32[8,1024]{1,0:T(8,128)S(1)}, u32[]{:S(2)}, u32[]{:S(2)}) collective-permute-start(f32[8,1024]{1,0:T(8,128)S(1)} %add.15.refs_0_.refs_1_), channel_id=1, source_target_pairs={{0,32},{16,48},{32,0},{48,16},{64,96},{80,112},{96,64},{112,80},{1... | collective-permute-start | bytes 98312 | tf_op jit(solution)/shard_map/ppermute | solution.py:370
  51.3 3.8 %collective-permute-start.4 = (f32[8,1024]{1,0:T(8,128)S(1)}, f32[8,1024]{1,0:T(8,128)S(1)}, u32[]{:S(2)}, u32[]{:S(2)}) collective-permute-start(f32[8,1024]{1,0:T(8,128)S(1)} %col_pass.2), channel_id=1, source_target_pairs={{0,16},{16,0},{32,48},{48,32},{64,80},{80,64},{96,112},{112,96},{1... | collective-permute-start | bytes 98312 | tf_op jit(solution)/shard_map/ppermute | solution.py:370
  55.1 7.1 %collective-permute-start.7 = (f32[8,1024]{1,0:T(8,128)S(1)}, f32[8,1024]{1,0:T(8,128)S(1)}, u32[]{:S(2)}, u32[]{:S(2)}) collective-permute-start(f32[8,1024]{1,0:T(8,128)S(1)} %add.16.refs_0_.refs_1_), channel_id=1, source_target_pairs={{0,96},{16,112},{32,64},{48,80},{64,32},{80,48},{96,0},{112,16},{1... | collective-permute-start | bytes 98312 | tf_op jit(solution)/shard_map/ppermute | solution.py:370
  57.3 4.8 %collective-permute-start.6 = (f32[8,1024]{1,0:T(8,128)S(1)}, f32[8,1024]{1,0:T(8,128)S(1)}, u32[]{:S(2)}, u32[]{:S(2)}) collective-permute-start(f32[8,1024]{1,0:T(8,128)S(1)} %add.16.refs_0_.refs_1_), channel_id=1, source_target_pairs={{0,64},{16,80},{32,96},{48,112},{64,0},{80,16},{96,32},{112,48},{1... | collective-permute-start | bytes 98312 | tf_op jit(solution)/shard_map/ppermute | solution.py:370
  57.8 4.3 %collective-permute-start.5 = (f32[8,1024]{1,0:T(8,128)S(1)}, f32[8,1024]{1,0:T(8,128)S(1)}, u32[]{:S(2)}, u32[]{:S(2)}) collective-permute-start(f32[8,1024]{1,0:T(8,128)S(1)} %add.16.refs_0_.refs_1_), channel_id=1, source_target_pairs={{0,32},{16,48},{32,0},{48,16},{64,96},{80,112},{96,64},{112,80},{1... | collective-permute-start | bytes 98312 | tf_op jit(solution)/shard_map/ppermute | solution.py:370
  75.1 3.6 %collective-permute-start.8 = (f32[8,1024]{1,0:T(8,128)S(1)}, f32[8,1024]{1,0:T(8,128)S(1)}, u32[]{:S(2)}, u32[]{:S(2)}) collective-permute-start(f32[8,1024]{1,0:T(8,128)S(1)} %col_pass.3), channel_id=1, source_target_pairs={{0,16},{16,0},{32,48},{48,32},{64,80},{80,64},{96,112},{112,96},{1... | collective-permute-start | bytes 98312 | tf_op jit(solution)/shard_map/ppermute | solution.py:370
  78.7 6.3 %collective-permute-start.11 = (f32[8,1024]{1,0:T(8,128)S(1)}, f32[8,1024]{1,0:T(8,128)S(1)}, u32[]{:S(2)}, u32[]{:S(2)}) collective-permute-start(f32[8,1024]{1,0:T(8,128)S(1)} %add.17.refs_0_.refs_3_.refs_1_), channel_id=1, source_target_pairs={{0,96},{16,112},{32,64},{48,80},{64,32},{80,48},{96,0},{112,16},{1... | collective-permute-start | bytes 98312 | tf_op jit(solution)/shard_map/ppermute | solution.py:370
  80.9 4.3 %collective-permute-start.10 = (f32[8,1024]{1,0:T(8,128)S(1)}, f32[8,1024]{1,0:T(8,128)S(1)}, u32[]{:S(2)}, u32[]{:S(2)}) collective-permute-start(f32[8,1024]{1,0:T(8,128)S(1)} %add.17.refs_0_.refs_3_.refs_1_), channel_id=1, source_target_pairs={{0,64},{16,80},{32,96},{48,112},{64,0},{80,16},{96,32},{112,48},{1... | collective-permute-start | bytes 98312 | tf_op jit(solution)/shard_map/ppermute | solution.py:370
  81.4 3.8 %collective-permute-start.9 = (f32[8,1024]{1,0:T(8,128)S(1)}, f32[8,1024]{1,0:T(8,128)S(1)}, u32[]{:S(2)}, u32[]{:S(2)}) collective-permute-start(f32[8,1024]{1,0:T(8,128)S(1)} %add.17.refs_0_.refs_3_.refs_1_), channel_id=1, source_target_pairs={{0,32},{16,48},{32,0},{48,16},{64,96},{80,112},{96,64},{112,80},{1... | collective-permute-start | bytes 98312 | tf_op jit(solution)/shard_map/ppermute | solution.py:370
  107.8 7.4 %collective-permute-start.12 = (bf16[4,32,8192]{2,1,0:T(8,128)(2,1)S(1)}, bf16[4,32,8192]{2,1,0:T(8,128)(2,1)S(1)}, u32[]{:S(2)}, u32[]{:S(2)}) collective-permute-start(bf16[4,32,8192]{2,1,0:T(8,128)(2,1)S(1)} %get-tuple-element.44), channel_id=1, source_target_pairs={{0,16},{16,0},{32,48},{48,32},{64,80},{80,64},{96,112},{112,96},{1... | collective-permute-start | bytes 6291464 | tf_op jit(solution)/shard_map/ppermute | solution.py:370
  116.5 0.8 copy-start
  118.5 16.3 %all-to-all-start.4 = ((f32[16,40,256]{2,1,0:T(8,128)}), f32[16,40,256]{2,1,0:T(8,128)S(1)}, u32[]{:S(2)}, u32[]{:S(2)}) async-start(f32[16,40,256]{2,1,0:T(8,128)} %feature.1), calls=%async_computation.4 | async-start | bytes 1310720 | tf_op jit(solution)/shard_map/all_to_all | solution.py:367
  122.1 18.0 %collective-permute-start.13 = (bf16[32,8192]{1,0:T(8,128)(2,1)}, bf16[32,8192]{1,0:T(8,128)(2,1)S(1)}, u32[]{:S(2)}, u32[]{:S(2)}) collective-permute-start(bf16[32,8192]{1,0:T(8,128)(2,1)} %get-tuple-element.52), channel_id=1, source_target_pairs={{0,32},{16,48},{32,0},{48,16},{64,96},{80,112},{96,64},{112,80},{1... | collective-permute-start | bytes 1572872 | tf_op jit(solution)/shard_map/ppermute | solution.py:370
  122.3 26.0 %collective-permute-start.14 = (bf16[32,8192]{1,0:T(8,128)(2,1)}, bf16[32,8192]{1,0:T(8,128)(2,1)S(1)}, u32[]{:S(2)}, u32[]{:S(2)}) collective-permute-start(bf16[32,8192]{1,0:T(8,128)(2,1)} %get-tuple-element.53), channel_id=1, source_target_pairs={{0,64},{16,80},{32,96},{48,112},{64,0},{80,16},{96,32},{112,48},{1... | collective-permute-start | bytes 1572872 | tf_op jit(solution)/shard_map/ppermute | solution.py:370
  124.8 25.7 %collective-permute-start.15 = (bf16[32,8192]{1,0:T(8,128)(2,1)}, bf16[32,8192]{1,0:T(8,128)(2,1)S(1)}, u32[]{:S(2)}, u32[]{:S(2)}) collective-permute-start(bf16[32,8192]{1,0:T(8,128)(2,1)} %copy-done), channel_id=1, source_target_pairs={{0,96},{16,112},{32,64},{48,80},{64,32},{80,48},{96,0},{112,16},{1... | collective-permute-start | bytes 1572872 | tf_op jit(solution)/shard_map/ppermute | solution.py:370
  135.6 16.0 %all-to-all-start.5 = ((f32[8,8,128]{2,1,0:T(8,128)}), f32[8,8,128]{2,1,0:T(8,128)S(1)}, u32[]{:S(2)}, u32[]{:S(2)}) async-start(f32[8,8,128]{2,1,0:T(8,128)} %get-tuple-element.51.refs_0_), calls=%async_computation.5 | async-start | bytes 65536 | tf_op jit(solution)/shard_map/all_to_all | solution.py:367
where the time goes:
time: 155 us
  Pallas kernels  51.8 us (33%)
  starting transfers between devices  41.3 us (27%)
  waiting for transfers between devices  28.9 us (19%)
  blocking collectives  27.9 us (18%)
  between operations  3.28 us (2%)
    pallas_call x17, Pallas kernels, call(): pl.pallas_call(ordered, name=name, out_shape=out_shape, in_specs=[ANY] *...  51.8 us
    all_to_all x3, blocking collectives, exchange(): return lax.all_to_all(array, axis, 0, 0)  27.9 us
    ppermute x16, starting transfers between devices, hop(): return lax.ppermute(array, 'patch', [(i, i ^ bits) for i in range(n_patch)])  24.7 us
    all_to_all x3, starting transfers between devices, exchange(): return lax.all_to_all(array, axis, 0, 0)  16.6 us
    all_to_all x3, waiting for transfers between devices, exchange(): return lax.all_to_all(array, axis, 0, 0)  15.6 us
    ppermute x16, waiting for transfers between devices, hop(): return lax.ppermute(array, 'patch', [(i, i ^ bits) for i in range(n_patch)])  13.3 us
  transfers between devices with their start and end apart: 19, of which 8 were waited for; matrix products, arithmetic and copies ran while one was open for 0% of the time, Pallas kernels for 13%

commit v1 on v0

--- a/solution.py
+++ b/solution.py
@@ -15,6 +15,7 @@
 BF16 = jnp.bfloat16
 LANES = 128
 PIECES = (3, 3, 2)
+PARTS = (3, 5)
 VMEM_LIMIT = 20 * 1024 * 1024
 
 NN = (((1,), (0,)), ((), ()))
@@ -85,19 +86,25 @@
     return [(j, pl.ds(j * width, width)) for j in range(count)]
 
 
-def move(source, start, target, sems, count):
+def move(source, target, sems, count):
     width = target.shape[1] // count
     copies = [
         pltpu.make_async_copy(
-            source.at[:, pl.ds(start + j * width, width)],
+            source.at[:, pl.ds(j * width, width)],
             target.at[:, pl.ds(j * width, width)],
             sems.at[j],
         )
         for j in range(count)
     ]
-    for copy in copies:
+    for copy in copies[:2]:
         copy.start()
     return copies
+
+
+def arrive(copies, j):
+    copies[j].wait()
+    if j + 2 < len(copies):
+        copies[j + 2].start()
 
 
 def store(source, target, cols, sem):
@@ -162,10 +169,10 @@
 
 
 def proto_body(w_hbm, unit_hbm, inverse_ref, w_ref, unit_ref, in_sems, out_sems):
-    copies = move(w_hbm, 0, w_ref, in_sems, 8)
+    copies = move(w_hbm, w_ref, in_sems, 8)
     stores = []
     for j, cols in chunks(w_ref):
-        copies[j].wait()
+        arrive(copies, j)
         w = w_ref[:, cols].astype(F32)
         inverse = lax.rsqrt(jnp.sum(w * w, axis=0, keepdims=True) + EPS)
         inverse_ref[pl.ds(j, 1), :] = inverse
@@ -176,11 +183,11 @@
 
 
 def table_body(rows_ref, unit_hbm, table_ref, sums_ref, unit_ref, sems):
-    copies = move(unit_hbm, 0, unit_ref, sems, 8)
+    copies = move(unit_hbm, unit_ref, sems, 8)
     half = rows_ref.shape[1] // 2
     teacher = rows_ref[:, :half, :].reshape(-1, rows_ref.shape[2])
     for j, cols in chunks(table_ref):
-        copies[j].wait()
+        arrive(copies, j)
         table = jnp.exp(mm(teacher, unit_ref[:, cols]) * (1.0 / TEACHER_TEMP)).astype(BF16)
         table_ref[:, cols] = table
         sums_ref[pl.ds(j, 1), :] = jnp.sum(table.astype(F32), axis=0, keepdims=True)
@@ -203,17 +210,15 @@
         out_ref[pl.ds(j, 1), :] = jnp.sum(mm(terms, table_ref[:, cols]), axis=0, keepdims=True)
 
 
-def student_body(first, rows_ref, unit_hbm, table_ref, sums_ref, feature_ref, *refs):
-    unit_ref, sems = refs[-2:]
+def student_body(first, rows_ref, unit_ref, table_ref, sums_ref, feature_ref, *turned_refs):
     count = PIECES[first]
     width = table_ref.shape[1] // count
-    copies = move(unit_hbm, sum(PIECES[:first]) * width, unit_ref, sems, count)
+    start = sum(PIECES[:first]) * width
     half = rows_ref.shape[1] // 2
     student = rows_ref[:, half:, :].reshape(-1, rows_ref.shape[2])
     total = jnp.zeros((16, student.shape[0]), F32)
     for j, cols in chunks(table_ref, count):
-        copies[j].wait()
-        unit = unit_ref[:, cols]
+        unit = unit_ref[:, pl.ds(start + j * width, width)]
         table = jnp.exp(mm(student, unit) * (1.0 / STUDENT_TEMP)).astype(BF16)
         table_ref[:, cols] = table
         total += mm(jnp.ones((16, table.shape[1]), BF16), table, NT)
@@ -223,21 +228,19 @@
         else:
             feature_ref[...] += part
     sums_ref[...] = total[0:8]
-    if len(refs) > 2:
+    for turned_ref in turned_refs:
         d = student.shape[1]
         eye = (
             lax.broadcasted_iota(jnp.int32, (d, d), 0)
             == lax.broadcasted_iota(jnp.int32, (d, d), 1)
         ).astype(BF16)
-        refs[0][...] = mm(eye, student, NT).astype(BF16)
+        turned_ref[...] = mm(eye, student, NT).astype(BF16)
 
 
 def codes_feature_body(*refs):
-    *sums_refs, table_ref, unit_hbm, feature_ref, unit_ref, sems = refs
-    copies = move(unit_hbm, 0, unit_ref, sems, 8)
+    *sums_refs, table_ref, unit_ref, feature_ref = refs
     scale = 1.0 / column_sum(sums_refs)
     for j, cols in chunks(table_ref):
-        copies[j].wait()
         scaled = (unit_ref[:, cols].astype(F32) * scale[j : j + 1, :]).astype(BF16)
         part = mm(scaled, table_ref[:, cols], NT)
         if j == 0:
@@ -251,51 +254,36 @@
     return read_rows(first_ref, tile, n), read_rows(last_ref, tile, n), read_rows(last_ref, 0, n)
 
 
-def head_body(parts, *refs):
+def head_body(first, count, parts, *refs):
     place_ref, first_ref, last_ref = refs[:3]
     sums_refs = refs[3 : 3 + parts]
-    turned_ref, inverse_ref, codes_ref, *piece_refs, w_hbm = refs[3 + parts : -6]
-    own_ref, keep_ref, near_ref, turn_ref, w_ref, sems = refs[-6:]
+    turned_ref, inverse_ref, codes_ref, *piece_refs, w_ref = refs[3 + parts : -4]
+    own_ref, keep_ref, near_ref, turn_ref = refs[-4:]
     x, core = place_ref[1], place_ref[2]
-    chips = near_ref.shape[0]
-    share = near_ref.shape[1]
-    protos = codes_ref.shape[1]
-    count = 8
-    width = protos // count
+    chips, share, span = near_ref.shape
+    width = span // count
     spots = []
     for k in range(chips):
-        spots += [2 * (x ^ k) + core, 2 * (x ^ k) + 1 - core]
-    copies = []
-    for j in range(count):
-        copies.append([])
-        for m, spot in enumerate(spots):
-            copy = pltpu.make_async_copy(
-                w_hbm.at[pl.ds(pl.multiple_of(spot * share, share), share), pl.ds(j * width, width)],
-                w_ref.at[pl.ds(m * share, share), pl.ds(j * width, width)],
-                sems.at[j, m],
-            )
-            copy.start()
-            copies[j].append(copy)
+        for side in (core, 1 - core):
+            spots.append(pl.ds(pl.multiple_of((2 * (x ^ k) + side) * share, share), share))
     for m, spot in enumerate(spots):
-        turn_ref[pl.ds(m * share, share), :] = turned_ref[
-            pl.ds(pl.multiple_of(spot * share, share), share), :
-        ]
+        turn_ref[pl.ds(m * share, share), :] = turned_ref[spot, :]
     weights, exp_total, total = row_factors(first_ref, last_ref, codes_ref.shape[0])
     turned = turn_ref[...].astype(F32)
     left_probs = (turned * (weights / exp_total * (1.0 / STUDENT_TEMP))).astype(BF16)
     left_codes = (turned * (weights / total * (1.0 / STUDENT_TEMP))).astype(BF16)
     scale = 1.0 / column_sum(sums_refs)
-    piece, at = 0, 0
-    for j, cols in chunks(codes_ref, count):
-        probs = piece_refs[piece][:, pl.ds(at * width, width)]
-        at += 1
-        if at == PIECES[piece]:
-            piece, at = piece + 1, 0
-        head = mm(left_probs, probs) - scale[j : j + 1, :] * mm(left_codes, codes_ref[:, cols])
-        for copy in copies[j]:
-            copy.wait()
-        inverse = inverse_ref[pl.ds(j, 1), :]
-        unit = w_ref[:, cols].astype(F32) * inverse
+    where = [(p, at) for p, size in enumerate(PIECES) for at in range(size)]
+    for j, cols in chunks(own_ref, count):
+        row = first + j
+        here = pl.ds(row * width, width)
+        piece, at = where[row]
+        head = mm(left_probs, piece_refs[piece][:, pl.ds(at * width, width)]) - scale[
+            row : row + 1, :
+        ] * mm(left_codes, codes_ref[:, here])
+        inverse = inverse_ref[pl.ds(row, 1), :]
+        w = jnp.concatenate([w_ref[spot, here] for spot in spots], axis=0)
+        unit = w.astype(F32) * inverse
         inner = jnp.sum(unit * head, axis=0, keepdims=True)
         grad = inverse * (head - unit * inner)
         own_ref[:, cols] = grad[0:share]
@@ -312,12 +300,22 @@
         pair_ref[...] = (keep_ref[k] + near_ref[k + 1].astype(F32)).astype(BF16)
 
 
-def final_body(own_ref, *refs):
-    *far_refs, out_ref = refs
+def left_body(*refs):
+    own_ref, *far_refs, out_ref = refs
     total = own_ref[...]
     for far_ref in far_refs:
         total = total + far_ref[...].astype(F32)
     out_ref[...] = total
+
+
+def final_body(left_ref, own_ref, *refs):
+    *far_refs, out_ref = refs
+    span = left_ref.shape[1]
+    total = own_ref[...]
+    for far_ref in far_refs:
+        total = total + far_ref[...].astype(F32)
+    out_ref[:, :span] = left_ref[...]
+    out_ref[:, span:] = total
 
 
 def owner_body(sent_ref, x_ref, grad_ref, tail_ref):
@@ -428,9 +426,7 @@
                 + ((shape((d, rows), BF16),) if last else ()),
                 (all_rows, unit),
                 product,
-                specs=[VMEM, HBM],
                 after=(sums,),
-                scratch=[pltpu.VMEM((d, span), BF16), pltpu.SemaphoreType.DMA((PIECES[sweep],))],
             )
         )
         part = call(
@@ -453,60 +449,75 @@
 
     turned = pieces[-1][3]
     factors = (messages[0], messages[-1])
-    own_block, keep, near = call(
-        functools.partial(head_body, chips),
-        "head",
-        (
-            shape((share, protos), F32),
-            shape((chips - 1, share, protos), F32),
-            shape((chips, share, protos), BF16),
-        ),
-        (
-            place,
-            *factors,
-            *parts,
-            turned,
-            inverse,
-            codes,
-            *[piece[0] for piece in pieces],
-            proto_weight,
-        ),
-        4 * product,
-        specs=[SMEM] + [VMEM] * (len(factors) + chips + 3 + len(pieces)) + [HBM],
-        scratch=[
-            pltpu.VMEM((d, rows), BF16),
-            pltpu.VMEM((d, protos), BF16),
-            pltpu.SemaphoreType.DMA((8, n_patch)),
-        ],
-    )
+    heads = []
+    for index, count in enumerate(PARTS):
+        span = count * width
+        heads.append(
+            call(
+                functools.partial(head_body, sum(PARTS[:index]), count, chips),
+                "head",
+                (
+                    shape((share, span), F32),
+                    shape((chips - 1, share, span), F32),
+                    shape((chips, share, span), BF16),
+                ),
+                (
+                    place,
+                    *factors,
+                    *parts,
+                    turned,
+                    inverse,
+                    codes,
+                    *[piece[0] for piece in pieces],
+                    proto_weight,
+                ),
+                2 * product,
+                specs=[SMEM] + [VMEM] * (len(factors) + chips + 4 + len(pieces)),
+                after=(heads[-1][0],) if heads else (),
+                scratch=[pltpu.VMEM((d, rows), BF16)],
+            )
+        )
+
+    def send_part(index, after):
+        own_part, keep, near = heads[index]
+        span = own_part.shape[1]
+        own_part, *pairs = call(
+            pair_body,
+            "pair_sums",
+            (shape((share, span), F32),)
+            + tuple(shape((share, span), BF16) for _ in range(chips - 1)),
+            (own_part, keep, hop(near, 1)),
+            product // 8,
+            after=after,
+        )
+        return [own_part] + [hop(pair, 2 * (k + 1)) for k, pair in enumerate(pairs)]
+
+    left = send_part(0, (heads[1][0],))
     codes_feature = call(
         codes_feature_body,
         "codes_feature",
         shape((d, rows), F32),
         (*parts, codes, unit),
         product,
-        specs=[VMEM] * (chips + 1) + [HBM],
-        after=(own_block,),
-        scratch=[pltpu.VMEM((d, protos), BF16), pltpu.SemaphoreType.DMA((8,))],
-    )
-    own_block, *pairs = call(
-        pair_body,
-        "pair_sums",
-        (shape((share, protos), F32),)
-        + tuple(shape((share, protos), BF16) for _ in range(chips - 1)),
-        (own_block, keep, hop(near, 1)),
-        product // 4,
+        after=(left[0],),
+    )
+    left_sum = call(
+        left_body,
+        "left_sum",
+        shape((share, PARTS[0] * width), F32),
+        tuple(left),
+        product // 8,
         after=(codes_feature,),
     )
-    far = [hop(pair, 2 * (k + 1)) for k, pair in enumerate(pairs)]
     feature_part = call(
         feature_body,
         "feature",
         shape((n_proto, own + 8, d), F32),
         (*factors, codes_feature, turned, *[piece[2] for piece in pieces]),
         product // 4,
-        after=(own_block,),
-    )
+        after=(left_sum,),
+    )
+    right = send_part(1, (feature_part,))
     grad_student, tails = call(
         owner_body,
         "owner",
@@ -518,7 +529,7 @@
         final_body,
         "assemble",
         shape((share, protos), F32),
-        (own_block, *far),
+        (left_sum, *right),
         product // 4,
         after=(tails,),
     )

time: 155 us -> 157 us (1.013)
  blocking collectives: 27.9 us -> 38.5 us
  waiting for transfers between devices: 28.9 us -> 20.3 us
  Pallas kernels: 51.8 us -> 49.1 us
    all_to_all x3 -> x4, blocking collectives: 27.9 us -> 38.5 us  [exchange(): return lax.all_to_all(array, axis, 0, 0)]
    all_to_all x3 -> x2, waiting for transfers between devices: 15.6 us -> 8.92 us  [exchange(): return lax.all_to_all(array, axis, 0, 0)]
    ppermute x16 -> x20, starting transfers between devices: 24.7 us -> 29.1 us  [hop(): return lax.ppermute(array, 'patch', [(i, i ^ bits) for i in range(n_patch)])]
    all_to_all x3 -> x2, starting transfers between devices: 16.6 us -> 12.9 us  [exchange(): return lax.all_to_all(array, axis, 0, 0)]
    pallas_call x17 -> x20, Pallas kernels: 51.8 us -> 49.1 us  [call(): pl.pallas_call(ordered, name=name, out_shape=out_shape, in_specs=[ANY] *...]
    ppermute x16 -> x20, waiting for transfers between devices: 13.3 us -> 11.3 us  [hop(): return lax.ppermute(array, 'patch', [(i, i ^ bits) for i in range(n_patch)])]
  transfers between devices with their start and end apart: 19 -> 22, of which waited for: 8 -> 9; matrix products, arithmetic and copies ran while one was open for 0% -> 0% of each run, Pallas kernels for 13% -> 17%
where the time goes in v1:
time: 157 us; the launch traced here: 156 us
  Pallas kernels  49.1 us (31%)
  starting transfers between devices  42 us (27%)
  blocking collectives  38.5 us (25%)
  waiting for transfers between devices  20.3 us (13%)
  between operations  3.36 us (2%)
  local copies, waits for them, and re-layouts  2.52 us (2%)
    pallas_call x20, Pallas kernels, call(): pl.pallas_call(ordered, name=name, out_shape=out_shape, in_specs=[ANY] *...  49.1 us
    all_to_all x4, blocking collectives, exchange(): return lax.all_to_all(array, axis, 0, 0)  38.5 us
    ppermute x20, starting transfers between devices, hop(): return lax.ppermute(array, 'patch', [(i, i ^ bits) for i in range(n_patch)])  29.1 us
    all_to_all x2, starting transfers between devices, exchange(): return lax.all_to_all(array, axis, 0, 0)  12.9 us
    ppermute x20, waiting for transfers between devices, hop(): return lax.ppermute(array, 'patch', [(i, i ^ bits) for i in range(n_patch)])  11.3 us
    all_to_all x2, waiting for transfers between devices, exchange(): return lax.all_to_all(array, axis, 0, 0)  8.92 us
  transfers between devices with their start and end apart: 22, of which 9 were waited for; matrix products, arithmetic and copies ran while one was open for 0% of the time, Pallas kernels for 17%

profile of v1, /device:TPU:1, one launch (start us, length us, event | category | flops | bytes accessed | tf_op | source)
XLA Modules:
  0.0 155.8 jit_solution(11428979159826090585)
XLA Ops:
  0.6 0.1 pad_add_fusion.refs_0_.refs_1_
  0.7 2.7 %own_rows.1 = (bf16[16,64,256]{2,1,0:T(8,128)(2,1)}, f32[32,256]{1,0:T(8,128)S(1)}, f32[8,512]{1,0:T(8,128)S(1)}) custom-call(s32[3]{0:T(128)S(1)} %pad_add_fusion.refs_0_.refs_1_, bf16[256,256]{1,0:T(8,128)(2,1)} %refs_1_.1, bf16[256,256]{1,0:T(8,128)(2,1)} %refs_2_.1, s32[1,32]{1,0:T(1,128)} %bitcast.6, bf16[1,32]{1,0:T(2,128)(2,1)} %bitcast.7), custom_call_target="tpu_custom_call" | custom-call | flops 268435456 | bytes 65536 | tf_op jit(solution)/shard_map/own_rows/pallas_call | solution.py:53
  3.4 8.6 %all-to-all-start = ((bf16[16,64,256]{2,1,0:T(8,128)(2,1)}), bf16[16,64,256]{2,1,0:T(8,128)(2,1)S(1)}, u32[]{:S(2)}, u32[]{:S(2)}) async-start(bf16[16,64,256]{2,1,0:T(8,128)(2,1)} %get-tuple-element.36), calls=%async_computation | async-start | bytes 1048576 | tf_op jit(solution)/shard_map/all_to_all | solution.py:365
  12.0 6.0 %proto_unit.1 = (bf16[256,8192]{1,0:T(8,128)(2,1)}, f32[8,1024]{1,0:T(8,128)S(1)}) custom-call(bf16[256,8192]{1,0:T(8,128)(2,1)} %refs_14_.1), custom_call_target="tpu_custom_call" | custom-call | flops 2147483648 | bytes 65536 | tf_op jit(solution)/shard_map/proto_unit/pallas_call | solution.py:53
  18.1 4.5 %all-to-all-done.refs_0_.refs_1_ = bf16[16,64,256]{2,1,0:T(8,128)(2,1)S(1)} async-done(((bf16[16,64,256]{2,1,0:T(8,128)(2,1)}), bf16[16,64,256]{2,1,0:T(8,128)(2,1)S(1)}, u32[]{:S(2)}, u32[]{:S(2)}) %all-to-all-start) | async-done | bytes 524320 | tf_op jit(solution)/shard_map/all_to_all | solution.py:365
  22.5 6.2 %teacher_table.1 = (bf16[512,8192]{1,0:T(8,128)(2,1)S(1)}, f32[8,1024]{1,0:T(8,128)S(1)}) custom-call(bf16[16,64,256]{2,1,0:T(8,128)(2,1)S(1)} %all-to-all-done.refs_0_.refs_1_, bf16[256,8192]{1,0:T(8,128)(2,1)} %get-tuple-element.37.refs_1_.refs_2_.refs_6_), custom_call_target="tpu_custom_call" | custom-call | flops 4294967296 | bytes 65536 | tf_op jit(solution)/shard_map/teacher_table/pallas_call | solution.py:53
  28.7 2.1 %collective-permute-start = (f32[8,1024]{1,0:T(8,128)S(1)}, f32[8,1024]{1,0:T(8,128)S(1)}, u32[]{:S(2)}, u32[]{:S(2)}) collective-permute-start(f32[8,1024]{1,0:T(8,128)S(1)} %get-tuple-element.38), channel_id=1, source_target_pairs={{0,16},{16,0},{32,48},{48,32},{64,80},{80,64},{96,112},{112,96},{1... | collective-permute-start | bytes 98312 | tf_op jit(solution)/shard_map/ppermute | solution.py:368
  30.8 0.9 collective-permute-done
  31.7 2.5 %collective-permute-start.3 = (f32[8,1024]{1,0:T(8,128)S(1)}, f32[8,1024]{1,0:T(8,128)S(1)}, u32[]{:S(2)}, u32[]{:S(2)}) collective-permute-start(f32[8,1024]{1,0:T(8,128)S(1)} %add.15.refs_0_.refs_1_), channel_id=1, source_target_pairs={{0,96},{16,112},{32,64},{48,80},{64,32},{80,48},{96,0},{112,16},{1... | collective-permute-start | bytes 98312 | tf_op jit(solution)/shard_map/ppermute | solution.py:368
  34.1 0.5 collective-permute-start.2
  34.7 0.3 collective-permute-start.1
  34.9 2.7 %student_table.3 = (bf16[512,3072]{1,0:T(8,128)(2,1)S(1)}, f32[8,512]{1,0:T(8,128)S(1)}, f32[256,512]{1,0:T(8,128)S(1)}) custom-call(f32[8,1024]{1,0:T(8,128)S(1)} %add.15.refs_0_.refs_1_, bf16[16,64,256]{2,1,0:T(8,128)(2,1)S(1)} %all-to-all-done.refs_0_.refs_1_, bf16[256,8192]{1,0:T(8,128)(2,1)S(1)} %copy-done.1), custom_call_target="tpu_custom_call" | custom-call | flops 2147483648 | bytes 65536 | tf_op jit(solution)/shard_map/student_table/pallas_call | solution.py:53
  37.6 0.0 collective-permute-done.3.refs_4_
  37.6 0.8 collective-permute-done.2.refs_3_
  38.4 0.0 collective-permute-done.1.refs_2_
  38.4 2.3 %row_pass.3 = f32[16,8,128]{2,1,0:T(8,128)S(1)} custom-call(f32[8,512]{1,0:T(8,128)S(1)} %get-tuple-element.39.refs_0_.refs_5_, f32[8,1024]{1,0:T(8,128)S(1)} %add.15.refs_0_.refs_1_, f32[8,1024]{1,0:T(8,128)S(1)} %collective-permute-done.1.refs_2_, f32[8,1024]{1,0:T(8,128)S(1)} %collective-permute-done.2.refs_3_, ...), custom_call_target="tpu_custom_call" | custom-call | flops 2147483648 | bytes 65536 | tf_op jit(solution)/shard_map/row_pass/pallas_call | solution.py:53
  40.7 9.2 %all_to_all.30.refs_0_.refs_1_.refs_2_ = f32[16,8,128]{2,1,0:T(8,128)S(1)} all-to-all(f32[16,8,128]{2,1,0:T(8,128)S(1)} %row_pass.3), channel_id=1, replica_groups=mesh['patch'=8,'proto'=16] {'proto'}, dimensions={0} | all-to-all | bytes 131072 | tf_op jit(solution)/shard_map/all_to_all | solution.py:365
  49.9 1.2 col_pass.2
  51.1 3.3 %collective-permute-start.4 = (f32[8,1024]{1,0:T(8,128)S(1)}, f32[8,1024]{1,0:T(8,128)S(1)}, u32[]{:S(2)}, u32[]{:S(2)}) collective-permute-start(f32[8,1024]{1,0:T(8,128)S(1)} %col_pass.2), channel_id=1, source_target_pairs={{0,16},{16,0},{32,48},{48,32},{64,80},{80,64},{96,112},{112,96},{1... | collective-permute-start | bytes 98312 | tf_op jit(solution)/shard_map/ppermute | solution.py:368
  54.4 0.9 collective-permute-done.4
  55.3 1.1 collective-permute-start.7
  56.4 0.8 collective-permute-start.6
  57.2 1.3 collective-permute-start.5
  58.5 2.7 %student_table.4 = (bf16[512,3072]{1,0:T(8,128)(2,1)S(1)}, f32[8,512]{1,0:T(8,128)S(1)}, f32[256,512]{1,0:T(8,128)S(1)}) custom-call(f32[8,1024]{1,0:T(8,128)S(1)} %add.16.refs_0_.refs_1_, bf16[16,64,256]{2,1,0:T(8,128)(2,1)S(1)} %all-to-all-done.refs_0_.refs_1_, bf16[256,8192]{1,0:T(8,128)(2,1)S(1)} %copy-done.1), custom_call_target="tpu_custom_call" | custom-call | flops 2147483648 | bytes 65536 | tf_op jit(solution)/shard_map/student_table/pallas_call | solution.py:53
  61.2 0.0 collective-permute-done.7.refs_4_
  61.2 0.0 collective-permute-done.5.refs_2_
  61.3 2.3 %row_pass.4 = f32[16,8,128]{2,1,0:T(8,128)S(1)} custom-call(f32[8,512]{1,0:T(8,128)S(1)} %get-tuple-element.42.refs_0_.refs_6_, f32[8,1024]{1,0:T(8,128)S(1)} %add.16.refs_0_.refs_1_, f32[8,1024]{1,0:T(8,128)S(1)} %collective-permute-done.5.refs_2_, f32[8,1024]{1,0:T(8,128)S(1)} %collective-permute-done.6.refs_3_, ...), custom_call_target="tpu_custom_call" | custom-call | flops 2147483648 | bytes 65536 | tf_op jit(solution)/shard_map/row_pass/pallas_call | solution.py:53
  63.6 9.4 %all_to_all.31.refs_0_ = f32[16,8,128]{2,1,0:T(8,128)S(1)} all-to-all(f32[16,8,128]{2,1,0:T(8,128)S(1)} %row_pass.4), channel_id=1, replica_groups=mesh['patch'=8,'proto'=16] {'proto'}, dimensions={0} | all-to-all | bytes 131072 | tf_op jit(solution)/shard_map/all_to_all | solution.py:365
  72.9 1.2 col_pass.3
  74.2 2.9 %collective-permute-start.8 = (f32[8,1024]{1,0:T(8,128)S(1)}, f32[8,1024]{1,0:T(8,128)S(1)}, u32[]{:S(2)}, u32[]{:S(2)}) collective-permute-start(f32[8,1024]{1,0:T(8,128)S(1)} %col_pass.3), channel_id=1, source_target_pairs={{0,16},{16,0},{32,48},{48,32},{64,80},{80,64},{96,112},{112,96},{1... | collective-permute-start | bytes 98312 | tf_op jit(solution)/shard_map/ppermute | solution.py:368
  77.1 0.9 collective-permute-done.8
  77.9 1.4 collective-permute-start.11
  79.3 1.1 collective-permute-start.10
  80.4 0.7 collective-permute-start.9
  81.2 1.9 %student_table.5 = (bf16[512,2048]{1,0:T(8,128)(2,1)S(1)}, f32[8,512]{1,0:T(8,128)S(1)}, f32[256,512]{1,0:T(8,128)S(1)}, bf16[256,512]{1,0:T(8,128)(2,1)S(1)}) custom-call(f32[8,1024]{1,0:T(8,128)S(1)} %add.17.refs_0_.refs_3_.refs_4_.refs_1_, bf16[16,64,256]{2,1,0:T(8,128)(2,1)S(1)} %all-to-all-done.refs_0_.refs_1_, bf16[256,8192]{1,0:T(8,128)(2,1)S(1)} %copy-done.1), custom_call_target="tpu_custom_call" | custom-call | flops 2147483648 | bytes 65536 | tf_op jit(solution)/shard_map/student_table/pallas_call | solution.py:53
  83.1 0.0 collective-permute-done.11.refs_3_.refs_6_.refs_7_.refs_4_
  83.1 0.5 collective-permute-done.10.refs_2_.refs_5_.refs_6_.refs_3_
  83.6 0.0 collective-permute-done.9.refs_1_.refs_4_.refs_5_.refs_2_
  83.6 2.3 %row_pass.5 = f32[16,8,128]{2,1,0:T(8,128)S(1)} custom-call(f32[8,1024]{1,0:T(8,128)S(1)} %add.17.refs_0_.refs_3_.refs_4_.refs_1_, f32[8,1024]{1,0:T(8,128)S(1)} %collective-permute-done.9.refs_1_.refs_4_.refs_5_.refs_2_, f32[8,1024]{1,0:T(8,128)S(1)} %collective-permute-done.10.refs_2_.refs_5_.refs_6_.refs_3_, ...), custom_call_target="tpu_custom_call" | custom-call | flops 2147483648 | bytes 65536 | tf_op jit(solution)/shard_map/row_pass/pallas_call | solution.py:53
  85.9 9.4 %all_to_all.32.refs_2_.refs_3_ = f32[16,8,128]{2,1,0:T(8,128)S(1)} all-to-all(f32[16,8,128]{2,1,0:T(8,128)S(1)} %row_pass.5), channel_id=1, replica_groups=mesh['patch'=8,'proto'=16] {'proto'}, dimensions={0} | all-to-all | bytes 131072 | tf_op jit(solution)/shard_map/all_to_all | solution.py:365
  95.3 2.9 %head.2 = (f32[32,3072]{1,0:T(8,128)S(1)}, f32[3,32,3072]{2,1,0:T(8,128)S(1)}, bf16[4,32,3072]{2,1,0:T(8,128)(2,1)S(1)}) custom-call(s32[3]{0:T(128)S(1)} %pad_add_fusion.refs_0_.refs_1_, f32[16,8,128]{2,1,0:T(8,128)S(1)} %all_to_all.30.refs_0_.refs_1_.refs_2_, f32[16,8,128]{2,1,0:T(8,128)S(1)} %all_to_all.32.refs_2_.refs_3_, ...), custom_call_target="tpu_custom_call" | custom-call | flops 4294967296 | bytes 65536 | tf_op jit(solution)/shard_map/head/pallas_call | solution.py:53
  98.2 3.3 %collective-permute-start.12 = (bf16[4,32,3072]{2,1,0:T(8,128)(2,1)S(1)}, bf16[4,32,3072]{2,1,0:T(8,128)(2,1)S(1)}, u32[]{:S(2)}, u32[]{:S(2)}) collective-permute-start(bf16[4,32,3072]{2,1,0:T(8,128)(2,1)S(1)} %get-tuple-element.52), channel_id=1, source_target_pairs={{0,16},{16,0},{32,48},{48,32},{64,80},{80,64},{96,112},{112,96},{1... | collective-permute-start | bytes 2359304 | tf_op jit(solution)/shard_map/ppermute | solution.py:368
  101.5 5.5 %head.3 = (f32[32,5120]{1,0:T(8,128)S(1)}, f32[3,32,5120]{2,1,0:T(8,128)S(1)}, bf16[4,32,5120]{2,1,0:T(8,128)(2,1)}) custom-call(f32[32,3072]{1,0:T(8,128)S(1)} %get-tuple-element.49.refs_0_.refs_1_, s32[3]{0:T(128)S(1)} %pad_add_fusion.refs_0_.refs_1_, f32[16,8,128]{2,1,0:T(8,128)S(1)} %all_to_all.30.refs_0_.refs_1_.refs_2_, ...), custom_call_target="tpu_custom_call" | custom-call | flops 4294967296 | bytes 65536 | tf_op jit(solution)/shard_map/head/pallas_call | solution.py:53
  107.0 0.0 collective-permute-start.16
  107.0 0.2 pair_sums.2
  107.2 0.7 collective-permute-start.13
  107.9 1.8 %collective-permute-start.14 = (bf16[32,3072]{1,0:T(8,128)(2,1)S(1)}, bf16[32,3072]{1,0:T(8,128)(2,1)S(1)}, u32[]{:S(2)}, u32[]{:S(2)}) collective-permute-start(bf16[32,3072]{1,0:T(8,128)(2,1)S(1)} %get-tuple-element.55), channel_id=1, source_target_pairs={{0,64},{16,80},{32,96},{48,112},{64,0},{80,16},{96,32},{112,48},{1... | collective-permute-start | bytes 589832 | tf_op jit(solution)/shard_map/ppermute | solution.py:368
  109.7 1.4 collective-permute-start.15
  111.1 2.4 %codes_feature.1.refs_0_.refs_3_ = f32[256,512]{1,0:T(8,128)S(1)} custom-call(f32[32,3072]{1,0:T(8,128)S(1)} %get-tuple-element.53.refs_0_.refs_1_, f32[8,1024]{1,0:T(8,128)S(1)} %add.17.refs_0_.refs_3_.refs_4_.refs_1_, f32[8,1024]{1,0:T(8,128)S(1)} %collective-permute-done.9.refs_1_.refs_4_.refs_5_.refs_2_, ...), custom_call_target="tpu_custom_call" | custom-call | flops 2147483648 | bytes 65536 | tf_op jit(solution)/shard_map/codes_feature/pallas_call | solution.py:53
  113.5 5.0 %collective-permute-done.14.refs_3_ = bf16[32,3072]{1,0:T(8,128)(2,1)S(1)} collective-permute-done((bf16[32,3072]{1,0:T(8,128)(2,1)S(1)}, bf16[32,3072]{1,0:T(8,128)(2,1)S(1)}, u32[]{:S(2)}, u32[]{:S(2)}) %collective-permute-start.14) | collective-permute-done | bytes 196640 | tf_op jit(solution)/shard_map/ppermute | solution.py:368
  118.5 2.5 %collective-permute-done.15.refs_4_ = bf16[32,3072]{1,0:T(8,128)(2,1)S(1)} collective-permute-done((bf16[32,3072]{1,0:T(8,128)(2,1)S(1)}, bf16[32,3072]{1,0:T(8,128)(2,1)S(1)}, u32[]{:S(2)}, u32[]{:S(2)}) %collective-permute-start.15) | collective-permute-done | bytes 196640 | tf_op jit(solution)/shard_map/ppermute | solution.py:368
  121.0 0.1 left_sum.1.refs_0_.refs_1_
  121.0 1.2 feature.1.refs_0_
  122.2 4.3 %all-to-all-start.4 = ((f32[16,40,256]{2,1,0:T(8,128)}), f32[16,40,256]{2,1,0:T(8,128)}, u32[]{:S(2)}, u32[]{:S(2)}) async-start(f32[16,40,256]{2,1,0:T(8,128)} %feature.1.refs_0_), calls=%async_computation.4 | async-start | bytes 1310720 | tf_op jit(solution)/shard_map/all_to_all | solution.py:365
  126.5 2.3 %pair_sums.3 = (f32[32,5120]{1,0:T(8,128)S(1)}, bf16[32,5120]{1,0:T(8,128)(2,1)}, bf16[32,5120]{1,0:T(8,128)(2,1)}, bf16[32,5120]{1,0:T(8,128)(2,1)S(1)}) custom-call(f32[16,40,256]{2,1,0:T(8,128)} %feature.1.refs_0_, f32[32,5120]{1,0:T(8,128)S(1)} %get-tuple-element.50.refs_0_.refs_1_, f32[3,32,5120]{2,1,0:T(8,128)S(1)} %get-tuple-element.63.refs_2_, ...), custom_call_target="tpu_custom_call" | custom-call | flops 268435456 | bytes 65536 | tf_op jit(solution)/shard_map/pair_sums/pallas_call | solution.py:53
  128.8 0.8 copy-done.2
  129.7 2.6 %collective-permute-start.18 = (bf16[32,5120]{1,0:T(8,128)(2,1)}, bf16[32,5120]{1,0:T(8,128)(2,1)S(1)}, u32[]{:S(2)}, u32[]{:S(2)}) collective-permute-start(bf16[32,5120]{1,0:T(8,128)(2,1)} %get-tuple-element.67), channel_id=1, source_target_pairs={{0,64},{16,80},{32,96},{48,112},{64,0},{80,16},{96,32},{112,48},{1... | collective-permute-start | bytes 983048 | tf_op jit(solution)/shard_map/ppermute | solution.py:368
  132.3 1.3 collective-permute-start.19
  133.6 4.5 %all-to-all-done.4.refs_0_ = f32[16,40,256]{2,1,0:T(8,128)} async-done(((f32[16,40,256]{2,1,0:T(8,128)}), f32[16,40,256]{2,1,0:T(8,128)}, u32[]{:S(2)}, u32[]{:S(2)}) %all-to-all-start.4) | async-done | bytes 655392 | tf_op jit(solution)/shard_map/all_to_all | solution.py:365
  138.0 1.9 %owner.1 = (f32[32,256]{1,0:T(8,128)}, f32[8,8,128]{2,1,0:T(8,128)S(1)}) custom-call(f32[16,40,256]{2,1,0:T(8,128)} %all-to-all-done.4.refs_0_, f32[32,256]{1,0:T(8,128)S(1)} %get-tuple-element.60.refs_1_), custom_call_target="tpu_custom_call" | custom-call | flops 268435456 | bytes 65536 | tf_op jit(solution)/shard_map/owner/pallas_call | solution.py:53
  139.9 10.6 %all_to_all.33 = f32[8,8,128]{2,1,0:T(8,128)S(1)} all-to-all(f32[8,8,128]{2,1,0:T(8,128)S(1)} %get-tuple-element.62.refs_0_), channel_id=1, replica_groups=mesh['patch'=8,'proto'=16] {'patch'}, dimensions={0} | all-to-all | bytes 65536 | tf_op jit(solution)/shard_map/all_to_all | solution.py:365
  150.5 0.6 fusion
  152.5 1.1 copy-done.3
  153.5 1.1 assemble.1
  (18 shorter events, 0.1 us)
Async XLA Ops:
  3.4 19.1 %all-to-all-start = ((bf16[16,64,256]{2,1,0:T(8,128)(2,1)}), bf16[16,64,256]{2,1,0:T(8,128)(2,1)S(1)}, u32[]{:S(2)}, u32[]{:S(2)}) async-start(bf16[16,64,256]{2,1,0:T(8,128)(2,1)} %get-tuple-element.36), calls=%async_computation | async-start | bytes 1048576 | tf_op jit(solution)/shard_map/all_to_all | solution.py:365
  22.5 12.4 %copy-start.1 = (bf16[256,8192]{1,0:T(8,128)(2,1)S(1)}, bf16[256,8192]{1,0:T(8,128)(2,1)}, u32[]{:S(2)}) copy-start(bf16[256,8192]{1,0:T(8,128)(2,1)} %get-tuple-element.37.refs_1_.refs_2_.refs_6_) | copy-start | bytes 12582916
  28.7 2.9 %collective-permute-start = (f32[8,1024]{1,0:T(8,128)S(1)}, f32[8,1024]{1,0:T(8,128)S(1)}, u32[]{:S(2)}, u32[]{:S(2)}) collective-permute-start(f32[8,1024]{1,0:T(8,128)S(1)} %get-tuple-element.38), channel_id=1, source_target_pairs={{0,16},{16,0},{32,48},{48,32},{64,80},{80,64},{96,112},{112,96},{1... | collective-permute-start | bytes 98312 | tf_op jit(solution)/shard_map/ppermute | solution.py:368
  31.7 5.9 %collective-permute-start.3 = (f32[8,1024]{1,0:T(8,128)S(1)}, f32[8,1024]{1,0:T(8,128)S(1)}, u32[]{:S(2)}, u32[]{:S(2)}) collective-permute-start(f32[8,1024]{1,0:T(8,128)S(1)} %add.15.refs_0_.refs_1_), channel_id=1, source_target_pairs={{0,96},{16,112},{32,64},{48,80},{64,32},{80,48},{96,0},{112,16},{1... | collective-permute-start | bytes 98312 | tf_op jit(solution)/shard_map/ppermute | solution.py:368
  34.1 4.3 %collective-permute-start.2 = (f32[8,1024]{1,0:T(8,128)S(1)}, f32[8,1024]{1,0:T(8,128)S(1)}, u32[]{:S(2)}, u32[]{:S(2)}) collective-permute-start(f32[8,1024]{1,0:T(8,128)S(1)} %add.15.refs_0_.refs_1_), channel_id=1, source_target_pairs={{0,64},{16,80},{32,96},{48,112},{64,0},{80,16},{96,32},{112,48},{1... | collective-permute-start | bytes 98312 | tf_op jit(solution)/shard_map/ppermute | solution.py:368
  34.7 3.8 %collective-permute-start.1 = (f32[8,1024]{1,0:T(8,128)S(1)}, f32[8,1024]{1,0:T(8,128)S(1)}, u32[]{:S(2)}, u32[]{:S(2)}) collective-permute-start(f32[8,1024]{1,0:T(8,128)S(1)} %add.15.refs_0_.refs_1_), channel_id=1, source_target_pairs={{0,32},{16,48},{32,0},{48,16},{64,96},{80,112},{96,64},{112,80},{1... | collective-permute-start | bytes 98312 | tf_op jit(solution)/shard_map/ppermute | solution.py:368
  51.1 4.1 %collective-permute-start.4 = (f32[8,1024]{1,0:T(8,128)S(1)}, f32[8,1024]{1,0:T(8,128)S(1)}, u32[]{:S(2)}, u32[]{:S(2)}) collective-permute-start(f32[8,1024]{1,0:T(8,128)S(1)} %col_pass.2), channel_id=1, source_target_pairs={{0,16},{16,0},{32,48},{48,32},{64,80},{80,64},{96,112},{112,96},{1... | collective-permute-start | bytes 98312 | tf_op jit(solution)/shard_map/ppermute | solution.py:368
  55.3 5.9 %collective-permute-start.7 = (f32[8,1024]{1,0:T(8,128)S(1)}, f32[8,1024]{1,0:T(8,128)S(1)}, u32[]{:S(2)}, u32[]{:S(2)}) collective-permute-start(f32[8,1024]{1,0:T(8,128)S(1)} %add.16.refs_0_.refs_1_), channel_id=1, source_target_pairs={{0,96},{16,112},{32,64},{48,80},{64,32},{80,48},{96,0},{112,16},{1... | collective-permute-start | bytes 98312 | tf_op jit(solution)/shard_map/ppermute | solution.py:368
  56.4 4.8 %collective-permute-start.6 = (f32[8,1024]{1,0:T(8,128)S(1)}, f32[8,1024]{1,0:T(8,128)S(1)}, u32[]{:S(2)}, u32[]{:S(2)}) collective-permute-start(f32[8,1024]{1,0:T(8,128)S(1)} %add.16.refs_0_.refs_1_), channel_id=1, source_target_pairs={{0,64},{16,80},{32,96},{48,112},{64,0},{80,16},{96,32},{112,48},{1... | collective-permute-start | bytes 98312 | tf_op jit(solution)/shard_map/ppermute | solution.py:368
  57.2 4.0 %collective-permute-start.5 = (f32[8,1024]{1,0:T(8,128)S(1)}, f32[8,1024]{1,0:T(8,128)S(1)}, u32[]{:S(2)}, u32[]{:S(2)}) collective-permute-start(f32[8,1024]{1,0:T(8,128)S(1)} %add.16.refs_0_.refs_1_), channel_id=1, source_target_pairs={{0,32},{16,48},{32,0},{48,16},{64,96},{80,112},{96,64},{112,80},{1... | collective-permute-start | bytes 98312 | tf_op jit(solution)/shard_map/ppermute | solution.py:368
  74.2 3.7 %collective-permute-start.8 = (f32[8,1024]{1,0:T(8,128)S(1)}, f32[8,1024]{1,0:T(8,128)S(1)}, u32[]{:S(2)}, u32[]{:S(2)}) collective-permute-start(f32[8,1024]{1,0:T(8,128)S(1)} %col_pass.3), channel_id=1, source_target_pairs={{0,16},{16,0},{32,48},{48,32},{64,80},{80,64},{96,112},{112,96},{1... | collective-permute-start | bytes 98312 | tf_op jit(solution)/shard_map/ppermute | solution.py:368
  77.9 5.2 %collective-permute-start.11 = (f32[8,1024]{1,0:T(8,128)S(1)}, f32[8,1024]{1,0:T(8,128)S(1)}, u32[]{:S(2)}, u32[]{:S(2)}) collective-permute-start(f32[8,1024]{1,0:T(8,128)S(1)} %add.17.refs_0_.refs_3_.refs_4_.refs_1_), channel_id=1, source_target_pairs={{0,96},{16,112},{32,64},{48,80},{64,32},{80,48},{96,0},{112,16},{1... | collective-permute-start | bytes 98312 | tf_op jit(solution)/shard_map/ppermute | solution.py:368
  79.3 4.3 %collective-permute-start.10 = (f32[8,1024]{1,0:T(8,128)S(1)}, f32[8,1024]{1,0:T(8,128)S(1)}, u32[]{:S(2)}, u32[]{:S(2)}) collective-permute-start(f32[8,1024]{1,0:T(8,128)S(1)} %add.17.refs_0_.refs_3_.refs_4_.refs_1_), channel_id=1, source_target_pairs={{0,64},{16,80},{32,96},{48,112},{64,0},{80,16},{96,32},{112,48},{1... | collective-permute-start | bytes 98312 | tf_op jit(solution)/shard_map/ppermute | solution.py:368
  80.4 3.1 %collective-permute-start.9 = (f32[8,1024]{1,0:T(8,128)S(1)}, f32[8,1024]{1,0:T(8,128)S(1)}, u32[]{:S(2)}, u32[]{:S(2)}) collective-permute-start(f32[8,1024]{1,0:T(8,128)S(1)} %add.17.refs_0_.refs_3_.refs_4_.refs_1_), channel_id=1, source_target_pairs={{0,32},{16,48},{32,0},{48,16},{64,96},{80,112},{96,64},{112,80},{1... | collective-permute-start | bytes 98312 | tf_op jit(solution)/shard_map/ppermute | solution.py:368
  83.6 11.7 %copy-start = (bf16[256,8192]{1,0:T(8,128)(2,1)S(1)}, bf16[256,8192]{1,0:T(8,128)(2,1)}, u32[]{:S(2)}) copy-start(bf16[256,8192]{1,0:T(8,128)(2,1)} %refs_14_.1) | copy-start | bytes 12582916
  98.2 8.8 %collective-permute-start.12 = (bf16[4,32,3072]{2,1,0:T(8,128)(2,1)S(1)}, bf16[4,32,3072]{2,1,0:T(8,128)(2,1)S(1)}, u32[]{:S(2)}, u32[]{:S(2)}) collective-permute-start(bf16[4,32,3072]{2,1,0:T(8,128)(2,1)S(1)} %get-tuple-element.52), channel_id=1, source_target_pairs={{0,16},{16,0},{32,48},{48,32},{64,80},{80,64},{96,112},{112,96},{1... | collective-permute-start | bytes 2359304 | tf_op jit(solution)/shard_map/ppermute | solution.py:368
  107.0 19.5 %collective-permute-start.16 = (bf16[4,32,5120]{2,1,0:T(8,128)(2,1)}, bf16[4,32,5120]{2,1,0:T(8,128)(2,1)}, u32[]{:S(2)}, u32[]{:S(2)}) collective-permute-start(bf16[4,32,5120]{2,1,0:T(8,128)(2,1)} %get-tuple-element.64), channel_id=1, source_target_pairs={{0,16},{16,0},{32,48},{48,32},{64,80},{80,64},{96,112},{112,96},{1... | collective-permute-start | bytes 3932168 | tf_op jit(solution)/shard_map/ppermute | solution.py:368
  107.2 6.3 %collective-permute-start.13 = (bf16[32,3072]{1,0:T(8,128)(2,1)S(1)}, bf16[32,3072]{1,0:T(8,128)(2,1)S(1)}, u32[]{:S(2)}, u32[]{:S(2)}) collective-permute-start(bf16[32,3072]{1,0:T(8,128)(2,1)S(1)} %get-tuple-element.54), channel_id=1, source_target_pairs={{0,32},{16,48},{32,0},{48,16},{64,96},{80,112},{96,64},{112,80},{1... | collective-permute-start | bytes 589832 | tf_op jit(solution)/shard_map/ppermute | solution.py:368
  107.9 10.6 %collective-permute-start.14 = (bf16[32,3072]{1,0:T(8,128)(2,1)S(1)}, bf16[32,3072]{1,0:T(8,128)(2,1)S(1)}, u32[]{:S(2)}, u32[]{:S(2)}) collective-permute-start(bf16[32,3072]{1,0:T(8,128)(2,1)S(1)} %get-tuple-element.55), channel_id=1, source_target_pairs={{0,64},{16,80},{32,96},{48,112},{64,0},{80,16},{96,32},{112,48},{1... | collective-permute-start | bytes 589832 | tf_op jit(solution)/shard_map/ppermute | solution.py:368
  109.7 11.2 %collective-permute-start.15 = (bf16[32,3072]{1,0:T(8,128)(2,1)S(1)}, bf16[32,3072]{1,0:T(8,128)(2,1)S(1)}, u32[]{:S(2)}, u32[]{:S(2)}) collective-permute-start(bf16[32,3072]{1,0:T(8,128)(2,1)S(1)} %get-tuple-element.56), channel_id=1, source_target_pairs={{0,96},{16,112},{32,64},{48,80},{64,32},{80,48},{96,0},{112,16},{1... | collective-permute-start | bytes 589832 | tf_op jit(solution)/shard_map/ppermute | solution.py:368
  122.2 15.8 %all-to-all-start.4 = ((f32[16,40,256]{2,1,0:T(8,128)}), f32[16,40,256]{2,1,0:T(8,128)}, u32[]{:S(2)}, u32[]{:S(2)}) async-start(f32[16,40,256]{2,1,0:T(8,128)} %feature.1.refs_0_), calls=%async_computation.4 | async-start | bytes 1310720 | tf_op jit(solution)/shard_map/all_to_all | solution.py:365
  128.8 0.8 copy-start.2
  129.7 22.7 %collective-permute-start.17 = (bf16[32,5120]{1,0:T(8,128)(2,1)}, bf16[32,5120]{1,0:T(8,128)(2,1)S(1)}, u32[]{:S(2)}, u32[]{:S(2)}) collective-permute-start(bf16[32,5120]{1,0:T(8,128)(2,1)} %get-tuple-element.66), channel_id=1, source_target_pairs={{0,32},{16,48},{32,0},{48,16},{64,96},{80,112},{96,64},{112,80},{1... | collective-permute-start | bytes 983048 | tf_op jit(solution)/shard_map/ppermute | solution.py:368
  129.7 22.7 %collective-permute-start.18 = (bf16[32,5120]{1,0:T(8,128)(2,1)}, bf16[32,5120]{1,0:T(8,128)(2,1)S(1)}, u32[]{:S(2)}, u32[]{:S(2)}) collective-permute-start(bf16[32,5120]{1,0:T(8,128)(2,1)} %get-tuple-element.67), channel_id=1, source_target_pairs={{0,64},{16,80},{32,96},{48,112},{64,0},{80,16},{96,32},{112,48},{1... | collective-permute-start | bytes 983048 | tf_op jit(solution)/shard_map/ppermute | solution.py:368
  132.3 20.2 %collective-permute-start.19 = (bf16[32,5120]{1,0:T(8,128)(2,1)S(1)}, bf16[32,5120]{1,0:T(8,128)(2,1)S(1)}, u32[]{:S(2)}, u32[]{:S(2)}) collective-permute-start(bf16[32,5120]{1,0:T(8,128)(2,1)S(1)} %get-tuple-element.68), channel_id=1, source_target_pairs={{0,96},{16,112},{32,64},{48,80},{64,32},{80,48},{96,0},{112,16},{1... | collective-permute-start | bytes 983048 | tf_op jit(solution)/shard_map/ppermute | solution.py:368
  152.5 1.1 copy-start.3

commit v2 on v0

--- a/solution.py
+++ b/solution.py
@@ -85,25 +85,13 @@
     return [(j, pl.ds(j * width, width)) for j in range(count)]
 
 
-def move(source, start, target, sems, count):
-    width = target.shape[1] // count
-    copies = [
-        pltpu.make_async_copy(
-            source.at[:, pl.ds(start + j * width, width)],
-            target.at[:, pl.ds(j * width, width)],
-            sems.at[j],
-        )
-        for j in range(count)
-    ]
-    for copy in copies:
-        copy.start()
-    return copies
-
-
-def store(source, target, cols, sem):
-    copy = pltpu.make_async_copy(source.at[:, cols], target.at[:, cols], sem)
-    copy.start()
-    return copy
+def arrive(copies, j, ahead):
+    if j == 0:
+        for copy in copies[:ahead]:
+            copy.start()
+    copies[j].wait()
+    if j + ahead < len(copies):
+        copies[j + ahead].start()
 
 
 def read_rows(message_ref, start, n):
@@ -162,26 +150,35 @@
 
 
 def proto_body(w_hbm, unit_hbm, inverse_ref, w_ref, unit_ref, in_sems, out_sems):
-    copies = move(w_hbm, 0, w_ref, in_sems, 8)
+    count = unit_ref.shape[0]
+    copies = [
+        pltpu.make_async_copy(w_hbm.at[:, cols], w_ref.at[:, cols], in_sems.at[j])
+        for j, cols in chunks(w_ref, count)
+    ]
     stores = []
-    for j, cols in chunks(w_ref):
-        copies[j].wait()
+    for j, cols in chunks(w_ref, count):
+        arrive(copies, j, 4)
         w = w_ref[:, cols].astype(F32)
         inverse = lax.rsqrt(jnp.sum(w * w, axis=0, keepdims=True) + EPS)
         inverse_ref[pl.ds(j, 1), :] = inverse
-        unit_ref[:, cols] = (w * inverse).astype(BF16)
-        stores.append(store(unit_ref, unit_hbm, cols, out_sems.at[j]))
-    for copy in stores:
-        copy.wait()
+        unit_ref[j] = (w * inverse).astype(BF16)
+        store = pltpu.make_async_copy(unit_ref.at[j], unit_hbm.at[j], out_sems.at[j])
+        store.start()
+        stores.append(store)
+    for store in stores:
+        store.wait()
 
 
 def table_body(rows_ref, unit_hbm, table_ref, sums_ref, unit_ref, sems):
-    copies = move(unit_hbm, 0, unit_ref, sems, 8)
+    copies = [
+        pltpu.make_async_copy(unit_hbm.at[j], unit_ref.at[j], sems.at[j])
+        for j in range(unit_ref.shape[0])
+    ]
     half = rows_ref.shape[1] // 2
     teacher = rows_ref[:, :half, :].reshape(-1, rows_ref.shape[2])
     for j, cols in chunks(table_ref):
-        copies[j].wait()
-        table = jnp.exp(mm(teacher, unit_ref[:, cols]) * (1.0 / TEACHER_TEMP)).astype(BF16)
+        arrive(copies, j, 3)
+        table = jnp.exp(mm(teacher, unit_ref[j]) * (1.0 / TEACHER_TEMP)).astype(BF16)
         table_ref[:, cols] = table
         sums_ref[pl.ds(j, 1), :] = jnp.sum(table.astype(F32), axis=0, keepdims=True)
 
@@ -203,17 +200,14 @@
         out_ref[pl.ds(j, 1), :] = jnp.sum(mm(terms, table_ref[:, cols]), axis=0, keepdims=True)
 
 
-def student_body(first, rows_ref, unit_hbm, table_ref, sums_ref, feature_ref, *refs):
-    unit_ref, sems = refs[-2:]
+def student_body(first, rows_ref, unit_ref, table_ref, sums_ref, feature_ref, *turned_refs):
     count = PIECES[first]
-    width = table_ref.shape[1] // count
-    copies = move(unit_hbm, sum(PIECES[:first]) * width, unit_ref, sems, count)
+    start = sum(PIECES[:first])
     half = rows_ref.shape[1] // 2
     student = rows_ref[:, half:, :].reshape(-1, rows_ref.shape[2])
     total = jnp.zeros((16, student.shape[0]), F32)
     for j, cols in chunks(table_ref, count):
-        copies[j].wait()
-        unit = unit_ref[:, cols]
+        unit = unit_ref[start + j]
         table = jnp.exp(mm(student, unit) * (1.0 / STUDENT_TEMP)).astype(BF16)
         table_ref[:, cols] = table
         total += mm(jnp.ones((16, table.shape[1]), BF16), table, NT)
@@ -223,22 +217,20 @@
         else:
             feature_ref[...] += part
     sums_ref[...] = total[0:8]
-    if len(refs) > 2:
+    for turned_ref in turned_refs:
         d = student.shape[1]
         eye = (
             lax.broadcasted_iota(jnp.int32, (d, d), 0)
             == lax.broadcasted_iota(jnp.int32, (d, d), 1)
         ).astype(BF16)
-        refs[0][...] = mm(eye, student, NT).astype(BF16)
+        turned_ref[...] = mm(eye, student, NT).astype(BF16)
 
 
 def codes_feature_body(*refs):
-    *sums_refs, table_ref, unit_hbm, feature_ref, unit_ref, sems = refs
-    copies = move(unit_hbm, 0, unit_ref, sems, 8)
+    *sums_refs, table_ref, unit_ref, feature_ref = refs
     scale = 1.0 / column_sum(sums_refs)
     for j, cols in chunks(table_ref):
-        copies[j].wait()
-        scaled = (unit_ref[:, cols].astype(F32) * scale[j : j + 1, :]).astype(BF16)
+        scaled = (unit_ref[j].astype(F32) * scale[j : j + 1, :]).astype(BF16)
         part = mm(scaled, table_ref[:, cols], NT)
         if j == 0:
             feature_ref[...] = part
@@ -254,62 +246,55 @@
 def head_body(parts, *refs):
     place_ref, first_ref, last_ref = refs[:3]
     sums_refs = refs[3 : 3 + parts]
-    turned_ref, inverse_ref, codes_ref, *piece_refs, w_hbm = refs[3 + parts : -6]
-    own_ref, keep_ref, near_ref, turn_ref, w_ref, sems = refs[-6:]
+    turned_ref, inverse_ref, codes_ref, *piece_refs, w_ref = refs[3 + parts : -7]
+    own_hbm, own_near_ref, keep_ref, near_ref, turn_ref, own_ref, sems = refs[-7:]
     x, core = place_ref[1], place_ref[2]
-    chips = near_ref.shape[0]
     share = near_ref.shape[1]
-    protos = codes_ref.shape[1]
-    count = 8
-    width = protos // count
+    chips = near_ref.shape[0] + 1
     spots = []
     for k in range(chips):
-        spots += [2 * (x ^ k) + core, 2 * (x ^ k) + 1 - core]
-    copies = []
-    for j in range(count):
-        copies.append([])
-        for m, spot in enumerate(spots):
-            copy = pltpu.make_async_copy(
-                w_hbm.at[pl.ds(pl.multiple_of(spot * share, share), share), pl.ds(j * width, width)],
-                w_ref.at[pl.ds(m * share, share), pl.ds(j * width, width)],
-                sems.at[j, m],
-            )
-            copy.start()
-            copies[j].append(copy)
+        for side in (core, 1 - core):
+            spots.append(pl.ds(pl.multiple_of((2 * (x ^ k) + side) * share, share), share))
     for m, spot in enumerate(spots):
-        turn_ref[pl.ds(m * share, share), :] = turned_ref[
-            pl.ds(pl.multiple_of(spot * share, share), share), :
-        ]
+        turn_ref[pl.ds(m * share, share), :] = turned_ref[spot, :]
     weights, exp_total, total = row_factors(first_ref, last_ref, codes_ref.shape[0])
     turned = turn_ref[...].astype(F32)
     left_probs = (turned * (weights / exp_total * (1.0 / STUDENT_TEMP))).astype(BF16)
     left_codes = (turned * (weights / total * (1.0 / STUDENT_TEMP))).astype(BF16)
     scale = 1.0 / column_sum(sums_refs)
-    piece, at = 0, 0
-    for j, cols in chunks(codes_ref, count):
-        probs = piece_refs[piece][:, pl.ds(at * width, width)]
-        at += 1
-        if at == PIECES[piece]:
-            piece, at = piece + 1, 0
-        head = mm(left_probs, probs) - scale[j : j + 1, :] * mm(left_codes, codes_ref[:, cols])
-        for copy in copies[j]:
-            copy.wait()
+    where = [(p, at) for p, size in enumerate(PIECES) for at in range(size)]
+    stores = []
+    for j, cols in chunks(codes_ref):
+        piece, at = where[j]
+        width = codes_ref.shape[1] // len(where)
+        head = mm(left_probs, piece_refs[piece][:, pl.ds(at * width, width)]) - scale[
+            j : j + 1, :
+        ] * mm(left_codes, codes_ref[:, cols])
         inverse = inverse_ref[pl.ds(j, 1), :]
-        unit = w_ref[:, cols].astype(F32) * inverse
+        w = jnp.concatenate([w_ref[spot, cols] for spot in spots], axis=0)
+        unit = w.astype(F32) * inverse
         inner = jnp.sum(unit * head, axis=0, keepdims=True)
         grad = inverse * (head - unit * inner)
         own_ref[:, cols] = grad[0:share]
-        for k in range(chips):
+        store = pltpu.make_async_copy(own_ref.at[:, cols], own_hbm.at[:, cols], sems.at[j])
+        store.start()
+        stores.append(store)
+        own_near_ref[:, cols] = grad[share : 2 * share].astype(BF16)
+        for k in range(1, chips):
             low = 2 * k * share
-            if k:
-                keep_ref[k - 1, :, cols] = grad[low : low + share]
-            near_ref[k, :, cols] = grad[low + share : low + 2 * share].astype(BF16)
-
-
-def pair_body(own_ref, keep_ref, near_ref, out_ref, *pair_refs):
-    out_ref[...] = own_ref[...] + near_ref[0].astype(F32)
+            keep_ref[k - 1, :, cols] = grad[low : low + share].astype(BF16)
+            near_ref[k - 1, :, cols] = grad[low + share : low + 2 * share].astype(BF16)
+    for store in stores:
+        store.wait()
+
+
+def pair_body(keep_ref, near_ref, *pair_refs):
     for k, pair_ref in enumerate(pair_refs):
-        pair_ref[...] = (keep_ref[k] + near_ref[k + 1].astype(F32)).astype(BF16)
+        pair_ref[...] = (keep_ref[k].astype(F32) + near_ref[k].astype(F32)).astype(BF16)
+
+
+def own_sum_body(own_ref, near_ref, out_ref):
+    out_ref[...] = own_ref[...] + near_ref[...].astype(F32)
 
 
 def final_body(own_ref, *refs):
@@ -392,13 +377,13 @@
     unit, inverse = call(
         proto_body,
         "proto_unit",
-        (pltpu.HBM((d, protos), BF16), shape((8, width), F32)),
+        (pltpu.HBM((8, d, width), BF16), shape((8, width), F32)),
         (proto_weight,),
         product,
         specs=[HBM],
         scratch=[
             pltpu.VMEM((d, protos), BF16),
-            pltpu.VMEM((d, protos), BF16),
+            pltpu.VMEM((8, d, width), BF16),
             pltpu.SemaphoreType.DMA((8,)),
             pltpu.SemaphoreType.DMA((8,)),
         ],
@@ -410,7 +395,7 @@
         (all_rows, unit),
         2 * product,
         specs=[VMEM, HBM],
-        scratch=[pltpu.VMEM((d, protos), BF16), pltpu.SemaphoreType.DMA((8,))],
+        scratch=[pltpu.VMEM((8, d, width), BF16), pltpu.SemaphoreType.DMA((8,))],
     )
 
     messages = []
@@ -428,9 +413,7 @@
                 + ((shape((d, rows), BF16),) if last else ()),
                 (all_rows, unit),
                 product,
-                specs=[VMEM, HBM],
                 after=(sums,),
-                scratch=[pltpu.VMEM((d, span), BF16), pltpu.SemaphoreType.DMA((PIECES[sweep],))],
             )
         )
         part = call(
@@ -453,13 +436,14 @@
 
     turned = pieces[-1][3]
     factors = (messages[0], messages[-1])
-    own_block, keep, near = call(
+    own_block, own_near, keep, near = call(
         functools.partial(head_body, chips),
         "head",
         (
-            shape((share, protos), F32),
-            shape((chips - 1, share, protos), F32),
-            shape((chips, share, protos), BF16),
+            pltpu.HBM((share, protos), F32),
+            shape((share, protos), BF16),
+            shape((chips - 1, share, protos), BF16),
+            shape((chips - 1, share, protos), BF16),
         ),
         (
             place,
@@ -472,11 +456,11 @@
             proto_weight,
         ),
         4 * product,
-        specs=[SMEM] + [VMEM] * (len(factors) + chips + 3 + len(pieces)) + [HBM],
+        specs=[SMEM] + [VMEM] * (len(factors) + chips + 4 + len(pieces)),
         scratch=[
             pltpu.VMEM((d, rows), BF16),
-            pltpu.VMEM((d, protos), BF16),
-            pltpu.SemaphoreType.DMA((8, n_patch)),
+            pltpu.VMEM((share, protos), F32),
+            pltpu.SemaphoreType.DMA((8,)),
         ],
     )
     codes_feature = call(
@@ -485,28 +469,24 @@
         shape((d, rows), F32),
         (*parts, codes, unit),
         product,
-        specs=[VMEM] * (chips + 1) + [HBM],
-        after=(own_block,),
-        scratch=[pltpu.VMEM((d, protos), BF16), pltpu.SemaphoreType.DMA((8,))],
-    )
-    own_block, *pairs = call(
-        pair_body,
-        "pair_sums",
-        (shape((share, protos), F32),)
-        + tuple(shape((share, protos), BF16) for _ in range(chips - 1)),
-        (own_block, keep, hop(near, 1)),
-        product // 4,
-        after=(codes_feature,),
-    )
-    far = [hop(pair, 2 * (k + 1)) for k, pair in enumerate(pairs)]
+        after=(keep,),
+    )
     feature_part = call(
         feature_body,
         "feature",
         shape((n_proto, own + 8, d), F32),
         (*factors, codes_feature, turned, *[piece[2] for piece in pieces]),
         product // 4,
-        after=(own_block,),
-    )
+    )
+    pairs = call(
+        pair_body,
+        "pair_sums",
+        tuple(shape((share, protos), BF16) for _ in range(chips - 1)),
+        (keep, hop(near, 1)),
+        product // 8,
+        after=(feature_part,),
+    )
+    far = [hop(pair, 2 * (k + 1)) for k, pair in enumerate(pairs)]
     grad_student, tails = call(
         owner_body,
         "owner",
@@ -514,13 +494,20 @@
         (exchange(feature_part, "proto"), x_rows),
         product // 8,
     )
+    own_sum = call(
+        own_sum_body,
+        "own_sum",
+        shape((share, protos), F32),
+        (own_block, hop(own_near, 1)),
+        product // 8,
+        after=(tails,),
+    )
     grad_proto = call(
         final_body,
         "assemble",
         shape((share, protos), F32),
-        (own_block, *far),
+        (own_sum, *far),
         product // 4,
-        after=(tails,),
     )
     losses = jnp.sum(exchange(tails, "patch"), axis=0)
     return (grad_student, grad_proto, losses[0, 0] / losses[0, 1])

time: 155 us -> 151 us (0.974)
  Pallas kernels: 51.8 us -> 47.6 us
  waiting for transfers between devices: 28.9 us -> 26.8 us
    ppermute x16 -> x17, waiting for transfers between devices: 13.3 us -> 3.88 us  [hop(): return lax.ppermute(array, 'patch', [(i, i ^ bits) for i in range(n_patch)])]
    all_to_all x3, waiting for transfers between devices: 15.6 us -> 23 us  [exchange(): return lax.all_to_all(array, axis, 0, 0)]
    pallas_call x17 -> x18, Pallas kernels: 51.8 us -> 47.6 us  [call(): pl.pallas_call(ordered, name=name, out_shape=out_shape, in_specs=[ANY] *...]
    ppermute x16 -> x17, starting transfers between devices: 24.7 us -> 25.2 us  [hop(): return lax.ppermute(array, 'patch', [(i, i ^ bits) for i in range(n_patch)])]
  transfers between devices with their start and end apart: 19 -> 20, of which waited for: 8 -> 8; matrix products, arithmetic and copies ran while one was open for 0% -> 0% of each run, Pallas kernels for 13% -> 13%
where the time goes in v2:
time: 151 us; the launch traced here: 150 us
  Pallas kernels  47.6 us (32%)
  starting transfers between devices  42.2 us (28%)
  blocking collectives  27.9 us (18%)
  waiting for transfers between devices  26.8 us (18%)
  between operations  3.35 us (2%)
  local copies, waits for them, and re-layouts  1.82 us (1%)
    pallas_call x18, Pallas kernels, call(): pl.pallas_call(ordered, name=name, out_shape=out_shape, in_specs=[ANY] *...  47.6 us
    all_to_all x3, blocking collectives, exchange(): return lax.all_to_all(array, axis, 0, 0)  27.9 us
    ppermute x17, starting transfers between devices, hop(): return lax.ppermute(array, 'patch', [(i, i ^ bits) for i in range(n_patch)])  25.2 us
    all_to_all x3, waiting for transfers between devices, exchange(): return lax.all_to_all(array, axis, 0, 0)  23 us
    all_to_all x3, starting transfers between devices, exchange(): return lax.all_to_all(array, axis, 0, 0)  17 us
    ppermute x17, waiting for transfers between devices, hop(): return lax.ppermute(array, 'patch', [(i, i ^ bits) for i in range(n_patch)])  3.88 us
  transfers between devices with their start and end apart: 20, of which 8 were waited for; matrix products, arithmetic and copies ran while one was open for 0% of the time, Pallas kernels for 13%

profile of v2, /device:TPU:1, one launch (start us, length us, event | category | flops | bytes accessed | tf_op | source)
XLA Modules:
  0.0 149.8 jit_solution(11382809763146442457)
XLA Ops:
  0.6 0.1 pad_add_fusion.refs_0_
  0.7 2.7 %own_rows.1 = (bf16[16,64,256]{2,1,0:T(8,128)(2,1)}, f32[32,256]{1,0:T(8,128)S(1)}, f32[8,512]{1,0:T(8,128)S(1)}) custom-call(s32[3]{0:T(128)S(1)} %pad_add_fusion.refs_0_, bf16[256,256]{1,0:T(8,128)(2,1)} %refs_1_.1, bf16[256,256]{1,0:T(8,128)(2,1)} %refs_2_.1, s32[1,32]{1,0:T(1,128)} %bitcast.6, bf16[1,32]{1,0:T(2,128)(2,1)} %bitcast.7), custom_call_target="tpu_custom_call" | custom-call | flops 268435456 | bytes 65536 | tf_op jit(solution)/shard_map/own_rows/pallas_call | solution.py:52
  3.4 8.6 %all-to-all-start = ((bf16[16,64,256]{2,1,0:T(8,128)(2,1)}), bf16[16,64,256]{2,1,0:T(8,128)(2,1)S(1)}, u32[]{:S(2)}, u32[]{:S(2)}) async-start(bf16[16,64,256]{2,1,0:T(8,128)(2,1)} %get-tuple-element.29), calls=%async_computation | async-start | bytes 1048576 | tf_op jit(solution)/shard_map/all_to_all | solution.py:352
  12.0 4.7 %proto_unit.1 = (bf16[8,256,1024]{2,1,0:T(8,128)(2,1)}, f32[8,1024]{1,0:T(8,128)S(1)}) custom-call(bf16[256,8192]{1,0:T(8,128)(2,1)} %refs_13_.1), custom_call_target="tpu_custom_call" | custom-call | flops 2147483648 | bytes 65536 | tf_op jit(solution)/shard_map/proto_unit/pallas_call | solution.py:52
  16.7 5.8 %all-to-all-done.refs_0_.refs_1_ = bf16[16,64,256]{2,1,0:T(8,128)(2,1)S(1)} async-done(((bf16[16,64,256]{2,1,0:T(8,128)(2,1)}), bf16[16,64,256]{2,1,0:T(8,128)(2,1)S(1)}, u32[]{:S(2)}, u32[]{:S(2)}) %all-to-all-start) | async-done | bytes 524320 | tf_op jit(solution)/shard_map/all_to_all | solution.py:352
  22.5 6.1 %teacher_table.1 = (bf16[512,8192]{1,0:T(8,128)(2,1)S(1)}, f32[8,1024]{1,0:T(8,128)S(1)}) custom-call(bf16[16,64,256]{2,1,0:T(8,128)(2,1)S(1)} %all-to-all-done.refs_0_.refs_1_, bf16[8,256,1024]{2,1,0:T(8,128)(2,1)} %get-tuple-element.30.refs_1_.refs_2_.refs_6_), custom_call_target="tpu_custom_call" | custom-call | flops 4294967296 | bytes 65536 | tf_op jit(solution)/shard_map/teacher_table/pallas_call | solution.py:52
  28.7 2.1 %collective-permute-start = (f32[8,1024]{1,0:T(8,128)S(1)}, f32[8,1024]{1,0:T(8,128)S(1)}, u32[]{:S(2)}, u32[]{:S(2)}) collective-permute-start(f32[8,1024]{1,0:T(8,128)S(1)} %get-tuple-element.31), channel_id=1, source_target_pairs={{0,16},{16,0},{32,48},{48,32},{64,80},{80,64},{96,112},{112,96},{1... | collective-permute-start | bytes 98312 | tf_op jit(solution)/shard_map/ppermute | solution.py:355
  30.7 0.9 collective-permute-done
  31.6 2.5 %collective-permute-start.3 = (f32[8,1024]{1,0:T(8,128)S(1)}, f32[8,1024]{1,0:T(8,128)S(1)}, u32[]{:S(2)}, u32[]{:S(2)}) collective-permute-start(f32[8,1024]{1,0:T(8,128)S(1)} %add.15.refs_0_.refs_1_), channel_id=1, source_target_pairs={{0,96},{16,112},{32,64},{48,80},{64,32},{80,48},{96,0},{112,16},{1... | collective-permute-start | bytes 98312 | tf_op jit(solution)/shard_map/ppermute | solution.py:355
  34.1 0.5 collective-permute-start.2
  34.6 0.3 collective-permute-start.1
  34.9 2.7 %student_table.3 = (bf16[512,3072]{1,0:T(8,128)(2,1)S(1)}, f32[8,512]{1,0:T(8,128)S(1)}, f32[256,512]{1,0:T(8,128)S(1)}) custom-call(f32[8,1024]{1,0:T(8,128)S(1)} %add.15.refs_0_.refs_1_, bf16[16,64,256]{2,1,0:T(8,128)(2,1)S(1)} %all-to-all-done.refs_0_.refs_1_, bf16[8,256,1024]{2,1,0:T(8,128)(2,1)S(1)} %copy-done), custom_call_target="tpu_custom_call" | custom-call | flops 2147483648 | bytes 65536 | tf_op jit(solution)/shard_map/student_table/pallas_call | solution.py:52
  37.5 0.0 collective-permute-done.3.refs_4_
  37.5 0.8 collective-permute-done.2.refs_3_
  38.3 0.0 collective-permute-done.1.refs_2_
  38.3 2.3 %row_pass.3 = f32[16,8,128]{2,1,0:T(8,128)S(1)} custom-call(f32[8,512]{1,0:T(8,128)S(1)} %get-tuple-element.32.refs_0_.refs_5_, f32[8,1024]{1,0:T(8,128)S(1)} %add.15.refs_0_.refs_1_, f32[8,1024]{1,0:T(8,128)S(1)} %collective-permute-done.1.refs_2_, f32[8,1024]{1,0:T(8,128)S(1)} %collective-permute-done.2.refs_3_, ...), custom_call_target="tpu_custom_call" | custom-call | flops 2147483648 | bytes 65536 | tf_op jit(solution)/shard_map/row_pass/pallas_call | solution.py:52
  40.7 9.2 %all_to_all.30.refs_0_.refs_1_ = f32[16,8,128]{2,1,0:T(8,128)S(1)} all-to-all(f32[16,8,128]{2,1,0:T(8,128)S(1)} %row_pass.3), channel_id=1, replica_groups=mesh['patch'=8,'proto'=16] {'proto'}, dimensions={0} | all-to-all | bytes 131072 | tf_op jit(solution)/shard_map/all_to_all | solution.py:352
  49.8 1.2 col_pass.2
  51.1 3.3 %collective-permute-start.4 = (f32[8,1024]{1,0:T(8,128)S(1)}, f32[8,1024]{1,0:T(8,128)S(1)}, u32[]{:S(2)}, u32[]{:S(2)}) collective-permute-start(f32[8,1024]{1,0:T(8,128)S(1)} %col_pass.2), channel_id=1, source_target_pairs={{0,16},{16,0},{32,48},{48,32},{64,80},{80,64},{96,112},{112,96},{1... | collective-permute-start | bytes 98312 | tf_op jit(solution)/shard_map/ppermute | solution.py:355
  54.4 0.9 collective-permute-done.4
  55.2 1.1 collective-permute-start.7
  56.3 0.8 collective-permute-start.6
  57.1 1.3 collective-permute-start.5
  58.5 2.7 %student_table.4 = (bf16[512,3072]{1,0:T(8,128)(2,1)S(1)}, f32[8,512]{1,0:T(8,128)S(1)}, f32[256,512]{1,0:T(8,128)S(1)}) custom-call(f32[8,1024]{1,0:T(8,128)S(1)} %add.16.refs_0_.refs_1_, bf16[16,64,256]{2,1,0:T(8,128)(2,1)S(1)} %all-to-all-done.refs_0_.refs_1_, bf16[8,256,1024]{2,1,0:T(8,128)(2,1)S(1)} %copy-done), custom_call_target="tpu_custom_call" | custom-call | flops 2147483648 | bytes 65536 | tf_op jit(solution)/shard_map/student_table/pallas_call | solution.py:52
  61.2 0.0 collective-permute-done.7.refs_4_
  61.2 0.0 collective-permute-done.6.refs_3_
  61.2 0.0 collective-permute-done.5.refs_2_
  61.2 2.3 %row_pass.4 = f32[16,8,128]{2,1,0:T(8,128)S(1)} custom-call(f32[8,512]{1,0:T(8,128)S(1)} %get-tuple-element.35.refs_0_.refs_6_, f32[8,1024]{1,0:T(8,128)S(1)} %add.16.refs_0_.refs_1_, f32[8,1024]{1,0:T(8,128)S(1)} %collective-permute-done.5.refs_2_, f32[8,1024]{1,0:T(8,128)S(1)} %collective-permute-done.6.refs_3_, ...), custom_call_target="tpu_custom_call" | custom-call | flops 2147483648 | bytes 65536 | tf_op jit(solution)/shard_map/row_pass/pallas_call | solution.py:52
  63.5 9.4 %all_to_all.31.refs_0_ = f32[16,8,128]{2,1,0:T(8,128)S(1)} all-to-all(f32[16,8,128]{2,1,0:T(8,128)S(1)} %row_pass.4), channel_id=1, replica_groups=mesh['patch'=8,'proto'=16] {'proto'}, dimensions={0} | all-to-all | bytes 131072 | tf_op jit(solution)/shard_map/all_to_all | solution.py:352
  72.9 1.2 col_pass.3
  74.1 2.9 %collective-permute-start.8 = (f32[8,1024]{1,0:T(8,128)S(1)}, f32[8,1024]{1,0:T(8,128)S(1)}, u32[]{:S(2)}, u32[]{:S(2)}) collective-permute-start(f32[8,1024]{1,0:T(8,128)S(1)} %col_pass.3), channel_id=1, source_target_pairs={{0,16},{16,0},{32,48},{48,32},{64,80},{80,64},{96,112},{112,96},{1... | collective-permute-start | bytes 98312 | tf_op jit(solution)/shard_map/ppermute | solution.py:355
  77.0 0.9 collective-permute-done.8
  77.8 1.4 collective-permute-start.11
  79.2 1.1 collective-permute-start.10
  80.4 0.7 collective-permute-start.9
  81.1 1.9 %student_table.5 = (bf16[512,2048]{1,0:T(8,128)(2,1)S(1)}, f32[8,512]{1,0:T(8,128)S(1)}, f32[256,512]{1,0:T(8,128)S(1)}, bf16[256,512]{1,0:T(8,128)(2,1)S(1)}) custom-call(f32[8,1024]{1,0:T(8,128)S(1)} %add.17.refs_0_.refs_3_.refs_1_, bf16[16,64,256]{2,1,0:T(8,128)(2,1)S(1)} %all-to-all-done.refs_0_.refs_1_, bf16[8,256,1024]{2,1,0:T(8,128)(2,1)S(1)} %copy-done), custom_call_target="tpu_custom_call" | custom-call | flops 2147483648 | bytes 65536 | tf_op jit(solution)/shard_map/student_table/pallas_call | solution.py:52
  83.0 0.0 collective-permute-done.11.refs_3_.refs_6_.refs_4_
  83.0 0.5 collective-permute-done.10.refs_2_.refs_5_.refs_3_
  83.5 0.0 collective-permute-done.9.refs_1_.refs_4_.refs_2_
  83.5 2.3 %row_pass.5 = f32[16,8,128]{2,1,0:T(8,128)S(1)} custom-call(f32[8,1024]{1,0:T(8,128)S(1)} %add.17.refs_0_.refs_3_.refs_1_, f32[8,1024]{1,0:T(8,128)S(1)} %collective-permute-done.9.refs_1_.refs_4_.refs_2_, f32[8,1024]{1,0:T(8,128)S(1)} %collective-permute-done.10.refs_2_.refs_5_.refs_3_, f32[8,1024]{1,0:T(8,128)S(1)} %collective-permute-done.11.refs_3_.refs_6_.refs_4_, ...), custom_call_target="tpu_custom_call" | custom-call | flops 2147483648 | bytes 65536 | tf_op jit(solution)/shard_map/row_pass/pallas_call | solution.py:52
  85.8 9.4 %all_to_all.32.refs_2_.refs_1_ = f32[16,8,128]{2,1,0:T(8,128)S(1)} all-to-all(f32[16,8,128]{2,1,0:T(8,128)S(1)} %row_pass.5), channel_id=1, replica_groups=mesh['patch'=8,'proto'=16] {'proto'}, dimensions={0} | all-to-all | bytes 131072 | tf_op jit(solution)/shard_map/all_to_all | solution.py:352
  95.2 8.4 %head.1 = (f32[32,8192]{1,0:T(8,128)}, bf16[32,8192]{1,0:T(8,128)(2,1)S(1)}, bf16[3,32,8192]{2,1,0:T(8,128)(2,1)S(1)}, bf16[3,32,8192]{2,1,0:T(8,128)(2,1)}) custom-call(s32[3]{0:T(128)S(1)} %pad_add_fusion.refs_0_, f32[16,8,128]{2,1,0:T(8,128)S(1)} %all_to_all.30.refs_0_.refs_1_, f32[16,8,128]{2,1,0:T(8,128)S(1)} %all_to_all.32.refs_2_.refs_1_, ...), custom_call_target="tpu_custom_call" | custom-call | flops 8589934592 | bytes 65536 | tf_op jit(solution)/shard_map/head/pallas_call | solution.py:52
  103.6 3.3 %collective-permute-start.13 = (bf16[3,32,8192]{2,1,0:T(8,128)(2,1)}, bf16[3,32,8192]{2,1,0:T(8,128)(2,1)S(1)}, u32[]{:S(2)}, u32[]{:S(2)}) collective-permute-start(bf16[3,32,8192]{2,1,0:T(8,128)(2,1)} %get-tuple-element.51), channel_id=1, source_target_pairs={{0,16},{16,0},{32,48},{48,32},{64,80},{80,64},{96,112},{112,96},{1... | collective-permute-start | bytes 4718600 | tf_op jit(solution)/shard_map/ppermute | solution.py:355
  106.9 2.4 %codes_feature.1.refs_2_ = f32[256,512]{1,0:T(8,128)S(1)} custom-call(bf16[3,32,8192]{2,1,0:T(8,128)(2,1)S(1)} %get-tuple-element.42.refs_0_.refs_1_, f32[8,1024]{1,0:T(8,128)S(1)} %add.17.refs_0_.refs_3_.refs_1_, f32[8,1024]{1,0:T(8,128)S(1)} %collective-permute-done.9.refs_1_.refs_4_.refs_2_, ...), custom_call_target="tpu_custom_call" | custom-call | flops 2147483648 | bytes 65536 | tf_op jit(solution)/shard_map/codes_feature/pallas_call | solution.py:52
  109.2 1.2 feature.1.refs_0_
  110.4 4.3 %all-to-all-start.4 = ((f32[16,40,256]{2,1,0:T(8,128)}), f32[16,40,256]{2,1,0:T(8,128)}, u32[]{:S(2)}, u32[]{:S(2)}) async-start(f32[16,40,256]{2,1,0:T(8,128)} %feature.1.refs_0_), calls=%async_computation.4 | async-start | bytes 1310720 | tf_op jit(solution)/shard_map/all_to_all | solution.py:352
  114.7 0.1 collective-permute-start.12
  114.8 0.0 collective-permute-done.13.refs_2_
  114.8 1.4 pair_sums.1
  116.2 0.6 collective-permute-start.14
  116.9 1.8 %collective-permute-start.15 = (bf16[32,8192]{1,0:T(8,128)(2,1)}, bf16[32,8192]{1,0:T(8,128)(2,1)S(1)}, u32[]{:S(2)}, u32[]{:S(2)}) collective-permute-start(bf16[32,8192]{1,0:T(8,128)(2,1)} %get-tuple-element.53), channel_id=1, source_target_pairs={{0,64},{16,80},{32,96},{48,112},{64,0},{80,16},{96,32},{112,48},{1... | collective-permute-start | bytes 1572872 | tf_op jit(solution)/shard_map/ppermute | solution.py:355
  118.7 1.4 collective-permute-start.16
  120.1 7.8 %all-to-all-done.4.refs_0_ = f32[16,40,256]{2,1,0:T(8,128)} async-done(((f32[16,40,256]{2,1,0:T(8,128)}), f32[16,40,256]{2,1,0:T(8,128)}, u32[]{:S(2)}, u32[]{:S(2)}) %all-to-all-start.4) | async-done | bytes 655392 | tf_op jit(solution)/shard_map/all_to_all | solution.py:352
  127.9 1.9 %owner.1 = (f32[32,256]{1,0:T(8,128)}, f32[8,8,128]{2,1,0:T(8,128)}) custom-call(f32[16,40,256]{2,1,0:T(8,128)} %all-to-all-done.4.refs_0_, f32[32,256]{1,0:T(8,128)S(1)} %get-tuple-element.46.refs_1_), custom_call_target="tpu_custom_call" | custom-call | flops 268435456 | bytes 65536 | tf_op jit(solution)/shard_map/owner/pallas_call | solution.py:52
  129.8 4.1 %all-to-all-start.5 = ((f32[8,8,128]{2,1,0:T(8,128)}), f32[8,8,128]{2,1,0:T(8,128)S(1)}, u32[]{:S(2)}, u32[]{:S(2)}) async-start(f32[8,8,128]{2,1,0:T(8,128)} %get-tuple-element.48.refs_0_), calls=%async_computation.5 | async-start | bytes 65536 | tf_op jit(solution)/shard_map/all_to_all | solution.py:352
  133.9 0.0 collective-permute-done.12.refs_2_
  133.9 1.2 copy-done.1
  135.1 1.1 own_sum.1.refs_0_
  136.2 9.3 %all-to-all-done.5 = f32[8,8,128]{2,1,0:T(8,128)S(1)} async-done(((f32[8,8,128]{2,1,0:T(8,128)}), f32[8,8,128]{2,1,0:T(8,128)S(1)}, u32[]{:S(2)}, u32[]{:S(2)}) %all-to-all-start.5) | async-done | bytes 32800 | tf_op jit(solution)/shard_map/all_to_all | solution.py:352
  145.6 0.6 fusion
  147.5 0.0 collective-permute-done.14.refs_1_
  147.5 0.0 collective-permute-done.15.refs_2_
  147.5 0.0 collective-permute-done.16.refs_3_
  147.5 1.2 assemble.1
  (11 shorter events, 0.0 us)
Async XLA Ops:
  3.4 19.1 %all-to-all-start = ((bf16[16,64,256]{2,1,0:T(8,128)(2,1)}), bf16[16,64,256]{2,1,0:T(8,128)(2,1)S(1)}, u32[]{:S(2)}, u32[]{:S(2)}) async-start(bf16[16,64,256]{2,1,0:T(8,128)(2,1)} %get-tuple-element.29), calls=%async_computation | async-start | bytes 1048576 | tf_op jit(solution)/shard_map/all_to_all | solution.py:352
  22.5 12.3 %copy-start = (bf16[8,256,1024]{2,1,0:T(8,128)(2,1)S(1)}, bf16[8,256,1024]{2,1,0:T(8,128)(2,1)}, u32[]{:S(2)}) copy-start(bf16[8,256,1024]{2,1,0:T(8,128)(2,1)} %get-tuple-element.30.refs_1_.refs_2_.refs_6_) | copy-start | bytes 12582916
  28.7 2.9 %collective-permute-start = (f32[8,1024]{1,0:T(8,128)S(1)}, f32[8,1024]{1,0:T(8,128)S(1)}, u32[]{:S(2)}, u32[]{:S(2)}) collective-permute-start(f32[8,1024]{1,0:T(8,128)S(1)} %get-tuple-element.31), channel_id=1, source_target_pairs={{0,16},{16,0},{32,48},{48,32},{64,80},{80,64},{96,112},{112,96},{1... | collective-permute-start | bytes 98312 | tf_op jit(solution)/shard_map/ppermute | solution.py:355
  31.6 5.9 %collective-permute-start.3 = (f32[8,1024]{1,0:T(8,128)S(1)}, f32[8,1024]{1,0:T(8,128)S(1)}, u32[]{:S(2)}, u32[]{:S(2)}) collective-permute-start(f32[8,1024]{1,0:T(8,128)S(1)} %add.15.refs_0_.refs_1_), channel_id=1, source_target_pairs={{0,96},{16,112},{32,64},{48,80},{64,32},{80,48},{96,0},{112,16},{1... | collective-permute-start | bytes 98312 | tf_op jit(solution)/shard_map/ppermute | solution.py:355
  34.1 4.3 %collective-permute-start.2 = (f32[8,1024]{1,0:T(8,128)S(1)}, f32[8,1024]{1,0:T(8,128)S(1)}, u32[]{:S(2)}, u32[]{:S(2)}) collective-permute-start(f32[8,1024]{1,0:T(8,128)S(1)} %add.15.refs_0_.refs_1_), channel_id=1, source_target_pairs={{0,64},{16,80},{32,96},{48,112},{64,0},{80,16},{96,32},{112,48},{1... | collective-permute-start | bytes 98312 | tf_op jit(solution)/shard_map/ppermute | solution.py:355
  34.6 3.8 %collective-permute-start.1 = (f32[8,1024]{1,0:T(8,128)S(1)}, f32[8,1024]{1,0:T(8,128)S(1)}, u32[]{:S(2)}, u32[]{:S(2)}) collective-permute-start(f32[8,1024]{1,0:T(8,128)S(1)} %add.15.refs_0_.refs_1_), channel_id=1, source_target_pairs={{0,32},{16,48},{32,0},{48,16},{64,96},{80,112},{96,64},{112,80},{1... | collective-permute-start | bytes 98312 | tf_op jit(solution)/shard_map/ppermute | solution.py:355
  51.1 4.1 %collective-permute-start.4 = (f32[8,1024]{1,0:T(8,128)S(1)}, f32[8,1024]{1,0:T(8,128)S(1)}, u32[]{:S(2)}, u32[]{:S(2)}) collective-permute-start(f32[8,1024]{1,0:T(8,128)S(1)} %col_pass.2), channel_id=1, source_target_pairs={{0,16},{16,0},{32,48},{48,32},{64,80},{80,64},{96,112},{112,96},{1... | collective-permute-start | bytes 98312 | tf_op jit(solution)/shard_map/ppermute | solution.py:355
  55.2 5.9 %collective-permute-start.7 = (f32[8,1024]{1,0:T(8,128)S(1)}, f32[8,1024]{1,0:T(8,128)S(1)}, u32[]{:S(2)}, u32[]{:S(2)}) collective-permute-start(f32[8,1024]{1,0:T(8,128)S(1)} %add.16.refs_0_.refs_1_), channel_id=1, source_target_pairs={{0,96},{16,112},{32,64},{48,80},{64,32},{80,48},{96,0},{112,16},{1... | collective-permute-start | bytes 98312 | tf_op jit(solution)/shard_map/ppermute | solution.py:355
  56.3 4.8 %collective-permute-start.6 = (f32[8,1024]{1,0:T(8,128)S(1)}, f32[8,1024]{1,0:T(8,128)S(1)}, u32[]{:S(2)}, u32[]{:S(2)}) collective-permute-start(f32[8,1024]{1,0:T(8,128)S(1)} %add.16.refs_0_.refs_1_), channel_id=1, source_target_pairs={{0,64},{16,80},{32,96},{48,112},{64,0},{80,16},{96,32},{112,48},{1... | collective-permute-start | bytes 98312 | tf_op jit(solution)/shard_map/ppermute | solution.py:355
  57.1 4.0 %collective-permute-start.5 = (f32[8,1024]{1,0:T(8,128)S(1)}, f32[8,1024]{1,0:T(8,128)S(1)}, u32[]{:S(2)}, u32[]{:S(2)}) collective-permute-start(f32[8,1024]{1,0:T(8,128)S(1)} %add.16.refs_0_.refs_1_), channel_id=1, source_target_pairs={{0,32},{16,48},{32,0},{48,16},{64,96},{80,112},{96,64},{112,80},{1... | collective-permute-start | bytes 98312 | tf_op jit(solution)/shard_map/ppermute | solution.py:355
  74.1 3.7 %collective-permute-start.8 = (f32[8,1024]{1,0:T(8,128)S(1)}, f32[8,1024]{1,0:T(8,128)S(1)}, u32[]{:S(2)}, u32[]{:S(2)}) collective-permute-start(f32[8,1024]{1,0:T(8,128)S(1)} %col_pass.3), channel_id=1, source_target_pairs={{0,16},{16,0},{32,48},{48,32},{64,80},{80,64},{96,112},{112,96},{1... | collective-permute-start | bytes 98312 | tf_op jit(solution)/shard_map/ppermute | solution.py:355
  77.8 5.2 %collective-permute-start.11 = (f32[8,1024]{1,0:T(8,128)S(1)}, f32[8,1024]{1,0:T(8,128)S(1)}, u32[]{:S(2)}, u32[]{:S(2)}) collective-permute-start(f32[8,1024]{1,0:T(8,128)S(1)} %add.17.refs_0_.refs_3_.refs_1_), channel_id=1, source_target_pairs={{0,96},{16,112},{32,64},{48,80},{64,32},{80,48},{96,0},{112,16},{1... | collective-permute-start | bytes 98312 | tf_op jit(solution)/shard_map/ppermute | solution.py:355
  79.2 4.3 %collective-permute-start.10 = (f32[8,1024]{1,0:T(8,128)S(1)}, f32[8,1024]{1,0:T(8,128)S(1)}, u32[]{:S(2)}, u32[]{:S(2)}) collective-permute-start(f32[8,1024]{1,0:T(8,128)S(1)} %add.17.refs_0_.refs_3_.refs_1_), channel_id=1, source_target_pairs={{0,64},{16,80},{32,96},{48,112},{64,0},{80,16},{96,32},{112,48},{1... | collective-permute-start | bytes 98312 | tf_op jit(solution)/shard_map/ppermute | solution.py:355
  80.4 3.1 %collective-permute-start.9 = (f32[8,1024]{1,0:T(8,128)S(1)}, f32[8,1024]{1,0:T(8,128)S(1)}, u32[]{:S(2)}, u32[]{:S(2)}) collective-permute-start(f32[8,1024]{1,0:T(8,128)S(1)} %add.17.refs_0_.refs_3_.refs_1_), channel_id=1, source_target_pairs={{0,32},{16,48},{32,0},{48,16},{64,96},{80,112},{96,64},{112,80},{1... | collective-permute-start | bytes 98312 | tf_op jit(solution)/shard_map/ppermute | solution.py:355
  83.5 11.7 %copy-start.2 = (bf16[256,8192]{1,0:T(8,128)(2,1)S(1)}, bf16[256,8192]{1,0:T(8,128)(2,1)}, u32[]{:S(2)}) copy-start(bf16[256,8192]{1,0:T(8,128)(2,1)} %refs_13_.1) | copy-start | bytes 12582916
  103.6 5.7 %copy-start.3 = (bf16[32,8192]{1,0:T(8,128)(2,1)}, bf16[32,8192]{1,0:T(8,128)(2,1)S(1)}, u32[]{:S(2)}) copy-start(bf16[32,8192]{1,0:T(8,128)(2,1)S(1)} %get-tuple-element.50) | copy-start | bytes 1572868
  103.6 11.2 %collective-permute-start.13 = (bf16[3,32,8192]{2,1,0:T(8,128)(2,1)}, bf16[3,32,8192]{2,1,0:T(8,128)(2,1)S(1)}, u32[]{:S(2)}, u32[]{:S(2)}) collective-permute-start(bf16[3,32,8192]{2,1,0:T(8,128)(2,1)} %get-tuple-element.51), channel_id=1, source_target_pairs={{0,16},{16,0},{32,48},{48,32},{64,80},{80,64},{96,112},{112,96},{1... | collective-permute-start | bytes 4718600 | tf_op jit(solution)/shard_map/ppermute | solution.py:355
  110.4 17.5 %all-to-all-start.4 = ((f32[16,40,256]{2,1,0:T(8,128)}), f32[16,40,256]{2,1,0:T(8,128)}, u32[]{:S(2)}, u32[]{:S(2)}) async-start(f32[16,40,256]{2,1,0:T(8,128)} %feature.1.refs_0_), calls=%async_computation.4 | async-start | bytes 1310720 | tf_op jit(solution)/shard_map/all_to_all | solution.py:352
  114.7 19.2 %collective-permute-start.12 = (bf16[32,8192]{1,0:T(8,128)(2,1)}, bf16[32,8192]{1,0:T(8,128)(2,1)}, u32[]{:S(2)}, u32[]{:S(2)}) collective-permute-start(bf16[32,8192]{1,0:T(8,128)(2,1)} %copy-done.3), channel_id=1, source_target_pairs={{0,16},{16,0},{32,48},{48,32},{64,80},{80,64},{96,112},{112,96},{1... | collective-permute-start | bytes 1572872 | tf_op jit(solution)/shard_map/ppermute | solution.py:355
  116.2 31.3 %collective-permute-start.14 = (bf16[32,8192]{1,0:T(8,128)(2,1)}, bf16[32,8192]{1,0:T(8,128)(2,1)S(1)}, u32[]{:S(2)}, u32[]{:S(2)}) collective-permute-start(bf16[32,8192]{1,0:T(8,128)(2,1)} %get-tuple-element.52), channel_id=1, source_target_pairs={{0,32},{16,48},{32,0},{48,16},{64,96},{80,112},{96,64},{112,80},{1... | collective-permute-start | bytes 1572872 | tf_op jit(solution)/shard_map/ppermute | solution.py:355
  116.9 30.7 %collective-permute-start.15 = (bf16[32,8192]{1,0:T(8,128)(2,1)}, bf16[32,8192]{1,0:T(8,128)(2,1)S(1)}, u32[]{:S(2)}, u32[]{:S(2)}) collective-permute-start(bf16[32,8192]{1,0:T(8,128)(2,1)} %get-tuple-element.53), channel_id=1, source_target_pairs={{0,64},{16,80},{32,96},{48,112},{64,0},{80,16},{96,32},{112,48},{1... | collective-permute-start | bytes 1572872 | tf_op jit(solution)/shard_map/ppermute | solution.py:355
  118.7 28.8 %collective-permute-start.16 = (bf16[32,8192]{1,0:T(8,128)(2,1)}, bf16[32,8192]{1,0:T(8,128)(2,1)S(1)}, u32[]{:S(2)}, u32[]{:S(2)}) collective-permute-start(bf16[32,8192]{1,0:T(8,128)(2,1)} %get-tuple-element.54), channel_id=1, source_target_pairs={{0,96},{16,112},{32,64},{48,80},{64,32},{80,48},{96,0},{112,16},{1... | collective-permute-start | bytes 1572872 | tf_op jit(solution)/shard_map/ppermute | solution.py:355
  129.8 15.8 %all-to-all-start.5 = ((f32[8,8,128]{2,1,0:T(8,128)}), f32[8,8,128]{2,1,0:T(8,128)S(1)}, u32[]{:S(2)}, u32[]{:S(2)}) async-start(f32[8,8,128]{2,1,0:T(8,128)} %get-tuple-element.48.refs_0_), calls=%async_computation.5 | async-start | bytes 65536 | tf_op jit(solution)/shard_map/all_to_all | solution.py:352
  133.9 1.2 copy-start.1

commit v3 on v2

--- a/solution.py
+++ b/solution.py
@@ -15,6 +15,7 @@
 BF16 = jnp.bfloat16
 LANES = 128
 PIECES = (3, 3, 2)
+FIRST = 2
 VMEM_LIMIT = 20 * 1024 * 1024
 
 NN = (((1,), (0,)), ((), ()))
@@ -149,7 +150,7 @@
     w_ref[...] = jnp.broadcast_to(mm(weight_ref[...], spread), w_ref.shape)
 
 
-def proto_body(w_hbm, unit_hbm, inverse_ref, w_ref, unit_ref, in_sems, out_sems):
+def proto_body(w_hbm, unit_hbm, first_ref, inverse_ref, w_ref, unit_ref, in_sems, out_sems):
     count = unit_ref.shape[0]
     copies = [
         pltpu.make_async_copy(w_hbm.at[:, cols], w_ref.at[:, cols], in_sems.at[j])
@@ -161,7 +162,10 @@
         w = w_ref[:, cols].astype(F32)
         inverse = lax.rsqrt(jnp.sum(w * w, axis=0, keepdims=True) + EPS)
         inverse_ref[pl.ds(j, 1), :] = inverse
-        unit_ref[j] = (w * inverse).astype(BF16)
+        unit = (w * inverse).astype(BF16)
+        unit_ref[j] = unit
+        if j < first_ref.shape[0]:
+            first_ref[j] = unit
         store = pltpu.make_async_copy(unit_ref.at[j], unit_hbm.at[j], out_sems.at[j])
         store.start()
         stores.append(store)
@@ -169,16 +173,23 @@
         store.wait()
 
 
-def table_body(rows_ref, unit_hbm, table_ref, sums_ref, unit_ref, sems):
+def table_body(rows_ref, first_ref, unit_hbm, table_ref, sums_ref, unit_ref, sems):
+    skip = first_ref.shape[0]
     copies = [
-        pltpu.make_async_copy(unit_hbm.at[j], unit_ref.at[j], sems.at[j])
+        pltpu.make_async_copy(unit_hbm.at[skip + j], unit_ref.at[j], sems.at[j])
         for j in range(unit_ref.shape[0])
     ]
+    for copy in copies:
+        copy.start()
     half = rows_ref.shape[1] // 2
     teacher = rows_ref[:, :half, :].reshape(-1, rows_ref.shape[2])
     for j, cols in chunks(table_ref):
-        arrive(copies, j, 3)
-        table = jnp.exp(mm(teacher, unit_ref[j]) * (1.0 / TEACHER_TEMP)).astype(BF16)
+        if j < skip:
+            unit = first_ref[j]
+        else:
+            copies[j - skip].wait()
+            unit = unit_ref[j - skip]
+        table = jnp.exp(mm(teacher, unit) * (1.0 / TEACHER_TEMP)).astype(BF16)
         table_ref[:, cols] = table
         sums_ref[pl.ds(j, 1), :] = jnp.sum(table.astype(F32), axis=0, keepdims=True)
 
@@ -293,8 +304,9 @@
         pair_ref[...] = (keep_ref[k].astype(F32) + near_ref[k].astype(F32)).astype(BF16)
 
 
-def own_sum_body(own_ref, near_ref, out_ref):
+def own_sum_body(own_ref, near_ref, tails_ref, out_ref, tails_out_ref):
     out_ref[...] = own_ref[...] + near_ref[...].astype(F32)
+    tails_out_ref[...] = tails_ref[...]
 
 
 def final_body(own_ref, *refs):
@@ -306,33 +318,43 @@
 
 
 def owner_body(sent_ref, x_ref, grad_ref, tail_ref):
-    sent = jnp.sum(sent_ref[...], axis=0)
+    sent = jnp.sum(sent_ref[...].astype(F32), axis=0)
     own = x_ref.shape[0]
     x = x_ref[...]
     feature = sent[:own]
     inverse = lax.rsqrt(jnp.sum(x * x, axis=1, keepdims=True) + EPS)
     unit = x * inverse
     grad_ref[...] = inverse * (feature - unit * jnp.sum(unit * feature, axis=1, keepdims=True))
-    tail_ref[...] = jnp.broadcast_to(sent[own:, :LANES][None], tail_ref.shape)
+    tail_ref[...] = jnp.broadcast_to(sent[own : own + 8, :LANES][None], tail_ref.shape)
+
+
+def split(value):
+    row = jnp.broadcast_to(value, (8, LANES))
+    high = row.astype(BF16).astype(F32)
+    mid = (row - high).astype(BF16).astype(F32)
+    return [term[0:1, 0:1] for term in (high, mid, row - high - mid)]
 
 
 def feature_body(first_ref, last_ref, codes_ref, turned_ref, *refs):
     *probs_refs, out_ref = refs
     n = codes_ref.shape[1]
+    count = out_ref.shape[0]
+    own = n // count
     weights, exp_total, total = row_factors(first_ref, last_ref, n)
     codes = codes_ref[...]
-    probs = column_sum(probs_refs)
     over = weights / total * (1.0 / STUDENT_TEMP)
-    feature = probs * (weights / exp_total * (1.0 / STUDENT_TEMP)) - codes * over
-    own = n // out_ref.shape[0]
-    out_ref[:, :own, :] = feature.T.reshape(out_ref.shape[0], own, out_ref.shape[2])
-    share = 1.0 / out_ref.shape[0]
+    probs = column_sum(probs_refs) * (weights / exp_total * (1.0 / STUDENT_TEMP))
+    feature = (probs - codes * over).T.astype(BF16)
+    out_ref[:, :own, :] = feature.reshape(count, own, feature.shape[1])
+    share = 1.0 / count
     cross = jnp.sum(turned_ref[...].astype(F32) * codes, axis=0, keepdims=True)
     part = jnp.sum(weights * jnp.log(exp_total) * share - over * cross)
-    count = jnp.sum(weights) * share
-    tail = (out_ref.shape[0], out_ref.shape[1] - own, out_ref.shape[2])
-    lane = lax.broadcasted_iota(jnp.int32, tail, 2)
-    out_ref[:, own:, :] = jnp.where(lane == 0, part, jnp.where(lane == 1, count, 0.0))
+    tail = (out_ref.shape[1] - own, out_ref.shape[2])
+    lane = lax.broadcasted_iota(jnp.int32, tail, 1)
+    row = jnp.zeros(tail, F32)
+    for k, term in enumerate(split(part) + split(jnp.sum(weights) * share)):
+        row = jnp.where(lane == k, term, row)
+    out_ref[:, own:, :] = jnp.broadcast_to(row.astype(BF16)[None], (count,) + tail)
 
 
 def on_device(student_feats, teacher_feats, proto_weight, mask_index, row_weight):
@@ -374,10 +396,14 @@
         ],
     )
     all_rows = exchange(own_rows, "proto")
-    unit, inverse = call(
+    unit, unit_first, inverse = call(
         proto_body,
         "proto_unit",
-        (pltpu.HBM((8, d, width), BF16), shape((8, width), F32)),
+        (
+            pltpu.HBM((8, d, width), BF16),
+            shape((FIRST, d, width), BF16),
+            shape((8, width), F32),
+        ),
         (proto_weight,),
         product,
         specs=[HBM],
@@ -392,10 +418,10 @@
         table_body,
         "teacher_table",
         (shape((rows, protos), BF16), shape((8, width), F32)),
-        (all_rows, unit),
+        (all_rows, unit_first, unit),
         2 * product,
-        specs=[VMEM, HBM],
-        scratch=[pltpu.VMEM((8, d, width), BF16), pltpu.SemaphoreType.DMA((8,))],
+        specs=[VMEM, VMEM, HBM],
+        scratch=[pltpu.VMEM((8 - FIRST, d, width), BF16), pltpu.SemaphoreType.DMA((8 - FIRST,))],
     )
 
     messages = []
@@ -474,7 +500,7 @@
     feature_part = call(
         feature_body,
         "feature",
-        shape((n_proto, own + 8, d), F32),
+        shape((n_proto, own + 16, d), BF16),
         (*factors, codes_feature, turned, *[piece[2] for piece in pieces]),
         product // 4,
     )
@@ -486,7 +512,7 @@
         product // 8,
         after=(feature_part,),
     )
-    far = [hop(pair, 2 * (k + 1)) for k, pair in enumerate(pairs)]
+    far = [hop(pairs[k - 1], 2 * k) for k in sorted(range(1, chips), key=lambda k: k % 2)]
     grad_student, tails = call(
         owner_body,
         "owner",
@@ -494,13 +520,12 @@
         (exchange(feature_part, "proto"), x_rows),
         product // 8,
     )
-    own_sum = call(
+    own_sum, tails = call(
         own_sum_body,
         "own_sum",
-        shape((share, protos), F32),
-        (own_block, hop(own_near, 1)),
+        (shape((share, protos), F32), shape((n_patch, 8, LANES), F32)),
+        (own_block, hop(own_near, 1), tails),
         product // 8,
-        after=(tails,),
     )
     grad_proto = call(
         final_body,
@@ -509,8 +534,9 @@
         (own_sum, *far),
         product // 4,
     )
-    losses = jnp.sum(exchange(tails, "patch"), axis=0)
-    return (grad_student, grad_proto, losses[0, 0] / losses[0, 1])
+    totals = jnp.sum(exchange(tails, "patch"), axis=0)[0]
+    loss = jnp.sum(totals[0:3]) / jnp.sum(totals[3:6])
+    return (grad_student, grad_proto, loss)
 
 
 def solution(mesh):

time: 151 us -> 148 us (0.980)
  blocking collectives: 27.9 us -> 43.2 us
  waiting for transfers between devices: 26.8 us -> 14.4 us
  starting transfers between devices: 42.2 us -> 36.8 us
    all_to_all x3 -> x4, blocking collectives: 27.9 us -> 43.2 us  [exchange(): return lax.all_to_all(array, axis, 0, 0)]
    all_to_all x3 -> x2, waiting for transfers between devices: 23 us -> 10.5 us  [exchange(): return lax.all_to_all(array, axis, 0, 0)]
    all_to_all x3 -> x2, starting transfers between devices: 17 us -> 12.2 us  [exchange(): return lax.all_to_all(array, axis, 0, 0)]
  transfers between devices with their start and end apart: 20 -> 19, of which waited for: 8 -> 7; matrix products, arithmetic and copies ran while one was open for 0% -> 0% of each run, Pallas kernels for 13% -> 13%
where the time goes in v3:
time: 148 us; the launch traced here: 147 us
  Pallas kernels  46.9 us (32%)
  blocking collectives  43.2 us (29%)
  starting transfers between devices  36.8 us (25%)
  waiting for transfers between devices  14.4 us (10%)
  between operations  3.35 us (2%)
  local copies, waits for them, and re-layouts  2 us (1%)
    pallas_call x18, Pallas kernels, call(): pl.pallas_call(ordered, name=name, out_shape=out_shape, in_specs=[ANY] *...  46.9 us
    all_to_all x4, blocking collectives, exchange(): return lax.all_to_all(array, axis, 0, 0)  43.2 us
    ppermute x17, starting transfers between devices, hop(): return lax.ppermute(array, 'patch', [(i, i ^ bits) for i in range(n_patch)])  24.6 us
    all_to_all x2, starting transfers between devices, exchange(): return lax.all_to_all(array, axis, 0, 0)  12.2 us
    all_to_all x2, waiting for transfers between devices, exchange(): return lax.all_to_all(array, axis, 0, 0)  10.5 us
    ppermute x17, waiting for transfers between devices, hop(): return lax.ppermute(array, 'patch', [(i, i ^ bits) for i in range(n_patch)])  3.89 us
  transfers between devices with their start and end apart: 19, of which 7 were waited for; matrix products, arithmetic and copies ran while one was open for 0% of the time, Pallas kernels for 13%

profile of v3, /device:TPU:1, one launch (start us, length us, event | category | flops | bytes accessed | tf_op | source)
XLA Modules:
  0.0 147.4 jit_solution(6783702694572289285)
XLA Ops:
  0.6 0.1 pad_add_fusion.refs_0_
  0.7 2.7 %own_rows.1 = (bf16[16,64,256]{2,1,0:T(8,128)(2,1)}, f32[32,256]{1,0:T(8,128)S(1)}, f32[8,512]{1,0:T(8,128)S(1)}) custom-call(s32[3]{0:T(128)S(1)} %pad_add_fusion.refs_0_, bf16[256,256]{1,0:T(8,128)(2,1)} %refs_1_.1, bf16[256,256]{1,0:T(8,128)(2,1)} %refs_2_.1, s32[1,32]{1,0:T(1,128)} %bitcast.5, bf16[1,32]{1,0:T(2,128)(2,1)} %bitcast.6), custom_call_target="tpu_custom_call" | custom-call | flops 268435456 | bytes 65536 | tf_op jit(solution)/shard_map/own_rows/pallas_call | solution.py:53
  3.4 0.0 copy-start.3
  3.4 8.6 %all-to-all-start = ((bf16[16,64,256]{2,1,0:T(8,128)(2,1)}), bf16[16,64,256]{2,1,0:T(8,128)(2,1)S(1)}, u32[]{:S(2)}, u32[]{:S(2)}) async-start(bf16[16,64,256]{2,1,0:T(8,128)(2,1)} %get-tuple-element.32), calls=%async_computation | async-start | bytes 1048576 | tf_op jit(solution)/shard_map/all_to_all | solution.py:374
  12.0 4.7 %proto_unit.1 = (bf16[8,256,1024]{2,1,0:T(8,128)(2,1)}, bf16[2,256,1024]{2,1,0:T(8,128)(2,1)S(1)}, f32[8,1024]{1,0:T(8,128)S(1)}) custom-call(bf16[256,8192]{1,0:T(8,128)(2,1)} %refs_13_.1), custom_call_target="tpu_custom_call" | custom-call | flops 2147483648 | bytes 65536 | tf_op jit(solution)/shard_map/proto_unit/pallas_call | solution.py:53
  16.8 5.8 %all-to-all-done.refs_0_.refs_1_ = bf16[16,64,256]{2,1,0:T(8,128)(2,1)S(1)} async-done(((bf16[16,64,256]{2,1,0:T(8,128)(2,1)}), bf16[16,64,256]{2,1,0:T(8,128)(2,1)S(1)}, u32[]{:S(2)}, u32[]{:S(2)}) %all-to-all-start) | async-done | bytes 524320 | tf_op jit(solution)/shard_map/all_to_all | solution.py:374
  22.5 6.0 %teacher_table.1 = (bf16[512,8192]{1,0:T(8,128)(2,1)S(1)}, f32[8,1024]{1,0:T(8,128)S(1)}) custom-call(bf16[16,64,256]{2,1,0:T(8,128)(2,1)S(1)} %all-to-all-done.refs_0_.refs_1_, bf16[2,256,1024]{2,1,0:T(8,128)(2,1)S(1)} %get-tuple-element.33.refs_1_, bf16[8,256,1024]{2,1,0:T(8,128)(2,1)} %get-tuple-element.34.refs_2_.refs_6_), custom_call_target="tpu_custom_call" | custom-call | flops 4294967296 | bytes 65536 | tf_op jit(solution)/shard_map/teacher_table/pallas_call | solution.py:53
  28.6 2.1 %collective-permute-start = (f32[8,1024]{1,0:T(8,128)S(1)}, f32[8,1024]{1,0:T(8,128)S(1)}, u32[]{:S(2)}, u32[]{:S(2)}) collective-permute-start(f32[8,1024]{1,0:T(8,128)S(1)} %get-tuple-element.35), channel_id=1, source_target_pairs={{0,16},{16,0},{32,48},{48,32},{64,80},{80,64},{96,112},{112,96},{1... | collective-permute-start | bytes 98312 | tf_op jit(solution)/shard_map/ppermute | solution.py:377
  30.6 0.9 collective-permute-done
  31.5 2.5 %collective-permute-start.3 = (f32[8,1024]{1,0:T(8,128)S(1)}, f32[8,1024]{1,0:T(8,128)S(1)}, u32[]{:S(2)}, u32[]{:S(2)}) collective-permute-start(f32[8,1024]{1,0:T(8,128)S(1)} %add.15.refs_0_.refs_1_), channel_id=1, source_target_pairs={{0,96},{16,112},{32,64},{48,80},{64,32},{80,48},{96,0},{112,16},{1... | collective-permute-start | bytes 98312 | tf_op jit(solution)/shard_map/ppermute | solution.py:377
  34.0 0.5 collective-permute-start.2
  34.5 0.3 collective-permute-start.1
  34.7 2.7 %student_table.3 = (bf16[512,3072]{1,0:T(8,128)(2,1)S(1)}, f32[8,512]{1,0:T(8,128)S(1)}, f32[256,512]{1,0:T(8,128)S(1)}) custom-call(f32[8,1024]{1,0:T(8,128)S(1)} %add.15.refs_0_.refs_1_, bf16[16,64,256]{2,1,0:T(8,128)(2,1)S(1)} %all-to-all-done.refs_0_.refs_1_, bf16[8,256,1024]{2,1,0:T(8,128)(2,1)S(1)} %copy-done), custom_call_target="tpu_custom_call" | custom-call | flops 2147483648 | bytes 65536 | tf_op jit(solution)/shard_map/student_table/pallas_call | solution.py:53
  37.4 0.0 collective-permute-done.3.refs_4_
  37.4 0.8 collective-permute-done.2.refs_3_
  38.2 0.0 collective-permute-done.1.refs_2_
  38.2 2.3 %row_pass.3 = f32[16,8,128]{2,1,0:T(8,128)S(1)} custom-call(f32[8,512]{1,0:T(8,128)S(1)} %get-tuple-element.36.refs_0_.refs_5_, f32[8,1024]{1,0:T(8,128)S(1)} %add.15.refs_0_.refs_1_, f32[8,1024]{1,0:T(8,128)S(1)} %collective-permute-done.1.refs_2_, f32[8,1024]{1,0:T(8,128)S(1)} %collective-permute-done.2.refs_3_, ...), custom_call_target="tpu_custom_call" | custom-call | flops 2147483648 | bytes 65536 | tf_op jit(solution)/shard_map/row_pass/pallas_call | solution.py:53
  40.5 9.2 %all_to_all.30.refs_0_.refs_1_ = f32[16,8,128]{2,1,0:T(8,128)S(1)} all-to-all(f32[16,8,128]{2,1,0:T(8,128)S(1)} %row_pass.3), channel_id=1, replica_groups=mesh['patch'=8,'proto'=16] {'proto'}, dimensions={0} | all-to-all | bytes 131072 | tf_op jit(solution)/shard_map/all_to_all | solution.py:374
  49.7 1.2 col_pass.2
  51.0 3.3 %collective-permute-start.4 = (f32[8,1024]{1,0:T(8,128)S(1)}, f32[8,1024]{1,0:T(8,128)S(1)}, u32[]{:S(2)}, u32[]{:S(2)}) collective-permute-start(f32[8,1024]{1,0:T(8,128)S(1)} %col_pass.2), channel_id=1, source_target_pairs={{0,16},{16,0},{32,48},{48,32},{64,80},{80,64},{96,112},{112,96},{1... | collective-permute-start | bytes 98312 | tf_op jit(solution)/shard_map/ppermute | solution.py:377
  54.2 0.9 collective-permute-done.4
  55.1 1.1 collective-permute-start.7
  56.2 0.8 collective-permute-start.6
  57.0 1.3 collective-permute-start.5
  58.4 2.7 %student_table.4 = (bf16[512,3072]{1,0:T(8,128)(2,1)S(1)}, f32[8,512]{1,0:T(8,128)S(1)}, f32[256,512]{1,0:T(8,128)S(1)}) custom-call(f32[8,1024]{1,0:T(8,128)S(1)} %add.16.refs_0_.refs_1_, bf16[16,64,256]{2,1,0:T(8,128)(2,1)S(1)} %all-to-all-done.refs_0_.refs_1_, bf16[8,256,1024]{2,1,0:T(8,128)(2,1)S(1)} %copy-done), custom_call_target="tpu_custom_call" | custom-call | flops 2147483648 | bytes 65536 | tf_op jit(solution)/shard_map/student_table/pallas_call | solution.py:53
  61.0 0.0 collective-permute-done.7.refs_4_
  61.1 0.0 collective-permute-done.6.refs_3_
  61.1 0.0 collective-permute-done.5.refs_2_
  61.1 2.3 %row_pass.4 = f32[16,8,128]{2,1,0:T(8,128)S(1)} custom-call(f32[8,512]{1,0:T(8,128)S(1)} %get-tuple-element.39.refs_0_.refs_6_, f32[8,1024]{1,0:T(8,128)S(1)} %add.16.refs_0_.refs_1_, f32[8,1024]{1,0:T(8,128)S(1)} %collective-permute-done.5.refs_2_, f32[8,1024]{1,0:T(8,128)S(1)} %collective-permute-done.6.refs_3_, ...), custom_call_target="tpu_custom_call" | custom-call | flops 2147483648 | bytes 65536 | tf_op jit(solution)/shard_map/row_pass/pallas_call | solution.py:53
  63.4 9.4 %all_to_all.31.refs_0_ = f32[16,8,128]{2,1,0:T(8,128)S(1)} all-to-all(f32[16,8,128]{2,1,0:T(8,128)S(1)} %row_pass.4), channel_id=1, replica_groups=mesh['patch'=8,'proto'=16] {'proto'}, dimensions={0} | all-to-all | bytes 131072 | tf_op jit(solution)/shard_map/all_to_all | solution.py:374
  72.8 1.2 col_pass.3
  74.0 2.9 %collective-permute-start.8 = (f32[8,1024]{1,0:T(8,128)S(1)}, f32[8,1024]{1,0:T(8,128)S(1)}, u32[]{:S(2)}, u32[]{:S(2)}) collective-permute-start(f32[8,1024]{1,0:T(8,128)S(1)} %col_pass.3), channel_id=1, source_target_pairs={{0,16},{16,0},{32,48},{48,32},{64,80},{80,64},{96,112},{112,96},{1... | collective-permute-start | bytes 98312 | tf_op jit(solution)/shard_map/ppermute | solution.py:377
  76.9 0.9 collective-permute-done.8
  77.7 1.4 collective-permute-start.11
  79.1 1.1 collective-permute-start.10
  80.3 0.7 collective-permute-start.9
  81.0 1.9 %student_table.5 = (bf16[512,2048]{1,0:T(8,128)(2,1)S(1)}, f32[8,512]{1,0:T(8,128)S(1)}, f32[256,512]{1,0:T(8,128)S(1)}, bf16[256,512]{1,0:T(8,128)(2,1)S(1)}) custom-call(f32[8,1024]{1,0:T(8,128)S(1)} %add.17.refs_0_.refs_3_.refs_1_, bf16[16,64,256]{2,1,0:T(8,128)(2,1)S(1)} %all-to-all-done.refs_0_.refs_1_, bf16[8,256,1024]{2,1,0:T(8,128)(2,1)S(1)} %copy-done), custom_call_target="tpu_custom_call" | custom-call | flops 2147483648 | bytes 65536 | tf_op jit(solution)/shard_map/student_table/pallas_call | solution.py:53
  82.9 0.0 collective-permute-done.11.refs_3_.refs_6_.refs_4_
  82.9 0.5 collective-permute-done.10.refs_2_.refs_5_.refs_3_
  83.4 0.0 collective-permute-done.9.refs_1_.refs_4_.refs_2_
  83.4 2.3 %row_pass.5 = f32[16,8,128]{2,1,0:T(8,128)S(1)} custom-call(f32[8,1024]{1,0:T(8,128)S(1)} %add.17.refs_0_.refs_3_.refs_1_, f32[8,1024]{1,0:T(8,128)S(1)} %collective-permute-done.9.refs_1_.refs_4_.refs_2_, f32[8,1024]{1,0:T(8,128)S(1)} %collective-permute-done.10.refs_2_.refs_5_.refs_3_, f32[8,1024]{1,0:T(8,128)S(1)} %collective-permute-done.11.refs_3_.refs_6_.refs_4_, ...), custom_call_target="tpu_custom_call" | custom-call | flops 2147483648 | bytes 65536 | tf_op jit(solution)/shard_map/row_pass/pallas_call | solution.py:53
  85.7 9.4 %all_to_all.32.refs_2_.refs_1_ = f32[16,8,128]{2,1,0:T(8,128)S(1)} all-to-all(f32[16,8,128]{2,1,0:T(8,128)S(1)} %row_pass.5), channel_id=1, replica_groups=mesh['patch'=8,'proto'=16] {'proto'}, dimensions={0} | all-to-all | bytes 131072 | tf_op jit(solution)/shard_map/all_to_all | solution.py:374
  95.1 8.9 %head.1 = (f32[32,8192]{1,0:T(8,128)}, bf16[32,8192]{1,0:T(8,128)(2,1)}, bf16[3,32,8192]{2,1,0:T(8,128)(2,1)S(1)}, bf16[3,32,8192]{2,1,0:T(8,128)(2,1)}) custom-call(s32[3]{0:T(128)S(1)} %pad_add_fusion.refs_0_, f32[16,8,128]{2,1,0:T(8,128)S(1)} %all_to_all.30.refs_0_.refs_1_, f32[16,8,128]{2,1,0:T(8,128)S(1)} %all_to_all.32.refs_2_.refs_1_, ...), custom_call_target="tpu_custom_call" | custom-call | flops 8589934592 | bytes 65536 | tf_op jit(solution)/shard_map/head/pallas_call | solution.py:53
  104.0 3.3 %collective-permute-start.13 = (bf16[3,32,8192]{2,1,0:T(8,128)(2,1)}, bf16[3,32,8192]{2,1,0:T(8,128)(2,1)S(1)}, u32[]{:S(2)}, u32[]{:S(2)}) collective-permute-start(bf16[3,32,8192]{2,1,0:T(8,128)(2,1)} %get-tuple-element.56), channel_id=1, source_target_pairs={{0,16},{16,0},{32,48},{48,32},{64,80},{80,64},{96,112},{112,96},{1... | collective-permute-start | bytes 4718600 | tf_op jit(solution)/shard_map/ppermute | solution.py:377
  107.3 0.1 collective-permute-start.12
  107.4 2.4 %codes_feature.1.refs_2_ = f32[256,512]{1,0:T(8,128)S(1)} custom-call(bf16[3,32,8192]{2,1,0:T(8,128)(2,1)S(1)} %get-tuple-element.46.refs_0_.refs_1_, f32[8,1024]{1,0:T(8,128)S(1)} %add.17.refs_0_.refs_3_.refs_1_, f32[8,1024]{1,0:T(8,128)S(1)} %collective-permute-done.9.refs_1_.refs_4_.refs_2_, ...), custom_call_target="tpu_custom_call" | custom-call | flops 2147483648 | bytes 65536 | tf_op jit(solution)/shard_map/codes_feature/pallas_call | solution.py:53
  109.8 1.1 feature.1.refs_0_
  110.9 3.6 %all-to-all-start.4 = ((bf16[16,48,256]{2,1,0:T(8,128)(2,1)}), bf16[16,48,256]{2,1,0:T(8,128)(2,1)S(1)}, u32[]{:S(2)}, u32[]{:S(2)}) async-start(bf16[16,48,256]{2,1,0:T(8,128)(2,1)} %feature.1.refs_0_), calls=%async_computation.4 | async-start | bytes 786432 | tf_op jit(solution)/shard_map/all_to_all | solution.py:374
  114.4 0.0 collective-permute-done.13.refs_2_
  114.4 1.5 pair_sums.1
  115.9 1.7 %collective-permute-start.14 = (bf16[32,8192]{1,0:T(8,128)(2,1)}, bf16[32,8192]{1,0:T(8,128)(2,1)S(1)}, u32[]{:S(2)}, u32[]{:S(2)}) collective-permute-start(bf16[32,8192]{1,0:T(8,128)(2,1)} %get-tuple-element.57), channel_id=1, source_target_pairs={{0,64},{16,80},{32,96},{48,112},{64,0},{80,16},{96,32},{112,48},{1... | collective-permute-start | bytes 1572872 | tf_op jit(solution)/shard_map/ppermute | solution.py:377
  117.6 0.1 collective-permute-start.15
  117.8 1.4 collective-permute-start.16
  119.2 4.7 %all-to-all-done.4.refs_0_ = bf16[16,48,256]{2,1,0:T(8,128)(2,1)S(1)} async-done(((bf16[16,48,256]{2,1,0:T(8,128)(2,1)}), bf16[16,48,256]{2,1,0:T(8,128)(2,1)S(1)}, u32[]{:S(2)}, u32[]{:S(2)}) %all-to-all-start.4) | async-done | bytes 393248 | tf_op jit(solution)/shard_map/all_to_all | solution.py:374
  123.9 0.8 copy-done.4
  124.6 0.8 owner.1
  125.4 0.0 collective-permute-done.12.refs_1_
  125.4 1.2 copy-done.1
  126.6 1.1 own_sum.1
  127.8 15.2 %all_to_all.33 = f32[8,8,128]{2,1,0:T(8,128)S(1)} all-to-all(f32[8,8,128]{2,1,0:T(8,128)S(1)} %get-tuple-element.60), channel_id=1, replica_groups=mesh['patch'=8,'proto'=16] {'patch'}, dimensions={0} | all-to-all | bytes 65536 | tf_op jit(solution)/shard_map/all_to_all | solution.py:374
  143.0 0.7 slice_reduce_fusion
  145.1 0.0 collective-permute-done.15.refs_2_
  145.1 0.0 collective-permute-done.16.refs_3_
  145.1 1.2 assemble.1
  (12 shorter events, 0.0 us)
Async XLA Ops:
  3.4 13.4 %copy-start.3 = (f32[32,256]{1,0:T(8,128)}, f32[32,256]{1,0:T(8,128)S(1)}, u32[]{:S(2)}) copy-start(f32[32,256]{1,0:T(8,128)S(1)} %get-tuple-element.50.refs_1_) | copy-start | bytes 98308
  3.4 19.1 %all-to-all-start = ((bf16[16,64,256]{2,1,0:T(8,128)(2,1)}), bf16[16,64,256]{2,1,0:T(8,128)(2,1)S(1)}, u32[]{:S(2)}, u32[]{:S(2)}) async-start(bf16[16,64,256]{2,1,0:T(8,128)(2,1)} %get-tuple-element.32), calls=%async_computation | async-start | bytes 1048576 | tf_op jit(solution)/shard_map/all_to_all | solution.py:374
  22.5 12.2 %copy-start = (bf16[8,256,1024]{2,1,0:T(8,128)(2,1)S(1)}, bf16[8,256,1024]{2,1,0:T(8,128)(2,1)}, u32[]{:S(2)}) copy-start(bf16[8,256,1024]{2,1,0:T(8,128)(2,1)} %get-tuple-element.34.refs_2_.refs_6_) | copy-start | bytes 12582916
  28.6 2.9 %collective-permute-start = (f32[8,1024]{1,0:T(8,128)S(1)}, f32[8,1024]{1,0:T(8,128)S(1)}, u32[]{:S(2)}, u32[]{:S(2)}) collective-permute-start(f32[8,1024]{1,0:T(8,128)S(1)} %get-tuple-element.35), channel_id=1, source_target_pairs={{0,16},{16,0},{32,48},{48,32},{64,80},{80,64},{96,112},{112,96},{1... | collective-permute-start | bytes 98312 | tf_op jit(solution)/shard_map/ppermute | solution.py:377
  31.5 5.9 %collective-permute-start.3 = (f32[8,1024]{1,0:T(8,128)S(1)}, f32[8,1024]{1,0:T(8,128)S(1)}, u32[]{:S(2)}, u32[]{:S(2)}) collective-permute-start(f32[8,1024]{1,0:T(8,128)S(1)} %add.15.refs_0_.refs_1_), channel_id=1, source_target_pairs={{0,96},{16,112},{32,64},{48,80},{64,32},{80,48},{96,0},{112,16},{1... | collective-permute-start | bytes 98312 | tf_op jit(solution)/shard_map/ppermute | solution.py:377
  34.0 4.3 %collective-permute-start.2 = (f32[8,1024]{1,0:T(8,128)S(1)}, f32[8,1024]{1,0:T(8,128)S(1)}, u32[]{:S(2)}, u32[]{:S(2)}) collective-permute-start(f32[8,1024]{1,0:T(8,128)S(1)} %add.15.refs_0_.refs_1_), channel_id=1, source_target_pairs={{0,64},{16,80},{32,96},{48,112},{64,0},{80,16},{96,32},{112,48},{1... | collective-permute-start | bytes 98312 | tf_op jit(solution)/shard_map/ppermute | solution.py:377
  34.5 3.8 %collective-permute-start.1 = (f32[8,1024]{1,0:T(8,128)S(1)}, f32[8,1024]{1,0:T(8,128)S(1)}, u32[]{:S(2)}, u32[]{:S(2)}) collective-permute-start(f32[8,1024]{1,0:T(8,128)S(1)} %add.15.refs_0_.refs_1_), channel_id=1, source_target_pairs={{0,32},{16,48},{32,0},{48,16},{64,96},{80,112},{96,64},{112,80},{1... | collective-permute-start | bytes 98312 | tf_op jit(solution)/shard_map/ppermute | solution.py:377
  51.0 4.1 %collective-permute-start.4 = (f32[8,1024]{1,0:T(8,128)S(1)}, f32[8,1024]{1,0:T(8,128)S(1)}, u32[]{:S(2)}, u32[]{:S(2)}) collective-permute-start(f32[8,1024]{1,0:T(8,128)S(1)} %col_pass.2), channel_id=1, source_target_pairs={{0,16},{16,0},{32,48},{48,32},{64,80},{80,64},{96,112},{112,96},{1... | collective-permute-start | bytes 98312 | tf_op jit(solution)/shard_map/ppermute | solution.py:377
  55.1 5.9 %collective-permute-start.7 = (f32[8,1024]{1,0:T(8,128)S(1)}, f32[8,1024]{1,0:T(8,128)S(1)}, u32[]{:S(2)}, u32[]{:S(2)}) collective-permute-start(f32[8,1024]{1,0:T(8,128)S(1)} %add.16.refs_0_.refs_1_), channel_id=1, source_target_pairs={{0,96},{16,112},{32,64},{48,80},{64,32},{80,48},{96,0},{112,16},{1... | collective-permute-start | bytes 98312 | tf_op jit(solution)/shard_map/ppermute | solution.py:377
  56.2 4.8 %collective-permute-start.6 = (f32[8,1024]{1,0:T(8,128)S(1)}, f32[8,1024]{1,0:T(8,128)S(1)}, u32[]{:S(2)}, u32[]{:S(2)}) collective-permute-start(f32[8,1024]{1,0:T(8,128)S(1)} %add.16.refs_0_.refs_1_), channel_id=1, source_target_pairs={{0,64},{16,80},{32,96},{48,112},{64,0},{80,16},{96,32},{112,48},{1... | collective-permute-start | bytes 98312 | tf_op jit(solution)/shard_map/ppermute | solution.py:377
  57.0 4.0 %collective-permute-start.5 = (f32[8,1024]{1,0:T(8,128)S(1)}, f32[8,1024]{1,0:T(8,128)S(1)}, u32[]{:S(2)}, u32[]{:S(2)}) collective-permute-start(f32[8,1024]{1,0:T(8,128)S(1)} %add.16.refs_0_.refs_1_), channel_id=1, source_target_pairs={{0,32},{16,48},{32,0},{48,16},{64,96},{80,112},{96,64},{112,80},{1... | collective-permute-start | bytes 98312 | tf_op jit(solution)/shard_map/ppermute | solution.py:377
  74.0 3.7 %collective-permute-start.8 = (f32[8,1024]{1,0:T(8,128)S(1)}, f32[8,1024]{1,0:T(8,128)S(1)}, u32[]{:S(2)}, u32[]{:S(2)}) collective-permute-start(f32[8,1024]{1,0:T(8,128)S(1)} %col_pass.3), channel_id=1, source_target_pairs={{0,16},{16,0},{32,48},{48,32},{64,80},{80,64},{96,112},{112,96},{1... | collective-permute-start | bytes 98312 | tf_op jit(solution)/shard_map/ppermute | solution.py:377
  77.7 5.2 %collective-permute-start.11 = (f32[8,1024]{1,0:T(8,128)S(1)}, f32[8,1024]{1,0:T(8,128)S(1)}, u32[]{:S(2)}, u32[]{:S(2)}) collective-permute-start(f32[8,1024]{1,0:T(8,128)S(1)} %add.17.refs_0_.refs_3_.refs_1_), channel_id=1, source_target_pairs={{0,96},{16,112},{32,64},{48,80},{64,32},{80,48},{96,0},{112,16},{1... | collective-permute-start | bytes 98312 | tf_op jit(solution)/shard_map/ppermute | solution.py:377
  79.1 4.3 %collective-permute-start.10 = (f32[8,1024]{1,0:T(8,128)S(1)}, f32[8,1024]{1,0:T(8,128)S(1)}, u32[]{:S(2)}, u32[]{:S(2)}) collective-permute-start(f32[8,1024]{1,0:T(8,128)S(1)} %add.17.refs_0_.refs_3_.refs_1_), channel_id=1, source_target_pairs={{0,64},{16,80},{32,96},{48,112},{64,0},{80,16},{96,32},{112,48},{1... | collective-permute-start | bytes 98312 | tf_op jit(solution)/shard_map/ppermute | solution.py:377
  80.3 3.1 %collective-permute-start.9 = (f32[8,1024]{1,0:T(8,128)S(1)}, f32[8,1024]{1,0:T(8,128)S(1)}, u32[]{:S(2)}, u32[]{:S(2)}) collective-permute-start(f32[8,1024]{1,0:T(8,128)S(1)} %add.17.refs_0_.refs_3_.refs_1_), channel_id=1, source_target_pairs={{0,32},{16,48},{32,0},{48,16},{64,96},{80,112},{96,64},{112,80},{1... | collective-permute-start | bytes 98312 | tf_op jit(solution)/shard_map/ppermute | solution.py:377
  83.4 11.7 %copy-start.2 = (bf16[256,8192]{1,0:T(8,128)(2,1)S(1)}, bf16[256,8192]{1,0:T(8,128)(2,1)}, u32[]{:S(2)}) copy-start(bf16[256,8192]{1,0:T(8,128)(2,1)} %refs_13_.1) | copy-start | bytes 12582916
  104.0 10.4 %collective-permute-start.13 = (bf16[3,32,8192]{2,1,0:T(8,128)(2,1)}, bf16[3,32,8192]{2,1,0:T(8,128)(2,1)S(1)}, u32[]{:S(2)}, u32[]{:S(2)}) collective-permute-start(bf16[3,32,8192]{2,1,0:T(8,128)(2,1)} %get-tuple-element.56), channel_id=1, source_target_pairs={{0,16},{16,0},{32,48},{48,32},{64,80},{80,64},{96,112},{112,96},{1... | collective-permute-start | bytes 4718600 | tf_op jit(solution)/shard_map/ppermute | solution.py:377
  107.3 18.1 %collective-permute-start.12 = (bf16[32,8192]{1,0:T(8,128)(2,1)}, bf16[32,8192]{1,0:T(8,128)(2,1)}, u32[]{:S(2)}, u32[]{:S(2)}) collective-permute-start(bf16[32,8192]{1,0:T(8,128)(2,1)} %get-tuple-element.53), channel_id=1, source_target_pairs={{0,16},{16,0},{32,48},{48,32},{64,80},{80,64},{96,112},{112,96},{1... | collective-permute-start | bytes 1572872 | tf_op jit(solution)/shard_map/ppermute | solution.py:377
  110.9 13.0 %all-to-all-start.4 = ((bf16[16,48,256]{2,1,0:T(8,128)(2,1)}), bf16[16,48,256]{2,1,0:T(8,128)(2,1)S(1)}, u32[]{:S(2)}, u32[]{:S(2)}) async-start(bf16[16,48,256]{2,1,0:T(8,128)(2,1)} %feature.1.refs_0_), calls=%async_computation.4 | async-start | bytes 786432 | tf_op jit(solution)/shard_map/all_to_all | solution.py:374
  115.9 29.1 %collective-permute-start.14 = (bf16[32,8192]{1,0:T(8,128)(2,1)}, bf16[32,8192]{1,0:T(8,128)(2,1)S(1)}, u32[]{:S(2)}, u32[]{:S(2)}) collective-permute-start(bf16[32,8192]{1,0:T(8,128)(2,1)} %get-tuple-element.57), channel_id=1, source_target_pairs={{0,64},{16,80},{32,96},{48,112},{64,0},{80,16},{96,32},{112,48},{1... | collective-permute-start | bytes 1572872 | tf_op jit(solution)/shard_map/ppermute | solution.py:377
  117.6 27.4 %collective-permute-start.15 = (bf16[32,8192]{1,0:T(8,128)(2,1)}, bf16[32,8192]{1,0:T(8,128)(2,1)S(1)}, u32[]{:S(2)}, u32[]{:S(2)}) collective-permute-start(bf16[32,8192]{1,0:T(8,128)(2,1)} %get-tuple-element.58), channel_id=1, source_target_pairs={{0,32},{16,48},{32,0},{48,16},{64,96},{80,112},{96,64},{112,80},{1... | collective-permute-start | bytes 1572872 | tf_op jit(solution)/shard_map/ppermute | solution.py:377
  117.8 27.3 %collective-permute-start.16 = (bf16[32,8192]{1,0:T(8,128)(2,1)}, bf16[32,8192]{1,0:T(8,128)(2,1)S(1)}, u32[]{:S(2)}, u32[]{:S(2)}) collective-permute-start(bf16[32,8192]{1,0:T(8,128)(2,1)} %get-tuple-element.59), channel_id=1, source_target_pairs={{0,96},{16,112},{32,64},{48,80},{64,32},{80,48},{96,0},{112,16},{1... | collective-permute-start | bytes 1572872 | tf_op jit(solution)/shard_map/ppermute | solution.py:377
  123.9 0.8 copy-start.4
  125.4 1.2 copy-start.1

commit v4 on v3

--- a/solution.py
+++ b/solution.py
@@ -173,25 +173,26 @@
         store.wait()
 
 
-def table_body(rows_ref, first_ref, unit_hbm, table_ref, sums_ref, unit_ref, sems):
-    skip = first_ref.shape[0]
+def table_body(rows_ref, first_ref, unit_hbm, table_ref, unit_ref, sums_ref, sems):
+    skip, count = first_ref.shape[0], unit_ref.shape[0]
     copies = [
-        pltpu.make_async_copy(unit_hbm.at[skip + j], unit_ref.at[j], sems.at[j])
-        for j in range(unit_ref.shape[0])
+        pltpu.make_async_copy(unit_hbm.at[j], unit_ref.at[j], sems.at[j]) for j in range(count)
     ]
-    for copy in copies:
+    for copy in copies[skip:] + copies[:skip]:
         copy.start()
     half = rows_ref.shape[1] // 2
     teacher = rows_ref[:, :half, :].reshape(-1, rows_ref.shape[2])
-    for j, cols in chunks(table_ref):
+    for j, cols in chunks(table_ref, count):
         if j < skip:
             unit = first_ref[j]
         else:
-            copies[j - skip].wait()
-            unit = unit_ref[j - skip]
+            copies[j].wait()
+            unit = unit_ref[j]
         table = jnp.exp(mm(teacher, unit) * (1.0 / TEACHER_TEMP)).astype(BF16)
         table_ref[:, cols] = table
         sums_ref[pl.ds(j, 1), :] = jnp.sum(table.astype(F32), axis=0, keepdims=True)
+    for copy in copies[:skip]:
+        copy.wait()
 
 
 def row_pass_body(parts, *refs):
@@ -237,16 +238,24 @@
         turned_ref[...] = mm(eye, student, NT).astype(BF16)
 
 
-def codes_feature_body(*refs):
-    *sums_refs, table_ref, unit_ref, feature_ref = refs
+def last_row_pass_body(parts, *refs):
+    sums_refs, table_ref, unit_ref = refs[:parts], refs[parts], refs[parts + 1]
+    *extra_refs, out_ref, feature_ref = refs[parts + 2 :]
     scale = 1.0 / column_sum(sums_refs)
+    n, d = table_ref.shape[0], unit_ref.shape[1]
+    total = jnp.zeros((16, n), F32)
     for j, cols in chunks(table_ref):
-        scaled = (unit_ref[j].astype(F32) * scale[j : j + 1, :]).astype(BF16)
-        part = mm(scaled, table_ref[:, cols], NT)
+        factor = scale[j : j + 1, :]
+        scaled = (unit_ref[j].astype(F32) * factor).astype(BF16)
+        left = jnp.concatenate([scaled, three_terms(factor)], axis=0)
+        part = mm(left, table_ref[:, cols], NT)
+        total += part[d:]
         if j == 0:
-            feature_ref[...] = part
+            feature_ref[...] = part[:d]
         else:
-            feature_ref[...] += part
+            feature_ref[...] += part[:d]
+    write_rows(out_ref, 0, jnp.sum(total, axis=0, keepdims=True))
+    write_rows(out_ref, n // LANES, column_sum(extra_refs)[0:1, :])
 
 
 def row_factors(first_ref, last_ref, n):
@@ -309,12 +318,17 @@
     tails_out_ref[...] = tails_ref[...]
 
 
-def final_body(own_ref, *refs):
-    *far_refs, out_ref = refs
+def final_body(own_ref, tails_ref, *refs):
+    *far_refs, out_ref, loss_ref = refs
     total = own_ref[...]
     for far_ref in far_refs:
         total = total + far_ref[...].astype(F32)
     out_ref[...] = total
+    terms = jnp.sum(tails_ref[...], axis=0)[0:1, :]
+    lane = lax.broadcasted_iota(jnp.int32, terms.shape, 1)
+    part = jnp.sum(jnp.where(lane < 3, terms, 0.0), axis=1, keepdims=True)
+    count = jnp.sum(jnp.where((lane >= 3) & (lane < 6), terms, 0.0), axis=1, keepdims=True)
+    loss_ref[...] = part / count
 
 
 def owner_body(sent_ref, x_ref, grad_ref, tail_ref):
@@ -414,14 +428,18 @@
             pltpu.SemaphoreType.DMA((8,)),
         ],
     )
-    codes, sums = call(
+    codes, unit, sums = call(
         table_body,
         "teacher_table",
-        (shape((rows, protos), BF16), shape((8, width), F32)),
+        (
+            shape((rows, protos), BF16),
+            shape((8, d, width), BF16),
+            shape((8, width), F32),
+        ),
         (all_rows, unit_first, unit),
         2 * product,
         specs=[VMEM, VMEM, HBM],
-        scratch=[pltpu.VMEM((8 - FIRST, d, width), BF16), pltpu.SemaphoreType.DMA((8 - FIRST,))],
+        scratch=[pltpu.SemaphoreType.DMA((8,))],
     )
 
     messages = []
@@ -442,14 +460,23 @@
                 after=(sums,),
             )
         )
-        part = call(
-            functools.partial(row_pass_body, chips),
-            "row_pass",
-            shape((n_proto, 8, LANES), F32),
-            (*parts, codes, *([piece[1] for piece in pieces] if last else [own_weights])),
-            product,
-            after=() if last else (pieces[-1][1],),
-        )
+        if last:
+            part, codes_feature = call(
+                functools.partial(last_row_pass_body, chips),
+                "last_row_pass",
+                (shape((n_proto, 8, LANES), F32), shape((d, rows), F32)),
+                (*parts, codes, unit, *[piece[1] for piece in pieces]),
+                product,
+            )
+        else:
+            part = call(
+                functools.partial(row_pass_body, chips),
+                "row_pass",
+                shape((n_proto, 8, LANES), F32),
+                (*parts, codes, own_weights),
+                product,
+                after=(pieces[-1][1],),
+            )
         messages.append(exchange(part, "proto"))
         if not last:
             sums = call(
@@ -489,20 +516,13 @@
             pltpu.SemaphoreType.DMA((8,)),
         ],
     )
-    codes_feature = call(
-        codes_feature_body,
-        "codes_feature",
-        shape((d, rows), F32),
-        (*parts, codes, unit),
-        product,
-        after=(keep,),
-    )
     feature_part = call(
         feature_body,
         "feature",
         shape((n_proto, own + 16, d), BF16),
         (*factors, codes_feature, turned, *[piece[2] for piece in pieces]),
         product // 4,
+        after=(keep,),
     )
     pairs = call(
         pair_body,
@@ -527,16 +547,14 @@
         (own_block, hop(own_near, 1), tails),
         product // 8,
     )
-    grad_proto = call(
+    grad_proto, loss = call(
         final_body,
         "assemble",
-        shape((share, protos), F32),
-        (own_sum, *far),
+        (shape((share, protos), F32), shape((1, 1), F32)),
+        (own_sum, exchange(tails, "patch"), *far),
         product // 4,
     )
-    totals = jnp.sum(exchange(tails, "patch"), axis=0)[0]
-    loss = jnp.sum(totals[0:3]) / jnp.sum(totals[3:6])
-    return (grad_student, grad_proto, loss)
+    return (grad_student, grad_proto, loss.reshape(()))
 
 
 def solution(mesh):

time: 148 us -> 137 us (0.926)
  blocking collectives: 43.2 us -> 50.7 us
  Pallas kernels: 46.9 us -> 39.5 us
  starting transfers between devices: 36.8 us -> 33.3 us
  between operations: 3.35 us -> 0.83 us
  waiting for transfers between devices: 14.4 us -> 12.3 us
  local copies, waits for them, and re-layouts: 2 us -> 0.01 us
    all_to_all x4 -> x5, blocking collectives: 43.2 us -> 50.7 us  [exchange(): return lax.all_to_all(array, axis, 0, 0)]
    pallas_call x18 -> x17, Pallas kernels: 46.9 us -> 39.5 us  [call(): pl.pallas_call(ordered, name=name, out_shape=out_shape, in_specs=[ANY] *...]
    all_to_all x2 -> x1, waiting for transfers between devices: 10.5 us -> 5.76 us  [exchange(): return lax.all_to_all(array, axis, 0, 0)]
    all_to_all x2 -> x1, starting transfers between devices: 12.2 us -> 8.61 us  [exchange(): return lax.all_to_all(array, axis, 0, 0)]
    ppermute x17, waiting for transfers between devices: 3.89 us -> 6.5 us  [hop(): return lax.ppermute(array, 'patch', [(i, i ^ bits) for i in range(n_patch)])]
    unnamed x10 -> x4, local copies, waits for them, and re-layouts: 2 us -> 0.01 us
  transfers between devices with their start and end apart: 19 -> 18, of which waited for: 7 -> 7; matrix products, arithmetic and copies ran while one was open for 0% -> 0% of each run, Pallas kernels for 13% -> 10%
where the time goes in v4:
time: 137 us
  blocking collectives  50.7 us (37%)
  Pallas kernels  39.5 us (29%)
  starting transfers between devices  33.3 us (24%)
  waiting for transfers between devices  12.3 us (9%)
    all_to_all x5, blocking collectives, exchange(): return lax.all_to_all(array, axis, 0, 0)  50.7 us
    pallas_call x17, Pallas kernels, call(): pl.pallas_call(ordered, name=name, out_shape=out_shape, in_specs=[ANY] *...  39.5 us
    ppermute x17, starting transfers between devices, hop(): return lax.ppermute(array, 'patch', [(i, i ^ bits) for i in range(n_patch)])  24.7 us
    all_to_all x1, starting transfers between devices, exchange(): return lax.all_to_all(array, axis, 0, 0)  8.61 us
    ppermute x17, waiting for transfers between devices, hop(): return lax.ppermute(array, 'patch', [(i, i ^ bits) for i in range(n_patch)])  6.5 us
    all_to_all x1, waiting for transfers between devices, exchange(): return lax.all_to_all(array, axis, 0, 0)  5.76 us
  transfers between devices with their start and end apart: 18, of which 7 were waited for; matrix products, arithmetic and copies ran while one was open for 0% of the time, Pallas kernels for 10%

profile of v4, /device:TPU:1, one launch (start us, length us, event | category | flops | bytes accessed | tf_op | source)
XLA Modules:
  0.0 136.7 jit_solution(17536215192894660918)
XLA Ops:
  0.6 0.1 pad_add_fusion.refs_0_
  0.7 2.7 %own_rows.1 = (bf16[16,64,256]{2,1,0:T(8,128)(2,1)}, f32[32,256]{1,0:T(8,128)S(1)}, f32[8,512]{1,0:T(8,128)S(1)}) custom-call(s32[3]{0:T(128)S(1)} %pad_add_fusion.refs_0_, bf16[256,256]{1,0:T(8,128)(2,1)} %refs_1_.1, bf16[256,256]{1,0:T(8,128)(2,1)} %refs_2_.1, s32[1,32]{1,0:T(1,128)} %bitcast.6, bf16[1,32]{1,0:T(2,128)(2,1)} %bitcast.7), custom_call_target="tpu_custom_call" | custom-call | flops 268435456 | bytes 65536 | tf_op jit(solution)/shard_map/own_rows/pallas_call | solution.py:53
  3.4 8.6 %all-to-all-start = ((bf16[16,64,256]{2,1,0:T(8,128)(2,1)}), bf16[16,64,256]{2,1,0:T(8,128)(2,1)S(1)}, u32[]{:S(2)}, u32[]{:S(2)}) async-start(bf16[16,64,256]{2,1,0:T(8,128)(2,1)} %get-tuple-element.37), calls=%async_computation | async-start | bytes 1048576 | tf_op jit(solution)/shard_map/all_to_all | solution.py:388
  12.0 4.7 %proto_unit.1 = (bf16[8,256,1024]{2,1,0:T(8,128)(2,1)}, bf16[2,256,1024]{2,1,0:T(8,128)(2,1)S(1)}, f32[8,1024]{1,0:T(8,128)S(1)}) custom-call(bf16[256,8192]{1,0:T(8,128)(2,1)} %refs_13_.1), custom_call_target="tpu_custom_call" | custom-call | flops 2147483648 | bytes 65536 | tf_op jit(solution)/shard_map/proto_unit/pallas_call | solution.py:53
  16.8 5.8 %all-to-all-done.refs_0_.refs_1_ = bf16[16,64,256]{2,1,0:T(8,128)(2,1)S(1)} async-done(((bf16[16,64,256]{2,1,0:T(8,128)(2,1)}), bf16[16,64,256]{2,1,0:T(8,128)(2,1)S(1)}, u32[]{:S(2)}, u32[]{:S(2)}) %all-to-all-start) | async-done | bytes 524320 | tf_op jit(solution)/shard_map/all_to_all | solution.py:388
  22.5 4.9 %teacher_table.1 = (bf16[512,8192]{1,0:T(8,128)(2,1)S(1)}, bf16[8,256,1024]{2,1,0:T(8,128)(2,1)S(1)}, f32[8,1024]{1,0:T(8,128)S(1)}) custom-call(bf16[16,64,256]{2,1,0:T(8,128)(2,1)S(1)} %all-to-all-done.refs_0_.refs_1_, bf16[2,256,1024]{2,1,0:T(8,128)(2,1)S(1)} %get-tuple-element.38.refs_1_, bf16[8,256,1024]{2,1,0:T(8,128)(2,1)} %get-tuple-element.39.refs_2_), custom_call_target="tpu_custom_call" | custom-call | flops 4294967296 | bytes 65536 | tf_op jit(solution)/shard_map/teacher_table/pallas_call | solution.py:53
  27.4 2.1 %collective-permute-start = (f32[8,1024]{1,0:T(8,128)S(1)}, f32[8,1024]{1,0:T(8,128)S(1)}, u32[]{:S(2)}, u32[]{:S(2)}) collective-permute-start(f32[8,1024]{1,0:T(8,128)S(1)} %get-tuple-element.40), channel_id=1, source_target_pairs={{0,16},{16,0},{32,48},{48,32},{64,80},{80,64},{96,112},{112,96},{1... | collective-permute-start | bytes 98312 | tf_op jit(solution)/shard_map/ppermute | solution.py:391
  29.5 0.9 collective-permute-done
  30.3 2.5 %collective-permute-start.3 = (f32[8,1024]{1,0:T(8,128)S(1)}, f32[8,1024]{1,0:T(8,128)S(1)}, u32[]{:S(2)}, u32[]{:S(2)}) collective-permute-start(f32[8,1024]{1,0:T(8,128)S(1)} %add.15.refs_0_.refs_1_), channel_id=1, source_target_pairs={{0,96},{16,112},{32,64},{48,80},{64,32},{80,48},{96,0},{112,16},{1... | collective-permute-start | bytes 98312 | tf_op jit(solution)/shard_map/ppermute | solution.py:391
  32.8 0.5 collective-permute-start.2
  33.3 0.3 collective-permute-start.1
  33.6 2.7 %student_table.3 = (bf16[512,3072]{1,0:T(8,128)(2,1)S(1)}, f32[8,512]{1,0:T(8,128)S(1)}, f32[256,512]{1,0:T(8,128)S(1)}) custom-call(f32[8,1024]{1,0:T(8,128)S(1)} %add.15.refs_0_.refs_1_, bf16[16,64,256]{2,1,0:T(8,128)(2,1)S(1)} %all-to-all-done.refs_0_.refs_1_, bf16[8,256,1024]{2,1,0:T(8,128)(2,1)S(1)} %get-tuple-element.41.refs_2_.refs_5_), custom_call_target="tpu_custom_call" | custom-call | flops 2147483648 | bytes 65536 | tf_op jit(solution)/shard_map/student_table/pallas_call | solution.py:53
  36.3 0.0 collective-permute-done.3.refs_4_
  36.3 0.8 collective-permute-done.2.refs_3_
  37.1 0.0 collective-permute-done.1.refs_2_
  37.1 2.3 %row_pass.2 = f32[16,8,128]{2,1,0:T(8,128)S(1)} custom-call(f32[8,512]{1,0:T(8,128)S(1)} %get-tuple-element.42.refs_0_.refs_6_, f32[8,1024]{1,0:T(8,128)S(1)} %add.15.refs_0_.refs_1_, f32[8,1024]{1,0:T(8,128)S(1)} %collective-permute-done.1.refs_2_, f32[8,1024]{1,0:T(8,128)S(1)} %collective-permute-done.2.refs_3_, ...), custom_call_target="tpu_custom_call" | custom-call | flops 2147483648 | bytes 65536 | tf_op jit(solution)/shard_map/row_pass/pallas_call | solution.py:53
  39.4 9.2 %all_to_all.30.refs_0_.refs_1_ = f32[16,8,128]{2,1,0:T(8,128)S(1)} all-to-all(f32[16,8,128]{2,1,0:T(8,128)S(1)} %row_pass.2), channel_id=1, replica_groups=mesh['patch'=8,'proto'=16] {'proto'}, dimensions={0} | all-to-all | bytes 131072 | tf_op jit(solution)/shard_map/all_to_all | solution.py:388
  48.6 1.2 col_pass.2
  49.8 3.3 %collective-permute-start.4 = (f32[8,1024]{1,0:T(8,128)S(1)}, f32[8,1024]{1,0:T(8,128)S(1)}, u32[]{:S(2)}, u32[]{:S(2)}) collective-permute-start(f32[8,1024]{1,0:T(8,128)S(1)} %col_pass.2), channel_id=1, source_target_pairs={{0,16},{16,0},{32,48},{48,32},{64,80},{80,64},{96,112},{112,96},{1... | collective-permute-start | bytes 98312 | tf_op jit(solution)/shard_map/ppermute | solution.py:391
  53.1 0.9 collective-permute-done.4
  53.9 1.1 collective-permute-start.7
  55.1 0.8 collective-permute-start.6
  55.9 1.3 collective-permute-start.5
  57.2 2.7 %student_table.4 = (bf16[512,3072]{1,0:T(8,128)(2,1)S(1)}, f32[8,512]{1,0:T(8,128)S(1)}, f32[256,512]{1,0:T(8,128)S(1)}) custom-call(f32[8,1024]{1,0:T(8,128)S(1)} %add.16.refs_0_.refs_1_, bf16[16,64,256]{2,1,0:T(8,128)(2,1)S(1)} %all-to-all-done.refs_0_.refs_1_, bf16[8,256,1024]{2,1,0:T(8,128)(2,1)S(1)} %get-tuple-element.41.refs_2_.refs_5_), custom_call_target="tpu_custom_call" | custom-call | flops 2147483648 | bytes 65536 | tf_op jit(solution)/shard_map/student_table/pallas_call | solution.py:53
  59.9 0.0 collective-permute-done.7.refs_4_
  59.9 0.0 collective-permute-done.6.refs_3_
  59.9 0.0 collective-permute-done.5.refs_2_
  59.9 2.3 %row_pass.3 = f32[16,8,128]{2,1,0:T(8,128)S(1)} custom-call(f32[8,512]{1,0:T(8,128)S(1)} %get-tuple-element.45.refs_0_.refs_7_, f32[8,1024]{1,0:T(8,128)S(1)} %add.16.refs_0_.refs_1_, f32[8,1024]{1,0:T(8,128)S(1)} %collective-permute-done.5.refs_2_, f32[8,1024]{1,0:T(8,128)S(1)} %collective-permute-done.6.refs_3_, ...), custom_call_target="tpu_custom_call" | custom-call | flops 2147483648 | bytes 65536 | tf_op jit(solution)/shard_map/row_pass/pallas_call | solution.py:53
  62.2 9.4 %all_to_all.31.refs_0_ = f32[16,8,128]{2,1,0:T(8,128)S(1)} all-to-all(f32[16,8,128]{2,1,0:T(8,128)S(1)} %row_pass.3), channel_id=1, replica_groups=mesh['patch'=8,'proto'=16] {'proto'}, dimensions={0} | all-to-all | bytes 131072 | tf_op jit(solution)/shard_map/all_to_all | solution.py:388
  71.6 1.2 col_pass.3
  72.8 2.9 %collective-permute-start.8 = (f32[8,1024]{1,0:T(8,128)S(1)}, f32[8,1024]{1,0:T(8,128)S(1)}, u32[]{:S(2)}, u32[]{:S(2)}) collective-permute-start(f32[8,1024]{1,0:T(8,128)S(1)} %col_pass.3), channel_id=1, source_target_pairs={{0,16},{16,0},{32,48},{48,32},{64,80},{80,64},{96,112},{112,96},{1... | collective-permute-start | bytes 98312 | tf_op jit(solution)/shard_map/ppermute | solution.py:391
  75.7 0.9 collective-permute-done.8
  76.6 1.4 %collective-permute-start.11 = (f32[8,1024]{1,0:T(8,128)S(1)}, f32[8,1024]{1,0:T(8,128)S(1)}, u32[]{:S(2)}, u32[]{:S(2)}) collective-permute-start(f32[8,1024]{1,0:T(8,128)S(1)} %add.17.refs_0_.refs_3_), channel_id=1, source_target_pairs={{0,96},{16,112},{32,64},{48,80},{64,32},{80,48},{96,0},{112,16},{1... | collective-permute-start | bytes 98312 | tf_op jit(solution)/shard_map/ppermute | solution.py:391
  78.0 1.1 collective-permute-start.10
  79.1 0.7 collective-permute-start.9
  79.8 1.9 %student_table.5 = (bf16[512,2048]{1,0:T(8,128)(2,1)S(1)}, f32[8,512]{1,0:T(8,128)S(1)}, f32[256,512]{1,0:T(8,128)S(1)}, bf16[256,512]{1,0:T(8,128)(2,1)S(1)}) custom-call(f32[8,1024]{1,0:T(8,128)S(1)} %add.17.refs_0_.refs_3_, bf16[16,64,256]{2,1,0:T(8,128)(2,1)S(1)} %all-to-all-done.refs_0_.refs_1_, bf16[8,256,1024]{2,1,0:T(8,128)(2,1)S(1)} %get-tuple-element.41.refs_2_.refs_5_), custom_call_target="tpu_custom_call" | custom-call | flops 2147483648 | bytes 65536 | tf_op jit(solution)/shard_map/student_table/pallas_call | solution.py:53
  81.7 0.0 collective-permute-done.11.refs_3_.refs_6_
  81.7 0.5 collective-permute-done.10.refs_2_.refs_5_
  82.2 0.0 collective-permute-done.9.refs_1_.refs_4_
  82.2 0.0 copy-start.1
  82.2 2.5 %last_row_pass.1 = (f32[16,8,128]{2,1,0:T(8,128)S(1)}, f32[256,512]{1,0:T(8,128)S(1)}) custom-call(f32[8,1024]{1,0:T(8,128)S(1)} %add.17.refs_0_.refs_3_, f32[8,1024]{1,0:T(8,128)S(1)} %collective-permute-done.9.refs_1_.refs_4_, f32[8,1024]{1,0:T(8,128)S(1)} %collective-permute-done.10.refs_2_.refs_5_, ...), custom_call_target="tpu_custom_call" | custom-call | flops 2147483648 | bytes 65536 | tf_op jit(solution)/shard_map/last_row_pass/pallas_call | solution.py:53
  84.8 9.4 %all_to_all.32.refs_2_ = f32[16,8,128]{2,1,0:T(8,128)S(1)} all-to-all(f32[16,8,128]{2,1,0:T(8,128)S(1)} %get-tuple-element.47), channel_id=1, replica_groups=mesh['patch'=8,'proto'=16] {'proto'}, dimensions={0} | all-to-all | bytes 131072 | tf_op jit(solution)/shard_map/all_to_all | solution.py:388
  94.1 0.0 copy-done.1
  94.1 7.6 %head.1 = (f32[32,8192]{1,0:T(8,128)}, bf16[32,8192]{1,0:T(8,128)(2,1)S(1)}, bf16[3,32,8192]{2,1,0:T(8,128)(2,1)S(1)}, bf16[3,32,8192]{2,1,0:T(8,128)(2,1)S(1)}) custom-call(s32[3]{0:T(128)S(1)} %pad_add_fusion.refs_0_, f32[16,8,128]{2,1,0:T(8,128)S(1)} %all_to_all.30.refs_0_.refs_1_, f32[16,8,128]{2,1,0:T(8,128)S(1)} %all_to_all.32.refs_2_, ...), custom_call_target="tpu_custom_call" | custom-call | flops 8589934592 | bytes 65536 | tf_op jit(solution)/shard_map/head/pallas_call | solution.py:53
  101.7 3.3 %collective-permute-start.13 = (bf16[3,32,8192]{2,1,0:T(8,128)(2,1)S(1)}, bf16[3,32,8192]{2,1,0:T(8,128)(2,1)S(1)}, u32[]{:S(2)}, u32[]{:S(2)}) collective-permute-start(bf16[3,32,8192]{2,1,0:T(8,128)(2,1)S(1)} %get-tuple-element.65), channel_id=1, source_target_pairs={{0,16},{16,0},{32,48},{48,32},{64,80},{80,64},{96,112},{112,96},{1... | collective-permute-start | bytes 4718600 | tf_op jit(solution)/shard_map/ppermute | solution.py:391
  105.0 0.1 collective-permute-start.12
  105.1 0.3 feature.1.refs_0_
  105.4 0.0 copy-start
  105.4 2.6 %collective-permute-done.13.refs_2_ = bf16[3,32,8192]{2,1,0:T(8,128)(2,1)S(1)} collective-permute-done((bf16[3,32,8192]{2,1,0:T(8,128)(2,1)S(1)}, bf16[3,32,8192]{2,1,0:T(8,128)(2,1)S(1)}, u32[]{:S(2)}, u32[]{:S(2)}) %collective-permute-start.13) | collective-permute-done | bytes 1572896 | tf_op jit(solution)/shard_map/ppermute | solution.py:391
  108.0 0.4 pair_sums.1
  108.4 1.8 %collective-permute-start.14 = (bf16[32,8192]{1,0:T(8,128)(2,1)S(1)}, bf16[32,8192]{1,0:T(8,128)(2,1)S(1)}, u32[]{:S(2)}, u32[]{:S(2)}) collective-permute-start(bf16[32,8192]{1,0:T(8,128)(2,1)S(1)} %get-tuple-element.66), channel_id=1, source_target_pairs={{0,64},{16,80},{32,96},{48,112},{64,0},{80,16},{96,32},{112,48},{1... | collective-permute-start | bytes 1572872 | tf_op jit(solution)/shard_map/ppermute | solution.py:391
  110.2 0.1 collective-permute-start.15
  110.3 1.4 %collective-permute-start.16 = (bf16[32,8192]{1,0:T(8,128)(2,1)S(1)}, bf16[32,8192]{1,0:T(8,128)(2,1)S(1)}, u32[]{:S(2)}, u32[]{:S(2)}) collective-permute-start(bf16[32,8192]{1,0:T(8,128)(2,1)S(1)} %get-tuple-element.68), channel_id=1, source_target_pairs={{0,96},{16,112},{32,64},{48,80},{64,32},{80,48},{96,0},{112,16},{1... | collective-permute-start | bytes 1572872 | tf_op jit(solution)/shard_map/ppermute | solution.py:391
  111.7 11.3 %all_to_all.33.refs_0_ = bf16[16,48,256]{2,1,0:T(8,128)(2,1)S(1)} all-to-all(bf16[16,48,256]{2,1,0:T(8,128)(2,1)S(1)} %feature.1.refs_0_), channel_id=1, replica_groups=mesh['patch'=8,'proto'=16] {'proto'}, dimensions={0} | all-to-all | bytes 786432 | tf_op jit(solution)/shard_map/all_to_all | solution.py:388
  123.0 0.8 owner.1
  123.8 0.0 collective-permute-done.12.refs_1_
  123.8 0.0 copy-done
  123.8 0.1 own_sum.1
  123.9 11.5 %all_to_all.34.refs_1_ = f32[8,8,128]{2,1,0:T(8,128)S(1)} all-to-all(f32[8,8,128]{2,1,0:T(8,128)S(1)} %get-tuple-element.64), channel_id=1, replica_groups=mesh['patch'=8,'proto'=16] {'patch'}, dimensions={0} | all-to-all | bytes 65536 | tf_op jit(solution)/shard_map/all_to_all | solution.py:388
  135.4 0.0 collective-permute-done.14.refs_2_
  135.4 0.0 collective-permute-done.15.refs_3_
  135.4 0.0 collective-permute-done.16.refs_4_
  135.4 1.3 assemble.1
  (3 shorter events, 0.0 us)
Async XLA Ops:
  3.4 19.1 %all-to-all-start = ((bf16[16,64,256]{2,1,0:T(8,128)(2,1)}), bf16[16,64,256]{2,1,0:T(8,128)(2,1)S(1)}, u32[]{:S(2)}, u32[]{:S(2)}) async-start(bf16[16,64,256]{2,1,0:T(8,128)(2,1)} %get-tuple-element.37), calls=%async_computation | async-start | bytes 1048576 | tf_op jit(solution)/shard_map/all_to_all | solution.py:388
  27.4 2.9 %collective-permute-start = (f32[8,1024]{1,0:T(8,128)S(1)}, f32[8,1024]{1,0:T(8,128)S(1)}, u32[]{:S(2)}, u32[]{:S(2)}) collective-permute-start(f32[8,1024]{1,0:T(8,128)S(1)} %get-tuple-element.40), channel_id=1, source_target_pairs={{0,16},{16,0},{32,48},{48,32},{64,80},{80,64},{96,112},{112,96},{1... | collective-permute-start | bytes 98312 | tf_op jit(solution)/shard_map/ppermute | solution.py:391
  30.3 5.9 %collective-permute-start.3 = (f32[8,1024]{1,0:T(8,128)S(1)}, f32[8,1024]{1,0:T(8,128)S(1)}, u32[]{:S(2)}, u32[]{:S(2)}) collective-permute-start(f32[8,1024]{1,0:T(8,128)S(1)} %add.15.refs_0_.refs_1_), channel_id=1, source_target_pairs={{0,96},{16,112},{32,64},{48,80},{64,32},{80,48},{96,0},{112,16},{1... | collective-permute-start | bytes 98312 | tf_op jit(solution)/shard_map/ppermute | solution.py:391
  32.8 4.3 %collective-permute-start.2 = (f32[8,1024]{1,0:T(8,128)S(1)}, f32[8,1024]{1,0:T(8,128)S(1)}, u32[]{:S(2)}, u32[]{:S(2)}) collective-permute-start(f32[8,1024]{1,0:T(8,128)S(1)} %add.15.refs_0_.refs_1_), channel_id=1, source_target_pairs={{0,64},{16,80},{32,96},{48,112},{64,0},{80,16},{96,32},{112,48},{1... | collective-permute-start | bytes 98312 | tf_op jit(solution)/shard_map/ppermute | solution.py:391
  33.3 3.8 %collective-permute-start.1 = (f32[8,1024]{1,0:T(8,128)S(1)}, f32[8,1024]{1,0:T(8,128)S(1)}, u32[]{:S(2)}, u32[]{:S(2)}) collective-permute-start(f32[8,1024]{1,0:T(8,128)S(1)} %add.15.refs_0_.refs_1_), channel_id=1, source_target_pairs={{0,32},{16,48},{32,0},{48,16},{64,96},{80,112},{96,64},{112,80},{1... | collective-permute-start | bytes 98312 | tf_op jit(solution)/shard_map/ppermute | solution.py:391
  49.8 4.1 %collective-permute-start.4 = (f32[8,1024]{1,0:T(8,128)S(1)}, f32[8,1024]{1,0:T(8,128)S(1)}, u32[]{:S(2)}, u32[]{:S(2)}) collective-permute-start(f32[8,1024]{1,0:T(8,128)S(1)} %col_pass.2), channel_id=1, source_target_pairs={{0,16},{16,0},{32,48},{48,32},{64,80},{80,64},{96,112},{112,96},{1... | collective-permute-start | bytes 98312 | tf_op jit(solution)/shard_map/ppermute | solution.py:391
  53.9 5.9 %collective-permute-start.7 = (f32[8,1024]{1,0:T(8,128)S(1)}, f32[8,1024]{1,0:T(8,128)S(1)}, u32[]{:S(2)}, u32[]{:S(2)}) collective-permute-start(f32[8,1024]{1,0:T(8,128)S(1)} %add.16.refs_0_.refs_1_), channel_id=1, source_target_pairs={{0,96},{16,112},{32,64},{48,80},{64,32},{80,48},{96,0},{112,16},{1... | collective-permute-start | bytes 98312 | tf_op jit(solution)/shard_map/ppermute | solution.py:391
  55.1 4.8 %collective-permute-start.6 = (f32[8,1024]{1,0:T(8,128)S(1)}, f32[8,1024]{1,0:T(8,128)S(1)}, u32[]{:S(2)}, u32[]{:S(2)}) collective-permute-start(f32[8,1024]{1,0:T(8,128)S(1)} %add.16.refs_0_.refs_1_), channel_id=1, source_target_pairs={{0,64},{16,80},{32,96},{48,112},{64,0},{80,16},{96,32},{112,48},{1... | collective-permute-start | bytes 98312 | tf_op jit(solution)/shard_map/ppermute | solution.py:391
  55.9 4.0 %collective-permute-start.5 = (f32[8,1024]{1,0:T(8,128)S(1)}, f32[8,1024]{1,0:T(8,128)S(1)}, u32[]{:S(2)}, u32[]{:S(2)}) collective-permute-start(f32[8,1024]{1,0:T(8,128)S(1)} %add.16.refs_0_.refs_1_), channel_id=1, source_target_pairs={{0,32},{16,48},{32,0},{48,16},{64,96},{80,112},{96,64},{112,80},{1... | collective-permute-start | bytes 98312 | tf_op jit(solution)/shard_map/ppermute | solution.py:391
  72.8 3.7 %collective-permute-start.8 = (f32[8,1024]{1,0:T(8,128)S(1)}, f32[8,1024]{1,0:T(8,128)S(1)}, u32[]{:S(2)}, u32[]{:S(2)}) collective-permute-start(f32[8,1024]{1,0:T(8,128)S(1)} %col_pass.3), channel_id=1, source_target_pairs={{0,16},{16,0},{32,48},{48,32},{64,80},{80,64},{96,112},{112,96},{1... | collective-permute-start | bytes 98312 | tf_op jit(solution)/shard_map/ppermute | solution.py:391
  76.6 5.2 %collective-permute-start.11 = (f32[8,1024]{1,0:T(8,128)S(1)}, f32[8,1024]{1,0:T(8,128)S(1)}, u32[]{:S(2)}, u32[]{:S(2)}) collective-permute-start(f32[8,1024]{1,0:T(8,128)S(1)} %add.17.refs_0_.refs_3_), channel_id=1, source_target_pairs={{0,96},{16,112},{32,64},{48,80},{64,32},{80,48},{96,0},{112,16},{1... | collective-permute-start | bytes 98312 | tf_op jit(solution)/shard_map/ppermute | solution.py:391
  78.0 4.3 %collective-permute-start.10 = (f32[8,1024]{1,0:T(8,128)S(1)}, f32[8,1024]{1,0:T(8,128)S(1)}, u32[]{:S(2)}, u32[]{:S(2)}) collective-permute-start(f32[8,1024]{1,0:T(8,128)S(1)} %add.17.refs_0_.refs_3_), channel_id=1, source_target_pairs={{0,64},{16,80},{32,96},{48,112},{64,0},{80,16},{96,32},{112,48},{1... | collective-permute-start | bytes 98312 | tf_op jit(solution)/shard_map/ppermute | solution.py:391
  79.1 3.1 %collective-permute-start.9 = (f32[8,1024]{1,0:T(8,128)S(1)}, f32[8,1024]{1,0:T(8,128)S(1)}, u32[]{:S(2)}, u32[]{:S(2)}) collective-permute-start(f32[8,1024]{1,0:T(8,128)S(1)} %add.17.refs_0_.refs_3_), channel_id=1, source_target_pairs={{0,32},{16,48},{32,0},{48,16},{64,96},{80,112},{96,64},{112,80},{1... | collective-permute-start | bytes 98312 | tf_op jit(solution)/shard_map/ppermute | solution.py:391
  82.2 11.9 %copy-start.1 = (bf16[256,8192]{1,0:T(8,128)(2,1)S(1)}, bf16[256,8192]{1,0:T(8,128)(2,1)}, u32[]{:S(2)}) copy-start(bf16[256,8192]{1,0:T(8,128)(2,1)} %refs_13_.1) | copy-start | bytes 12582916
  101.7 6.3 %collective-permute-start.13 = (bf16[3,32,8192]{2,1,0:T(8,128)(2,1)S(1)}, bf16[3,32,8192]{2,1,0:T(8,128)(2,1)S(1)}, u32[]{:S(2)}, u32[]{:S(2)}) collective-permute-start(bf16[3,32,8192]{2,1,0:T(8,128)(2,1)S(1)} %get-tuple-element.65), channel_id=1, source_target_pairs={{0,16},{16,0},{32,48},{48,32},{64,80},{80,64},{96,112},{112,96},{1... | collective-permute-start | bytes 4718600 | tf_op jit(solution)/shard_map/ppermute | solution.py:391
  105.0 18.8 %collective-permute-start.12 = (bf16[32,8192]{1,0:T(8,128)(2,1)S(1)}, bf16[32,8192]{1,0:T(8,128)(2,1)S(1)}, u32[]{:S(2)}, u32[]{:S(2)}) collective-permute-start(bf16[32,8192]{1,0:T(8,128)(2,1)S(1)} %get-tuple-element.61), channel_id=1, source_target_pairs={{0,16},{16,0},{32,48},{48,32},{64,80},{80,64},{96,112},{112,96},{1... | collective-permute-start | bytes 1572872 | tf_op jit(solution)/shard_map/ppermute | solution.py:391
  105.4 18.4 %copy-start = (f32[32,8192]{1,0:T(8,128)S(1)}, f32[32,8192]{1,0:T(8,128)}, u32[]{:S(2)}) copy-start(f32[32,8192]{1,0:T(8,128)} %get-tuple-element.60.refs_0_) | copy-start | bytes 3145732
  108.4 27.0 %collective-permute-start.14 = (bf16[32,8192]{1,0:T(8,128)(2,1)S(1)}, bf16[32,8192]{1,0:T(8,128)(2,1)S(1)}, u32[]{:S(2)}, u32[]{:S(2)}) collective-permute-start(bf16[32,8192]{1,0:T(8,128)(2,1)S(1)} %get-tuple-element.66), channel_id=1, source_target_pairs={{0,64},{16,80},{32,96},{48,112},{64,0},{80,16},{96,32},{112,48},{1... | collective-permute-start | bytes 1572872 | tf_op jit(solution)/shard_map/ppermute | solution.py:391
  110.2 25.2 %collective-permute-start.15 = (bf16[32,8192]{1,0:T(8,128)(2,1)S(1)}, bf16[32,8192]{1,0:T(8,128)(2,1)S(1)}, u32[]{:S(2)}, u32[]{:S(2)}) collective-permute-start(bf16[32,8192]{1,0:T(8,128)(2,1)S(1)} %get-tuple-element.67), channel_id=1, source_target_pairs={{0,32},{16,48},{32,0},{48,16},{64,96},{80,112},{96,64},{112,80},{1... | collective-permute-start | bytes 1572872 | tf_op jit(solution)/shard_map/ppermute | solution.py:391
  110.3 25.1 %collective-permute-start.16 = (bf16[32,8192]{1,0:T(8,128)(2,1)S(1)}, bf16[32,8192]{1,0:T(8,128)(2,1)S(1)}, u32[]{:S(2)}, u32[]{:S(2)}) collective-permute-start(bf16[32,8192]{1,0:T(8,128)(2,1)S(1)} %get-tuple-element.68), channel_id=1, source_target_pairs={{0,96},{16,112},{32,64},{48,80},{64,32},{80,48},{96,0},{112,16},{1... | collective-permute-start | bytes 1572872 | tf_op jit(solution)/shard_map/ppermute | solution.py:391

commit v5 on v4

--- a/solution.py
+++ b/solution.py
@@ -16,6 +16,7 @@
 LANES = 128
 PIECES = (3, 3, 2)
 FIRST = 2
+PARTS = (6, 2)
 VMEM_LIMIT = 20 * 1024 * 1024
 
 NN = (((1,), (0,)), ((), ()))
@@ -263,14 +264,14 @@
     return read_rows(first_ref, tile, n), read_rows(last_ref, tile, n), read_rows(last_ref, 0, n)
 
 
-def head_body(parts, *refs):
+def head_body(first, parts, *refs):
     place_ref, first_ref, last_ref = refs[:3]
     sums_refs = refs[3 : 3 + parts]
-    turned_ref, inverse_ref, codes_ref, *piece_refs, w_ref = refs[3 + parts : -7]
-    own_hbm, own_near_ref, keep_ref, near_ref, turn_ref, own_ref, sems = refs[-7:]
+    turned_ref, inverse_ref, codes_ref, *piece_refs, w_ref = refs[3 + parts : -6]
+    own_hbm, keep_ref, near_ref, turn_ref, own_ref, sems = refs[-6:]
     x, core = place_ref[1], place_ref[2]
-    share = near_ref.shape[1]
-    chips = near_ref.shape[0] + 1
+    chips, share = near_ref.shape[:2]
+    width = inverse_ref.shape[1]
     spots = []
     for k in range(chips):
         for side in (core, 1 - core):
@@ -284,38 +285,51 @@
     scale = 1.0 / column_sum(sums_refs)
     where = [(p, at) for p, size in enumerate(PIECES) for at in range(size)]
     stores = []
-    for j, cols in chunks(codes_ref):
-        piece, at = where[j]
-        width = codes_ref.shape[1] // len(where)
-        head = mm(left_probs, piece_refs[piece][:, pl.ds(at * width, width)]) - scale[
-            j : j + 1, :
-        ] * mm(left_codes, codes_ref[:, cols])
-        inverse = inverse_ref[pl.ds(j, 1), :]
-        w = jnp.concatenate([w_ref[spot, cols] for spot in spots], axis=0)
-        unit = w.astype(F32) * inverse
-        inner = jnp.sum(unit * head, axis=0, keepdims=True)
-        grad = inverse * (head - unit * inner)
+    for j, cols in chunks(own_ref, own_ref.shape[1] // width):
+        row = first + j
+        here = pl.ds(row * width, width)
+        piece, at = where[row]
+        inverse = inverse_ref[pl.ds(row, 1), :]
+        head = inverse * mm(left_probs, piece_refs[piece][:, pl.ds(at * width, width)]) - (
+            inverse * scale[row : row + 1, :]
+        ) * mm(left_codes, codes_ref[:, here])
+        w = jnp.concatenate([w_ref[spot, here] for spot in spots], axis=0).astype(F32)
+        inner = jnp.sum(w * head, axis=0, keepdims=True)
+        grad = head - w * (inverse * inverse * inner)
         own_ref[:, cols] = grad[0:share]
         store = pltpu.make_async_copy(own_ref.at[:, cols], own_hbm.at[:, cols], sems.at[j])
         store.start()
         stores.append(store)
-        own_near_ref[:, cols] = grad[share : 2 * share].astype(BF16)
-        for k in range(1, chips):
+        for k in range(chips):
             low = 2 * k * share
-            keep_ref[k - 1, :, cols] = grad[low : low + share].astype(BF16)
-            near_ref[k - 1, :, cols] = grad[low + share : low + 2 * share].astype(BF16)
+            if k:
+                keep_ref[k - 1, :, cols] = grad[low : low + share].astype(BF16)
+            near_ref[k, :, cols] = grad[low + share : low + 2 * share].astype(BF16)
     for store in stores:
         store.wait()
 
 
-def pair_body(keep_ref, near_ref, *pair_refs):
-    for k, pair_ref in enumerate(pair_refs):
-        pair_ref[...] = (keep_ref[k].astype(F32) + near_ref[k].astype(F32)).astype(BF16)
-
-
-def own_sum_body(own_ref, near_ref, tails_ref, out_ref, tails_out_ref):
-    out_ref[...] = own_ref[...] + near_ref[...].astype(F32)
-    tails_out_ref[...] = tails_ref[...]
+def pair_body(*refs):
+    count = len(PARTS)
+    start = 0
+    for part in range(count):
+        keep_ref, near_ref = refs[2 * part : 2 * part + 2]
+        span = keep_ref.shape[2]
+        for k, pair_ref in enumerate(refs[2 * count :]):
+            total = keep_ref[k].astype(F32) + near_ref[k + 1].astype(F32)
+            pair_ref[:, start : start + span] = total.astype(BF16)
+        start += span
+
+
+def own_sum_body(tails_ref, *refs):
+    count = len(PARTS)
+    start = 0
+    for part in range(count):
+        own_ref, near_ref = refs[2 * part : 2 * part + 2]
+        span = own_ref.shape[1]
+        refs[-2][:, start : start + span] = own_ref[...] + near_ref[0].astype(F32)
+        start += span
+    refs[-1][...] = tails_ref[...]
 
 
 def final_body(own_ref, tails_ref, *refs):
@@ -489,46 +503,56 @@
 
     turned = pieces[-1][3]
     factors = (messages[0], messages[-1])
-    own_block, own_near, keep, near = call(
-        functools.partial(head_body, chips),
-        "head",
-        (
-            pltpu.HBM((share, protos), F32),
-            shape((share, protos), BF16),
-            shape((chips - 1, share, protos), BF16),
-            shape((chips - 1, share, protos), BF16),
-        ),
-        (
-            place,
-            *factors,
-            *parts,
-            turned,
-            inverse,
-            codes,
-            *[piece[0] for piece in pieces],
-            proto_weight,
-        ),
-        4 * product,
-        specs=[SMEM] + [VMEM] * (len(factors) + chips + 4 + len(pieces)),
-        scratch=[
-            pltpu.VMEM((d, rows), BF16),
-            pltpu.VMEM((share, protos), F32),
-            pltpu.SemaphoreType.DMA((8,)),
-        ],
-    )
+    heads = []
+    for index, count in enumerate(PARTS):
+        span = count * width
+        heads.append(
+            call(
+                functools.partial(head_body, sum(PARTS[:index]), chips),
+                "head",
+                (
+                    pltpu.HBM((share, span), F32),
+                    shape((chips - 1, share, span), BF16),
+                    shape((chips, share, span), BF16),
+                ),
+                (
+                    place,
+                    *factors,
+                    *parts,
+                    turned,
+                    inverse,
+                    codes,
+                    *[piece[0] for piece in pieces],
+                    proto_weight,
+                ),
+                2 * product,
+                specs=[SMEM] + [VMEM] * (len(factors) + chips + 4 + len(pieces)),
+                after=(heads[-1][1],) if heads else (),
+                scratch=[
+                    pltpu.VMEM((d, rows), BF16),
+                    pltpu.VMEM((share, span), F32),
+                    pltpu.SemaphoreType.DMA((count,)),
+                ],
+            )
+        )
     feature_part = call(
         feature_body,
         "feature",
         shape((n_proto, own + 16, d), BF16),
         (*factors, codes_feature, turned, *[piece[2] for piece in pieces]),
         product // 4,
-        after=(keep,),
-    )
+        after=(heads[-1][1],),
+    )
+    ends, nears = [], []
+    for own_block, keep, near in heads:
+        near = hop(near, 1)
+        ends += [keep, near]
+        nears += [own_block, near]
     pairs = call(
         pair_body,
         "pair_sums",
         tuple(shape((share, protos), BF16) for _ in range(chips - 1)),
-        (keep, hop(near, 1)),
+        tuple(ends),
         product // 8,
         after=(feature_part,),
     )
@@ -544,7 +568,7 @@
         own_sum_body,
         "own_sum",
         (shape((share, protos), F32), shape((n_patch, 8, LANES), F32)),
-        (own_block, hop(own_near, 1), tails),
+        (tails, *nears),
         product // 8,
     )
     grad_proto, loss = call(

time: 137 us -> 138 us (level)
  Pallas kernels: 39.5 us -> 41.6 us
    pallas_call x17 -> x18, Pallas kernels: 39.5 us -> 41.6 us  [call(): pl.pallas_call(ordered, name=name, out_shape=out_shape, in_specs=[ANY] *...]
  transfers between devices with their start and end apart: 18 -> 18, of which waited for: 7 -> 7; matrix products, arithmetic and copies ran while one was open for 0% -> 0% of each run, Pallas kernels for 10% -> 12%
where the time goes in v5:
time: 138 us
  blocking collectives  50.7 us (37%)
  Pallas kernels  41.6 us (30%)
  starting transfers between devices  33.3 us (24%)
  waiting for transfers between devices  11.2 us (8%)
    all_to_all x5, blocking collectives, exchange(): return lax.all_to_all(array, axis, 0, 0)  50.7 us
    pallas_call x18, Pallas kernels, call(): pl.pallas_call(ordered, name=name, out_shape=out_shape, in_specs=[ANY] *...  41.6 us
    ppermute x17, starting transfers between devices, hop(): return lax.ppermute(array, 'patch', [(i, i ^ bits) for i in range(n_patch)])  24.7 us
    all_to_all x1, starting transfers between devices, exchange(): return lax.all_to_all(array, axis, 0, 0)  8.61 us
    all_to_all x1, waiting for transfers between devices, exchange(): return lax.all_to_all(array, axis, 0, 0)  5.76 us
    ppermute x17, waiting for transfers between devices, hop(): return lax.ppermute(array, 'patch', [(i, i ^ bits) for i in range(n_patch)])  5.43 us
  transfers between devices with their start and end apart: 18, of which 7 were waited for; matrix products, arithmetic and copies ran while one was open for 0% of the time, Pallas kernels for 12%

profile of v5, /device:TPU:1, one launch (start us, length us, event | category | flops | bytes accessed | tf_op | source)
XLA Modules:
  0.0 137.8 jit_solution(5392392970425265077)
XLA Ops:
  0.6 0.1 pad_add_fusion.refs_0_.refs_1_
  0.7 2.7 %own_rows.1 = (bf16[16,64,256]{2,1,0:T(8,128)(2,1)}, f32[32,256]{1,0:T(8,128)S(1)}, f32[8,512]{1,0:T(8,128)S(1)}) custom-call(s32[3]{0:T(128)S(1)} %pad_add_fusion.refs_0_.refs_1_, bf16[256,256]{1,0:T(8,128)(2,1)} %refs_1_.1, bf16[256,256]{1,0:T(8,128)(2,1)} %refs_2_.1, s32[1,32]{1,0:T(1,128)} %bitcast.6, bf16[1,32]{1,0:T(2,128)(2,1)} %bitcast.7), custom_call_target="tpu_custom_call" | custom-call | flops 268435456 | bytes 65536 | tf_op jit(solution)/shard_map/own_rows/pallas_call | solution.py:54
  3.4 8.6 %all-to-all-start = ((bf16[16,64,256]{2,1,0:T(8,128)(2,1)}), bf16[16,64,256]{2,1,0:T(8,128)(2,1)S(1)}, u32[]{:S(2)}, u32[]{:S(2)}) async-start(bf16[16,64,256]{2,1,0:T(8,128)(2,1)} %get-tuple-element.39), calls=%async_computation | async-start | bytes 1048576 | tf_op jit(solution)/shard_map/all_to_all | solution.py:402
  12.0 4.7 %proto_unit.1 = (bf16[8,256,1024]{2,1,0:T(8,128)(2,1)}, bf16[2,256,1024]{2,1,0:T(8,128)(2,1)S(1)}, f32[8,1024]{1,0:T(8,128)S(1)}) custom-call(bf16[256,8192]{1,0:T(8,128)(2,1)} %refs_14_.1), custom_call_target="tpu_custom_call" | custom-call | flops 2147483648 | bytes 65536 | tf_op jit(solution)/shard_map/proto_unit/pallas_call | solution.py:54
  16.8 5.8 %all-to-all-done.refs_0_.refs_1_ = bf16[16,64,256]{2,1,0:T(8,128)(2,1)S(1)} async-done(((bf16[16,64,256]{2,1,0:T(8,128)(2,1)}), bf16[16,64,256]{2,1,0:T(8,128)(2,1)S(1)}, u32[]{:S(2)}, u32[]{:S(2)}) %all-to-all-start) | async-done | bytes 524320 | tf_op jit(solution)/shard_map/all_to_all | solution.py:402
  22.5 4.9 %teacher_table.1 = (bf16[512,8192]{1,0:T(8,128)(2,1)S(1)}, bf16[8,256,1024]{2,1,0:T(8,128)(2,1)S(1)}, f32[8,1024]{1,0:T(8,128)S(1)}) custom-call(bf16[16,64,256]{2,1,0:T(8,128)(2,1)S(1)} %all-to-all-done.refs_0_.refs_1_, bf16[2,256,1024]{2,1,0:T(8,128)(2,1)S(1)} %get-tuple-element.40.refs_1_, bf16[8,256,1024]{2,1,0:T(8,128)(2,1)} %get-tuple-element.41.refs_2_), custom_call_target="tpu_custom_call" | custom-call | flops 4294967296 | bytes 65536 | tf_op jit(solution)/shard_map/teacher_table/pallas_call | solution.py:54
  27.4 2.1 %collective-permute-start = (f32[8,1024]{1,0:T(8,128)S(1)}, f32[8,1024]{1,0:T(8,128)S(1)}, u32[]{:S(2)}, u32[]{:S(2)}) collective-permute-start(f32[8,1024]{1,0:T(8,128)S(1)} %get-tuple-element.42), channel_id=1, source_target_pairs={{0,16},{16,0},{32,48},{48,32},{64,80},{80,64},{96,112},{112,96},{1... | collective-permute-start | bytes 98312 | tf_op jit(solution)/shard_map/ppermute | solution.py:405
  29.5 0.9 collective-permute-done
  30.3 2.5 %collective-permute-start.3 = (f32[8,1024]{1,0:T(8,128)S(1)}, f32[8,1024]{1,0:T(8,128)S(1)}, u32[]{:S(2)}, u32[]{:S(2)}) collective-permute-start(f32[8,1024]{1,0:T(8,128)S(1)} %add.15.refs_0_.refs_1_), channel_id=1, source_target_pairs={{0,96},{16,112},{32,64},{48,80},{64,32},{80,48},{96,0},{112,16},{1... | collective-permute-start | bytes 98312 | tf_op jit(solution)/shard_map/ppermute | solution.py:405
  32.8 0.5 collective-permute-start.2
  33.3 0.3 collective-permute-start.1
  33.6 2.7 %student_table.3 = (bf16[512,3072]{1,0:T(8,128)(2,1)S(1)}, f32[8,512]{1,0:T(8,128)S(1)}, f32[256,512]{1,0:T(8,128)S(1)}) custom-call(f32[8,1024]{1,0:T(8,128)S(1)} %add.15.refs_0_.refs_1_, bf16[16,64,256]{2,1,0:T(8,128)(2,1)S(1)} %all-to-all-done.refs_0_.refs_1_, bf16[8,256,1024]{2,1,0:T(8,128)(2,1)S(1)} %get-tuple-element.43.refs_2_.refs_5_), custom_call_target="tpu_custom_call" | custom-call | flops 2147483648 | bytes 65536 | tf_op jit(solution)/shard_map/student_table/pallas_call | solution.py:54
  36.3 0.0 collective-permute-done.3.refs_4_
  36.3 0.8 collective-permute-done.2.refs_3_
  37.1 0.0 collective-permute-done.1.refs_2_
  37.1 2.3 %row_pass.2 = f32[16,8,128]{2,1,0:T(8,128)S(1)} custom-call(f32[8,512]{1,0:T(8,128)S(1)} %get-tuple-element.44.refs_0_.refs_6_, f32[8,1024]{1,0:T(8,128)S(1)} %add.15.refs_0_.refs_1_, f32[8,1024]{1,0:T(8,128)S(1)} %collective-permute-done.1.refs_2_, f32[8,1024]{1,0:T(8,128)S(1)} %collective-permute-done.2.refs_3_, ...), custom_call_target="tpu_custom_call" | custom-call | flops 2147483648 | bytes 65536 | tf_op jit(solution)/shard_map/row_pass/pallas_call | solution.py:54
  39.4 9.2 %all_to_all.30.refs_0_.refs_1_.refs_2_ = f32[16,8,128]{2,1,0:T(8,128)S(1)} all-to-all(f32[16,8,128]{2,1,0:T(8,128)S(1)} %row_pass.2), channel_id=1, replica_groups=mesh['patch'=8,'proto'=16] {'proto'}, dimensions={0} | all-to-all | bytes 131072 | tf_op jit(solution)/shard_map/all_to_all | solution.py:402
  48.6 1.2 col_pass.2
  49.8 3.3 %collective-permute-start.4 = (f32[8,1024]{1,0:T(8,128)S(1)}, f32[8,1024]{1,0:T(8,128)S(1)}, u32[]{:S(2)}, u32[]{:S(2)}) collective-permute-start(f32[8,1024]{1,0:T(8,128)S(1)} %col_pass.2), channel_id=1, source_target_pairs={{0,16},{16,0},{32,48},{48,32},{64,80},{80,64},{96,112},{112,96},{1... | collective-permute-start | bytes 98312 | tf_op jit(solution)/shard_map/ppermute | solution.py:405
  53.1 0.9 collective-permute-done.4
  53.9 1.1 collective-permute-start.7
  55.1 0.8 collective-permute-start.6
  55.9 1.3 collective-permute-start.5
  57.2 2.7 %student_table.4 = (bf16[512,3072]{1,0:T(8,128)(2,1)S(1)}, f32[8,512]{1,0:T(8,128)S(1)}, f32[256,512]{1,0:T(8,128)S(1)}) custom-call(f32[8,1024]{1,0:T(8,128)S(1)} %add.16.refs_0_.refs_1_, bf16[16,64,256]{2,1,0:T(8,128)(2,1)S(1)} %all-to-all-done.refs_0_.refs_1_, bf16[8,256,1024]{2,1,0:T(8,128)(2,1)S(1)} %get-tuple-element.43.refs_2_.refs_5_), custom_call_target="tpu_custom_call" | custom-call | flops 2147483648 | bytes 65536 | tf_op jit(solution)/shard_map/student_table/pallas_call | solution.py:54
  59.9 0.0 collective-permute-done.7.refs_4_
  59.9 0.0 collective-permute-done.6.refs_3_
  59.9 0.0 collective-permute-done.5.refs_2_
  59.9 2.3 %row_pass.3 = f32[16,8,128]{2,1,0:T(8,128)S(1)} custom-call(f32[8,512]{1,0:T(8,128)S(1)} %get-tuple-element.47.refs_0_.refs_7_, f32[8,1024]{1,0:T(8,128)S(1)} %add.16.refs_0_.refs_1_, f32[8,1024]{1,0:T(8,128)S(1)} %collective-permute-done.5.refs_2_, f32[8,1024]{1,0:T(8,128)S(1)} %collective-permute-done.6.refs_3_, ...), custom_call_target="tpu_custom_call" | custom-call | flops 2147483648 | bytes 65536 | tf_op jit(solution)/shard_map/row_pass/pallas_call | solution.py:54
  62.2 9.4 %all_to_all.31.refs_0_ = f32[16,8,128]{2,1,0:T(8,128)S(1)} all-to-all(f32[16,8,128]{2,1,0:T(8,128)S(1)} %row_pass.3), channel_id=1, replica_groups=mesh['patch'=8,'proto'=16] {'proto'}, dimensions={0} | all-to-all | bytes 131072 | tf_op jit(solution)/shard_map/all_to_all | solution.py:402
  71.6 1.2 col_pass.3
  72.8 2.9 %collective-permute-start.8 = (f32[8,1024]{1,0:T(8,128)S(1)}, f32[8,1024]{1,0:T(8,128)S(1)}, u32[]{:S(2)}, u32[]{:S(2)}) collective-permute-start(f32[8,1024]{1,0:T(8,128)S(1)} %col_pass.3), channel_id=1, source_target_pairs={{0,16},{16,0},{32,48},{48,32},{64,80},{80,64},{96,112},{112,96},{1... | collective-permute-start | bytes 98312 | tf_op jit(solution)/shard_map/ppermute | solution.py:405
  75.7 0.9 collective-permute-done.8
  76.6 1.4 %collective-permute-start.11 = (f32[8,1024]{1,0:T(8,128)S(1)}, f32[8,1024]{1,0:T(8,128)S(1)}, u32[]{:S(2)}, u32[]{:S(2)}) collective-permute-start(f32[8,1024]{1,0:T(8,128)S(1)} %add.17.refs_0_.refs_3_.refs_4_), channel_id=1, source_target_pairs={{0,96},{16,112},{32,64},{48,80},{64,32},{80,48},{96,0},{112,16},{1... | collective-permute-start | bytes 98312 | tf_op jit(solution)/shard_map/ppermute | solution.py:405
  78.0 1.1 collective-permute-start.10
  79.1 0.7 collective-permute-start.9
  79.8 1.9 %student_table.5 = (bf16[512,2048]{1,0:T(8,128)(2,1)S(1)}, f32[8,512]{1,0:T(8,128)S(1)}, f32[256,512]{1,0:T(8,128)S(1)}, bf16[256,512]{1,0:T(8,128)(2,1)S(1)}) custom-call(f32[8,1024]{1,0:T(8,128)S(1)} %add.17.refs_0_.refs_3_.refs_4_, bf16[16,64,256]{2,1,0:T(8,128)(2,1)S(1)} %all-to-all-done.refs_0_.refs_1_, ...), custom_call_target="tpu_custom_call" | custom-call | flops 2147483648 | bytes 65536 | tf_op jit(solution)/shard_map/student_table/pallas_call | solution.py:54
  81.7 0.0 collective-permute-done.11.refs_3_.refs_6_.refs_7_
  81.7 0.5 collective-permute-done.10.refs_2_.refs_5_.refs_6_
  82.2 0.0 collective-permute-done.9.refs_1_.refs_4_.refs_5_
  82.2 2.5 %last_row_pass.1 = (f32[16,8,128]{2,1,0:T(8,128)S(1)}, f32[256,512]{1,0:T(8,128)S(1)}) custom-call(f32[8,1024]{1,0:T(8,128)S(1)} %add.17.refs_0_.refs_3_.refs_4_, f32[8,1024]{1,0:T(8,128)S(1)} %collective-permute-done.9.refs_1_.refs_4_.refs_5_, f32[8,1024]{1,0:T(8,128)S(1)} %collective-permute-done.10.refs_2_.refs_5_.refs_6_, ...), custom_call_target="tpu_custom_call" | custom-call | flops 2147483648 | bytes 65536 | tf_op jit(solution)/shard_map/last_row_pass/pallas_call | solution.py:54
  84.8 9.4 %all_to_all.32.refs_2_.refs_3_ = f32[16,8,128]{2,1,0:T(8,128)S(1)} all-to-all(f32[16,8,128]{2,1,0:T(8,128)S(1)} %get-tuple-element.49), channel_id=1, replica_groups=mesh['patch'=8,'proto'=16] {'proto'}, dimensions={0} | all-to-all | bytes 131072 | tf_op jit(solution)/shard_map/all_to_all | solution.py:402
  94.1 0.0 copy-done
  94.1 6.6 %head.2 = (f32[32,6144]{1,0:T(8,128)}, bf16[3,32,6144]{2,1,0:T(8,128)(2,1)S(1)}, bf16[4,32,6144]{2,1,0:T(8,128)(2,1)S(1)}) custom-call(s32[3]{0:T(128)S(1)} %pad_add_fusion.refs_0_.refs_1_, f32[16,8,128]{2,1,0:T(8,128)S(1)} %all_to_all.30.refs_0_.refs_1_.refs_2_, f32[16,8,128]{2,1,0:T(8,128)S(1)} %all_to_all.32.refs_2_.refs_3_, ...), custom_call_target="tpu_custom_call" | custom-call | flops 4294967296 | bytes 65536 | tf_op jit(solution)/shard_map/head/pallas_call | solution.py:54
  100.7 3.3 %collective-permute-start.12 = (bf16[4,32,6144]{2,1,0:T(8,128)(2,1)S(1)}, bf16[4,32,6144]{2,1,0:T(8,128)(2,1)S(1)}, u32[]{:S(2)}, u32[]{:S(2)}) collective-permute-start(bf16[4,32,6144]{2,1,0:T(8,128)(2,1)S(1)} %get-tuple-element.65), channel_id=1, source_target_pairs={{0,16},{16,0},{32,48},{48,32},{64,80},{80,64},{96,112},{112,96},{1... | collective-permute-start | bytes 4718600 | tf_op jit(solution)/shard_map/ppermute | solution.py:405
  104.0 3.0 %head.3 = (f32[32,2048]{1,0:T(8,128)}, bf16[3,32,2048]{2,1,0:T(8,128)(2,1)S(1)}, bf16[4,32,2048]{2,1,0:T(8,128)(2,1)S(1)}) custom-call(bf16[3,32,6144]{2,1,0:T(8,128)(2,1)S(1)} %get-tuple-element.55.refs_0_.refs_1_, s32[3]{0:T(128)S(1)} %pad_add_fusion.refs_0_.refs_1_, f32[16,8,128]{2,1,0:T(8,128)S(1)} %all_to_all.30.refs_0_.refs_1_.refs_2_, ...), custom_call_target="tpu_custom_call" | custom-call | flops 4294967296 | bytes 65536 | tf_op jit(solution)/shard_map/head/pallas_call | solution.py:54
  107.1 0.1 collective-permute-start.13
  107.2 0.3 feature.1.refs_0_
  107.5 0.0 copy-start.1
  107.5 0.0 copy-start.2
  107.5 1.5 %collective-permute-done.13.refs_4_ = bf16[4,32,2048]{2,1,0:T(8,128)(2,1)S(1)} collective-permute-done((bf16[4,32,2048]{2,1,0:T(8,128)(2,1)S(1)}, bf16[4,32,2048]{2,1,0:T(8,128)(2,1)S(1)}, u32[]{:S(2)}, u32[]{:S(2)}) %collective-permute-start.13) | collective-permute-done | bytes 524320 | tf_op jit(solution)/shard_map/ppermute | solution.py:405
  109.1 0.0 collective-permute-done.12.refs_2_
  109.1 0.4 pair_sums.1
  109.4 1.8 %collective-permute-start.14 = (bf16[32,8192]{1,0:T(8,128)(2,1)S(1)}, bf16[32,8192]{1,0:T(8,128)(2,1)S(1)}, u32[]{:S(2)}, u32[]{:S(2)}) collective-permute-start(bf16[32,8192]{1,0:T(8,128)(2,1)S(1)} %get-tuple-element.70), channel_id=1, source_target_pairs={{0,64},{16,80},{32,96},{48,112},{64,0},{80,16},{96,32},{112,48},{1... | collective-permute-start | bytes 1572872 | tf_op jit(solution)/shard_map/ppermute | solution.py:405
  111.3 0.1 collective-permute-start.15
  111.4 1.4 %collective-permute-start.16 = (bf16[32,8192]{1,0:T(8,128)(2,1)S(1)}, bf16[32,8192]{1,0:T(8,128)(2,1)S(1)}, u32[]{:S(2)}, u32[]{:S(2)}) collective-permute-start(bf16[32,8192]{1,0:T(8,128)(2,1)S(1)} %get-tuple-element.72), channel_id=1, source_target_pairs={{0,96},{16,112},{32,64},{48,80},{64,32},{80,48},{96,0},{112,16},{1... | collective-permute-start | bytes 1572872 | tf_op jit(solution)/shard_map/ppermute | solution.py:405
  112.8 11.7 %all_to_all.33.refs_0_ = bf16[16,48,256]{2,1,0:T(8,128)(2,1)S(1)} all-to-all(bf16[16,48,256]{2,1,0:T(8,128)(2,1)S(1)} %feature.1.refs_0_), channel_id=1, replica_groups=mesh['patch'=8,'proto'=16] {'proto'}, dimensions={0} | all-to-all | bytes 786432 | tf_op jit(solution)/shard_map/all_to_all | solution.py:402
  124.5 0.8 owner.1
  125.2 0.0 copy-done.2
  125.2 0.1 own_sum.1
  125.3 11.1 %all_to_all.34.refs_1_ = f32[8,8,128]{2,1,0:T(8,128)S(1)} all-to-all(f32[8,8,128]{2,1,0:T(8,128)S(1)} %get-tuple-element.69), channel_id=1, replica_groups=mesh['patch'=8,'proto'=16] {'patch'}, dimensions={0} | all-to-all | bytes 65536 | tf_op jit(solution)/shard_map/all_to_all | solution.py:402
  136.4 0.0 collective-permute-done.14.refs_2_
  136.4 0.0 collective-permute-done.15.refs_3_
  136.4 0.0 collective-permute-done.16.refs_4_
  136.4 1.3 assemble.1
  (5 shorter events, 0.0 us)
Async XLA Ops:
  3.4 19.1 %all-to-all-start = ((bf16[16,64,256]{2,1,0:T(8,128)(2,1)}), bf16[16,64,256]{2,1,0:T(8,128)(2,1)S(1)}, u32[]{:S(2)}, u32[]{:S(2)}) async-start(bf16[16,64,256]{2,1,0:T(8,128)(2,1)} %get-tuple-element.39), calls=%async_computation | async-start | bytes 1048576 | tf_op jit(solution)/shard_map/all_to_all | solution.py:402
  27.4 2.9 %collective-permute-start = (f32[8,1024]{1,0:T(8,128)S(1)}, f32[8,1024]{1,0:T(8,128)S(1)}, u32[]{:S(2)}, u32[]{:S(2)}) collective-permute-start(f32[8,1024]{1,0:T(8,128)S(1)} %get-tuple-element.42), channel_id=1, source_target_pairs={{0,16},{16,0},{32,48},{48,32},{64,80},{80,64},{96,112},{112,96},{1... | collective-permute-start | bytes 98312 | tf_op jit(solution)/shard_map/ppermute | solution.py:405
  30.3 5.9 %collective-permute-start.3 = (f32[8,1024]{1,0:T(8,128)S(1)}, f32[8,1024]{1,0:T(8,128)S(1)}, u32[]{:S(2)}, u32[]{:S(2)}) collective-permute-start(f32[8,1024]{1,0:T(8,128)S(1)} %add.15.refs_0_.refs_1_), channel_id=1, source_target_pairs={{0,96},{16,112},{32,64},{48,80},{64,32},{80,48},{96,0},{112,16},{1... | collective-permute-start | bytes 98312 | tf_op jit(solution)/shard_map/ppermute | solution.py:405
  32.8 4.3 %collective-permute-start.2 = (f32[8,1024]{1,0:T(8,128)S(1)}, f32[8,1024]{1,0:T(8,128)S(1)}, u32[]{:S(2)}, u32[]{:S(2)}) collective-permute-start(f32[8,1024]{1,0:T(8,128)S(1)} %add.15.refs_0_.refs_1_), channel_id=1, source_target_pairs={{0,64},{16,80},{32,96},{48,112},{64,0},{80,16},{96,32},{112,48},{1... | collective-permute-start | bytes 98312 | tf_op jit(solution)/shard_map/ppermute | solution.py:405
  33.3 3.7 %collective-permute-start.1 = (f32[8,1024]{1,0:T(8,128)S(1)}, f32[8,1024]{1,0:T(8,128)S(1)}, u32[]{:S(2)}, u32[]{:S(2)}) collective-permute-start(f32[8,1024]{1,0:T(8,128)S(1)} %add.15.refs_0_.refs_1_), channel_id=1, source_target_pairs={{0,32},{16,48},{32,0},{48,16},{64,96},{80,112},{96,64},{112,80},{1... | collective-permute-start | bytes 98312 | tf_op jit(solution)/shard_map/ppermute | solution.py:405
  49.8 4.1 %collective-permute-start.4 = (f32[8,1024]{1,0:T(8,128)S(1)}, f32[8,1024]{1,0:T(8,128)S(1)}, u32[]{:S(2)}, u32[]{:S(2)}) collective-permute-start(f32[8,1024]{1,0:T(8,128)S(1)} %col_pass.2), channel_id=1, source_target_pairs={{0,16},{16,0},{32,48},{48,32},{64,80},{80,64},{96,112},{112,96},{1... | collective-permute-start | bytes 98312 | tf_op jit(solution)/shard_map/ppermute | solution.py:405
  53.9 5.9 %collective-permute-start.7 = (f32[8,1024]{1,0:T(8,128)S(1)}, f32[8,1024]{1,0:T(8,128)S(1)}, u32[]{:S(2)}, u32[]{:S(2)}) collective-permute-start(f32[8,1024]{1,0:T(8,128)S(1)} %add.16.refs_0_.refs_1_), channel_id=1, source_target_pairs={{0,96},{16,112},{32,64},{48,80},{64,32},{80,48},{96,0},{112,16},{1... | collective-permute-start | bytes 98312 | tf_op jit(solution)/shard_map/ppermute | solution.py:405
  55.1 4.8 %collective-permute-start.6 = (f32[8,1024]{1,0:T(8,128)S(1)}, f32[8,1024]{1,0:T(8,128)S(1)}, u32[]{:S(2)}, u32[]{:S(2)}) collective-permute-start(f32[8,1024]{1,0:T(8,128)S(1)} %add.16.refs_0_.refs_1_), channel_id=1, source_target_pairs={{0,64},{16,80},{32,96},{48,112},{64,0},{80,16},{96,32},{112,48},{1... | collective-permute-start | bytes 98312 | tf_op jit(solution)/shard_map/ppermute | solution.py:405
  55.9 4.0 %collective-permute-start.5 = (f32[8,1024]{1,0:T(8,128)S(1)}, f32[8,1024]{1,0:T(8,128)S(1)}, u32[]{:S(2)}, u32[]{:S(2)}) collective-permute-start(f32[8,1024]{1,0:T(8,128)S(1)} %add.16.refs_0_.refs_1_), channel_id=1, source_target_pairs={{0,32},{16,48},{32,0},{48,16},{64,96},{80,112},{96,64},{112,80},{1... | collective-permute-start | bytes 98312 | tf_op jit(solution)/shard_map/ppermute | solution.py:405
  72.8 3.7 %collective-permute-start.8 = (f32[8,1024]{1,0:T(8,128)S(1)}, f32[8,1024]{1,0:T(8,128)S(1)}, u32[]{:S(2)}, u32[]{:S(2)}) collective-permute-start(f32[8,1024]{1,0:T(8,128)S(1)} %col_pass.3), channel_id=1, source_target_pairs={{0,16},{16,0},{32,48},{48,32},{64,80},{80,64},{96,112},{112,96},{1... | collective-permute-start | bytes 98312 | tf_op jit(solution)/shard_map/ppermute | solution.py:405
  76.6 5.2 %collective-permute-start.11 = (f32[8,1024]{1,0:T(8,128)S(1)}, f32[8,1024]{1,0:T(8,128)S(1)}, u32[]{:S(2)}, u32[]{:S(2)}) collective-permute-start(f32[8,1024]{1,0:T(8,128)S(1)} %add.17.refs_0_.refs_3_.refs_4_), channel_id=1, source_target_pairs={{0,96},{16,112},{32,64},{48,80},{64,32},{80,48},{96,0},{112,16},{1... | collective-permute-start | bytes 98312 | tf_op jit(solution)/shard_map/ppermute | solution.py:405
  78.0 4.3 %collective-permute-start.10 = (f32[8,1024]{1,0:T(8,128)S(1)}, f32[8,1024]{1,0:T(8,128)S(1)}, u32[]{:S(2)}, u32[]{:S(2)}) collective-permute-start(f32[8,1024]{1,0:T(8,128)S(1)} %add.17.refs_0_.refs_3_.refs_4_), channel_id=1, source_target_pairs={{0,64},{16,80},{32,96},{48,112},{64,0},{80,16},{96,32},{112,48},{1... | collective-permute-start | bytes 98312 | tf_op jit(solution)/shard_map/ppermute | solution.py:405
  79.1 3.1 %collective-permute-start.9 = (f32[8,1024]{1,0:T(8,128)S(1)}, f32[8,1024]{1,0:T(8,128)S(1)}, u32[]{:S(2)}, u32[]{:S(2)}) collective-permute-start(f32[8,1024]{1,0:T(8,128)S(1)} %add.17.refs_0_.refs_3_.refs_4_), channel_id=1, source_target_pairs={{0,32},{16,48},{32,0},{48,16},{64,96},{80,112},{96,64},{112,80},{1... | collective-permute-start | bytes 98312 | tf_op jit(solution)/shard_map/ppermute | solution.py:405
  82.2 11.9 %copy-start = (bf16[256,8192]{1,0:T(8,128)(2,1)S(1)}, bf16[256,8192]{1,0:T(8,128)(2,1)}, u32[]{:S(2)}) copy-start(bf16[256,8192]{1,0:T(8,128)(2,1)} %refs_14_.1) | copy-start | bytes 12582916
  100.7 8.3 %collective-permute-start.12 = (bf16[4,32,6144]{2,1,0:T(8,128)(2,1)S(1)}, bf16[4,32,6144]{2,1,0:T(8,128)(2,1)S(1)}, u32[]{:S(2)}, u32[]{:S(2)}) collective-permute-start(bf16[4,32,6144]{2,1,0:T(8,128)(2,1)S(1)} %get-tuple-element.65), channel_id=1, source_target_pairs={{0,16},{16,0},{32,48},{48,32},{64,80},{80,64},{96,112},{112,96},{1... | collective-permute-start | bytes 4718600 | tf_op jit(solution)/shard_map/ppermute | solution.py:405
  107.1 2.0 %collective-permute-start.13 = (bf16[4,32,2048]{2,1,0:T(8,128)(2,1)S(1)}, bf16[4,32,2048]{2,1,0:T(8,128)(2,1)S(1)}, u32[]{:S(2)}, u32[]{:S(2)}) collective-permute-start(bf16[4,32,2048]{2,1,0:T(8,128)(2,1)S(1)} %get-tuple-element.67), channel_id=1, source_target_pairs={{0,16},{16,0},{32,48},{48,32},{64,80},{80,64},{96,112},{112,96},{1... | collective-permute-start | bytes 1572872 | tf_op jit(solution)/shard_map/ppermute | solution.py:405
  107.5 17.7 %copy-start.1 = (f32[32,6144]{1,0:T(8,128)S(1)}, f32[32,6144]{1,0:T(8,128)}, u32[]{:S(2)}) copy-start(f32[32,6144]{1,0:T(8,128)} %get-tuple-element.64.refs_1_) | copy-start | bytes 2359300
  107.5 17.7 %copy-start.2 = (f32[32,2048]{1,0:T(8,128)S(1)}, f32[32,2048]{1,0:T(8,128)}, u32[]{:S(2)}) copy-start(f32[32,2048]{1,0:T(8,128)} %get-tuple-element.66.refs_3_) | copy-start | bytes 786436
  109.4 27.0 %collective-permute-start.14 = (bf16[32,8192]{1,0:T(8,128)(2,1)S(1)}, bf16[32,8192]{1,0:T(8,128)(2,1)S(1)}, u32[]{:S(2)}, u32[]{:S(2)}) collective-permute-start(bf16[32,8192]{1,0:T(8,128)(2,1)S(1)} %get-tuple-element.70), channel_id=1, source_target_pairs={{0,64},{16,80},{32,96},{48,112},{64,0},{80,16},{96,32},{112,48},{1... | collective-permute-start | bytes 1572872 | tf_op jit(solution)/shard_map/ppermute | solution.py:405
  111.3 25.2 %collective-permute-start.15 = (bf16[32,8192]{1,0:T(8,128)(2,1)S(1)}, bf16[32,8192]{1,0:T(8,128)(2,1)S(1)}, u32[]{:S(2)}, u32[]{:S(2)}) collective-permute-start(bf16[32,8192]{1,0:T(8,128)(2,1)S(1)} %get-tuple-element.71), channel_id=1, source_target_pairs={{0,32},{16,48},{32,0},{48,16},{64,96},{80,112},{96,64},{112,80},{1... | collective-permute-start | bytes 1572872 | tf_op jit(solution)/shard_map/ppermute | solution.py:405
  111.4 25.1 %collective-permute-start.16 = (bf16[32,8192]{1,0:T(8,128)(2,1)S(1)}, bf16[32,8192]{1,0:T(8,128)(2,1)S(1)}, u32[]{:S(2)}, u32[]{:S(2)}) collective-permute-start(bf16[32,8192]{1,0:T(8,128)(2,1)S(1)} %get-tuple-element.72), channel_id=1, source_target_pairs={{0,96},{16,112},{32,64},{48,80},{64,32},{80,48},{96,0},{112,16},{1... | collective-permute-start | bytes 1572872 | tf_op jit(solution)/shard_map/ppermute | solution.py:405

commit v6 on v5

--- a/solution.py
+++ b/solution.py
@@ -264,27 +264,38 @@
     return read_rows(first_ref, tile, n), read_rows(last_ref, tile, n), read_rows(last_ref, 0, n)
 
 
-def head_body(first, parts, *refs):
-    place_ref, first_ref, last_ref = refs[:3]
-    sums_refs = refs[3 : 3 + parts]
-    turned_ref, inverse_ref, codes_ref, *piece_refs, w_ref = refs[3 + parts : -6]
-    own_hbm, keep_ref, near_ref, turn_ref, own_ref, sems = refs[-6:]
+def targets(place_ref, chips, share):
     x, core = place_ref[1], place_ref[2]
-    chips, share = near_ref.shape[:2]
-    width = inverse_ref.shape[1]
     spots = []
     for k in range(chips):
         for side in (core, 1 - core):
             spots.append(pl.ds(pl.multiple_of((2 * (x ^ k) + side) * share, share), share))
-    for m, spot in enumerate(spots):
-        turn_ref[pl.ds(m * share, share), :] = turned_ref[spot, :]
-    weights, exp_total, total = row_factors(first_ref, last_ref, codes_ref.shape[0])
-    turned = turn_ref[...].astype(F32)
-    left_probs = (turned * (weights / exp_total * (1.0 / STUDENT_TEMP))).astype(BF16)
-    left_codes = (turned * (weights / total * (1.0 / STUDENT_TEMP))).astype(BF16)
+    return spots
+
+
+def left_body(chips, place_ref, first_ref, last_ref, turned_ref, probs_ref, codes_ref):
+    share = turned_ref.shape[0] // (2 * chips)
+    weights, exp_total, total = row_factors(first_ref, last_ref, turned_ref.shape[1])
+    over_probs = weights / exp_total * (1.0 / STUDENT_TEMP)
+    over_codes = weights / total * (1.0 / STUDENT_TEMP)
+    for m, spot in enumerate(targets(place_ref, chips, share)):
+        rows = pl.ds(m * share, share)
+        turned = turned_ref[spot, :].astype(F32)
+        probs_ref[rows, :] = (turned * over_probs).astype(BF16)
+        codes_ref[rows, :] = (turned * over_codes).astype(BF16)
+
+
+def head_body(first, parts, *refs):
+    place_ref, left_probs_ref, left_codes_ref = refs[:3]
+    sums_refs = refs[3 : 3 + parts]
+    inverse_ref, codes_ref, *piece_refs, w_ref = refs[3 + parts : -3]
+    own_ref, keep_ref, near_ref = refs[-3:]
+    chips, share = near_ref.shape[:2]
+    width = inverse_ref.shape[1]
+    spots = targets(place_ref, chips, share)
+    left_probs, left_codes = left_probs_ref[...], left_codes_ref[...]
     scale = 1.0 / column_sum(sums_refs)
     where = [(p, at) for p, size in enumerate(PIECES) for at in range(size)]
-    stores = []
     for j, cols in chunks(own_ref, own_ref.shape[1] // width):
         row = first + j
         here = pl.ds(row * width, width)
@@ -297,16 +308,11 @@
         inner = jnp.sum(w * head, axis=0, keepdims=True)
         grad = head - w * (inverse * inverse * inner)
         own_ref[:, cols] = grad[0:share]
-        store = pltpu.make_async_copy(own_ref.at[:, cols], own_hbm.at[:, cols], sems.at[j])
-        store.start()
-        stores.append(store)
         for k in range(chips):
             low = 2 * k * share
             if k:
                 keep_ref[k - 1, :, cols] = grad[low : low + share].astype(BF16)
             near_ref[k, :, cols] = grad[low + share : low + 2 * share].astype(BF16)
-    for store in stores:
-        store.wait()
 
 
 def pair_body(*refs):
@@ -503,6 +509,14 @@
 
     turned = pieces[-1][3]
     factors = (messages[0], messages[-1])
+    lefts = call(
+        functools.partial(left_body, chips),
+        "row_factors",
+        (shape((d, rows), BF16), shape((d, rows), BF16)),
+        (place, *factors, turned),
+        product // 8,
+        specs=[SMEM] + [VMEM] * (len(factors) + 1),
+    )
     heads = []
     for index, count in enumerate(PARTS):
         span = count * width
@@ -511,28 +525,22 @@
                 functools.partial(head_body, sum(PARTS[:index]), chips),
                 "head",
                 (
-                    pltpu.HBM((share, span), F32),
+                    shape((share, span), F32),
                     shape((chips - 1, share, span), BF16),
                     shape((chips, share, span), BF16),
                 ),
                 (
                     place,
-                    *factors,
+                    *lefts,
                     *parts,
-                    turned,
                     inverse,
                     codes,
                     *[piece[0] for piece in pieces],
                     proto_weight,
                 ),
                 2 * product,
-                specs=[SMEM] + [VMEM] * (len(factors) + chips + 4 + len(pieces)),
+                specs=[SMEM] + [VMEM] * (chips + 5 + len(pieces)),
                 after=(heads[-1][1],) if heads else (),
-                scratch=[
-                    pltpu.VMEM((d, rows), BF16),
-                    pltpu.VMEM((share, span), F32),
-                    pltpu.SemaphoreType.DMA((count,)),
-                ],
             )
         )
     feature_part = call(

time: 138 us -> 138 us (level)
    pallas_call x18 -> x19, Pallas kernels: 41.6 us -> 41.2 us  [call(): pl.pallas_call(ordered, name=name, out_shape=out_shape, in_specs=[ANY] *...]
  transfers between devices with their start and end apart: 18 -> 18, of which waited for: 7 -> 7; matrix products, arithmetic and copies ran while one was open for 0% -> 0% of each run, Pallas kernels for 12% -> 11%
where the time goes in v6:
time: 138 us; the launch traced here: 137 us
  blocking collectives  50.7 us (37%)
  Pallas kernels  41.2 us (30%)
  starting transfers between devices  33.3 us (24%)
  waiting for transfers between devices  11.1 us (8%)
    all_to_all x5, blocking collectives, exchange(): return lax.all_to_all(array, axis, 0, 0)  50.7 us
    pallas_call x19, Pallas kernels, call(): pl.pallas_call(ordered, name=name, out_shape=out_shape, in_specs=[ANY] *...  41.2 us
    ppermute x17, starting transfers between devices, hop(): return lax.ppermute(array, 'patch', [(i, i ^ bits) for i in range(n_patch)])  24.7 us
    all_to_all x1, starting transfers between devices, exchange(): return lax.all_to_all(array, axis, 0, 0)  8.61 us
    all_to_all x1, waiting for transfers between devices, exchange(): return lax.all_to_all(array, axis, 0, 0)  5.69 us
    ppermute x17, waiting for transfers between devices, hop(): return lax.ppermute(array, 'patch', [(i, i ^ bits) for i in range(n_patch)])  5.41 us
  transfers between devices with their start and end apart: 18, of which 7 were waited for; matrix products, arithmetic and copies ran while one was open for 0% of the time, Pallas kernels for 11%

profile of v6, /device:TPU:1, one launch (start us, length us, event | category | flops | bytes accessed | tf_op | source)
XLA Modules:
  0.0 137.3 jit_solution(4171972558111954361)
XLA Ops:
  0.6 0.1 pad_add_fusion.refs_0_.refs_1_
  0.7 2.7 %own_rows.1 = (bf16[16,64,256]{2,1,0:T(8,128)(2,1)}, f32[32,256]{1,0:T(8,128)S(1)}, f32[8,512]{1,0:T(8,128)S(1)}) custom-call(s32[3]{0:T(128)S(1)} %pad_add_fusion.refs_0_.refs_1_, bf16[256,256]{1,0:T(8,128)(2,1)} %refs_1_.1, bf16[256,256]{1,0:T(8,128)(2,1)} %refs_2_.1, s32[1,32]{1,0:T(1,128)} %bitcast.6, bf16[1,32]{1,0:T(2,128)(2,1)} %bitcast.7), custom_call_target="tpu_custom_call" | custom-call | flops 268435456 | bytes 65536 | tf_op jit(solution)/shard_map/own_rows/pallas_call | solution.py:54
  3.4 8.6 %all-to-all-start = ((bf16[16,64,256]{2,1,0:T(8,128)(2,1)}), bf16[16,64,256]{2,1,0:T(8,128)(2,1)S(1)}, u32[]{:S(2)}, u32[]{:S(2)}) async-start(bf16[16,64,256]{2,1,0:T(8,128)(2,1)} %get-tuple-element.41), calls=%async_computation | async-start | bytes 1048576 | tf_op jit(solution)/shard_map/all_to_all | solution.py:408
  12.0 4.8 %proto_unit.1 = (bf16[8,256,1024]{2,1,0:T(8,128)(2,1)}, bf16[2,256,1024]{2,1,0:T(8,128)(2,1)S(1)}, f32[8,1024]{1,0:T(8,128)S(1)}) custom-call(bf16[256,8192]{1,0:T(8,128)(2,1)} %refs_13_.1), custom_call_target="tpu_custom_call" | custom-call | flops 2147483648 | bytes 65536 | tf_op jit(solution)/shard_map/proto_unit/pallas_call | solution.py:54
  16.8 5.7 %all-to-all-done.refs_0_.refs_1_ = bf16[16,64,256]{2,1,0:T(8,128)(2,1)S(1)} async-done(((bf16[16,64,256]{2,1,0:T(8,128)(2,1)}), bf16[16,64,256]{2,1,0:T(8,128)(2,1)S(1)}, u32[]{:S(2)}, u32[]{:S(2)}) %all-to-all-start) | async-done | bytes 524320 | tf_op jit(solution)/shard_map/all_to_all | solution.py:408
  22.5 4.9 %teacher_table.1 = (bf16[512,8192]{1,0:T(8,128)(2,1)S(1)}, bf16[8,256,1024]{2,1,0:T(8,128)(2,1)S(1)}, f32[8,1024]{1,0:T(8,128)S(1)}) custom-call(bf16[16,64,256]{2,1,0:T(8,128)(2,1)S(1)} %all-to-all-done.refs_0_.refs_1_, bf16[2,256,1024]{2,1,0:T(8,128)(2,1)S(1)} %get-tuple-element.42.refs_1_, bf16[8,256,1024]{2,1,0:T(8,128)(2,1)} %get-tuple-element.43.refs_2_), custom_call_target="tpu_custom_call" | custom-call | flops 4294967296 | bytes 65536 | tf_op jit(solution)/shard_map/teacher_table/pallas_call | solution.py:54
  27.4 2.1 %collective-permute-start = (f32[8,1024]{1,0:T(8,128)S(1)}, f32[8,1024]{1,0:T(8,128)S(1)}, u32[]{:S(2)}, u32[]{:S(2)}) collective-permute-start(f32[8,1024]{1,0:T(8,128)S(1)} %get-tuple-element.44), channel_id=1, source_target_pairs={{0,16},{16,0},{32,48},{48,32},{64,80},{80,64},{96,112},{112,96},{1... | collective-permute-start | bytes 98312 | tf_op jit(solution)/shard_map/ppermute | solution.py:411
  29.4 0.9 collective-permute-done
  30.3 2.5 %collective-permute-start.3 = (f32[8,1024]{1,0:T(8,128)S(1)}, f32[8,1024]{1,0:T(8,128)S(1)}, u32[]{:S(2)}, u32[]{:S(2)}) collective-permute-start(f32[8,1024]{1,0:T(8,128)S(1)} %add.15.refs_0_.refs_1_), channel_id=1, source_target_pairs={{0,96},{16,112},{32,64},{48,80},{64,32},{80,48},{96,0},{112,16},{1... | collective-permute-start | bytes 98312 | tf_op jit(solution)/shard_map/ppermute | solution.py:411
  32.8 0.5 collective-permute-start.2
  33.3 0.3 collective-permute-start.1
  33.6 2.7 %student_table.3 = (bf16[512,3072]{1,0:T(8,128)(2,1)S(1)}, f32[8,512]{1,0:T(8,128)S(1)}, f32[256,512]{1,0:T(8,128)S(1)}) custom-call(f32[8,1024]{1,0:T(8,128)S(1)} %add.15.refs_0_.refs_1_, bf16[16,64,256]{2,1,0:T(8,128)(2,1)S(1)} %all-to-all-done.refs_0_.refs_1_, bf16[8,256,1024]{2,1,0:T(8,128)(2,1)S(1)} %get-tuple-element.45.refs_2_.refs_5_), custom_call_target="tpu_custom_call" | custom-call | flops 2147483648 | bytes 65536 | tf_op jit(solution)/shard_map/student_table/pallas_call | solution.py:54
  36.2 0.0 collective-permute-done.3.refs_4_
  36.3 0.8 collective-permute-done.2.refs_3_
  37.0 0.0 collective-permute-done.1.refs_2_
  37.1 2.3 %row_pass.2 = f32[16,8,128]{2,1,0:T(8,128)S(1)} custom-call(f32[8,512]{1,0:T(8,128)S(1)} %get-tuple-element.46.refs_0_.refs_6_, f32[8,1024]{1,0:T(8,128)S(1)} %add.15.refs_0_.refs_1_, f32[8,1024]{1,0:T(8,128)S(1)} %collective-permute-done.1.refs_2_, f32[8,1024]{1,0:T(8,128)S(1)} %collective-permute-done.2.refs_3_, ...), custom_call_target="tpu_custom_call" | custom-call | flops 2147483648 | bytes 65536 | tf_op jit(solution)/shard_map/row_pass/pallas_call | solution.py:54
  39.4 9.2 %all_to_all.30.refs_0_.refs_1_ = f32[16,8,128]{2,1,0:T(8,128)S(1)} all-to-all(f32[16,8,128]{2,1,0:T(8,128)S(1)} %row_pass.2), channel_id=1, replica_groups=mesh['patch'=8,'proto'=16] {'proto'}, dimensions={0} | all-to-all | bytes 131072 | tf_op jit(solution)/shard_map/all_to_all | solution.py:408
  48.5 1.2 col_pass.2
  49.8 3.3 %collective-permute-start.4 = (f32[8,1024]{1,0:T(8,128)S(1)}, f32[8,1024]{1,0:T(8,128)S(1)}, u32[]{:S(2)}, u32[]{:S(2)}) collective-permute-start(f32[8,1024]{1,0:T(8,128)S(1)} %col_pass.2), channel_id=1, source_target_pairs={{0,16},{16,0},{32,48},{48,32},{64,80},{80,64},{96,112},{112,96},{1... | collective-permute-start | bytes 98312 | tf_op jit(solution)/shard_map/ppermute | solution.py:411
  53.1 0.9 collective-permute-done.4
  53.9 1.1 collective-permute-start.7
  55.0 0.8 collective-permute-start.6
  55.8 1.3 collective-permute-start.5
  57.2 2.7 %student_table.4 = (bf16[512,3072]{1,0:T(8,128)(2,1)S(1)}, f32[8,512]{1,0:T(8,128)S(1)}, f32[256,512]{1,0:T(8,128)S(1)}) custom-call(f32[8,1024]{1,0:T(8,128)S(1)} %add.16.refs_0_.refs_1_, bf16[16,64,256]{2,1,0:T(8,128)(2,1)S(1)} %all-to-all-done.refs_0_.refs_1_, bf16[8,256,1024]{2,1,0:T(8,128)(2,1)S(1)} %get-tuple-element.45.refs_2_.refs_5_), custom_call_target="tpu_custom_call" | custom-call | flops 2147483648 | bytes 65536 | tf_op jit(solution)/shard_map/student_table/pallas_call | solution.py:54
  59.9 0.0 collective-permute-done.7.refs_4_
  59.9 0.0 collective-permute-done.6.refs_3_
  59.9 0.0 collective-permute-done.5.refs_2_
  59.9 2.3 %row_pass.3 = f32[16,8,128]{2,1,0:T(8,128)S(1)} custom-call(f32[8,512]{1,0:T(8,128)S(1)} %get-tuple-element.49.refs_0_.refs_7_, f32[8,1024]{1,0:T(8,128)S(1)} %add.16.refs_0_.refs_1_, f32[8,1024]{1,0:T(8,128)S(1)} %collective-permute-done.5.refs_2_, f32[8,1024]{1,0:T(8,128)S(1)} %collective-permute-done.6.refs_3_, ...), custom_call_target="tpu_custom_call" | custom-call | flops 2147483648 | bytes 65536 | tf_op jit(solution)/shard_map/row_pass/pallas_call | solution.py:54
  62.2 9.4 %all_to_all.31.refs_0_ = f32[16,8,128]{2,1,0:T(8,128)S(1)} all-to-all(f32[16,8,128]{2,1,0:T(8,128)S(1)} %row_pass.3), channel_id=1, replica_groups=mesh['patch'=8,'proto'=16] {'proto'}, dimensions={0} | all-to-all | bytes 131072 | tf_op jit(solution)/shard_map/all_to_all | solution.py:408
  71.6 1.2 col_pass.3
  72.8 2.9 %collective-permute-start.8 = (f32[8,1024]{1,0:T(8,128)S(1)}, f32[8,1024]{1,0:T(8,128)S(1)}, u32[]{:S(2)}, u32[]{:S(2)}) collective-permute-start(f32[8,1024]{1,0:T(8,128)S(1)} %col_pass.3), channel_id=1, source_target_pairs={{0,16},{16,0},{32,48},{48,32},{64,80},{80,64},{96,112},{112,96},{1... | collective-permute-start | bytes 98312 | tf_op jit(solution)/shard_map/ppermute | solution.py:411
  75.7 0.9 collective-permute-done.8
  76.6 1.4 %collective-permute-start.11 = (f32[8,1024]{1,0:T(8,128)S(1)}, f32[8,1024]{1,0:T(8,128)S(1)}, u32[]{:S(2)}, u32[]{:S(2)}) collective-permute-start(f32[8,1024]{1,0:T(8,128)S(1)} %add.17.refs_0_.refs_3_.refs_4_), channel_id=1, source_target_pairs={{0,96},{16,112},{32,64},{48,80},{64,32},{80,48},{96,0},{112,16},{1... | collective-permute-start | bytes 98312 | tf_op jit(solution)/shard_map/ppermute | solution.py:411
  77.9 1.1 collective-permute-start.10
  79.1 0.7 collective-permute-start.9
  79.8 1.9 %student_table.5 = (bf16[512,2048]{1,0:T(8,128)(2,1)S(1)}, f32[8,512]{1,0:T(8,128)S(1)}, f32[256,512]{1,0:T(8,128)S(1)}, bf16[256,512]{1,0:T(8,128)(2,1)S(1)}) custom-call(f32[8,1024]{1,0:T(8,128)S(1)} %add.17.refs_0_.refs_3_.refs_4_, bf16[16,64,256]{2,1,0:T(8,128)(2,1)S(1)} %all-to-all-done.refs_0_.refs_1_, ...), custom_call_target="tpu_custom_call" | custom-call | flops 2147483648 | bytes 65536 | tf_op jit(solution)/shard_map/student_table/pallas_call | solution.py:54
  81.7 0.0 collective-permute-done.11.refs_3_.refs_6_.refs_7_
  81.7 0.5 collective-permute-done.10.refs_2_.refs_5_.refs_6_
  82.2 0.0 collective-permute-done.9.refs_1_.refs_4_.refs_5_
  82.2 0.0 copy-start
  82.2 2.5 %last_row_pass.1 = (f32[16,8,128]{2,1,0:T(8,128)S(1)}, f32[256,512]{1,0:T(8,128)S(1)}) custom-call(f32[8,1024]{1,0:T(8,128)S(1)} %add.17.refs_0_.refs_3_.refs_4_, f32[8,1024]{1,0:T(8,128)S(1)} %collective-permute-done.9.refs_1_.refs_4_.refs_5_, f32[8,1024]{1,0:T(8,128)S(1)} %collective-permute-done.10.refs_2_.refs_5_.refs_6_, ...), custom_call_target="tpu_custom_call" | custom-call | flops 2147483648 | bytes 65536 | tf_op jit(solution)/shard_map/last_row_pass/pallas_call | solution.py:54
  84.7 9.4 %all_to_all.32.refs_2_ = f32[16,8,128]{2,1,0:T(8,128)S(1)} all-to-all(f32[16,8,128]{2,1,0:T(8,128)S(1)} %get-tuple-element.51), channel_id=1, replica_groups=mesh['patch'=8,'proto'=16] {'proto'}, dimensions={0} | all-to-all | bytes 131072 | tf_op jit(solution)/shard_map/all_to_all | solution.py:408
  94.1 0.7 row_factors.1
  94.8 0.0 copy-done
  94.8 6.0 %head.2 = (f32[32,6144]{1,0:T(8,128)S(1)}, bf16[3,32,6144]{2,1,0:T(8,128)(2,1)S(1)}, bf16[4,32,6144]{2,1,0:T(8,128)(2,1)S(1)}) custom-call(s32[3]{0:T(128)S(1)} %pad_add_fusion.refs_0_.refs_1_, bf16[256,512]{1,0:T(8,128)(2,1)S(1)} %get-tuple-element.53.refs_1_.refs_2_, bf16[256,512]{1,0:T(8,128)(2,1)S(1)} %get-tuple-element.54.refs_2_.refs_3_, ...), custom_call_target="tpu_custom_call" | custom-call | flops 4294967296 | bytes 65536 | tf_op jit(solution)/shard_map/head/pallas_call | solution.py:54
  100.8 3.3 %collective-permute-start.12 = (bf16[4,32,6144]{2,1,0:T(8,128)(2,1)S(1)}, bf16[4,32,6144]{2,1,0:T(8,128)(2,1)S(1)}, u32[]{:S(2)}, u32[]{:S(2)}) collective-permute-start(bf16[4,32,6144]{2,1,0:T(8,128)(2,1)S(1)} %get-tuple-element.69), channel_id=1, source_target_pairs={{0,16},{16,0},{32,48},{48,32},{64,80},{80,64},{96,112},{112,96},{1... | collective-permute-start | bytes 4718600 | tf_op jit(solution)/shard_map/ppermute | solution.py:411
  104.1 2.4 %head.3 = (f32[32,2048]{1,0:T(8,128)S(1)}, bf16[3,32,2048]{2,1,0:T(8,128)(2,1)S(1)}, bf16[4,32,2048]{2,1,0:T(8,128)(2,1)S(1)}) custom-call(bf16[3,32,6144]{2,1,0:T(8,128)(2,1)S(1)} %get-tuple-element.59.refs_0_.refs_1_, s32[3]{0:T(128)S(1)} %pad_add_fusion.refs_0_.refs_1_, bf16[256,512]{1,0:T(8,128)(2,1)S(1)} %get-tuple-element.53.refs_1_.refs_2_, ...), custom_call_target="tpu_custom_call" | custom-call | flops 4294967296 | bytes 65536 | tf_op jit(solution)/shard_map/head/pallas_call | solution.py:54
  106.6 0.1 collective-permute-start.13
  106.7 0.3 feature.1.refs_0_
  107.0 1.5 %collective-permute-done.13.refs_4_ = bf16[4,32,2048]{2,1,0:T(8,128)(2,1)S(1)} collective-permute-done((bf16[4,32,2048]{2,1,0:T(8,128)(2,1)S(1)}, bf16[4,32,2048]{2,1,0:T(8,128)(2,1)S(1)}, u32[]{:S(2)}, u32[]{:S(2)}) %collective-permute-start.13) | collective-permute-done | bytes 524320 | tf_op jit(solution)/shard_map/ppermute | solution.py:411
  108.5 0.0 collective-permute-done.12.refs_2_
  108.5 0.4 pair_sums.1
  108.9 1.8 %collective-permute-start.14 = (bf16[32,8192]{1,0:T(8,128)(2,1)S(1)}, bf16[32,8192]{1,0:T(8,128)(2,1)S(1)}, u32[]{:S(2)}, u32[]{:S(2)}) collective-permute-start(bf16[32,8192]{1,0:T(8,128)(2,1)S(1)} %get-tuple-element.74), channel_id=1, source_target_pairs={{0,64},{16,80},{32,96},{48,112},{64,0},{80,16},{96,32},{112,48},{1... | collective-permute-start | bytes 1572872 | tf_op jit(solution)/shard_map/ppermute | solution.py:411
  110.8 0.1 collective-permute-start.15
  110.9 1.4 %collective-permute-start.16 = (bf16[32,8192]{1,0:T(8,128)(2,1)S(1)}, bf16[32,8192]{1,0:T(8,128)(2,1)S(1)}, u32[]{:S(2)}, u32[]{:S(2)}) collective-permute-start(bf16[32,8192]{1,0:T(8,128)(2,1)S(1)} %get-tuple-element.76), channel_id=1, source_target_pairs={{0,96},{16,112},{32,64},{48,80},{64,32},{80,48},{96,0},{112,16},{1... | collective-permute-start | bytes 1572872 | tf_op jit(solution)/shard_map/ppermute | solution.py:411
  112.3 11.7 %all_to_all.33.refs_0_ = bf16[16,48,256]{2,1,0:T(8,128)(2,1)S(1)} all-to-all(bf16[16,48,256]{2,1,0:T(8,128)(2,1)S(1)} %feature.1.refs_0_), channel_id=1, replica_groups=mesh['patch'=8,'proto'=16] {'proto'}, dimensions={0} | all-to-all | bytes 786432 | tf_op jit(solution)/shard_map/all_to_all | solution.py:408
  124.0 0.8 owner.1
  124.8 0.1 own_sum.1
  124.9 11.1 %all_to_all.34.refs_1_ = f32[8,8,128]{2,1,0:T(8,128)S(1)} all-to-all(f32[8,8,128]{2,1,0:T(8,128)S(1)} %get-tuple-element.73), channel_id=1, replica_groups=mesh['patch'=8,'proto'=16] {'patch'}, dimensions={0} | all-to-all | bytes 65536 | tf_op jit(solution)/shard_map/all_to_all | solution.py:408
  135.9 0.0 collective-permute-done.14.refs_2_
  135.9 0.0 collective-permute-done.15.refs_3_
  135.9 0.0 collective-permute-done.16.refs_4_
  135.9 1.3 assemble.1
  (3 shorter events, 0.0 us)
Async XLA Ops:
  3.4 19.1 %all-to-all-start = ((bf16[16,64,256]{2,1,0:T(8,128)(2,1)}), bf16[16,64,256]{2,1,0:T(8,128)(2,1)S(1)}, u32[]{:S(2)}, u32[]{:S(2)}) async-start(bf16[16,64,256]{2,1,0:T(8,128)(2,1)} %get-tuple-element.41), calls=%async_computation | async-start | bytes 1048576 | tf_op jit(solution)/shard_map/all_to_all | solution.py:408
  27.4 2.9 %collective-permute-start = (f32[8,1024]{1,0:T(8,128)S(1)}, f32[8,1024]{1,0:T(8,128)S(1)}, u32[]{:S(2)}, u32[]{:S(2)}) collective-permute-start(f32[8,1024]{1,0:T(8,128)S(1)} %get-tuple-element.44), channel_id=1, source_target_pairs={{0,16},{16,0},{32,48},{48,32},{64,80},{80,64},{96,112},{112,96},{1... | collective-permute-start | bytes 98312 | tf_op jit(solution)/shard_map/ppermute | solution.py:411
  30.3 5.9 %collective-permute-start.3 = (f32[8,1024]{1,0:T(8,128)S(1)}, f32[8,1024]{1,0:T(8,128)S(1)}, u32[]{:S(2)}, u32[]{:S(2)}) collective-permute-start(f32[8,1024]{1,0:T(8,128)S(1)} %add.15.refs_0_.refs_1_), channel_id=1, source_target_pairs={{0,96},{16,112},{32,64},{48,80},{64,32},{80,48},{96,0},{112,16},{1... | collective-permute-start | bytes 98312 | tf_op jit(solution)/shard_map/ppermute | solution.py:411
  32.8 4.3 %collective-permute-start.2 = (f32[8,1024]{1,0:T(8,128)S(1)}, f32[8,1024]{1,0:T(8,128)S(1)}, u32[]{:S(2)}, u32[]{:S(2)}) collective-permute-start(f32[8,1024]{1,0:T(8,128)S(1)} %add.15.refs_0_.refs_1_), channel_id=1, source_target_pairs={{0,64},{16,80},{32,96},{48,112},{64,0},{80,16},{96,32},{112,48},{1... | collective-permute-start | bytes 98312 | tf_op jit(solution)/shard_map/ppermute | solution.py:411
  33.3 3.7 %collective-permute-start.1 = (f32[8,1024]{1,0:T(8,128)S(1)}, f32[8,1024]{1,0:T(8,128)S(1)}, u32[]{:S(2)}, u32[]{:S(2)}) collective-permute-start(f32[8,1024]{1,0:T(8,128)S(1)} %add.15.refs_0_.refs_1_), channel_id=1, source_target_pairs={{0,32},{16,48},{32,0},{48,16},{64,96},{80,112},{96,64},{112,80},{1... | collective-permute-start | bytes 98312 | tf_op jit(solution)/shard_map/ppermute | solution.py:411
  49.8 4.1 %collective-permute-start.4 = (f32[8,1024]{1,0:T(8,128)S(1)}, f32[8,1024]{1,0:T(8,128)S(1)}, u32[]{:S(2)}, u32[]{:S(2)}) collective-permute-start(f32[8,1024]{1,0:T(8,128)S(1)} %col_pass.2), channel_id=1, source_target_pairs={{0,16},{16,0},{32,48},{48,32},{64,80},{80,64},{96,112},{112,96},{1... | collective-permute-start | bytes 98312 | tf_op jit(solution)/shard_map/ppermute | solution.py:411
  53.9 5.9 %collective-permute-start.7 = (f32[8,1024]{1,0:T(8,128)S(1)}, f32[8,1024]{1,0:T(8,128)S(1)}, u32[]{:S(2)}, u32[]{:S(2)}) collective-permute-start(f32[8,1024]{1,0:T(8,128)S(1)} %add.16.refs_0_.refs_1_), channel_id=1, source_target_pairs={{0,96},{16,112},{32,64},{48,80},{64,32},{80,48},{96,0},{112,16},{1... | collective-permute-start | bytes 98312 | tf_op jit(solution)/shard_map/ppermute | solution.py:411
  55.0 4.8 %collective-permute-start.6 = (f32[8,1024]{1,0:T(8,128)S(1)}, f32[8,1024]{1,0:T(8,128)S(1)}, u32[]{:S(2)}, u32[]{:S(2)}) collective-permute-start(f32[8,1024]{1,0:T(8,128)S(1)} %add.16.refs_0_.refs_1_), channel_id=1, source_target_pairs={{0,64},{16,80},{32,96},{48,112},{64,0},{80,16},{96,32},{112,48},{1... | collective-permute-start | bytes 98312 | tf_op jit(solution)/shard_map/ppermute | solution.py:411
  55.8 4.0 %collective-permute-start.5 = (f32[8,1024]{1,0:T(8,128)S(1)}, f32[8,1024]{1,0:T(8,128)S(1)}, u32[]{:S(2)}, u32[]{:S(2)}) collective-permute-start(f32[8,1024]{1,0:T(8,128)S(1)} %add.16.refs_0_.refs_1_), channel_id=1, source_target_pairs={{0,32},{16,48},{32,0},{48,16},{64,96},{80,112},{96,64},{112,80},{1... | collective-permute-start | bytes 98312 | tf_op jit(solution)/shard_map/ppermute | solution.py:411
  72.8 3.7 %collective-permute-start.8 = (f32[8,1024]{1,0:T(8,128)S(1)}, f32[8,1024]{1,0:T(8,128)S(1)}, u32[]{:S(2)}, u32[]{:S(2)}) collective-permute-start(f32[8,1024]{1,0:T(8,128)S(1)} %col_pass.3), channel_id=1, source_target_pairs={{0,16},{16,0},{32,48},{48,32},{64,80},{80,64},{96,112},{112,96},{1... | collective-permute-start | bytes 98312 | tf_op jit(solution)/shard_map/ppermute | solution.py:411
  76.6 5.2 %collective-permute-start.11 = (f32[8,1024]{1,0:T(8,128)S(1)}, f32[8,1024]{1,0:T(8,128)S(1)}, u32[]{:S(2)}, u32[]{:S(2)}) collective-permute-start(f32[8,1024]{1,0:T(8,128)S(1)} %add.17.refs_0_.refs_3_.refs_4_), channel_id=1, source_target_pairs={{0,96},{16,112},{32,64},{48,80},{64,32},{80,48},{96,0},{112,16},{1... | collective-permute-start | bytes 98312 | tf_op jit(solution)/shard_map/ppermute | solution.py:411
  77.9 4.3 %collective-permute-start.10 = (f32[8,1024]{1,0:T(8,128)S(1)}, f32[8,1024]{1,0:T(8,128)S(1)}, u32[]{:S(2)}, u32[]{:S(2)}) collective-permute-start(f32[8,1024]{1,0:T(8,128)S(1)} %add.17.refs_0_.refs_3_.refs_4_), channel_id=1, source_target_pairs={{0,64},{16,80},{32,96},{48,112},{64,0},{80,16},{96,32},{112,48},{1... | collective-permute-start | bytes 98312 | tf_op jit(solution)/shard_map/ppermute | solution.py:411
  79.1 3.1 %collective-permute-start.9 = (f32[8,1024]{1,0:T(8,128)S(1)}, f32[8,1024]{1,0:T(8,128)S(1)}, u32[]{:S(2)}, u32[]{:S(2)}) collective-permute-start(f32[8,1024]{1,0:T(8,128)S(1)} %add.17.refs_0_.refs_3_.refs_4_), channel_id=1, source_target_pairs={{0,32},{16,48},{32,0},{48,16},{64,96},{80,112},{96,64},{112,80},{1... | collective-permute-start | bytes 98312 | tf_op jit(solution)/shard_map/ppermute | solution.py:411
  82.2 12.6 %copy-start = (bf16[256,8192]{1,0:T(8,128)(2,1)S(1)}, bf16[256,8192]{1,0:T(8,128)(2,1)}, u32[]{:S(2)}) copy-start(bf16[256,8192]{1,0:T(8,128)(2,1)} %refs_13_.1) | copy-start | bytes 12582916
  100.8 7.7 %collective-permute-start.12 = (bf16[4,32,6144]{2,1,0:T(8,128)(2,1)S(1)}, bf16[4,32,6144]{2,1,0:T(8,128)(2,1)S(1)}, u32[]{:S(2)}, u32[]{:S(2)}) collective-permute-start(bf16[4,32,6144]{2,1,0:T(8,128)(2,1)S(1)} %get-tuple-element.69), channel_id=1, source_target_pairs={{0,16},{16,0},{32,48},{48,32},{64,80},{80,64},{96,112},{112,96},{1... | collective-permute-start | bytes 4718600 | tf_op jit(solution)/shard_map/ppermute | solution.py:411
  106.6 2.0 %collective-permute-start.13 = (bf16[4,32,2048]{2,1,0:T(8,128)(2,1)S(1)}, bf16[4,32,2048]{2,1,0:T(8,128)(2,1)S(1)}, u32[]{:S(2)}, u32[]{:S(2)}) collective-permute-start(bf16[4,32,2048]{2,1,0:T(8,128)(2,1)S(1)} %get-tuple-element.71), channel_id=1, source_target_pairs={{0,16},{16,0},{32,48},{48,32},{64,80},{80,64},{96,112},{112,96},{1... | collective-permute-start | bytes 1572872 | tf_op jit(solution)/shard_map/ppermute | solution.py:411
  108.9 27.0 %collective-permute-start.14 = (bf16[32,8192]{1,0:T(8,128)(2,1)S(1)}, bf16[32,8192]{1,0:T(8,128)(2,1)S(1)}, u32[]{:S(2)}, u32[]{:S(2)}) collective-permute-start(bf16[32,8192]{1,0:T(8,128)(2,1)S(1)} %get-tuple-element.74), channel_id=1, source_target_pairs={{0,64},{16,80},{32,96},{48,112},{64,0},{80,16},{96,32},{112,48},{1... | collective-permute-start | bytes 1572872 | tf_op jit(solution)/shard_map/ppermute | solution.py:411
  110.8 25.2 %collective-permute-start.15 = (bf16[32,8192]{1,0:T(8,128)(2,1)S(1)}, bf16[32,8192]{1,0:T(8,128)(2,1)S(1)}, u32[]{:S(2)}, u32[]{:S(2)}) collective-permute-start(bf16[32,8192]{1,0:T(8,128)(2,1)S(1)} %get-tuple-element.75), channel_id=1, source_target_pairs={{0,32},{16,48},{32,0},{48,16},{64,96},{80,112},{96,64},{112,80},{1... | collective-permute-start | bytes 1572872 | tf_op jit(solution)/shard_map/ppermute | solution.py:411
  110.9 25.0 %collective-permute-start.16 = (bf16[32,8192]{1,0:T(8,128)(2,1)S(1)}, bf16[32,8192]{1,0:T(8,128)(2,1)S(1)}, u32[]{:S(2)}, u32[]{:S(2)}) collective-permute-start(bf16[32,8192]{1,0:T(8,128)(2,1)S(1)} %get-tuple-element.76), channel_id=1, source_target_pairs={{0,96},{16,112},{32,64},{48,80},{64,32},{80,48},{96,0},{112,16},{1... | collective-permute-start | bytes 1572872 | tf_op jit(solution)/shard_map/ppermute | solution.py:411

commit v7 on v6

--- a/solution.py
+++ b/solution.py
@@ -301,12 +301,13 @@
         here = pl.ds(row * width, width)
         piece, at = where[row]
         inverse = inverse_ref[pl.ds(row, 1), :]
-        head = inverse * mm(left_probs, piece_refs[piece][:, pl.ds(at * width, width)]) - (
-            inverse * scale[row : row + 1, :]
-        ) * mm(left_codes, codes_ref[:, here])
-        w = jnp.concatenate([w_ref[spot, here] for spot in spots], axis=0).astype(F32)
-        inner = jnp.sum(w * head, axis=0, keepdims=True)
-        grad = head - w * (inverse * inverse * inner)
+        head = mm(left_probs, piece_refs[piece][:, pl.ds(at * width, width)]) - scale[
+            row : row + 1, :
+        ] * mm(left_codes, codes_ref[:, here])
+        w = jnp.concatenate([w_ref[spot, here] for spot in spots], axis=0)
+        unit = w.astype(F32) * inverse
+        inner = jnp.sum(unit * head, axis=0, keepdims=True)
+        grad = inverse * (head - unit * inner)
         own_ref[:, cols] = grad[0:share]
         for k in range(chips):
             low = 2 * k * share

time: 138 us -> 137 us (level)
  no operation moved by 1% of the time
where the time goes in v7:
time: 137 us; the launch traced here: 136 us
  blocking collectives  50.7 us (37%)
  Pallas kernels  40.3 us (29%)
  starting transfers between devices  33.3 us (24%)
  waiting for transfers between devices  11.1 us (8%)
    all_to_all x5, blocking collectives, exchange(): return lax.all_to_all(array, axis, 0, 0)  50.7 us
    pallas_call x19, Pallas kernels, call(): pl.pallas_call(ordered, name=name, out_shape=out_shape, in_specs=[ANY] *...  40.3 us
    ppermute x17, starting transfers between devices, hop(): return lax.ppermute(array, 'patch', [(i, i ^ bits) for i in range(n_patch)])  24.7 us
    all_to_all x1, starting transfers between devices, exchange(): return lax.all_to_all(array, axis, 0, 0)  8.61 us
    all_to_all x1, waiting for transfers between devices, exchange(): return lax.all_to_all(array, axis, 0, 0)  5.69 us
    ppermute x17, waiting for transfers between devices, hop(): return lax.ppermute(array, 'patch', [(i, i ^ bits) for i in range(n_patch)])  5.43 us
  transfers between devices with their start and end apart: 18, of which 7 were waited for; matrix products, arithmetic and copies ran while one was open for 0% of the time, Pallas kernels for 11%

profile of v7, /device:TPU:1, one launch (start us, length us, event | category | flops | bytes accessed | tf_op | source)
XLA Modules:
  0.0 136.3 jit_solution(16541487628525832484)
XLA Ops:
  0.6 0.1 pad_add_fusion.refs_0_.refs_1_
  0.7 2.7 %own_rows.1 = (bf16[16,64,256]{2,1,0:T(8,128)(2,1)}, f32[32,256]{1,0:T(8,128)S(1)}, f32[8,512]{1,0:T(8,128)S(1)}) custom-call(s32[3]{0:T(128)S(1)} %pad_add_fusion.refs_0_.refs_1_, bf16[256,256]{1,0:T(8,128)(2,1)} %refs_1_.1, bf16[256,256]{1,0:T(8,128)(2,1)} %refs_2_.1, s32[1,32]{1,0:T(1,128)} %bitcast.6, bf16[1,32]{1,0:T(2,128)(2,1)} %bitcast.7), custom_call_target="tpu_custom_call" | custom-call | flops 268435456 | bytes 65536 | tf_op jit(solution)/shard_map/own_rows/pallas_call | solution.py:54
  3.4 8.6 %all-to-all-start = ((bf16[16,64,256]{2,1,0:T(8,128)(2,1)}), bf16[16,64,256]{2,1,0:T(8,128)(2,1)S(1)}, u32[]{:S(2)}, u32[]{:S(2)}) async-start(bf16[16,64,256]{2,1,0:T(8,128)(2,1)} %get-tuple-element.41), calls=%async_computation | async-start | bytes 1048576 | tf_op jit(solution)/shard_map/all_to_all | solution.py:409
  12.0 4.8 %proto_unit.1 = (bf16[8,256,1024]{2,1,0:T(8,128)(2,1)}, bf16[2,256,1024]{2,1,0:T(8,128)(2,1)S(1)}, f32[8,1024]{1,0:T(8,128)S(1)}) custom-call(bf16[256,8192]{1,0:T(8,128)(2,1)} %refs_13_.1), custom_call_target="tpu_custom_call" | custom-call | flops 2147483648 | bytes 65536 | tf_op jit(solution)/shard_map/proto_unit/pallas_call | solution.py:54
  16.8 5.7 %all-to-all-done.refs_0_.refs_1_ = bf16[16,64,256]{2,1,0:T(8,128)(2,1)S(1)} async-done(((bf16[16,64,256]{2,1,0:T(8,128)(2,1)}), bf16[16,64,256]{2,1,0:T(8,128)(2,1)S(1)}, u32[]{:S(2)}, u32[]{:S(2)}) %all-to-all-start) | async-done | bytes 524320 | tf_op jit(solution)/shard_map/all_to_all | solution.py:409
  22.5 4.9 %teacher_table.1 = (bf16[512,8192]{1,0:T(8,128)(2,1)S(1)}, bf16[8,256,1024]{2,1,0:T(8,128)(2,1)S(1)}, f32[8,1024]{1,0:T(8,128)S(1)}) custom-call(bf16[16,64,256]{2,1,0:T(8,128)(2,1)S(1)} %all-to-all-done.refs_0_.refs_1_, bf16[2,256,1024]{2,1,0:T(8,128)(2,1)S(1)} %get-tuple-element.42.refs_1_, bf16[8,256,1024]{2,1,0:T(8,128)(2,1)} %get-tuple-element.43.refs_2_), custom_call_target="tpu_custom_call" | custom-call | flops 4294967296 | bytes 65536 | tf_op jit(solution)/shard_map/teacher_table/pallas_call | solution.py:54
  27.4 2.1 %collective-permute-start = (f32[8,1024]{1,0:T(8,128)S(1)}, f32[8,1024]{1,0:T(8,128)S(1)}, u32[]{:S(2)}, u32[]{:S(2)}) collective-permute-start(f32[8,1024]{1,0:T(8,128)S(1)} %get-tuple-element.44), channel_id=1, source_target_pairs={{0,16},{16,0},{32,48},{48,32},{64,80},{80,64},{96,112},{112,96},{1... | collective-permute-start | bytes 98312 | tf_op jit(solution)/shard_map/ppermute | solution.py:412
  29.4 0.9 collective-permute-done
  30.3 2.5 %collective-permute-start.3 = (f32[8,1024]{1,0:T(8,128)S(1)}, f32[8,1024]{1,0:T(8,128)S(1)}, u32[]{:S(2)}, u32[]{:S(2)}) collective-permute-start(f32[8,1024]{1,0:T(8,128)S(1)} %add.15.refs_0_.refs_1_), channel_id=1, source_target_pairs={{0,96},{16,112},{32,64},{48,80},{64,32},{80,48},{96,0},{112,16},{1... | collective-permute-start | bytes 98312 | tf_op jit(solution)/shard_map/ppermute | solution.py:412
  32.8 0.5 collective-permute-start.2
  33.3 0.3 collective-permute-start.1
  33.6 2.7 %student_table.3 = (bf16[512,3072]{1,0:T(8,128)(2,1)S(1)}, f32[8,512]{1,0:T(8,128)S(1)}, f32[256,512]{1,0:T(8,128)S(1)}) custom-call(f32[8,1024]{1,0:T(8,128)S(1)} %add.15.refs_0_.refs_1_, bf16[16,64,256]{2,1,0:T(8,128)(2,1)S(1)} %all-to-all-done.refs_0_.refs_1_, bf16[8,256,1024]{2,1,0:T(8,128)(2,1)S(1)} %get-tuple-element.45.refs_2_.refs_5_), custom_call_target="tpu_custom_call" | custom-call | flops 2147483648 | bytes 65536 | tf_op jit(solution)/shard_map/student_table/pallas_call | solution.py:54
  36.2 0.0 collective-permute-done.3.refs_4_
  36.3 0.8 collective-permute-done.2.refs_3_
  37.0 0.0 collective-permute-done.1.refs_2_
  37.1 2.3 %row_pass.2 = f32[16,8,128]{2,1,0:T(8,128)S(1)} custom-call(f32[8,512]{1,0:T(8,128)S(1)} %get-tuple-element.46.refs_0_.refs_6_, f32[8,1024]{1,0:T(8,128)S(1)} %add.15.refs_0_.refs_1_, f32[8,1024]{1,0:T(8,128)S(1)} %collective-permute-done.1.refs_2_, f32[8,1024]{1,0:T(8,128)S(1)} %collective-permute-done.2.refs_3_, ...), custom_call_target="tpu_custom_call" | custom-call | flops 2147483648 | bytes 65536 | tf_op jit(solution)/shard_map/row_pass/pallas_call | solution.py:54
  39.4 9.2 %all_to_all.30.refs_0_.refs_1_ = f32[16,8,128]{2,1,0:T(8,128)S(1)} all-to-all(f32[16,8,128]{2,1,0:T(8,128)S(1)} %row_pass.2), channel_id=1, replica_groups=mesh['patch'=8,'proto'=16] {'proto'}, dimensions={0} | all-to-all | bytes 131072 | tf_op jit(solution)/shard_map/all_to_all | solution.py:409
  48.5 1.2 col_pass.2
  49.8 3.3 %collective-permute-start.4 = (f32[8,1024]{1,0:T(8,128)S(1)}, f32[8,1024]{1,0:T(8,128)S(1)}, u32[]{:S(2)}, u32[]{:S(2)}) collective-permute-start(f32[8,1024]{1,0:T(8,128)S(1)} %col_pass.2), channel_id=1, source_target_pairs={{0,16},{16,0},{32,48},{48,32},{64,80},{80,64},{96,112},{112,96},{1... | collective-permute-start | bytes 98312 | tf_op jit(solution)/shard_map/ppermute | solution.py:412
  53.1 0.9 collective-permute-done.4
  53.9 1.1 collective-permute-start.7
  55.0 0.8 collective-permute-start.6
  55.8 1.3 collective-permute-start.5
  57.2 2.7 %student_table.4 = (bf16[512,3072]{1,0:T(8,128)(2,1)S(1)}, f32[8,512]{1,0:T(8,128)S(1)}, f32[256,512]{1,0:T(8,128)S(1)}) custom-call(f32[8,1024]{1,0:T(8,128)S(1)} %add.16.refs_0_.refs_1_, bf16[16,64,256]{2,1,0:T(8,128)(2,1)S(1)} %all-to-all-done.refs_0_.refs_1_, bf16[8,256,1024]{2,1,0:T(8,128)(2,1)S(1)} %get-tuple-element.45.refs_2_.refs_5_), custom_call_target="tpu_custom_call" | custom-call | flops 2147483648 | bytes 65536 | tf_op jit(solution)/shard_map/student_table/pallas_call | solution.py:54
  59.9 0.0 collective-permute-done.7.refs_4_
  59.9 0.0 collective-permute-done.6.refs_3_
  59.9 0.0 collective-permute-done.5.refs_2_
  59.9 2.3 %row_pass.3 = f32[16,8,128]{2,1,0:T(8,128)S(1)} custom-call(f32[8,512]{1,0:T(8,128)S(1)} %get-tuple-element.49.refs_0_.refs_7_, f32[8,1024]{1,0:T(8,128)S(1)} %add.16.refs_0_.refs_1_, f32[8,1024]{1,0:T(8,128)S(1)} %collective-permute-done.5.refs_2_, f32[8,1024]{1,0:T(8,128)S(1)} %collective-permute-done.6.refs_3_, ...), custom_call_target="tpu_custom_call" | custom-call | flops 2147483648 | bytes 65536 | tf_op jit(solution)/shard_map/row_pass/pallas_call | solution.py:54
  62.2 9.4 %all_to_all.31.refs_0_ = f32[16,8,128]{2,1,0:T(8,128)S(1)} all-to-all(f32[16,8,128]{2,1,0:T(8,128)S(1)} %row_pass.3), channel_id=1, replica_groups=mesh['patch'=8,'proto'=16] {'proto'}, dimensions={0} | all-to-all | bytes 131072 | tf_op jit(solution)/shard_map/all_to_all | solution.py:409
  71.6 1.2 col_pass.3
  72.8 2.9 %collective-permute-start.8 = (f32[8,1024]{1,0:T(8,128)S(1)}, f32[8,1024]{1,0:T(8,128)S(1)}, u32[]{:S(2)}, u32[]{:S(2)}) collective-permute-start(f32[8,1024]{1,0:T(8,128)S(1)} %col_pass.3), channel_id=1, source_target_pairs={{0,16},{16,0},{32,48},{48,32},{64,80},{80,64},{96,112},{112,96},{1... | collective-permute-start | bytes 98312 | tf_op jit(solution)/shard_map/ppermute | solution.py:412
  75.7 0.9 collective-permute-done.8
  76.6 1.4 %collective-permute-start.11 = (f32[8,1024]{1,0:T(8,128)S(1)}, f32[8,1024]{1,0:T(8,128)S(1)}, u32[]{:S(2)}, u32[]{:S(2)}) collective-permute-start(f32[8,1024]{1,0:T(8,128)S(1)} %add.17.refs_0_.refs_3_.refs_4_), channel_id=1, source_target_pairs={{0,96},{16,112},{32,64},{48,80},{64,32},{80,48},{96,0},{112,16},{1... | collective-permute-start | bytes 98312 | tf_op jit(solution)/shard_map/ppermute | solution.py:412
  77.9 1.1 collective-permute-start.10
  79.1 0.7 collective-permute-start.9
  79.8 1.9 %student_table.5 = (bf16[512,2048]{1,0:T(8,128)(2,1)S(1)}, f32[8,512]{1,0:T(8,128)S(1)}, f32[256,512]{1,0:T(8,128)S(1)}, bf16[256,512]{1,0:T(8,128)(2,1)S(1)}) custom-call(f32[8,1024]{1,0:T(8,128)S(1)} %add.17.refs_0_.refs_3_.refs_4_, bf16[16,64,256]{2,1,0:T(8,128)(2,1)S(1)} %all-to-all-done.refs_0_.refs_1_, ...), custom_call_target="tpu_custom_call" | custom-call | flops 2147483648 | bytes 65536 | tf_op jit(solution)/shard_map/student_table/pallas_call | solution.py:54
  81.7 0.0 collective-permute-done.11.refs_3_.refs_6_.refs_7_
  81.7 0.5 collective-permute-done.10.refs_2_.refs_5_.refs_6_
  82.2 0.0 collective-permute-done.9.refs_1_.refs_4_.refs_5_
  82.2 0.0 copy-start
  82.2 2.5 %last_row_pass.1 = (f32[16,8,128]{2,1,0:T(8,128)S(1)}, f32[256,512]{1,0:T(8,128)S(1)}) custom-call(f32[8,1024]{1,0:T(8,128)S(1)} %add.17.refs_0_.refs_3_.refs_4_, f32[8,1024]{1,0:T(8,128)S(1)} %collective-permute-done.9.refs_1_.refs_4_.refs_5_, f32[8,1024]{1,0:T(8,128)S(1)} %collective-permute-done.10.refs_2_.refs_5_.refs_6_, ...), custom_call_target="tpu_custom_call" | custom-call | flops 2147483648 | bytes 65536 | tf_op jit(solution)/shard_map/last_row_pass/pallas_call | solution.py:54
  84.7 9.4 %all_to_all.32.refs_2_ = f32[16,8,128]{2,1,0:T(8,128)S(1)} all-to-all(f32[16,8,128]{2,1,0:T(8,128)S(1)} %get-tuple-element.51), channel_id=1, replica_groups=mesh['patch'=8,'proto'=16] {'proto'}, dimensions={0} | all-to-all | bytes 131072 | tf_op jit(solution)/shard_map/all_to_all | solution.py:409
  94.1 0.7 row_factors.1
  94.8 0.0 copy-done
  94.8 5.3 %head.2 = (f32[32,6144]{1,0:T(8,128)S(1)}, bf16[3,32,6144]{2,1,0:T(8,128)(2,1)S(1)}, bf16[4,32,6144]{2,1,0:T(8,128)(2,1)S(1)}) custom-call(s32[3]{0:T(128)S(1)} %pad_add_fusion.refs_0_.refs_1_, bf16[256,512]{1,0:T(8,128)(2,1)S(1)} %get-tuple-element.53.refs_1_.refs_2_, bf16[256,512]{1,0:T(8,128)(2,1)S(1)} %get-tuple-element.54.refs_2_.refs_3_, ...), custom_call_target="tpu_custom_call" | custom-call | flops 4294967296 | bytes 65536 | tf_op jit(solution)/shard_map/head/pallas_call | solution.py:54
  100.1 3.3 %collective-permute-start.12 = (bf16[4,32,6144]{2,1,0:T(8,128)(2,1)S(1)}, bf16[4,32,6144]{2,1,0:T(8,128)(2,1)S(1)}, u32[]{:S(2)}, u32[]{:S(2)}) collective-permute-start(bf16[4,32,6144]{2,1,0:T(8,128)(2,1)S(1)} %get-tuple-element.69), channel_id=1, source_target_pairs={{0,16},{16,0},{32,48},{48,32},{64,80},{80,64},{96,112},{112,96},{1... | collective-permute-start | bytes 4718600 | tf_op jit(solution)/shard_map/ppermute | solution.py:412
  103.4 2.2 %head.3 = (f32[32,2048]{1,0:T(8,128)S(1)}, bf16[3,32,2048]{2,1,0:T(8,128)(2,1)S(1)}, bf16[4,32,2048]{2,1,0:T(8,128)(2,1)S(1)}) custom-call(bf16[3,32,6144]{2,1,0:T(8,128)(2,1)S(1)} %get-tuple-element.59.refs_0_.refs_1_, s32[3]{0:T(128)S(1)} %pad_add_fusion.refs_0_.refs_1_, bf16[256,512]{1,0:T(8,128)(2,1)S(1)} %get-tuple-element.53.refs_1_.refs_2_, ...), custom_call_target="tpu_custom_call" | custom-call | flops 4294967296 | bytes 65536 | tf_op jit(solution)/shard_map/head/pallas_call | solution.py:54
  105.6 0.1 collective-permute-start.13
  105.7 0.3 feature.1.refs_0_
  106.1 1.6 %collective-permute-done.13.refs_4_ = bf16[4,32,2048]{2,1,0:T(8,128)(2,1)S(1)} collective-permute-done((bf16[4,32,2048]{2,1,0:T(8,128)(2,1)S(1)}, bf16[4,32,2048]{2,1,0:T(8,128)(2,1)S(1)}, u32[]{:S(2)}, u32[]{:S(2)}) %collective-permute-start.13) | collective-permute-done | bytes 524320 | tf_op jit(solution)/shard_map/ppermute | solution.py:412
  107.6 0.0 collective-permute-done.12.refs_2_
  107.6 0.4 pair_sums.1
  108.0 1.8 %collective-permute-start.14 = (bf16[32,8192]{1,0:T(8,128)(2,1)S(1)}, bf16[32,8192]{1,0:T(8,128)(2,1)S(1)}, u32[]{:S(2)}, u32[]{:S(2)}) collective-permute-start(bf16[32,8192]{1,0:T(8,128)(2,1)S(1)} %get-tuple-element.74), channel_id=1, source_target_pairs={{0,64},{16,80},{32,96},{48,112},{64,0},{80,16},{96,32},{112,48},{1... | collective-permute-start | bytes 1572872 | tf_op jit(solution)/shard_map/ppermute | solution.py:412
  109.8 0.1 collective-permute-start.15
  109.9 1.4 %collective-permute-start.16 = (bf16[32,8192]{1,0:T(8,128)(2,1)S(1)}, bf16[32,8192]{1,0:T(8,128)(2,1)S(1)}, u32[]{:S(2)}, u32[]{:S(2)}) collective-permute-start(bf16[32,8192]{1,0:T(8,128)(2,1)S(1)} %get-tuple-element.76), channel_id=1, source_target_pairs={{0,96},{16,112},{32,64},{48,80},{64,32},{80,48},{96,0},{112,16},{1... | collective-permute-start | bytes 1572872 | tf_op jit(solution)/shard_map/ppermute | solution.py:412
  111.3 11.7 %all_to_all.33.refs_0_ = bf16[16,48,256]{2,1,0:T(8,128)(2,1)S(1)} all-to-all(bf16[16,48,256]{2,1,0:T(8,128)(2,1)S(1)} %feature.1.refs_0_), channel_id=1, replica_groups=mesh['patch'=8,'proto'=16] {'proto'}, dimensions={0} | all-to-all | bytes 786432 | tf_op jit(solution)/shard_map/all_to_all | solution.py:409
  123.0 0.8 owner.1
  123.8 0.1 own_sum.1
  123.9 11.1 %all_to_all.34.refs_1_ = f32[8,8,128]{2,1,0:T(8,128)S(1)} all-to-all(f32[8,8,128]{2,1,0:T(8,128)S(1)} %get-tuple-element.73), channel_id=1, replica_groups=mesh['patch'=8,'proto'=16] {'patch'}, dimensions={0} | all-to-all | bytes 65536 | tf_op jit(solution)/shard_map/all_to_all | solution.py:409
  135.0 0.0 collective-permute-done.14.refs_2_
  135.0 0.0 collective-permute-done.15.refs_3_
  135.0 0.0 collective-permute-done.16.refs_4_
  135.0 1.3 assemble.1
  (3 shorter events, 0.0 us)
Async XLA Ops:
  3.4 19.1 %all-to-all-start = ((bf16[16,64,256]{2,1,0:T(8,128)(2,1)}), bf16[16,64,256]{2,1,0:T(8,128)(2,1)S(1)}, u32[]{:S(2)}, u32[]{:S(2)}) async-start(bf16[16,64,256]{2,1,0:T(8,128)(2,1)} %get-tuple-element.41), calls=%async_computation | async-start | bytes 1048576 | tf_op jit(solution)/shard_map/all_to_all | solution.py:409
  27.4 2.9 %collective-permute-start = (f32[8,1024]{1,0:T(8,128)S(1)}, f32[8,1024]{1,0:T(8,128)S(1)}, u32[]{:S(2)}, u32[]{:S(2)}) collective-permute-start(f32[8,1024]{1,0:T(8,128)S(1)} %get-tuple-element.44), channel_id=1, source_target_pairs={{0,16},{16,0},{32,48},{48,32},{64,80},{80,64},{96,112},{112,96},{1... | collective-permute-start | bytes 98312 | tf_op jit(solution)/shard_map/ppermute | solution.py:412
  30.3 5.9 %collective-permute-start.3 = (f32[8,1024]{1,0:T(8,128)S(1)}, f32[8,1024]{1,0:T(8,128)S(1)}, u32[]{:S(2)}, u32[]{:S(2)}) collective-permute-start(f32[8,1024]{1,0:T(8,128)S(1)} %add.15.refs_0_.refs_1_), channel_id=1, source_target_pairs={{0,96},{16,112},{32,64},{48,80},{64,32},{80,48},{96,0},{112,16},{1... | collective-permute-start | bytes 98312 | tf_op jit(solution)/shard_map/ppermute | solution.py:412
  32.8 4.3 %collective-permute-start.2 = (f32[8,1024]{1,0:T(8,128)S(1)}, f32[8,1024]{1,0:T(8,128)S(1)}, u32[]{:S(2)}, u32[]{:S(2)}) collective-permute-start(f32[8,1024]{1,0:T(8,128)S(1)} %add.15.refs_0_.refs_1_), channel_id=1, source_target_pairs={{0,64},{16,80},{32,96},{48,112},{64,0},{80,16},{96,32},{112,48},{1... | collective-permute-start | bytes 98312 | tf_op jit(solution)/shard_map/ppermute | solution.py:412
  33.3 3.7 %collective-permute-start.1 = (f32[8,1024]{1,0:T(8,128)S(1)}, f32[8,1024]{1,0:T(8,128)S(1)}, u32[]{:S(2)}, u32[]{:S(2)}) collective-permute-start(f32[8,1024]{1,0:T(8,128)S(1)} %add.15.refs_0_.refs_1_), channel_id=1, source_target_pairs={{0,32},{16,48},{32,0},{48,16},{64,96},{80,112},{96,64},{112,80},{1... | collective-permute-start | bytes 98312 | tf_op jit(solution)/shard_map/ppermute | solution.py:412
  49.8 4.1 %collective-permute-start.4 = (f32[8,1024]{1,0:T(8,128)S(1)}, f32[8,1024]{1,0:T(8,128)S(1)}, u32[]{:S(2)}, u32[]{:S(2)}) collective-permute-start(f32[8,1024]{1,0:T(8,128)S(1)} %col_pass.2), channel_id=1, source_target_pairs={{0,16},{16,0},{32,48},{48,32},{64,80},{80,64},{96,112},{112,96},{1... | collective-permute-start | bytes 98312 | tf_op jit(solution)/shard_map/ppermute | solution.py:412
  53.9 5.9 %collective-permute-start.7 = (f32[8,1024]{1,0:T(8,128)S(1)}, f32[8,1024]{1,0:T(8,128)S(1)}, u32[]{:S(2)}, u32[]{:S(2)}) collective-permute-start(f32[8,1024]{1,0:T(8,128)S(1)} %add.16.refs_0_.refs_1_), channel_id=1, source_target_pairs={{0,96},{16,112},{32,64},{48,80},{64,32},{80,48},{96,0},{112,16},{1... | collective-permute-start | bytes 98312 | tf_op jit(solution)/shard_map/ppermute | solution.py:412
  55.0 4.8 %collective-permute-start.6 = (f32[8,1024]{1,0:T(8,128)S(1)}, f32[8,1024]{1,0:T(8,128)S(1)}, u32[]{:S(2)}, u32[]{:S(2)}) collective-permute-start(f32[8,1024]{1,0:T(8,128)S(1)} %add.16.refs_0_.refs_1_), channel_id=1, source_target_pairs={{0,64},{16,80},{32,96},{48,112},{64,0},{80,16},{96,32},{112,48},{1... | collective-permute-start | bytes 98312 | tf_op jit(solution)/shard_map/ppermute | solution.py:412
  55.8 4.0 %collective-permute-start.5 = (f32[8,1024]{1,0:T(8,128)S(1)}, f32[8,1024]{1,0:T(8,128)S(1)}, u32[]{:S(2)}, u32[]{:S(2)}) collective-permute-start(f32[8,1024]{1,0:T(8,128)S(1)} %add.16.refs_0_.refs_1_), channel_id=1, source_target_pairs={{0,32},{16,48},{32,0},{48,16},{64,96},{80,112},{96,64},{112,80},{1... | collective-permute-start | bytes 98312 | tf_op jit(solution)/shard_map/ppermute | solution.py:412
  72.8 3.7 %collective-permute-start.8 = (f32[8,1024]{1,0:T(8,128)S(1)}, f32[8,1024]{1,0:T(8,128)S(1)}, u32[]{:S(2)}, u32[]{:S(2)}) collective-permute-start(f32[8,1024]{1,0:T(8,128)S(1)} %col_pass.3), channel_id=1, source_target_pairs={{0,16},{16,0},{32,48},{48,32},{64,80},{80,64},{96,112},{112,96},{1... | collective-permute-start | bytes 98312 | tf_op jit(solution)/shard_map/ppermute | solution.py:412
  76.6 5.2 %collective-permute-start.11 = (f32[8,1024]{1,0:T(8,128)S(1)}, f32[8,1024]{1,0:T(8,128)S(1)}, u32[]{:S(2)}, u32[]{:S(2)}) collective-permute-start(f32[8,1024]{1,0:T(8,128)S(1)} %add.17.refs_0_.refs_3_.refs_4_), channel_id=1, source_target_pairs={{0,96},{16,112},{32,64},{48,80},{64,32},{80,48},{96,0},{112,16},{1... | collective-permute-start | bytes 98312 | tf_op jit(solution)/shard_map/ppermute | solution.py:412
  77.9 4.3 %collective-permute-start.10 = (f32[8,1024]{1,0:T(8,128)S(1)}, f32[8,1024]{1,0:T(8,128)S(1)}, u32[]{:S(2)}, u32[]{:S(2)}) collective-permute-start(f32[8,1024]{1,0:T(8,128)S(1)} %add.17.refs_0_.refs_3_.refs_4_), channel_id=1, source_target_pairs={{0,64},{16,80},{32,96},{48,112},{64,0},{80,16},{96,32},{112,48},{1... | collective-permute-start | bytes 98312 | tf_op jit(solution)/shard_map/ppermute | solution.py:412
  79.1 3.1 %collective-permute-start.9 = (f32[8,1024]{1,0:T(8,128)S(1)}, f32[8,1024]{1,0:T(8,128)S(1)}, u32[]{:S(2)}, u32[]{:S(2)}) collective-permute-start(f32[8,1024]{1,0:T(8,128)S(1)} %add.17.refs_0_.refs_3_.refs_4_), channel_id=1, source_target_pairs={{0,32},{16,48},{32,0},{48,16},{64,96},{80,112},{96,64},{112,80},{1... | collective-permute-start | bytes 98312 | tf_op jit(solution)/shard_map/ppermute | solution.py:412
  82.2 12.6 %copy-start = (bf16[256,8192]{1,0:T(8,128)(2,1)S(1)}, bf16[256,8192]{1,0:T(8,128)(2,1)}, u32[]{:S(2)}) copy-start(bf16[256,8192]{1,0:T(8,128)(2,1)} %refs_13_.1) | copy-start | bytes 12582916
  100.1 7.5 %collective-permute-start.12 = (bf16[4,32,6144]{2,1,0:T(8,128)(2,1)S(1)}, bf16[4,32,6144]{2,1,0:T(8,128)(2,1)S(1)}, u32[]{:S(2)}, u32[]{:S(2)}) collective-permute-start(bf16[4,32,6144]{2,1,0:T(8,128)(2,1)S(1)} %get-tuple-element.69), channel_id=1, source_target_pairs={{0,16},{16,0},{32,48},{48,32},{64,80},{80,64},{96,112},{112,96},{1... | collective-permute-start | bytes 4718600 | tf_op jit(solution)/shard_map/ppermute | solution.py:412
  105.6 2.0 %collective-permute-start.13 = (bf16[4,32,2048]{2,1,0:T(8,128)(2,1)S(1)}, bf16[4,32,2048]{2,1,0:T(8,128)(2,1)S(1)}, u32[]{:S(2)}, u32[]{:S(2)}) collective-permute-start(bf16[4,32,2048]{2,1,0:T(8,128)(2,1)S(1)} %get-tuple-element.71), channel_id=1, source_target_pairs={{0,16},{16,0},{32,48},{48,32},{64,80},{80,64},{96,112},{112,96},{1... | collective-permute-start | bytes 1572872 | tf_op jit(solution)/shard_map/ppermute | solution.py:412
  108.0 27.0 %collective-permute-start.14 = (bf16[32,8192]{1,0:T(8,128)(2,1)S(1)}, bf16[32,8192]{1,0:T(8,128)(2,1)S(1)}, u32[]{:S(2)}, u32[]{:S(2)}) collective-permute-start(bf16[32,8192]{1,0:T(8,128)(2,1)S(1)} %get-tuple-element.74), channel_id=1, source_target_pairs={{0,64},{16,80},{32,96},{48,112},{64,0},{80,16},{96,32},{112,48},{1... | collective-permute-start | bytes 1572872 | tf_op jit(solution)/shard_map/ppermute | solution.py:412
  109.8 25.2 %collective-permute-start.15 = (bf16[32,8192]{1,0:T(8,128)(2,1)S(1)}, bf16[32,8192]{1,0:T(8,128)(2,1)S(1)}, u32[]{:S(2)}, u32[]{:S(2)}) collective-permute-start(bf16[32,8192]{1,0:T(8,128)(2,1)S(1)} %get-tuple-element.75), channel_id=1, source_target_pairs={{0,32},{16,48},{32,0},{48,16},{64,96},{80,112},{96,64},{112,80},{1... | collective-permute-start | bytes 1572872 | tf_op jit(solution)/shard_map/ppermute | solution.py:412
  109.9 25.1 %collective-permute-start.16 = (bf16[32,8192]{1,0:T(8,128)(2,1)S(1)}, bf16[32,8192]{1,0:T(8,128)(2,1)S(1)}, u32[]{:S(2)}, u32[]{:S(2)}) collective-permute-start(bf16[32,8192]{1,0:T(8,128)(2,1)S(1)} %get-tuple-element.76), channel_id=1, source_target_pairs={{0,96},{16,112},{32,64},{48,80},{64,32},{80,48},{96,0},{112,16},{1... | collective-permute-start | bytes 1572872 | tf_op jit(solution)/shard_map/ppermute | solution.py:412

commit v8 on v7

--- a/solution.py
+++ b/solution.py
@@ -467,7 +467,8 @@
     pieces = []
     for sweep in range(SK_ITERS):
         sums = sums + hop(sums, 1)
-        parts = [sums] + [hop(sums, 2 * k) for k in range(1, chips)]
+        steps = sorted(range(1, chips), key=lambda k: k % 2, reverse=True)
+        parts = [sums] + [hop(sums, 2 * k) for k in steps]
         span = PIECES[sweep] * width
         last = sweep == SK_ITERS - 1
         pieces.append(

time: 137 us -> 138 us (level)
  transfers between devices with their start and end apart: 18 -> 18, of which waited for: 7 -> 8; matrix products, arithmetic and copies ran while one was open for 0% -> 0% of each run, Pallas kernels for 11% -> 11%
where the time goes in v8:
time: 138 us; the launch traced here: 137 us
  blocking collectives  50.7 us (37%)
  Pallas kernels  40.3 us (29%)
  starting transfers between devices  33.3 us (24%)
  waiting for transfers between devices  11.9 us (9%)
    all_to_all x5, blocking collectives, exchange(): return lax.all_to_all(array, axis, 0, 0)  50.7 us
    pallas_call x19, Pallas kernels, call(): pl.pallas_call(ordered, name=name, out_shape=out_shape, in_specs=[ANY] *...  40.3 us
    ppermute x17, starting transfers between devices, hop(): return lax.ppermute(array, 'patch', [(i, i ^ bits) for i in range(n_patch)])  24.7 us
    all_to_all x1, starting transfers between devices, exchange(): return lax.all_to_all(array, axis, 0, 0)  8.61 us
    ppermute x17, waiting for transfers between devices, hop(): return lax.ppermute(array, 'patch', [(i, i ^ bits) for i in range(n_patch)])  6.18 us
    all_to_all x1, waiting for transfers between devices, exchange(): return lax.all_to_all(array, axis, 0, 0)  5.69 us
  transfers between devices with their start and end apart: 18, of which 8 were waited for; matrix products, arithmetic and copies ran while one was open for 0% of the time, Pallas kernels for 11%

profile of v8, /device:TPU:1, one launch (start us, length us, event | category | flops | bytes accessed | tf_op | source)
XLA Modules:
  0.0 137.0 jit_solution(10713977219338106370)
XLA Ops:
  0.6 0.1 pad_add_fusion.refs_0_.refs_1_
  0.7 2.7 %own_rows.1 = (bf16[16,64,256]{2,1,0:T(8,128)(2,1)}, f32[32,256]{1,0:T(8,128)S(1)}, f32[8,512]{1,0:T(8,128)S(1)}) custom-call(s32[3]{0:T(128)S(1)} %pad_add_fusion.refs_0_.refs_1_, bf16[256,256]{1,0:T(8,128)(2,1)} %refs_1_.1, bf16[256,256]{1,0:T(8,128)(2,1)} %refs_2_.1, s32[1,32]{1,0:T(1,128)} %bitcast.6, bf16[1,32]{1,0:T(2,128)(2,1)} %bitcast.7), custom_call_target="tpu_custom_call" | custom-call | flops 268435456 | bytes 65536 | tf_op jit(solution)/shard_map/own_rows/pallas_call | solution.py:54
  3.4 8.6 %all-to-all-start = ((bf16[16,64,256]{2,1,0:T(8,128)(2,1)}), bf16[16,64,256]{2,1,0:T(8,128)(2,1)S(1)}, u32[]{:S(2)}, u32[]{:S(2)}) async-start(bf16[16,64,256]{2,1,0:T(8,128)(2,1)} %get-tuple-element.41), calls=%async_computation | async-start | bytes 1048576 | tf_op jit(solution)/shard_map/all_to_all | solution.py:409
  12.0 4.8 %proto_unit.1 = (bf16[8,256,1024]{2,1,0:T(8,128)(2,1)}, bf16[2,256,1024]{2,1,0:T(8,128)(2,1)S(1)}, f32[8,1024]{1,0:T(8,128)S(1)}) custom-call(bf16[256,8192]{1,0:T(8,128)(2,1)} %refs_13_.1), custom_call_target="tpu_custom_call" | custom-call | flops 2147483648 | bytes 65536 | tf_op jit(solution)/shard_map/proto_unit/pallas_call | solution.py:54
  16.8 5.7 %all-to-all-done.refs_0_.refs_1_ = bf16[16,64,256]{2,1,0:T(8,128)(2,1)S(1)} async-done(((bf16[16,64,256]{2,1,0:T(8,128)(2,1)}), bf16[16,64,256]{2,1,0:T(8,128)(2,1)S(1)}, u32[]{:S(2)}, u32[]{:S(2)}) %all-to-all-start) | async-done | bytes 524320 | tf_op jit(solution)/shard_map/all_to_all | solution.py:409
  22.5 4.9 %teacher_table.1 = (bf16[512,8192]{1,0:T(8,128)(2,1)S(1)}, bf16[8,256,1024]{2,1,0:T(8,128)(2,1)S(1)}, f32[8,1024]{1,0:T(8,128)S(1)}) custom-call(bf16[16,64,256]{2,1,0:T(8,128)(2,1)S(1)} %all-to-all-done.refs_0_.refs_1_, bf16[2,256,1024]{2,1,0:T(8,128)(2,1)S(1)} %get-tuple-element.42.refs_1_, bf16[8,256,1024]{2,1,0:T(8,128)(2,1)} %get-tuple-element.43.refs_2_), custom_call_target="tpu_custom_call" | custom-call | flops 4294967296 | bytes 65536 | tf_op jit(solution)/shard_map/teacher_table/pallas_call | solution.py:54
  27.4 2.1 %collective-permute-start = (f32[8,1024]{1,0:T(8,128)S(1)}, f32[8,1024]{1,0:T(8,128)S(1)}, u32[]{:S(2)}, u32[]{:S(2)}) collective-permute-start(f32[8,1024]{1,0:T(8,128)S(1)} %get-tuple-element.44), channel_id=1, source_target_pairs={{0,16},{16,0},{32,48},{48,32},{64,80},{80,64},{96,112},{112,96},{1... | collective-permute-start | bytes 98312 | tf_op jit(solution)/shard_map/ppermute | solution.py:412
  29.4 0.9 collective-permute-done
  30.3 2.7 %collective-permute-start.3 = (f32[8,1024]{1,0:T(8,128)S(1)}, f32[8,1024]{1,0:T(8,128)S(1)}, u32[]{:S(2)}, u32[]{:S(2)}) collective-permute-start(f32[8,1024]{1,0:T(8,128)S(1)} %add.15.refs_0_.refs_1_), channel_id=1, source_target_pairs={{0,64},{16,80},{32,96},{48,112},{64,0},{80,16},{96,32},{112,48},{1... | collective-permute-start | bytes 98312 | tf_op jit(solution)/shard_map/ppermute | solution.py:412
  33.1 0.9 collective-permute-start.2
  33.9 0.0 collective-permute-start.1
  33.9 2.7 %student_table.3 = (bf16[512,3072]{1,0:T(8,128)(2,1)S(1)}, f32[8,512]{1,0:T(8,128)S(1)}, f32[256,512]{1,0:T(8,128)S(1)}) custom-call(f32[8,1024]{1,0:T(8,128)S(1)} %add.15.refs_0_.refs_1_, bf16[16,64,256]{2,1,0:T(8,128)(2,1)S(1)} %all-to-all-done.refs_0_.refs_1_, bf16[8,256,1024]{2,1,0:T(8,128)(2,1)S(1)} %get-tuple-element.45.refs_2_.refs_5_), custom_call_target="tpu_custom_call" | custom-call | flops 2147483648 | bytes 65536 | tf_op jit(solution)/shard_map/student_table/pallas_call | solution.py:54
  36.6 0.0 collective-permute-done.3.refs_4_
  36.6 0.4 collective-permute-done.2.refs_3_
  37.0 0.0 collective-permute-done.1.refs_2_
  37.0 2.3 %row_pass.2 = f32[16,8,128]{2,1,0:T(8,128)S(1)} custom-call(f32[8,512]{1,0:T(8,128)S(1)} %get-tuple-element.46.refs_0_.refs_6_, f32[8,1024]{1,0:T(8,128)S(1)} %add.15.refs_0_.refs_1_, f32[8,1024]{1,0:T(8,128)S(1)} %collective-permute-done.1.refs_2_, f32[8,1024]{1,0:T(8,128)S(1)} %collective-permute-done.2.refs_3_, ...), custom_call_target="tpu_custom_call" | custom-call | flops 2147483648 | bytes 65536 | tf_op jit(solution)/shard_map/row_pass/pallas_call | solution.py:54
  39.3 9.2 %all_to_all.30.refs_0_.refs_1_ = f32[16,8,128]{2,1,0:T(8,128)S(1)} all-to-all(f32[16,8,128]{2,1,0:T(8,128)S(1)} %row_pass.2), channel_id=1, replica_groups=mesh['patch'=8,'proto'=16] {'proto'}, dimensions={0} | all-to-all | bytes 131072 | tf_op jit(solution)/shard_map/all_to_all | solution.py:409
  48.5 1.2 col_pass.2
  49.7 3.3 %collective-permute-start.4 = (f32[8,1024]{1,0:T(8,128)S(1)}, f32[8,1024]{1,0:T(8,128)S(1)}, u32[]{:S(2)}, u32[]{:S(2)}) collective-permute-start(f32[8,1024]{1,0:T(8,128)S(1)} %col_pass.2), channel_id=1, source_target_pairs={{0,16},{16,0},{32,48},{48,32},{64,80},{80,64},{96,112},{112,96},{1... | collective-permute-start | bytes 98312 | tf_op jit(solution)/shard_map/ppermute | solution.py:412
  53.0 0.9 collective-permute-done.4
  53.9 2.0 %collective-permute-start.7 = (f32[8,1024]{1,0:T(8,128)S(1)}, f32[8,1024]{1,0:T(8,128)S(1)}, u32[]{:S(2)}, u32[]{:S(2)}) collective-permute-start(f32[8,1024]{1,0:T(8,128)S(1)} %add.16.refs_0_.refs_1_), channel_id=1, source_target_pairs={{0,64},{16,80},{32,96},{48,112},{64,0},{80,16},{96,32},{112,48},{1... | collective-permute-start | bytes 98312 | tf_op jit(solution)/shard_map/ppermute | solution.py:412
  55.9 0.9 collective-permute-start.6
  56.8 0.0 collective-permute-start.5
  56.8 2.7 %student_table.4 = (bf16[512,3072]{1,0:T(8,128)(2,1)S(1)}, f32[8,512]{1,0:T(8,128)S(1)}, f32[256,512]{1,0:T(8,128)S(1)}) custom-call(f32[8,1024]{1,0:T(8,128)S(1)} %add.16.refs_0_.refs_1_, bf16[16,64,256]{2,1,0:T(8,128)(2,1)S(1)} %all-to-all-done.refs_0_.refs_1_, bf16[8,256,1024]{2,1,0:T(8,128)(2,1)S(1)} %get-tuple-element.45.refs_2_.refs_5_), custom_call_target="tpu_custom_call" | custom-call | flops 2147483648 | bytes 65536 | tf_op jit(solution)/shard_map/student_table/pallas_call | solution.py:54
  59.4 0.0 collective-permute-done.7.refs_4_
  59.5 0.4 collective-permute-done.6.refs_3_
  59.9 0.0 collective-permute-done.5.refs_2_
  59.9 2.3 %row_pass.3 = f32[16,8,128]{2,1,0:T(8,128)S(1)} custom-call(f32[8,512]{1,0:T(8,128)S(1)} %get-tuple-element.49.refs_0_.refs_7_, f32[8,1024]{1,0:T(8,128)S(1)} %add.16.refs_0_.refs_1_, f32[8,1024]{1,0:T(8,128)S(1)} %collective-permute-done.5.refs_2_, f32[8,1024]{1,0:T(8,128)S(1)} %collective-permute-done.6.refs_3_, ...), custom_call_target="tpu_custom_call" | custom-call | flops 2147483648 | bytes 65536 | tf_op jit(solution)/shard_map/row_pass/pallas_call | solution.py:54
  62.2 9.4 %all_to_all.31.refs_0_ = f32[16,8,128]{2,1,0:T(8,128)S(1)} all-to-all(f32[16,8,128]{2,1,0:T(8,128)S(1)} %row_pass.3), channel_id=1, replica_groups=mesh['patch'=8,'proto'=16] {'proto'}, dimensions={0} | all-to-all | bytes 131072 | tf_op jit(solution)/shard_map/all_to_all | solution.py:409
  71.6 1.2 col_pass.3
  72.8 3.3 %collective-permute-start.8 = (f32[8,1024]{1,0:T(8,128)S(1)}, f32[8,1024]{1,0:T(8,128)S(1)}, u32[]{:S(2)}, u32[]{:S(2)}) collective-permute-start(f32[8,1024]{1,0:T(8,128)S(1)} %col_pass.3), channel_id=1, source_target_pairs={{0,16},{16,0},{32,48},{48,32},{64,80},{80,64},{96,112},{112,96},{1... | collective-permute-start | bytes 98312 | tf_op jit(solution)/shard_map/ppermute | solution.py:412
  76.1 0.9 collective-permute-done.8
  76.9 2.0 %collective-permute-start.11 = (f32[8,1024]{1,0:T(8,128)S(1)}, f32[8,1024]{1,0:T(8,128)S(1)}, u32[]{:S(2)}, u32[]{:S(2)}) collective-permute-start(f32[8,1024]{1,0:T(8,128)S(1)} %add.17.refs_0_.refs_3_.refs_4_), channel_id=1, source_target_pairs={{0,64},{16,80},{32,96},{48,112},{64,0},{80,16},{96,32},{112,48},{1... | collective-permute-start | bytes 98312 | tf_op jit(solution)/shard_map/ppermute | solution.py:412
  78.9 0.9 collective-permute-start.10
  79.8 0.0 collective-permute-start.9
  79.8 1.9 %student_table.5 = (bf16[512,2048]{1,0:T(8,128)(2,1)S(1)}, f32[8,512]{1,0:T(8,128)S(1)}, f32[256,512]{1,0:T(8,128)S(1)}, bf16[256,512]{1,0:T(8,128)(2,1)S(1)}) custom-call(f32[8,1024]{1,0:T(8,128)S(1)} %add.17.refs_0_.refs_3_.refs_4_, bf16[16,64,256]{2,1,0:T(8,128)(2,1)S(1)} %all-to-all-done.refs_0_.refs_1_, ...), custom_call_target="tpu_custom_call" | custom-call | flops 2147483648 | bytes 65536 | tf_op jit(solution)/shard_map/student_table/pallas_call | solution.py:54
  81.7 0.0 collective-permute-done.11.refs_3_.refs_6_.refs_7_
  81.7 1.2 collective-permute-done.10.refs_2_.refs_5_.refs_6_
  82.9 0.0 collective-permute-done.9.refs_1_.refs_4_.refs_5_
  82.9 0.0 copy-start
  82.9 2.5 %last_row_pass.1 = (f32[16,8,128]{2,1,0:T(8,128)S(1)}, f32[256,512]{1,0:T(8,128)S(1)}) custom-call(f32[8,1024]{1,0:T(8,128)S(1)} %add.17.refs_0_.refs_3_.refs_4_, f32[8,1024]{1,0:T(8,128)S(1)} %collective-permute-done.9.refs_1_.refs_4_.refs_5_, f32[8,1024]{1,0:T(8,128)S(1)} %collective-permute-done.10.refs_2_.refs_5_.refs_6_, ...), custom_call_target="tpu_custom_call" | custom-call | flops 2147483648 | bytes 65536 | tf_op jit(solution)/shard_map/last_row_pass/pallas_call | solution.py:54
  85.5 9.4 %all_to_all.32.refs_2_ = f32[16,8,128]{2,1,0:T(8,128)S(1)} all-to-all(f32[16,8,128]{2,1,0:T(8,128)S(1)} %get-tuple-element.51), channel_id=1, replica_groups=mesh['patch'=8,'proto'=16] {'proto'}, dimensions={0} | all-to-all | bytes 131072 | tf_op jit(solution)/shard_map/all_to_all | solution.py:409
  94.8 0.7 row_factors.1
  95.5 0.0 copy-done
  95.5 5.3 %head.2 = (f32[32,6144]{1,0:T(8,128)S(1)}, bf16[3,32,6144]{2,1,0:T(8,128)(2,1)S(1)}, bf16[4,32,6144]{2,1,0:T(8,128)(2,1)S(1)}) custom-call(s32[3]{0:T(128)S(1)} %pad_add_fusion.refs_0_.refs_1_, bf16[256,512]{1,0:T(8,128)(2,1)S(1)} %get-tuple-element.53.refs_1_.refs_2_, bf16[256,512]{1,0:T(8,128)(2,1)S(1)} %get-tuple-element.54.refs_2_.refs_3_, ...), custom_call_target="tpu_custom_call" | custom-call | flops 4294967296 | bytes 65536 | tf_op jit(solution)/shard_map/head/pallas_call | solution.py:54
  100.8 3.3 %collective-permute-start.12 = (bf16[4,32,6144]{2,1,0:T(8,128)(2,1)S(1)}, bf16[4,32,6144]{2,1,0:T(8,128)(2,1)S(1)}, u32[]{:S(2)}, u32[]{:S(2)}) collective-permute-start(bf16[4,32,6144]{2,1,0:T(8,128)(2,1)S(1)} %get-tuple-element.69), channel_id=1, source_target_pairs={{0,16},{16,0},{32,48},{48,32},{64,80},{80,64},{96,112},{112,96},{1... | collective-permute-start | bytes 4718600 | tf_op jit(solution)/shard_map/ppermute | solution.py:412
  104.1 2.2 %head.3 = (f32[32,2048]{1,0:T(8,128)S(1)}, bf16[3,32,2048]{2,1,0:T(8,128)(2,1)S(1)}, bf16[4,32,2048]{2,1,0:T(8,128)(2,1)S(1)}) custom-call(bf16[3,32,6144]{2,1,0:T(8,128)(2,1)S(1)} %get-tuple-element.59.refs_0_.refs_1_, s32[3]{0:T(128)S(1)} %pad_add_fusion.refs_0_.refs_1_, bf16[256,512]{1,0:T(8,128)(2,1)S(1)} %get-tuple-element.53.refs_1_.refs_2_, ...), custom_call_target="tpu_custom_call" | custom-call | flops 4294967296 | bytes 65536 | tf_op jit(solution)/shard_map/head/pallas_call | solution.py:54
  106.3 0.1 collective-permute-start.13
  106.4 0.3 feature.1.refs_0_
  106.8 1.6 %collective-permute-done.13.refs_4_ = bf16[4,32,2048]{2,1,0:T(8,128)(2,1)S(1)} collective-permute-done((bf16[4,32,2048]{2,1,0:T(8,128)(2,1)S(1)}, bf16[4,32,2048]{2,1,0:T(8,128)(2,1)S(1)}, u32[]{:S(2)}, u32[]{:S(2)}) %collective-permute-start.13) | collective-permute-done | bytes 524320 | tf_op jit(solution)/shard_map/ppermute | solution.py:412
  108.3 0.0 collective-permute-done.12.refs_2_
  108.3 0.4 pair_sums.1
  108.7 1.3 collective-permute-start.14
  110.0 1.1 collective-permute-start.15
  111.1 0.9 collective-permute-start.16
  112.0 11.7 %all_to_all.33.refs_0_ = bf16[16,48,256]{2,1,0:T(8,128)(2,1)S(1)} all-to-all(bf16[16,48,256]{2,1,0:T(8,128)(2,1)S(1)} %feature.1.refs_0_), channel_id=1, replica_groups=mesh['patch'=8,'proto'=16] {'proto'}, dimensions={0} | all-to-all | bytes 786432 | tf_op jit(solution)/shard_map/all_to_all | solution.py:409
  123.7 0.8 owner.1
  124.5 0.1 own_sum.1
  124.6 11.1 %all_to_all.34.refs_1_ = f32[8,8,128]{2,1,0:T(8,128)S(1)} all-to-all(f32[8,8,128]{2,1,0:T(8,128)S(1)} %get-tuple-element.73), channel_id=1, replica_groups=mesh['patch'=8,'proto'=16] {'patch'}, dimensions={0} | all-to-all | bytes 65536 | tf_op jit(solution)/shard_map/all_to_all | solution.py:409
  135.7 0.0 collective-permute-done.14.refs_2_
  135.7 0.0 collective-permute-done.15.refs_3_
  135.7 0.0 collective-permute-done.16.refs_4_
  135.7 1.3 assemble.1
  (3 shorter events, 0.0 us)
Async XLA Ops:
  3.4 19.1 %all-to-all-start = ((bf16[16,64,256]{2,1,0:T(8,128)(2,1)}), bf16[16,64,256]{2,1,0:T(8,128)(2,1)S(1)}, u32[]{:S(2)}, u32[]{:S(2)}) async-start(bf16[16,64,256]{2,1,0:T(8,128)(2,1)} %get-tuple-element.41), calls=%async_computation | async-start | bytes 1048576 | tf_op jit(solution)/shard_map/all_to_all | solution.py:409
  27.4 2.9 %collective-permute-start = (f32[8,1024]{1,0:T(8,128)S(1)}, f32[8,1024]{1,0:T(8,128)S(1)}, u32[]{:S(2)}, u32[]{:S(2)}) collective-permute-start(f32[8,1024]{1,0:T(8,128)S(1)} %get-tuple-element.44), channel_id=1, source_target_pairs={{0,16},{16,0},{32,48},{48,32},{64,80},{80,64},{96,112},{112,96},{1... | collective-permute-start | bytes 98312 | tf_op jit(solution)/shard_map/ppermute | solution.py:412
  30.3 6.3 %collective-permute-start.3 = (f32[8,1024]{1,0:T(8,128)S(1)}, f32[8,1024]{1,0:T(8,128)S(1)}, u32[]{:S(2)}, u32[]{:S(2)}) collective-permute-start(f32[8,1024]{1,0:T(8,128)S(1)} %add.15.refs_0_.refs_1_), channel_id=1, source_target_pairs={{0,64},{16,80},{32,96},{48,112},{64,0},{80,16},{96,32},{112,48},{1... | collective-permute-start | bytes 98312 | tf_op jit(solution)/shard_map/ppermute | solution.py:412
  33.1 4.0 %collective-permute-start.2 = (f32[8,1024]{1,0:T(8,128)S(1)}, f32[8,1024]{1,0:T(8,128)S(1)}, u32[]{:S(2)}, u32[]{:S(2)}) collective-permute-start(f32[8,1024]{1,0:T(8,128)S(1)} %add.15.refs_0_.refs_1_), channel_id=1, source_target_pairs={{0,96},{16,112},{32,64},{48,80},{64,32},{80,48},{96,0},{112,16},{1... | collective-permute-start | bytes 98312 | tf_op jit(solution)/shard_map/ppermute | solution.py:412
  33.9 3.1 %collective-permute-start.1 = (f32[8,1024]{1,0:T(8,128)S(1)}, f32[8,1024]{1,0:T(8,128)S(1)}, u32[]{:S(2)}, u32[]{:S(2)}) collective-permute-start(f32[8,1024]{1,0:T(8,128)S(1)} %add.15.refs_0_.refs_1_), channel_id=1, source_target_pairs={{0,32},{16,48},{32,0},{48,16},{64,96},{80,112},{96,64},{112,80},{1... | collective-permute-start | bytes 98312 | tf_op jit(solution)/shard_map/ppermute | solution.py:412
  49.7 4.1 %collective-permute-start.4 = (f32[8,1024]{1,0:T(8,128)S(1)}, f32[8,1024]{1,0:T(8,128)S(1)}, u32[]{:S(2)}, u32[]{:S(2)}) collective-permute-start(f32[8,1024]{1,0:T(8,128)S(1)} %col_pass.2), channel_id=1, source_target_pairs={{0,16},{16,0},{32,48},{48,32},{64,80},{80,64},{96,112},{112,96},{1... | collective-permute-start | bytes 98312 | tf_op jit(solution)/shard_map/ppermute | solution.py:412
  53.9 5.6 %collective-permute-start.7 = (f32[8,1024]{1,0:T(8,128)S(1)}, f32[8,1024]{1,0:T(8,128)S(1)}, u32[]{:S(2)}, u32[]{:S(2)}) collective-permute-start(f32[8,1024]{1,0:T(8,128)S(1)} %add.16.refs_0_.refs_1_), channel_id=1, source_target_pairs={{0,64},{16,80},{32,96},{48,112},{64,0},{80,16},{96,32},{112,48},{1... | collective-permute-start | bytes 98312 | tf_op jit(solution)/shard_map/ppermute | solution.py:412
  55.9 4.0 %collective-permute-start.6 = (f32[8,1024]{1,0:T(8,128)S(1)}, f32[8,1024]{1,0:T(8,128)S(1)}, u32[]{:S(2)}, u32[]{:S(2)}) collective-permute-start(f32[8,1024]{1,0:T(8,128)S(1)} %add.16.refs_0_.refs_1_), channel_id=1, source_target_pairs={{0,96},{16,112},{32,64},{48,80},{64,32},{80,48},{96,0},{112,16},{1... | collective-permute-start | bytes 98312 | tf_op jit(solution)/shard_map/ppermute | solution.py:412
  56.8 3.1 %collective-permute-start.5 = (f32[8,1024]{1,0:T(8,128)S(1)}, f32[8,1024]{1,0:T(8,128)S(1)}, u32[]{:S(2)}, u32[]{:S(2)}) collective-permute-start(f32[8,1024]{1,0:T(8,128)S(1)} %add.16.refs_0_.refs_1_), channel_id=1, source_target_pairs={{0,32},{16,48},{32,0},{48,16},{64,96},{80,112},{96,64},{112,80},{1... | collective-permute-start | bytes 98312 | tf_op jit(solution)/shard_map/ppermute | solution.py:412
  72.8 4.1 %collective-permute-start.8 = (f32[8,1024]{1,0:T(8,128)S(1)}, f32[8,1024]{1,0:T(8,128)S(1)}, u32[]{:S(2)}, u32[]{:S(2)}) collective-permute-start(f32[8,1024]{1,0:T(8,128)S(1)} %col_pass.3), channel_id=1, source_target_pairs={{0,16},{16,0},{32,48},{48,32},{64,80},{80,64},{96,112},{112,96},{1... | collective-permute-start | bytes 98312 | tf_op jit(solution)/shard_map/ppermute | solution.py:412
  76.9 4.8 %collective-permute-start.11 = (f32[8,1024]{1,0:T(8,128)S(1)}, f32[8,1024]{1,0:T(8,128)S(1)}, u32[]{:S(2)}, u32[]{:S(2)}) collective-permute-start(f32[8,1024]{1,0:T(8,128)S(1)} %add.17.refs_0_.refs_3_.refs_4_), channel_id=1, source_target_pairs={{0,64},{16,80},{32,96},{48,112},{64,0},{80,16},{96,32},{112,48},{1... | collective-permute-start | bytes 98312 | tf_op jit(solution)/shard_map/ppermute | solution.py:412
  78.9 4.0 %collective-permute-start.10 = (f32[8,1024]{1,0:T(8,128)S(1)}, f32[8,1024]{1,0:T(8,128)S(1)}, u32[]{:S(2)}, u32[]{:S(2)}) collective-permute-start(f32[8,1024]{1,0:T(8,128)S(1)} %add.17.refs_0_.refs_3_.refs_4_), channel_id=1, source_target_pairs={{0,96},{16,112},{32,64},{48,80},{64,32},{80,48},{96,0},{112,16},{1... | collective-permute-start | bytes 98312 | tf_op jit(solution)/shard_map/ppermute | solution.py:412
  79.8 3.1 %collective-permute-start.9 = (f32[8,1024]{1,0:T(8,128)S(1)}, f32[8,1024]{1,0:T(8,128)S(1)}, u32[]{:S(2)}, u32[]{:S(2)}) collective-permute-start(f32[8,1024]{1,0:T(8,128)S(1)} %add.17.refs_0_.refs_3_.refs_4_), channel_id=1, source_target_pairs={{0,32},{16,48},{32,0},{48,16},{64,96},{80,112},{96,64},{112,80},{1... | collective-permute-start | bytes 98312 | tf_op jit(solution)/shard_map/ppermute | solution.py:412
  82.9 12.6 %copy-start = (bf16[256,8192]{1,0:T(8,128)(2,1)S(1)}, bf16[256,8192]{1,0:T(8,128)(2,1)}, u32[]{:S(2)}) copy-start(bf16[256,8192]{1,0:T(8,128)(2,1)} %refs_13_.1) | copy-start | bytes 12582916
  100.8 7.5 %collective-permute-start.12 = (bf16[4,32,6144]{2,1,0:T(8,128)(2,1)S(1)}, bf16[4,32,6144]{2,1,0:T(8,128)(2,1)S(1)}, u32[]{:S(2)}, u32[]{:S(2)}) collective-permute-start(bf16[4,32,6144]{2,1,0:T(8,128)(2,1)S(1)} %get-tuple-element.69), channel_id=1, source_target_pairs={{0,16},{16,0},{32,48},{48,32},{64,80},{80,64},{96,112},{112,96},{1... | collective-permute-start | bytes 4718600 | tf_op jit(solution)/shard_map/ppermute | solution.py:412
  106.3 2.0 %collective-permute-start.13 = (bf16[4,32,2048]{2,1,0:T(8,128)(2,1)S(1)}, bf16[4,32,2048]{2,1,0:T(8,128)(2,1)S(1)}, u32[]{:S(2)}, u32[]{:S(2)}) collective-permute-start(bf16[4,32,2048]{2,1,0:T(8,128)(2,1)S(1)} %get-tuple-element.71), channel_id=1, source_target_pairs={{0,16},{16,0},{32,48},{48,32},{64,80},{80,64},{96,112},{112,96},{1... | collective-permute-start | bytes 1572872 | tf_op jit(solution)/shard_map/ppermute | solution.py:412
  108.7 27.0 %collective-permute-start.14 = (bf16[32,8192]{1,0:T(8,128)(2,1)S(1)}, bf16[32,8192]{1,0:T(8,128)(2,1)S(1)}, u32[]{:S(2)}, u32[]{:S(2)}) collective-permute-start(bf16[32,8192]{1,0:T(8,128)(2,1)S(1)} %get-tuple-element.74), channel_id=1, source_target_pairs={{0,64},{16,80},{32,96},{48,112},{64,0},{80,16},{96,32},{112,48},{1... | collective-permute-start | bytes 1572872 | tf_op jit(solution)/shard_map/ppermute | solution.py:412
  110.0 25.7 %collective-permute-start.15 = (bf16[32,8192]{1,0:T(8,128)(2,1)S(1)}, bf16[32,8192]{1,0:T(8,128)(2,1)S(1)}, u32[]{:S(2)}, u32[]{:S(2)}) collective-permute-start(bf16[32,8192]{1,0:T(8,128)(2,1)S(1)} %get-tuple-element.75), channel_id=1, source_target_pairs={{0,32},{16,48},{32,0},{48,16},{64,96},{80,112},{96,64},{112,80},{1... | collective-permute-start | bytes 1572872 | tf_op jit(solution)/shard_map/ppermute | solution.py:412
  111.1 24.6 %collective-permute-start.16 = (bf16[32,8192]{1,0:T(8,128)(2,1)S(1)}, bf16[32,8192]{1,0:T(8,128)(2,1)S(1)}, u32[]{:S(2)}, u32[]{:S(2)}) collective-permute-start(bf16[32,8192]{1,0:T(8,128)(2,1)S(1)} %get-tuple-element.76), channel_id=1, source_target_pairs={{0,96},{16,112},{32,64},{48,80},{64,32},{80,48},{96,0},{112,16},{1... | collective-permute-start | bytes 1572872 | tf_op jit(solution)/shard_map/ppermute | solution.py:412

commit v9 on v7

--- a/solution.py
+++ b/solution.py
@@ -223,12 +223,13 @@
         unit = unit_ref[start + j]
         table = jnp.exp(mm(student, unit) * (1.0 / STUDENT_TEMP)).astype(BF16)
         table_ref[:, cols] = table
-        total += mm(jnp.ones((16, table.shape[1]), BF16), table, NT)
-        part = mm(unit, table, NT)
+        left = jnp.concatenate([unit, jnp.ones((16, unit.shape[1]), BF16)], axis=0)
+        part = mm(left, table, NT)
+        total += part[unit.shape[0] :]
         if j == 0:
-            feature_ref[...] = part
+            feature_ref[...] = part[: unit.shape[0]]
         else:
-            feature_ref[...] += part
+            feature_ref[...] += part[: unit.shape[0]]
     sums_ref[...] = total[0:8]
     for turned_ref in turned_refs:
         d = student.shape[1]

time: 137 us -> 137 us (level)
  Pallas kernels: 40.3 us -> 38.2 us
  waiting for transfers between devices: 11.1 us -> 12.6 us
    pallas_call x19, Pallas kernels: 40.3 us -> 38.2 us  [call(): pl.pallas_call(ordered, name=name, out_shape=out_shape, in_specs=[ANY] *...]
    ppermute x17, waiting for transfers between devices: 5.43 us -> 6.91 us  [hop(): return lax.ppermute(array, 'patch', [(i, i ^ bits) for i in range(n_patch)])]
  transfers between devices with their start and end apart: 18 -> 18, of which waited for: 7 -> 8; matrix products, arithmetic and copies ran while one was open for 0% -> 0% of each run, Pallas kernels for 11% -> 10%
where the time goes in v9:
time: 137 us
  blocking collectives  50.7 us (37%)
  Pallas kernels  38.2 us (28%)
  starting transfers between devices  34.1 us (25%)
  waiting for transfers between devices  12.6 us (9%)
    all_to_all x5, blocking collectives, exchange(): return lax.all_to_all(array, axis, 0, 0)  50.7 us
    pallas_call x19, Pallas kernels, call(): pl.pallas_call(ordered, name=name, out_shape=out_shape, in_specs=[ANY] *...  38.2 us
    ppermute x17, starting transfers between devices, hop(): return lax.ppermute(array, 'patch', [(i, i ^ bits) for i in range(n_patch)])  25.5 us
    all_to_all x1, starting transfers between devices, exchange(): return lax.all_to_all(array, axis, 0, 0)  8.61 us
    ppermute x17, waiting for transfers between devices, hop(): return lax.ppermute(array, 'patch', [(i, i ^ bits) for i in range(n_patch)])  6.91 us
    all_to_all x1, waiting for transfers between devices, exchange(): return lax.all_to_all(array, axis, 0, 0)  5.69 us
  transfers between devices with their start and end apart: 18, of which 8 were waited for; matrix products, arithmetic and copies ran while one was open for 0% of the time, Pallas kernels for 10%

profile of v9, /device:TPU:1, one launch (start us, length us, event | category | flops | bytes accessed | tf_op | source)
XLA Modules:
  0.0 136.5 jit_solution(14089223399389300501)
XLA Ops:
  0.6 0.1 pad_add_fusion.refs_0_.refs_1_
  0.7 2.7 %own_rows.1 = (bf16[16,64,256]{2,1,0:T(8,128)(2,1)}, f32[32,256]{1,0:T(8,128)S(1)}, f32[8,512]{1,0:T(8,128)S(1)}) custom-call(s32[3]{0:T(128)S(1)} %pad_add_fusion.refs_0_.refs_1_, bf16[256,256]{1,0:T(8,128)(2,1)} %refs_1_.1, bf16[256,256]{1,0:T(8,128)(2,1)} %refs_2_.1, s32[1,32]{1,0:T(1,128)} %bitcast.6, bf16[1,32]{1,0:T(2,128)(2,1)} %bitcast.7), custom_call_target="tpu_custom_call" | custom-call | flops 268435456 | bytes 65536 | tf_op jit(solution)/shard_map/own_rows/pallas_call | solution.py:54
  3.4 8.6 %all-to-all-start = ((bf16[16,64,256]{2,1,0:T(8,128)(2,1)}), bf16[16,64,256]{2,1,0:T(8,128)(2,1)S(1)}, u32[]{:S(2)}, u32[]{:S(2)}) async-start(bf16[16,64,256]{2,1,0:T(8,128)(2,1)} %get-tuple-element.41), calls=%async_computation | async-start | bytes 1048576 | tf_op jit(solution)/shard_map/all_to_all | solution.py:410
  12.0 4.8 %proto_unit.1 = (bf16[8,256,1024]{2,1,0:T(8,128)(2,1)}, bf16[2,256,1024]{2,1,0:T(8,128)(2,1)S(1)}, f32[8,1024]{1,0:T(8,128)S(1)}) custom-call(bf16[256,8192]{1,0:T(8,128)(2,1)} %refs_13_.1), custom_call_target="tpu_custom_call" | custom-call | flops 2147483648 | bytes 65536 | tf_op jit(solution)/shard_map/proto_unit/pallas_call | solution.py:54
  16.8 5.7 %all-to-all-done.refs_0_.refs_1_ = bf16[16,64,256]{2,1,0:T(8,128)(2,1)S(1)} async-done(((bf16[16,64,256]{2,1,0:T(8,128)(2,1)}), bf16[16,64,256]{2,1,0:T(8,128)(2,1)S(1)}, u32[]{:S(2)}, u32[]{:S(2)}) %all-to-all-start) | async-done | bytes 524320 | tf_op jit(solution)/shard_map/all_to_all | solution.py:410
  22.5 4.9 %teacher_table.1 = (bf16[512,8192]{1,0:T(8,128)(2,1)S(1)}, bf16[8,256,1024]{2,1,0:T(8,128)(2,1)S(1)}, f32[8,1024]{1,0:T(8,128)S(1)}) custom-call(bf16[16,64,256]{2,1,0:T(8,128)(2,1)S(1)} %all-to-all-done.refs_0_.refs_1_, bf16[2,256,1024]{2,1,0:T(8,128)(2,1)S(1)} %get-tuple-element.42.refs_1_, bf16[8,256,1024]{2,1,0:T(8,128)(2,1)} %get-tuple-element.43.refs_2_), custom_call_target="tpu_custom_call" | custom-call | flops 4294967296 | bytes 65536 | tf_op jit(solution)/shard_map/teacher_table/pallas_call | solution.py:54
  27.4 2.1 %collective-permute-start = (f32[8,1024]{1,0:T(8,128)S(1)}, f32[8,1024]{1,0:T(8,128)S(1)}, u32[]{:S(2)}, u32[]{:S(2)}) collective-permute-start(f32[8,1024]{1,0:T(8,128)S(1)} %get-tuple-element.44), channel_id=1, source_target_pairs={{0,16},{16,0},{32,48},{48,32},{64,80},{80,64},{96,112},{112,96},{1... | collective-permute-start | bytes 98312 | tf_op jit(solution)/shard_map/ppermute | solution.py:413
  29.4 0.9 collective-permute-done
  30.3 2.5 %collective-permute-start.3 = (f32[8,1024]{1,0:T(8,128)S(1)}, f32[8,1024]{1,0:T(8,128)S(1)}, u32[]{:S(2)}, u32[]{:S(2)}) collective-permute-start(f32[8,1024]{1,0:T(8,128)S(1)} %add.15.refs_0_.refs_1_), channel_id=1, source_target_pairs={{0,96},{16,112},{32,64},{48,80},{64,32},{80,48},{96,0},{112,16},{1... | collective-permute-start | bytes 98312 | tf_op jit(solution)/shard_map/ppermute | solution.py:413
  32.8 0.5 collective-permute-start.2
  33.3 0.3 collective-permute-start.1
  33.6 1.9 %student_table.3 = (bf16[512,3072]{1,0:T(8,128)(2,1)S(1)}, f32[8,512]{1,0:T(8,128)S(1)}, f32[256,512]{1,0:T(8,128)S(1)}) custom-call(f32[8,1024]{1,0:T(8,128)S(1)} %add.15.refs_0_.refs_1_, bf16[16,64,256]{2,1,0:T(8,128)(2,1)S(1)} %all-to-all-done.refs_0_.refs_1_, bf16[8,256,1024]{2,1,0:T(8,128)(2,1)S(1)} %get-tuple-element.45.refs_2_.refs_5_), custom_call_target="tpu_custom_call" | custom-call | flops 2147483648 | bytes 65536 | tf_op jit(solution)/shard_map/student_table/pallas_call | solution.py:54
  35.5 0.0 collective-permute-done.3.refs_4_
  35.5 1.6 %collective-permute-done.2.refs_3_ = f32[8,1024]{1,0:T(8,128)S(1)} collective-permute-done((f32[8,1024]{1,0:T(8,128)S(1)}, f32[8,1024]{1,0:T(8,128)S(1)}, u32[]{:S(2)}, u32[]{:S(2)}) %collective-permute-start.2) | collective-permute-done | bytes 32800 | tf_op jit(solution)/shard_map/ppermute | solution.py:413
  37.0 0.0 collective-permute-done.1.refs_2_
  37.1 2.3 %row_pass.2 = f32[16,8,128]{2,1,0:T(8,128)S(1)} custom-call(f32[8,512]{1,0:T(8,128)S(1)} %get-tuple-element.46.refs_0_.refs_6_, f32[8,1024]{1,0:T(8,128)S(1)} %add.15.refs_0_.refs_1_, f32[8,1024]{1,0:T(8,128)S(1)} %collective-permute-done.1.refs_2_, f32[8,1024]{1,0:T(8,128)S(1)} %collective-permute-done.2.refs_3_, ...), custom_call_target="tpu_custom_call" | custom-call | flops 2147483648 | bytes 65536 | tf_op jit(solution)/shard_map/row_pass/pallas_call | solution.py:54
  39.4 9.2 %all_to_all.30.refs_0_.refs_1_ = f32[16,8,128]{2,1,0:T(8,128)S(1)} all-to-all(f32[16,8,128]{2,1,0:T(8,128)S(1)} %row_pass.2), channel_id=1, replica_groups=mesh['patch'=8,'proto'=16] {'proto'}, dimensions={0} | all-to-all | bytes 131072 | tf_op jit(solution)/shard_map/all_to_all | solution.py:410
  48.5 1.2 col_pass.2
  49.8 3.5 %collective-permute-start.4 = (f32[8,1024]{1,0:T(8,128)S(1)}, f32[8,1024]{1,0:T(8,128)S(1)}, u32[]{:S(2)}, u32[]{:S(2)}) collective-permute-start(f32[8,1024]{1,0:T(8,128)S(1)} %col_pass.2), channel_id=1, source_target_pairs={{0,16},{16,0},{32,48},{48,32},{64,80},{80,64},{96,112},{112,96},{1... | collective-permute-start | bytes 98312 | tf_op jit(solution)/shard_map/ppermute | solution.py:413
  53.2 0.9 collective-permute-done.4
  54.1 1.1 collective-permute-start.7
  55.2 0.8 collective-permute-start.6
  56.0 1.3 collective-permute-start.5
  57.4 1.9 %student_table.4 = (bf16[512,3072]{1,0:T(8,128)(2,1)S(1)}, f32[8,512]{1,0:T(8,128)S(1)}, f32[256,512]{1,0:T(8,128)S(1)}) custom-call(f32[8,1024]{1,0:T(8,128)S(1)} %add.16.refs_0_.refs_1_, bf16[16,64,256]{2,1,0:T(8,128)(2,1)S(1)} %all-to-all-done.refs_0_.refs_1_, bf16[8,256,1024]{2,1,0:T(8,128)(2,1)S(1)} %get-tuple-element.45.refs_2_.refs_5_), custom_call_target="tpu_custom_call" | custom-call | flops 2147483648 | bytes 65536 | tf_op jit(solution)/shard_map/student_table/pallas_call | solution.py:54
  59.3 0.0 collective-permute-done.7.refs_4_
  59.3 0.2 collective-permute-done.6.refs_3_
  59.5 0.0 collective-permute-done.5.refs_2_
  59.5 2.3 %row_pass.3 = f32[16,8,128]{2,1,0:T(8,128)S(1)} custom-call(f32[8,512]{1,0:T(8,128)S(1)} %get-tuple-element.49.refs_0_.refs_7_, f32[8,1024]{1,0:T(8,128)S(1)} %add.16.refs_0_.refs_1_, f32[8,1024]{1,0:T(8,128)S(1)} %collective-permute-done.5.refs_2_, f32[8,1024]{1,0:T(8,128)S(1)} %collective-permute-done.6.refs_3_, ...), custom_call_target="tpu_custom_call" | custom-call | flops 2147483648 | bytes 65536 | tf_op jit(solution)/shard_map/row_pass/pallas_call | solution.py:54
  61.8 9.4 %all_to_all.31.refs_0_ = f32[16,8,128]{2,1,0:T(8,128)S(1)} all-to-all(f32[16,8,128]{2,1,0:T(8,128)S(1)} %row_pass.3), channel_id=1, replica_groups=mesh['patch'=8,'proto'=16] {'proto'}, dimensions={0} | all-to-all | bytes 131072 | tf_op jit(solution)/shard_map/all_to_all | solution.py:410
  71.2 1.2 col_pass.3
  72.4 3.5 %collective-permute-start.8 = (f32[8,1024]{1,0:T(8,128)S(1)}, f32[8,1024]{1,0:T(8,128)S(1)}, u32[]{:S(2)}, u32[]{:S(2)}) collective-permute-start(f32[8,1024]{1,0:T(8,128)S(1)} %col_pass.3), channel_id=1, source_target_pairs={{0,16},{16,0},{32,48},{48,32},{64,80},{80,64},{96,112},{112,96},{1... | collective-permute-start | bytes 98312 | tf_op jit(solution)/shard_map/ppermute | solution.py:413
  75.9 0.9 collective-permute-done.8
  76.7 1.4 %collective-permute-start.11 = (f32[8,1024]{1,0:T(8,128)S(1)}, f32[8,1024]{1,0:T(8,128)S(1)}, u32[]{:S(2)}, u32[]{:S(2)}) collective-permute-start(f32[8,1024]{1,0:T(8,128)S(1)} %add.17.refs_0_.refs_3_.refs_4_), channel_id=1, source_target_pairs={{0,96},{16,112},{32,64},{48,80},{64,32},{80,48},{96,0},{112,16},{1... | collective-permute-start | bytes 98312 | tf_op jit(solution)/shard_map/ppermute | solution.py:413
  78.1 1.1 collective-permute-start.10
  79.3 0.7 collective-permute-start.9
  80.0 1.4 %student_table.5 = (bf16[512,2048]{1,0:T(8,128)(2,1)S(1)}, f32[8,512]{1,0:T(8,128)S(1)}, f32[256,512]{1,0:T(8,128)S(1)}, bf16[256,512]{1,0:T(8,128)(2,1)S(1)}) custom-call(f32[8,1024]{1,0:T(8,128)S(1)} %add.17.refs_0_.refs_3_.refs_4_, bf16[16,64,256]{2,1,0:T(8,128)(2,1)S(1)} %all-to-all-done.refs_0_.refs_1_, ...), custom_call_target="tpu_custom_call" | custom-call | flops 2147483648 | bytes 65536 | tf_op jit(solution)/shard_map/student_table/pallas_call | solution.py:54
  81.4 0.0 collective-permute-done.11.refs_3_.refs_6_.refs_7_
  81.4 1.0 collective-permute-done.10.refs_2_.refs_5_.refs_6_
  82.4 0.0 collective-permute-done.9.refs_1_.refs_4_.refs_5_
  82.4 0.0 copy-start
  82.4 2.5 %last_row_pass.1 = (f32[16,8,128]{2,1,0:T(8,128)S(1)}, f32[256,512]{1,0:T(8,128)S(1)}) custom-call(f32[8,1024]{1,0:T(8,128)S(1)} %add.17.refs_0_.refs_3_.refs_4_, f32[8,1024]{1,0:T(8,128)S(1)} %collective-permute-done.9.refs_1_.refs_4_.refs_5_, f32[8,1024]{1,0:T(8,128)S(1)} %collective-permute-done.10.refs_2_.refs_5_.refs_6_, ...), custom_call_target="tpu_custom_call" | custom-call | flops 2147483648 | bytes 65536 | tf_op jit(solution)/shard_map/last_row_pass/pallas_call | solution.py:54
  84.9 9.4 %all_to_all.32.refs_2_ = f32[16,8,128]{2,1,0:T(8,128)S(1)} all-to-all(f32[16,8,128]{2,1,0:T(8,128)S(1)} %get-tuple-element.51), channel_id=1, replica_groups=mesh['patch'=8,'proto'=16] {'proto'}, dimensions={0} | all-to-all | bytes 131072 | tf_op jit(solution)/shard_map/all_to_all | solution.py:410
  94.3 0.7 row_factors.1
  95.0 0.0 copy-done
  95.0 5.3 %head.2 = (f32[32,6144]{1,0:T(8,128)S(1)}, bf16[3,32,6144]{2,1,0:T(8,128)(2,1)S(1)}, bf16[4,32,6144]{2,1,0:T(8,128)(2,1)S(1)}) custom-call(s32[3]{0:T(128)S(1)} %pad_add_fusion.refs_0_.refs_1_, bf16[256,512]{1,0:T(8,128)(2,1)S(1)} %get-tuple-element.53.refs_1_.refs_2_, bf16[256,512]{1,0:T(8,128)(2,1)S(1)} %get-tuple-element.54.refs_2_.refs_3_, ...), custom_call_target="tpu_custom_call" | custom-call | flops 4294967296 | bytes 65536 | tf_op jit(solution)/shard_map/head/pallas_call | solution.py:54
  100.3 3.3 %collective-permute-start.12 = (bf16[4,32,6144]{2,1,0:T(8,128)(2,1)S(1)}, bf16[4,32,6144]{2,1,0:T(8,128)(2,1)S(1)}, u32[]{:S(2)}, u32[]{:S(2)}) collective-permute-start(bf16[4,32,6144]{2,1,0:T(8,128)(2,1)S(1)} %get-tuple-element.69), channel_id=1, source_target_pairs={{0,16},{16,0},{32,48},{48,32},{64,80},{80,64},{96,112},{112,96},{1... | collective-permute-start | bytes 4718600 | tf_op jit(solution)/shard_map/ppermute | solution.py:413
  103.6 2.2 %head.3 = (f32[32,2048]{1,0:T(8,128)S(1)}, bf16[3,32,2048]{2,1,0:T(8,128)(2,1)S(1)}, bf16[4,32,2048]{2,1,0:T(8,128)(2,1)S(1)}) custom-call(bf16[3,32,6144]{2,1,0:T(8,128)(2,1)S(1)} %get-tuple-element.59.refs_0_.refs_1_, s32[3]{0:T(128)S(1)} %pad_add_fusion.refs_0_.refs_1_, bf16[256,512]{1,0:T(8,128)(2,1)S(1)} %get-tuple-element.53.refs_1_.refs_2_, ...), custom_call_target="tpu_custom_call" | custom-call | flops 4294967296 | bytes 65536 | tf_op jit(solution)/shard_map/head/pallas_call | solution.py:54
  105.8 0.1 collective-permute-start.13
  105.9 0.3 feature.1.refs_0_
  106.2 1.6 %collective-permute-done.13.refs_4_ = bf16[4,32,2048]{2,1,0:T(8,128)(2,1)S(1)} collective-permute-done((bf16[4,32,2048]{2,1,0:T(8,128)(2,1)S(1)}, bf16[4,32,2048]{2,1,0:T(8,128)(2,1)S(1)}, u32[]{:S(2)}, u32[]{:S(2)}) %collective-permute-start.13) | collective-permute-done | bytes 524320 | tf_op jit(solution)/shard_map/ppermute | solution.py:413
  107.8 0.0 collective-permute-done.12.refs_2_
  107.8 0.4 pair_sums.1
  108.2 1.8 %collective-permute-start.14 = (bf16[32,8192]{1,0:T(8,128)(2,1)S(1)}, bf16[32,8192]{1,0:T(8,128)(2,1)S(1)}, u32[]{:S(2)}, u32[]{:S(2)}) collective-permute-start(bf16[32,8192]{1,0:T(8,128)(2,1)S(1)} %get-tuple-element.74), channel_id=1, source_target_pairs={{0,64},{16,80},{32,96},{48,112},{64,0},{80,16},{96,32},{112,48},{1... | collective-permute-start | bytes 1572872 | tf_op jit(solution)/shard_map/ppermute | solution.py:413
  110.0 0.1 collective-permute-start.15
  110.1 1.4 %collective-permute-start.16 = (bf16[32,8192]{1,0:T(8,128)(2,1)S(1)}, bf16[32,8192]{1,0:T(8,128)(2,1)S(1)}, u32[]{:S(2)}, u32[]{:S(2)}) collective-permute-start(bf16[32,8192]{1,0:T(8,128)(2,1)S(1)} %get-tuple-element.76), channel_id=1, source_target_pairs={{0,96},{16,112},{32,64},{48,80},{64,32},{80,48},{96,0},{112,16},{1... | collective-permute-start | bytes 1572872 | tf_op jit(solution)/shard_map/ppermute | solution.py:413
  111.5 11.7 %all_to_all.33.refs_0_ = bf16[16,48,256]{2,1,0:T(8,128)(2,1)S(1)} all-to-all(bf16[16,48,256]{2,1,0:T(8,128)(2,1)S(1)} %feature.1.refs_0_), channel_id=1, replica_groups=mesh['patch'=8,'proto'=16] {'proto'}, dimensions={0} | all-to-all | bytes 786432 | tf_op jit(solution)/shard_map/all_to_all | solution.py:410
  123.2 0.8 owner.1
  124.0 0.1 own_sum.1
  124.1 11.1 %all_to_all.34.refs_1_ = f32[8,8,128]{2,1,0:T(8,128)S(1)} all-to-all(f32[8,8,128]{2,1,0:T(8,128)S(1)} %get-tuple-element.73), channel_id=1, replica_groups=mesh['patch'=8,'proto'=16] {'patch'}, dimensions={0} | all-to-all | bytes 65536 | tf_op jit(solution)/shard_map/all_to_all | solution.py:410
  135.2 0.0 collective-permute-done.14.refs_2_
  135.2 0.0 collective-permute-done.15.refs_3_
  135.2 0.0 collective-permute-done.16.refs_4_
  135.2 1.3 assemble.1
  (3 shorter events, 0.0 us)
Async XLA Ops:
  3.4 19.1 %all-to-all-start = ((bf16[16,64,256]{2,1,0:T(8,128)(2,1)}), bf16[16,64,256]{2,1,0:T(8,128)(2,1)S(1)}, u32[]{:S(2)}, u32[]{:S(2)}) async-start(bf16[16,64,256]{2,1,0:T(8,128)(2,1)} %get-tuple-element.41), calls=%async_computation | async-start | bytes 1048576 | tf_op jit(solution)/shard_map/all_to_all | solution.py:410
  27.4 2.9 %collective-permute-start = (f32[8,1024]{1,0:T(8,128)S(1)}, f32[8,1024]{1,0:T(8,128)S(1)}, u32[]{:S(2)}, u32[]{:S(2)}) collective-permute-start(f32[8,1024]{1,0:T(8,128)S(1)} %get-tuple-element.44), channel_id=1, source_target_pairs={{0,16},{16,0},{32,48},{48,32},{64,80},{80,64},{96,112},{112,96},{1... | collective-permute-start | bytes 98312 | tf_op jit(solution)/shard_map/ppermute | solution.py:413
  30.3 5.2 %collective-permute-start.3 = (f32[8,1024]{1,0:T(8,128)S(1)}, f32[8,1024]{1,0:T(8,128)S(1)}, u32[]{:S(2)}, u32[]{:S(2)}) collective-permute-start(f32[8,1024]{1,0:T(8,128)S(1)} %add.15.refs_0_.refs_1_), channel_id=1, source_target_pairs={{0,96},{16,112},{32,64},{48,80},{64,32},{80,48},{96,0},{112,16},{1... | collective-permute-start | bytes 98312 | tf_op jit(solution)/shard_map/ppermute | solution.py:413
  32.8 4.3 %collective-permute-start.2 = (f32[8,1024]{1,0:T(8,128)S(1)}, f32[8,1024]{1,0:T(8,128)S(1)}, u32[]{:S(2)}, u32[]{:S(2)}) collective-permute-start(f32[8,1024]{1,0:T(8,128)S(1)} %add.15.refs_0_.refs_1_), channel_id=1, source_target_pairs={{0,64},{16,80},{32,96},{48,112},{64,0},{80,16},{96,32},{112,48},{1... | collective-permute-start | bytes 98312 | tf_op jit(solution)/shard_map/ppermute | solution.py:413
  33.3 3.7 %collective-permute-start.1 = (f32[8,1024]{1,0:T(8,128)S(1)}, f32[8,1024]{1,0:T(8,128)S(1)}, u32[]{:S(2)}, u32[]{:S(2)}) collective-permute-start(f32[8,1024]{1,0:T(8,128)S(1)} %add.15.refs_0_.refs_1_), channel_id=1, source_target_pairs={{0,32},{16,48},{32,0},{48,16},{64,96},{80,112},{96,64},{112,80},{1... | collective-permute-start | bytes 98312 | tf_op jit(solution)/shard_map/ppermute | solution.py:413
  49.8 4.3 %collective-permute-start.4 = (f32[8,1024]{1,0:T(8,128)S(1)}, f32[8,1024]{1,0:T(8,128)S(1)}, u32[]{:S(2)}, u32[]{:S(2)}) collective-permute-start(f32[8,1024]{1,0:T(8,128)S(1)} %col_pass.2), channel_id=1, source_target_pairs={{0,16},{16,0},{32,48},{48,32},{64,80},{80,64},{96,112},{112,96},{1... | collective-permute-start | bytes 98312 | tf_op jit(solution)/shard_map/ppermute | solution.py:413
  54.1 5.2 %collective-permute-start.7 = (f32[8,1024]{1,0:T(8,128)S(1)}, f32[8,1024]{1,0:T(8,128)S(1)}, u32[]{:S(2)}, u32[]{:S(2)}) collective-permute-start(f32[8,1024]{1,0:T(8,128)S(1)} %add.16.refs_0_.refs_1_), channel_id=1, source_target_pairs={{0,96},{16,112},{32,64},{48,80},{64,32},{80,48},{96,0},{112,16},{1... | collective-permute-start | bytes 98312 | tf_op jit(solution)/shard_map/ppermute | solution.py:413
  55.2 4.3 %collective-permute-start.6 = (f32[8,1024]{1,0:T(8,128)S(1)}, f32[8,1024]{1,0:T(8,128)S(1)}, u32[]{:S(2)}, u32[]{:S(2)}) collective-permute-start(f32[8,1024]{1,0:T(8,128)S(1)} %add.16.refs_0_.refs_1_), channel_id=1, source_target_pairs={{0,64},{16,80},{32,96},{48,112},{64,0},{80,16},{96,32},{112,48},{1... | collective-permute-start | bytes 98312 | tf_op jit(solution)/shard_map/ppermute | solution.py:413
  56.0 3.5 %collective-permute-start.5 = (f32[8,1024]{1,0:T(8,128)S(1)}, f32[8,1024]{1,0:T(8,128)S(1)}, u32[]{:S(2)}, u32[]{:S(2)}) collective-permute-start(f32[8,1024]{1,0:T(8,128)S(1)} %add.16.refs_0_.refs_1_), channel_id=1, source_target_pairs={{0,32},{16,48},{32,0},{48,16},{64,96},{80,112},{96,64},{112,80},{1... | collective-permute-start | bytes 98312 | tf_op jit(solution)/shard_map/ppermute | solution.py:413
  72.4 4.3 %collective-permute-start.8 = (f32[8,1024]{1,0:T(8,128)S(1)}, f32[8,1024]{1,0:T(8,128)S(1)}, u32[]{:S(2)}, u32[]{:S(2)}) collective-permute-start(f32[8,1024]{1,0:T(8,128)S(1)} %col_pass.3), channel_id=1, source_target_pairs={{0,16},{16,0},{32,48},{48,32},{64,80},{80,64},{96,112},{112,96},{1... | collective-permute-start | bytes 98312 | tf_op jit(solution)/shard_map/ppermute | solution.py:413
  76.7 4.7 %collective-permute-start.11 = (f32[8,1024]{1,0:T(8,128)S(1)}, f32[8,1024]{1,0:T(8,128)S(1)}, u32[]{:S(2)}, u32[]{:S(2)}) collective-permute-start(f32[8,1024]{1,0:T(8,128)S(1)} %add.17.refs_0_.refs_3_.refs_4_), channel_id=1, source_target_pairs={{0,96},{16,112},{32,64},{48,80},{64,32},{80,48},{96,0},{112,16},{1... | collective-permute-start | bytes 98312 | tf_op jit(solution)/shard_map/ppermute | solution.py:413
  78.1 4.3 %collective-permute-start.10 = (f32[8,1024]{1,0:T(8,128)S(1)}, f32[8,1024]{1,0:T(8,128)S(1)}, u32[]{:S(2)}, u32[]{:S(2)}) collective-permute-start(f32[8,1024]{1,0:T(8,128)S(1)} %add.17.refs_0_.refs_3_.refs_4_), channel_id=1, source_target_pairs={{0,64},{16,80},{32,96},{48,112},{64,0},{80,16},{96,32},{112,48},{1... | collective-permute-start | bytes 98312 | tf_op jit(solution)/shard_map/ppermute | solution.py:413
  79.3 3.1 %collective-permute-start.9 = (f32[8,1024]{1,0:T(8,128)S(1)}, f32[8,1024]{1,0:T(8,128)S(1)}, u32[]{:S(2)}, u32[]{:S(2)}) collective-permute-start(f32[8,1024]{1,0:T(8,128)S(1)} %add.17.refs_0_.refs_3_.refs_4_), channel_id=1, source_target_pairs={{0,32},{16,48},{32,0},{48,16},{64,96},{80,112},{96,64},{112,80},{1... | collective-permute-start | bytes 98312 | tf_op jit(solution)/shard_map/ppermute | solution.py:413
  82.4 12.6 %copy-start = (bf16[256,8192]{1,0:T(8,128)(2,1)S(1)}, bf16[256,8192]{1,0:T(8,128)(2,1)}, u32[]{:S(2)}) copy-start(bf16[256,8192]{1,0:T(8,128)(2,1)} %refs_13_.1) | copy-start | bytes 12582916
  100.3 7.5 %collective-permute-start.12 = (bf16[4,32,6144]{2,1,0:T(8,128)(2,1)S(1)}, bf16[4,32,6144]{2,1,0:T(8,128)(2,1)S(1)}, u32[]{:S(2)}, u32[]{:S(2)}) collective-permute-start(bf16[4,32,6144]{2,1,0:T(8,128)(2,1)S(1)} %get-tuple-element.69), channel_id=1, source_target_pairs={{0,16},{16,0},{32,48},{48,32},{64,80},{80,64},{96,112},{112,96},{1... | collective-permute-start | bytes 4718600 | tf_op jit(solution)/shard_map/ppermute | solution.py:413
  105.8 2.0 %collective-permute-start.13 = (bf16[4,32,2048]{2,1,0:T(8,128)(2,1)S(1)}, bf16[4,32,2048]{2,1,0:T(8,128)(2,1)S(1)}, u32[]{:S(2)}, u32[]{:S(2)}) collective-permute-start(bf16[4,32,2048]{2,1,0:T(8,128)(2,1)S(1)} %get-tuple-element.71), channel_id=1, source_target_pairs={{0,16},{16,0},{32,48},{48,32},{64,80},{80,64},{96,112},{112,96},{1... | collective-permute-start | bytes 1572872 | tf_op jit(solution)/shard_map/ppermute | solution.py:413
  108.2 27.0 %collective-permute-start.14 = (bf16[32,8192]{1,0:T(8,128)(2,1)S(1)}, bf16[32,8192]{1,0:T(8,128)(2,1)S(1)}, u32[]{:S(2)}, u32[]{:S(2)}) collective-permute-start(bf16[32,8192]{1,0:T(8,128)(2,1)S(1)} %get-tuple-element.74), channel_id=1, source_target_pairs={{0,64},{16,80},{32,96},{48,112},{64,0},{80,16},{96,32},{112,48},{1... | collective-permute-start | bytes 1572872 | tf_op jit(solution)/shard_map/ppermute | solution.py:413
  110.0 25.2 %collective-permute-start.15 = (bf16[32,8192]{1,0:T(8,128)(2,1)S(1)}, bf16[32,8192]{1,0:T(8,128)(2,1)S(1)}, u32[]{:S(2)}, u32[]{:S(2)}) collective-permute-start(bf16[32,8192]{1,0:T(8,128)(2,1)S(1)} %get-tuple-element.75), channel_id=1, source_target_pairs={{0,32},{16,48},{32,0},{48,16},{64,96},{80,112},{96,64},{112,80},{1... | collective-permute-start | bytes 1572872 | tf_op jit(solution)/shard_map/ppermute | solution.py:413
  110.1 25.0 %collective-permute-start.16 = (bf16[32,8192]{1,0:T(8,128)(2,1)S(1)}, bf16[32,8192]{1,0:T(8,128)(2,1)S(1)}, u32[]{:S(2)}, u32[]{:S(2)}) collective-permute-start(bf16[32,8192]{1,0:T(8,128)(2,1)S(1)} %get-tuple-element.76), channel_id=1, source_target_pairs={{0,96},{16,112},{32,64},{48,80},{64,32},{80,48},{96,0},{112,16},{1... | collective-permute-start | bytes 1572872 | tf_op jit(solution)/shard_map/ppermute | solution.py:413

commit v10 on v7

--- a/solution.py
+++ b/solution.py
@@ -15,7 +15,7 @@
 BF16 = jnp.bfloat16
 LANES = 128
 PIECES = (3, 3, 2)
-FIRST = 2
+FIRST = 4
 PARTS = (6, 2)
 VMEM_LIMIT = 20 * 1024 * 1024
 

time: 137 us -> 138 us (level)
  local copies, waits for them, and re-layouts: 0.01 us -> 2.96 us
    unnamed x2 -> x6, local copies, waits for them, and re-layouts: 0.01 us -> 2.96 us
    all_to_all x1, waiting for transfers between devices: 5.69 us -> 4.3 us  [exchange(): return lax.all_to_all(array, axis, 0, 0)]
where the time goes in v10:
time: 138 us
  blocking collectives  50.7 us (37%)
  Pallas kernels  40.3 us (29%)
  starting transfers between devices  33.3 us (24%)
  waiting for transfers between devices  9.73 us (7%)
  local copies, waits for them, and re-layouts  2.96 us (2%)
    all_to_all x5, blocking collectives, exchange(): return lax.all_to_all(array, axis, 0, 0)  50.7 us
    pallas_call x19, Pallas kernels, call(): pl.pallas_call(ordered, name=name, out_shape=out_shape, in_specs=[ANY] *...  40.3 us
    ppermute x17, starting transfers between devices, hop(): return lax.ppermute(array, 'patch', [(i, i ^ bits) for i in range(n_patch)])  24.7 us
    all_to_all x1, starting transfers between devices, exchange(): return lax.all_to_all(array, axis, 0, 0)  8.61 us
    ppermute x17, waiting for transfers between devices, hop(): return lax.ppermute(array, 'patch', [(i, i ^ bits) for i in range(n_patch)])  5.43 us
    all_to_all x1, waiting for transfers between devices, exchange(): return lax.all_to_all(array, axis, 0, 0)  4.3 us
    unnamed x6, local copies, waits for them, and re-layouts  2.96 us
  transfers between devices with their start and end apart: 18, of which 7 were waited for; matrix products, arithmetic and copies ran while one was open for 0% of the time, Pallas kernels for 11%

profile of v10, /device:TPU:1, one launch (start us, length us, event | category | flops | bytes accessed | tf_op | source)
XLA Modules:
  0.0 137.9 jit_solution(8623092340023630598)
XLA Ops:
  0.6 0.1 pad_add_fusion.refs_0_.refs_1_
  0.7 2.7 %own_rows.1 = (bf16[16,64,256]{2,1,0:T(8,128)(2,1)}, f32[32,256]{1,0:T(8,128)S(1)}, f32[8,512]{1,0:T(8,128)S(1)}) custom-call(s32[3]{0:T(128)S(1)} %pad_add_fusion.refs_0_.refs_1_, bf16[256,256]{1,0:T(8,128)(2,1)} %refs_1_.1, bf16[256,256]{1,0:T(8,128)(2,1)} %refs_2_.1, s32[1,32]{1,0:T(1,128)} %bitcast.6, bf16[1,32]{1,0:T(2,128)(2,1)} %bitcast.7), custom_call_target="tpu_custom_call" | custom-call | flops 268435456 | bytes 65536 | tf_op jit(solution)/shard_map/own_rows/pallas_call | solution.py:54
  3.4 8.6 %all-to-all-start = ((bf16[16,64,256]{2,1,0:T(8,128)(2,1)}), bf16[16,64,256]{2,1,0:T(8,128)(2,1)S(1)}, u32[]{:S(2)}, u32[]{:S(2)}) async-start(bf16[16,64,256]{2,1,0:T(8,128)(2,1)} %get-tuple-element.41), calls=%async_computation | async-start | bytes 1048576 | tf_op jit(solution)/shard_map/all_to_all | solution.py:409
  12.0 4.8 %proto_unit.1 = (bf16[8,256,1024]{2,1,0:T(8,128)(2,1)}, bf16[4,256,1024]{2,1,0:T(8,128)(2,1)S(1)}, f32[8,1024]{1,0:T(8,128)S(1)}) custom-call(bf16[256,8192]{1,0:T(8,128)(2,1)} %refs_13_.1), custom_call_target="tpu_custom_call" | custom-call | flops 2147483648 | bytes 65536 | tf_op jit(solution)/shard_map/proto_unit/pallas_call | solution.py:54
  16.9 1.4 copy-done.1
  18.2 4.3 %all-to-all-done.refs_0_.refs_1_ = bf16[16,64,256]{2,1,0:T(8,128)(2,1)S(1)} async-done(((bf16[16,64,256]{2,1,0:T(8,128)(2,1)}), bf16[16,64,256]{2,1,0:T(8,128)(2,1)S(1)}, u32[]{:S(2)}, u32[]{:S(2)}) %all-to-all-start) | async-done | bytes 524320 | tf_op jit(solution)/shard_map/all_to_all | solution.py:409
  22.5 1.6 %copy-done.2 = bf16[4,256,1024]{2,1,0:T(8,128)(2,1)S(1)} copy-done((bf16[4,256,1024]{2,1,0:T(8,128)(2,1)S(1)}, bf16[4,256,1024]{2,1,0:T(8,128)(2,1)}, u32[]{:S(2)}) %copy-start.2) | copy-done | bytes 2097176
  24.1 4.7 %teacher_table.1 = (bf16[512,8192]{1,0:T(8,128)(2,1)S(1)}, bf16[8,256,1024]{2,1,0:T(8,128)(2,1)S(1)}, f32[8,1024]{1,0:T(8,128)S(1)}) custom-call(bf16[16,64,256]{2,1,0:T(8,128)(2,1)S(1)} %all-to-all-done.refs_0_.refs_1_, bf16[4,256,1024]{2,1,0:T(8,128)(2,1)S(1)} %copy-done.2, bf16[8,256,1024]{2,1,0:T(8,128)(2,1)} %get-tuple-element.43.refs_2_), custom_call_target="tpu_custom_call" | custom-call | flops 4294967296 | bytes 65536 | tf_op jit(solution)/shard_map/teacher_table/pallas_call | solution.py:54
  28.8 2.1 %collective-permute-start = (f32[8,1024]{1,0:T(8,128)S(1)}, f32[8,1024]{1,0:T(8,128)S(1)}, u32[]{:S(2)}, u32[]{:S(2)}) collective-permute-start(f32[8,1024]{1,0:T(8,128)S(1)} %get-tuple-element.44), channel_id=1, source_target_pairs={{0,16},{16,0},{32,48},{48,32},{64,80},{80,64},{96,112},{112,96},{1... | collective-permute-start | bytes 98312 | tf_op jit(solution)/shard_map/ppermute | solution.py:412
  30.8 0.9 collective-permute-done
  31.7 2.5 %collective-permute-start.3 = (f32[8,1024]{1,0:T(8,128)S(1)}, f32[8,1024]{1,0:T(8,128)S(1)}, u32[]{:S(2)}, u32[]{:S(2)}) collective-permute-start(f32[8,1024]{1,0:T(8,128)S(1)} %add.15.refs_0_.refs_1_), channel_id=1, source_target_pairs={{0,96},{16,112},{32,64},{48,80},{64,32},{80,48},{96,0},{112,16},{1... | collective-permute-start | bytes 98312 | tf_op jit(solution)/shard_map/ppermute | solution.py:412
  34.2 0.5 collective-permute-start.2
  34.7 0.3 collective-permute-start.1
  35.0 2.7 %student_table.3 = (bf16[512,3072]{1,0:T(8,128)(2,1)S(1)}, f32[8,512]{1,0:T(8,128)S(1)}, f32[256,512]{1,0:T(8,128)S(1)}) custom-call(f32[8,1024]{1,0:T(8,128)S(1)} %add.15.refs_0_.refs_1_, bf16[16,64,256]{2,1,0:T(8,128)(2,1)S(1)} %all-to-all-done.refs_0_.refs_1_, bf16[8,256,1024]{2,1,0:T(8,128)(2,1)S(1)} %get-tuple-element.45.refs_2_.refs_5_), custom_call_target="tpu_custom_call" | custom-call | flops 2147483648 | bytes 65536 | tf_op jit(solution)/shard_map/student_table/pallas_call | solution.py:54
  37.6 0.0 collective-permute-done.3.refs_4_
  37.7 0.8 collective-permute-done.2.refs_3_
  38.5 0.0 collective-permute-done.1.refs_2_
  38.5 2.3 %row_pass.2 = f32[16,8,128]{2,1,0:T(8,128)S(1)} custom-call(f32[8,512]{1,0:T(8,128)S(1)} %get-tuple-element.46.refs_0_.refs_6_, f32[8,1024]{1,0:T(8,128)S(1)} %add.15.refs_0_.refs_1_, f32[8,1024]{1,0:T(8,128)S(1)} %collective-permute-done.1.refs_2_, f32[8,1024]{1,0:T(8,128)S(1)} %collective-permute-done.2.refs_3_, ...), custom_call_target="tpu_custom_call" | custom-call | flops 2147483648 | bytes 65536 | tf_op jit(solution)/shard_map/row_pass/pallas_call | solution.py:54
  40.8 9.2 %all_to_all.30.refs_0_.refs_1_ = f32[16,8,128]{2,1,0:T(8,128)S(1)} all-to-all(f32[16,8,128]{2,1,0:T(8,128)S(1)} %row_pass.2), channel_id=1, replica_groups=mesh['patch'=8,'proto'=16] {'proto'}, dimensions={0} | all-to-all | bytes 131072 | tf_op jit(solution)/shard_map/all_to_all | solution.py:409
  50.0 1.2 col_pass.2
  51.2 3.3 %collective-permute-start.4 = (f32[8,1024]{1,0:T(8,128)S(1)}, f32[8,1024]{1,0:T(8,128)S(1)}, u32[]{:S(2)}, u32[]{:S(2)}) collective-permute-start(f32[8,1024]{1,0:T(8,128)S(1)} %col_pass.2), channel_id=1, source_target_pairs={{0,16},{16,0},{32,48},{48,32},{64,80},{80,64},{96,112},{112,96},{1... | collective-permute-start | bytes 98312 | tf_op jit(solution)/shard_map/ppermute | solution.py:412
  54.5 0.9 collective-permute-done.4
  55.3 1.1 collective-permute-start.7
  56.4 0.8 collective-permute-start.6
  57.3 1.3 collective-permute-start.5
  58.6 2.7 %student_table.4 = (bf16[512,3072]{1,0:T(8,128)(2,1)S(1)}, f32[8,512]{1,0:T(8,128)S(1)}, f32[256,512]{1,0:T(8,128)S(1)}) custom-call(f32[8,1024]{1,0:T(8,128)S(1)} %add.16.refs_0_.refs_1_, bf16[16,64,256]{2,1,0:T(8,128)(2,1)S(1)} %all-to-all-done.refs_0_.refs_1_, bf16[8,256,1024]{2,1,0:T(8,128)(2,1)S(1)} %get-tuple-element.45.refs_2_.refs_5_), custom_call_target="tpu_custom_call" | custom-call | flops 2147483648 | bytes 65536 | tf_op jit(solution)/shard_map/student_table/pallas_call | solution.py:54
  61.3 0.0 collective-permute-done.7.refs_4_
  61.3 0.0 collective-permute-done.6.refs_3_
  61.3 0.0 collective-permute-done.5.refs_2_
  61.3 2.3 %row_pass.3 = f32[16,8,128]{2,1,0:T(8,128)S(1)} custom-call(f32[8,512]{1,0:T(8,128)S(1)} %get-tuple-element.49.refs_0_.refs_7_, f32[8,1024]{1,0:T(8,128)S(1)} %add.16.refs_0_.refs_1_, f32[8,1024]{1,0:T(8,128)S(1)} %collective-permute-done.5.refs_2_, f32[8,1024]{1,0:T(8,128)S(1)} %collective-permute-done.6.refs_3_, ...), custom_call_target="tpu_custom_call" | custom-call | flops 2147483648 | bytes 65536 | tf_op jit(solution)/shard_map/row_pass/pallas_call | solution.py:54
  63.6 9.4 %all_to_all.31.refs_0_ = f32[16,8,128]{2,1,0:T(8,128)S(1)} all-to-all(f32[16,8,128]{2,1,0:T(8,128)S(1)} %row_pass.3), channel_id=1, replica_groups=mesh['patch'=8,'proto'=16] {'proto'}, dimensions={0} | all-to-all | bytes 131072 | tf_op jit(solution)/shard_map/all_to_all | solution.py:409
  73.0 1.2 col_pass.3
  74.2 2.9 %collective-permute-start.8 = (f32[8,1024]{1,0:T(8,128)S(1)}, f32[8,1024]{1,0:T(8,128)S(1)}, u32[]{:S(2)}, u32[]{:S(2)}) collective-permute-start(f32[8,1024]{1,0:T(8,128)S(1)} %col_pass.3), channel_id=1, source_target_pairs={{0,16},{16,0},{32,48},{48,32},{64,80},{80,64},{96,112},{112,96},{1... | collective-permute-start | bytes 98312 | tf_op jit(solution)/shard_map/ppermute | solution.py:412
  77.1 0.9 collective-permute-done.8
  78.0 1.4 %collective-permute-start.11 = (f32[8,1024]{1,0:T(8,128)S(1)}, f32[8,1024]{1,0:T(8,128)S(1)}, u32[]{:S(2)}, u32[]{:S(2)}) collective-permute-start(f32[8,1024]{1,0:T(8,128)S(1)} %add.17.refs_0_.refs_3_.refs_4_), channel_id=1, source_target_pairs={{0,96},{16,112},{32,64},{48,80},{64,32},{80,48},{96,0},{112,16},{1... | collective-permute-start | bytes 98312 | tf_op jit(solution)/shard_map/ppermute | solution.py:412
  79.3 1.1 collective-permute-start.10
  80.5 0.7 collective-permute-start.9
  81.2 1.9 %student_table.5 = (bf16[512,2048]{1,0:T(8,128)(2,1)S(1)}, f32[8,512]{1,0:T(8,128)S(1)}, f32[256,512]{1,0:T(8,128)S(1)}, bf16[256,512]{1,0:T(8,128)(2,1)S(1)}) custom-call(f32[8,1024]{1,0:T(8,128)S(1)} %add.17.refs_0_.refs_3_.refs_4_, bf16[16,64,256]{2,1,0:T(8,128)(2,1)S(1)} %all-to-all-done.refs_0_.refs_1_, ...), custom_call_target="tpu_custom_call" | custom-call | flops 2147483648 | bytes 65536 | tf_op jit(solution)/shard_map/student_table/pallas_call | solution.py:54
  83.1 0.0 collective-permute-done.11.refs_3_.refs_6_.refs_7_
  83.1 0.5 collective-permute-done.10.refs_2_.refs_5_.refs_6_
  83.6 0.0 collective-permute-done.9.refs_1_.refs_4_.refs_5_
  83.6 2.5 %last_row_pass.1 = (f32[16,8,128]{2,1,0:T(8,128)S(1)}, f32[256,512]{1,0:T(8,128)S(1)}) custom-call(f32[8,1024]{1,0:T(8,128)S(1)} %add.17.refs_0_.refs_3_.refs_4_, f32[8,1024]{1,0:T(8,128)S(1)} %collective-permute-done.9.refs_1_.refs_4_.refs_5_, f32[8,1024]{1,0:T(8,128)S(1)} %collective-permute-done.10.refs_2_.refs_5_.refs_6_, ...), custom_call_target="tpu_custom_call" | custom-call | flops 2147483648 | bytes 65536 | tf_op jit(solution)/shard_map/last_row_pass/pallas_call | solution.py:54
  86.2 9.4 %all_to_all.32.refs_2_ = f32[16,8,128]{2,1,0:T(8,128)S(1)} all-to-all(f32[16,8,128]{2,1,0:T(8,128)S(1)} %get-tuple-element.51), channel_id=1, replica_groups=mesh['patch'=8,'proto'=16] {'proto'}, dimensions={0} | all-to-all | bytes 131072 | tf_op jit(solution)/shard_map/all_to_all | solution.py:409
  95.5 0.7 row_factors.1
  96.2 0.0 copy-done
  96.2 5.5 %head.2 = (f32[32,6144]{1,0:T(8,128)S(1)}, bf16[3,32,6144]{2,1,0:T(8,128)(2,1)S(1)}, bf16[4,32,6144]{2,1,0:T(8,128)(2,1)S(1)}) custom-call(s32[3]{0:T(128)S(1)} %pad_add_fusion.refs_0_.refs_1_, bf16[256,512]{1,0:T(8,128)(2,1)S(1)} %get-tuple-element.53.refs_1_.refs_2_, bf16[256,512]{1,0:T(8,128)(2,1)S(1)} %get-tuple-element.54.refs_2_.refs_3_, ...), custom_call_target="tpu_custom_call" | custom-call | flops 4294967296 | bytes 65536 | tf_op jit(solution)/shard_map/head/pallas_call | solution.py:54
  101.7 3.3 %collective-permute-start.12 = (bf16[4,32,6144]{2,1,0:T(8,128)(2,1)S(1)}, bf16[4,32,6144]{2,1,0:T(8,128)(2,1)S(1)}, u32[]{:S(2)}, u32[]{:S(2)}) collective-permute-start(bf16[4,32,6144]{2,1,0:T(8,128)(2,1)S(1)} %get-tuple-element.69), channel_id=1, source_target_pairs={{0,16},{16,0},{32,48},{48,32},{64,80},{80,64},{96,112},{112,96},{1... | collective-permute-start | bytes 4718600 | tf_op jit(solution)/shard_map/ppermute | solution.py:412
  105.0 2.2 %head.3 = (f32[32,2048]{1,0:T(8,128)S(1)}, bf16[3,32,2048]{2,1,0:T(8,128)(2,1)S(1)}, bf16[4,32,2048]{2,1,0:T(8,128)(2,1)S(1)}) custom-call(bf16[3,32,6144]{2,1,0:T(8,128)(2,1)S(1)} %get-tuple-element.59.refs_0_.refs_1_, s32[3]{0:T(128)S(1)} %pad_add_fusion.refs_0_.refs_1_, bf16[256,512]{1,0:T(8,128)(2,1)S(1)} %get-tuple-element.53.refs_1_.refs_2_, ...), custom_call_target="tpu_custom_call" | custom-call | flops 4294967296 | bytes 65536 | tf_op jit(solution)/shard_map/head/pallas_call | solution.py:54
  107.2 0.1 collective-permute-start.13
  107.3 0.4 feature.1.refs_0_
  107.6 1.5 %collective-permute-done.13.refs_4_ = bf16[4,32,2048]{2,1,0:T(8,128)(2,1)S(1)} collective-permute-done((bf16[4,32,2048]{2,1,0:T(8,128)(2,1)S(1)}, bf16[4,32,2048]{2,1,0:T(8,128)(2,1)S(1)}, u32[]{:S(2)}, u32[]{:S(2)}) %collective-permute-start.13) | collective-permute-done | bytes 524320 | tf_op jit(solution)/shard_map/ppermute | solution.py:412
  109.2 0.0 collective-permute-done.12.refs_2_
  109.2 0.4 pair_sums.1
  109.6 1.8 %collective-permute-start.14 = (bf16[32,8192]{1,0:T(8,128)(2,1)S(1)}, bf16[32,8192]{1,0:T(8,128)(2,1)S(1)}, u32[]{:S(2)}, u32[]{:S(2)}) collective-permute-start(bf16[32,8192]{1,0:T(8,128)(2,1)S(1)} %get-tuple-element.74), channel_id=1, source_target_pairs={{0,64},{16,80},{32,96},{48,112},{64,0},{80,16},{96,32},{112,48},{1... | collective-permute-start | bytes 1572872 | tf_op jit(solution)/shard_map/ppermute | solution.py:412
  111.4 0.1 collective-permute-start.15
  111.5 1.4 %collective-permute-start.16 = (bf16[32,8192]{1,0:T(8,128)(2,1)S(1)}, bf16[32,8192]{1,0:T(8,128)(2,1)S(1)}, u32[]{:S(2)}, u32[]{:S(2)}) collective-permute-start(bf16[32,8192]{1,0:T(8,128)(2,1)S(1)} %get-tuple-element.76), channel_id=1, source_target_pairs={{0,96},{16,112},{32,64},{48,80},{64,32},{80,48},{96,0},{112,16},{1... | collective-permute-start | bytes 1572872 | tf_op jit(solution)/shard_map/ppermute | solution.py:412
  112.9 11.7 %all_to_all.33.refs_0_ = bf16[16,48,256]{2,1,0:T(8,128)(2,1)S(1)} all-to-all(bf16[16,48,256]{2,1,0:T(8,128)(2,1)S(1)} %feature.1.refs_0_), channel_id=1, replica_groups=mesh['patch'=8,'proto'=16] {'proto'}, dimensions={0} | all-to-all | bytes 786432 | tf_op jit(solution)/shard_map/all_to_all | solution.py:409
  124.6 0.8 owner.1
  125.4 0.1 own_sum.1
  125.5 11.1 %all_to_all.34.refs_1_ = f32[8,8,128]{2,1,0:T(8,128)S(1)} all-to-all(f32[8,8,128]{2,1,0:T(8,128)S(1)} %get-tuple-element.73), channel_id=1, replica_groups=mesh['patch'=8,'proto'=16] {'patch'}, dimensions={0} | all-to-all | bytes 65536 | tf_op jit(solution)/shard_map/all_to_all | solution.py:409
  136.6 0.0 collective-permute-done.14.refs_2_
  136.6 0.0 collective-permute-done.15.refs_3_
  136.6 0.0 collective-permute-done.16.refs_4_
  136.6 1.3 assemble.1
  (6 shorter events, 0.0 us)
Async XLA Ops:
  3.4 19.1 %all-to-all-start = ((bf16[16,64,256]{2,1,0:T(8,128)(2,1)}), bf16[16,64,256]{2,1,0:T(8,128)(2,1)S(1)}, u32[]{:S(2)}, u32[]{:S(2)}) async-start(bf16[16,64,256]{2,1,0:T(8,128)(2,1)} %get-tuple-element.41), calls=%async_computation | async-start | bytes 1048576 | tf_op jit(solution)/shard_map/all_to_all | solution.py:409
  16.8 1.4 copy-start.1
  22.5 1.6 %copy-start.2 = (bf16[4,256,1024]{2,1,0:T(8,128)(2,1)S(1)}, bf16[4,256,1024]{2,1,0:T(8,128)(2,1)}, u32[]{:S(2)}) copy-start(bf16[4,256,1024]{2,1,0:T(8,128)(2,1)} %copy-done.1) | copy-start | bytes 6291460
  28.8 2.9 %collective-permute-start = (f32[8,1024]{1,0:T(8,128)S(1)}, f32[8,1024]{1,0:T(8,128)S(1)}, u32[]{:S(2)}, u32[]{:S(2)}) collective-permute-start(f32[8,1024]{1,0:T(8,128)S(1)} %get-tuple-element.44), channel_id=1, source_target_pairs={{0,16},{16,0},{32,48},{48,32},{64,80},{80,64},{96,112},{112,96},{1... | collective-permute-start | bytes 98312 | tf_op jit(solution)/shard_map/ppermute | solution.py:412
  31.7 5.9 %collective-permute-start.3 = (f32[8,1024]{1,0:T(8,128)S(1)}, f32[8,1024]{1,0:T(8,128)S(1)}, u32[]{:S(2)}, u32[]{:S(2)}) collective-permute-start(f32[8,1024]{1,0:T(8,128)S(1)} %add.15.refs_0_.refs_1_), channel_id=1, source_target_pairs={{0,96},{16,112},{32,64},{48,80},{64,32},{80,48},{96,0},{112,16},{1... | collective-permute-start | bytes 98312 | tf_op jit(solution)/shard_map/ppermute | solution.py:412
  34.2 4.3 %collective-permute-start.2 = (f32[8,1024]{1,0:T(8,128)S(1)}, f32[8,1024]{1,0:T(8,128)S(1)}, u32[]{:S(2)}, u32[]{:S(2)}) collective-permute-start(f32[8,1024]{1,0:T(8,128)S(1)} %add.15.refs_0_.refs_1_), channel_id=1, source_target_pairs={{0,64},{16,80},{32,96},{48,112},{64,0},{80,16},{96,32},{112,48},{1... | collective-permute-start | bytes 98312 | tf_op jit(solution)/shard_map/ppermute | solution.py:412
  34.7 3.8 %collective-permute-start.1 = (f32[8,1024]{1,0:T(8,128)S(1)}, f32[8,1024]{1,0:T(8,128)S(1)}, u32[]{:S(2)}, u32[]{:S(2)}) collective-permute-start(f32[8,1024]{1,0:T(8,128)S(1)} %add.15.refs_0_.refs_1_), channel_id=1, source_target_pairs={{0,32},{16,48},{32,0},{48,16},{64,96},{80,112},{96,64},{112,80},{1... | collective-permute-start | bytes 98312 | tf_op jit(solution)/shard_map/ppermute | solution.py:412
  51.2 4.1 %collective-permute-start.4 = (f32[8,1024]{1,0:T(8,128)S(1)}, f32[8,1024]{1,0:T(8,128)S(1)}, u32[]{:S(2)}, u32[]{:S(2)}) collective-permute-start(f32[8,1024]{1,0:T(8,128)S(1)} %col_pass.2), channel_id=1, source_target_pairs={{0,16},{16,0},{32,48},{48,32},{64,80},{80,64},{96,112},{112,96},{1... | collective-permute-start | bytes 98312 | tf_op jit(solution)/shard_map/ppermute | solution.py:412
  55.3 5.9 %collective-permute-start.7 = (f32[8,1024]{1,0:T(8,128)S(1)}, f32[8,1024]{1,0:T(8,128)S(1)}, u32[]{:S(2)}, u32[]{:S(2)}) collective-permute-start(f32[8,1024]{1,0:T(8,128)S(1)} %add.16.refs_0_.refs_1_), channel_id=1, source_target_pairs={{0,96},{16,112},{32,64},{48,80},{64,32},{80,48},{96,0},{112,16},{1... | collective-permute-start | bytes 98312 | tf_op jit(solution)/shard_map/ppermute | solution.py:412
  56.4 4.8 %collective-permute-start.6 = (f32[8,1024]{1,0:T(8,128)S(1)}, f32[8,1024]{1,0:T(8,128)S(1)}, u32[]{:S(2)}, u32[]{:S(2)}) collective-permute-start(f32[8,1024]{1,0:T(8,128)S(1)} %add.16.refs_0_.refs_1_), channel_id=1, source_target_pairs={{0,64},{16,80},{32,96},{48,112},{64,0},{80,16},{96,32},{112,48},{1... | collective-permute-start | bytes 98312 | tf_op jit(solution)/shard_map/ppermute | solution.py:412
  57.3 4.0 %collective-permute-start.5 = (f32[8,1024]{1,0:T(8,128)S(1)}, f32[8,1024]{1,0:T(8,128)S(1)}, u32[]{:S(2)}, u32[]{:S(2)}) collective-permute-start(f32[8,1024]{1,0:T(8,128)S(1)} %add.16.refs_0_.refs_1_), channel_id=1, source_target_pairs={{0,32},{16,48},{32,0},{48,16},{64,96},{80,112},{96,64},{112,80},{1... | collective-permute-start | bytes 98312 | tf_op jit(solution)/shard_map/ppermute | solution.py:412
  74.2 3.7 %collective-permute-start.8 = (f32[8,1024]{1,0:T(8,128)S(1)}, f32[8,1024]{1,0:T(8,128)S(1)}, u32[]{:S(2)}, u32[]{:S(2)}) collective-permute-start(f32[8,1024]{1,0:T(8,128)S(1)} %col_pass.3), channel_id=1, source_target_pairs={{0,16},{16,0},{32,48},{48,32},{64,80},{80,64},{96,112},{112,96},{1... | collective-permute-start | bytes 98312 | tf_op jit(solution)/shard_map/ppermute | solution.py:412
  78.0 5.2 %collective-permute-start.11 = (f32[8,1024]{1,0:T(8,128)S(1)}, f32[8,1024]{1,0:T(8,128)S(1)}, u32[]{:S(2)}, u32[]{:S(2)}) collective-permute-start(f32[8,1024]{1,0:T(8,128)S(1)} %add.17.refs_0_.refs_3_.refs_4_), channel_id=1, source_target_pairs={{0,96},{16,112},{32,64},{48,80},{64,32},{80,48},{96,0},{112,16},{1... | collective-permute-start | bytes 98312 | tf_op jit(solution)/shard_map/ppermute | solution.py:412
  79.3 4.3 %collective-permute-start.10 = (f32[8,1024]{1,0:T(8,128)S(1)}, f32[8,1024]{1,0:T(8,128)S(1)}, u32[]{:S(2)}, u32[]{:S(2)}) collective-permute-start(f32[8,1024]{1,0:T(8,128)S(1)} %add.17.refs_0_.refs_3_.refs_4_), channel_id=1, source_target_pairs={{0,64},{16,80},{32,96},{48,112},{64,0},{80,16},{96,32},{112,48},{1... | collective-permute-start | bytes 98312 | tf_op jit(solution)/shard_map/ppermute | solution.py:412
  80.5 3.1 %collective-permute-start.9 = (f32[8,1024]{1,0:T(8,128)S(1)}, f32[8,1024]{1,0:T(8,128)S(1)}, u32[]{:S(2)}, u32[]{:S(2)}) collective-permute-start(f32[8,1024]{1,0:T(8,128)S(1)} %add.17.refs_0_.refs_3_.refs_4_), channel_id=1, source_target_pairs={{0,32},{16,48},{32,0},{48,16},{64,96},{80,112},{96,64},{112,80},{1... | collective-permute-start | bytes 98312 | tf_op jit(solution)/shard_map/ppermute | solution.py:412
  83.6 12.6 %copy-start = (bf16[256,8192]{1,0:T(8,128)(2,1)S(1)}, bf16[256,8192]{1,0:T(8,128)(2,1)}, u32[]{:S(2)}) copy-start(bf16[256,8192]{1,0:T(8,128)(2,1)} %refs_13_.1) | copy-start | bytes 12582916
  101.7 7.5 %collective-permute-start.12 = (bf16[4,32,6144]{2,1,0:T(8,128)(2,1)S(1)}, bf16[4,32,6144]{2,1,0:T(8,128)(2,1)S(1)}, u32[]{:S(2)}, u32[]{:S(2)}) collective-permute-start(bf16[4,32,6144]{2,1,0:T(8,128)(2,1)S(1)} %get-tuple-element.69), channel_id=1, source_target_pairs={{0,16},{16,0},{32,48},{48,32},{64,80},{80,64},{96,112},{112,96},{1... | collective-permute-start | bytes 4718600 | tf_op jit(solution)/shard_map/ppermute | solution.py:412
  107.2 2.0 %collective-permute-start.13 = (bf16[4,32,2048]{2,1,0:T(8,128)(2,1)S(1)}, bf16[4,32,2048]{2,1,0:T(8,128)(2,1)S(1)}, u32[]{:S(2)}, u32[]{:S(2)}) collective-permute-start(bf16[4,32,2048]{2,1,0:T(8,128)(2,1)S(1)} %get-tuple-element.71), channel_id=1, source_target_pairs={{0,16},{16,0},{32,48},{48,32},{64,80},{80,64},{96,112},{112,96},{1... | collective-permute-start | bytes 1572872 | tf_op jit(solution)/shard_map/ppermute | solution.py:412
  109.6 27.0 %collective-permute-start.14 = (bf16[32,8192]{1,0:T(8,128)(2,1)S(1)}, bf16[32,8192]{1,0:T(8,128)(2,1)S(1)}, u32[]{:S(2)}, u32[]{:S(2)}) collective-permute-start(bf16[32,8192]{1,0:T(8,128)(2,1)S(1)} %get-tuple-element.74), channel_id=1, source_target_pairs={{0,64},{16,80},{32,96},{48,112},{64,0},{80,16},{96,32},{112,48},{1... | collective-permute-start | bytes 1572872 | tf_op jit(solution)/shard_map/ppermute | solution.py:412
  111.4 25.2 %collective-permute-start.15 = (bf16[32,8192]{1,0:T(8,128)(2,1)S(1)}, bf16[32,8192]{1,0:T(8,128)(2,1)S(1)}, u32[]{:S(2)}, u32[]{:S(2)}) collective-permute-start(bf16[32,8192]{1,0:T(8,128)(2,1)S(1)} %get-tuple-element.75), channel_id=1, source_target_pairs={{0,32},{16,48},{32,0},{48,16},{64,96},{80,112},{96,64},{112,80},{1... | collective-permute-start | bytes 1572872 | tf_op jit(solution)/shard_map/ppermute | solution.py:412
  111.5 25.0 %collective-permute-start.16 = (bf16[32,8192]{1,0:T(8,128)(2,1)S(1)}, bf16[32,8192]{1,0:T(8,128)(2,1)S(1)}, u32[]{:S(2)}, u32[]{:S(2)}) collective-permute-start(bf16[32,8192]{1,0:T(8,128)(2,1)S(1)} %get-tuple-element.76), channel_id=1, source_target_pairs={{0,96},{16,112},{32,64},{48,80},{64,32},{80,48},{96,0},{112,16},{1... | collective-permute-start | bytes 1572872 | tf_op jit(solution)/shard_map/ppermute | solution.py:412
